TPU v7x, 32 devices: a whole 2x2x4 slice. The times are simulated.
32 devices in a mesh: row: 8 (over y, x, core), col: 4 (over z).
Axes of the slice: x: 2, y: 2, z: 4, core: 2. Of those that a mesh axis runs over, the one named last changes fastest.
Arguments:
- tokens: bfloat16 [1024, 2048], P('row', 'col'), may hold values from -6 to 6
- segment_ids: int32 [1024], replicated, may hold values from 0 to 15, never falling along the last dimension, each value on 1 to 128 neighbouring positions
- bucket_table: int32 [255], replicated, may hold values from 0 to 31
- slot_index: int32 [8, 1], P('row'), may hold values from 0 to 0, each once within a row
- gain_attn: float32 [2048], replicated, may hold values from 0.1 to 1.9
- w_qkv: bfloat16 [3, 2048, 2048], P(None, 'row', 'col'), may hold values from -0.09375 to 0.09375
- rel_bias: float32 [32, 32], P(None, 'col'), may hold values from -260 to 260
- w_out: bfloat16 [2048, 2048], P('col', 'row'), may hold values from -0.125 to 0.125
- gain_ffn: float32 [2048], replicated, may hold values from 0.1 to 1.9
- w_in: bfloat16 [2, 2048, 5120], P(None, 'row', 'col'), may hold values from -0.125 to 0.125
- w_down: bfloat16 [5120, 2048], P('col', 'row'), may hold values from -0.078125 to 0.078125
Outputs:
- output: bfloat16 [1024, 2048], P('row', 'col')
- kv_cache: bfloat16 [2, 1024, 2048], P(None, 'row', 'col')
Inputs may be any that keep to these rules, and one draw needn't show every extreme that they name: `segment_ids`: segment numbers never fall along the tokens; each prompt spans 1 to 128 tokens and one spans exactly 128. `slot_index`: each row names each of 0 to 0 once.
All inputs are finite; a program needn't handle non-finite values.
Results may differ from a plain program's by a relative error of at most 0.009.
Values may be sent and summed in bfloat16 or wider, within the bound.
No kernel may reach another device: no remote copies, remote signals or barrier semaphores. Data moves between devices by JAX's collectives and lax.ppermute only.
A program may use at most 128 MiB of HBM per device.

v0:
```python
import jax
import jax.numpy as jnp
from jax import lax
from jax.sharding import PartitionSpec as P

BLOCK = 128


epsilon = 1e-06
masked_score = -1e30


def extended(block, sides, width):
    for axis, dim in sides:
        count = lax.axis_size(axis)
        forward = [(i, i + 1) for i in range(count - 1)]
        backward = [(target, source) for source, target in forward]
        low = lax.ppermute(
            lax.slice_in_dim(block, block.shape[dim] - width, None, axis=dim), axis, forward
        )
        high = lax.ppermute(lax.slice_in_dim(block, 0, width, axis=dim), axis, backward)
        block = jnp.concatenate([low, block, high], axis=dim)
    return block


def normed_features(shard_part, gain_vector):
    gathered = lax.all_gather(shard_part, "col", axis=1, tiled=True)
    widened = gathered.astype(jnp.float32)
    factor = lax.rsqrt(jnp.mean(widened * widened, axis=1, keepdims=True) + epsilon)
    return (widened * factor * gain_vector).astype(jnp.bfloat16)


def project_rows(normed, stacked):
    return jnp.einsum(
        "td,kdc->ktc",
        normed,
        lax.all_gather(stacked, "row", axis=1, tiled=True),
        preferred_element_type=jnp.float32,
    )


def project_columns(hidden, weight):
    partial_terms = jnp.dot(
        hidden,
        lax.all_gather(weight, "row", axis=1, tiled=True),
        preferred_element_type=jnp.float32,
    )
    return lax.psum_scatter(partial_terms, "col", scatter_dimension=1, tiled=True)


def attend_tile(
    running, key_rows, value_rows, key_start, queries, query_pos, query_seg, segment_ids, bias_rows
):
    running_max, denominator, accumulated = running
    head_count, row_count, head_width = accumulated.shape
    key_count = key_rows.shape[0]
    token_total = segment_ids.shape[0]
    max_reach = (bias_rows.shape[1] + 1) // 2
    key_pos = key_start + jnp.arange(key_count, dtype=jnp.int32)
    inside = (key_pos >= 0) & (key_pos < token_total)
    key_seg = jnp.take(segment_ids, jnp.clip(key_pos, 0, token_total - 1))
    allowed = (query_seg[:, None] == key_seg[None, :]) & inside[None, :]
    offset = jnp.clip(key_pos[None, :] - query_pos[:, None] + max_reach - 1, 0, 2 * max_reach - 2)
    rel_terms = jnp.take(bias_rows, offset, axis=1)
    key_heads = key_rows.reshape(key_count, head_count, head_width)
    value_heads = value_rows.reshape(key_count, head_count, head_width)
    scores = (
        jnp.einsum("qhd,khd->hqk", queries, key_heads, preferred_element_type=jnp.float32)
        + rel_terms
    )
    scores = jnp.where(allowed[None], scores, masked_score)
    new_max = jnp.maximum(running_max, jnp.max(scores, axis=2))
    weights = jnp.where(allowed[None], jnp.exp(scores - new_max[:, :, None]), 0.0)
    denominator = jnp.sum(weights, axis=2)
    accumulated = jnp.einsum(
        "hqk,khd->hqd",
        weights.astype(jnp.bfloat16),
        value_heads,
        preferred_element_type=jnp.float32,
    )
    return (new_max, denominator, accumulated)


def per_device(
    tokens,
    segment_ids,
    bucket_table,
    slot_index,
    gain_attn,
    w_qkv,
    rel_bias,
    w_out,
    gain_ffn,
    w_in,
    w_down,
):
    row_count = tokens.shape[0]
    head_count = rel_bias.shape[1]
    normed = normed_features(tokens, gain_attn)
    projected = project_rows(normed, w_qkv).astype(jnp.bfloat16)
    queries = projected[0].reshape(row_count, head_count, -1)
    head_width = queries.shape[2]
    onehot = (
        bucket_table[:, None] == jnp.arange(rel_bias.shape[0], dtype=jnp.int32)[None, :]
    ).astype(jnp.float32)
    bias_rows = jnp.dot(onehot, rel_bias, precision=lax.Precision.HIGHEST).T
    first_row = lax.axis_index("row") * row_count
    query_pos = first_row + jnp.arange(row_count, dtype=jnp.int32)
    query_seg = lax.dynamic_slice_in_dim(segment_ids, first_row, row_count, 0)
    initial = (
        jnp.full((head_count, row_count), masked_score, jnp.float32),
        jnp.zeros((head_count, row_count), jnp.float32),
        jnp.zeros((head_count, row_count, head_width), jnp.float32),
    )
    padded = extended(projected[1:], (("row", 1),), row_count)
    running_max, denominator, accumulated = attend_tile(
        initial,
        padded[0],
        padded[1],
        first_row - row_count,
        queries,
        query_pos,
        query_seg,
        segment_ids,
        bias_rows,
    )
    context = (
        (accumulated / denominator[:, :, None])
        .transpose(1, 0, 2)
        .reshape(row_count, head_count * head_width)
        .astype(jnp.bfloat16)
    )
    attended = project_columns(context, w_out)
    residual_mid = (tokens.astype(jnp.float32) + attended).astype(jnp.bfloat16)
    normed_two = normed_features(residual_mid, gain_ffn)
    branches = project_rows(normed_two, w_in)
    hidden = (jax.nn.gelu(branches[0], approximate=True) * branches[1]).astype(jnp.bfloat16)
    output = (residual_mid.astype(jnp.float32) + project_columns(hidden, w_down)).astype(
        jnp.bfloat16
    )
    blocks = projected[1:].reshape(2, slot_index.shape[1], BLOCK, head_count * head_width)
    kv_cache = (
        jnp.zeros_like(blocks)
        .at[:, slot_index[0]]
        .set(blocks)
        .reshape(2, row_count, head_count * head_width)
    )
    return (output, kv_cache)


def solution(mesh):
    return jax.shard_map(
        per_device,
        mesh=mesh,
        in_specs=(
            P("row", "col"),
            P(),
            P(),
            P("row", None),
            P(),
            P(None, "row", "col"),
            P(None, "col"),
            P("col", "row"),
            P(),
            P(None, "row", "col"),
            P("col", "row"),
        ),
        out_specs=(P("row", "col"), P(None, "row", "col")),
        check_vma=False,
    )
```

profile of v0, /device:TPU:0, one launch (start us, length us, event | category | flops | bytes accessed | tf_op | source)
XLA Modules:
  0.0 428.6 jit_solution(3528855047510819238)
XLA Ops:
  7.2 0.0 copy-start
  7.2 0.0 copy-start.1
  7.2 0.0 copy-start.2
  7.2 0.0 all-gather.5.cloned.1.call-start
  7.2 0.7 all-gather.5.cloned.1.call-update
  7.9 0.0 all-gather.7.cloned.1.call-start
  8.0 0.7 all-gather.7.cloned.1.call-update
  8.7 0.0 reduce-scatter.3.cloned.1.call-start
  8.8 0.0 copy-done.1
  8.8 0.0 copy-start.5
  8.8 1.9 gather_fusion
  10.7 0.0 copy-start.4
  10.7 0.1 compare_select_fusion
  10.9 0.2 fusion.41
  11.7 0.7 and_reduce_fusion
  12.4 0.0 copy-done.2
  12.4 17.3 %all_gather.18 = bf16[128,2048]{1,0:T(8,128)(2,1)S(1)} all-gather(bf16[128,512]{1,0:T(8,128)(2,1)S(1)} %copy-done.2), channel_id=1, replica_groups=mesh['row'=8,'col'=4] {'col'}, dimensions={1}, use_global_device_ids=true | all-gather | bytes 655360 | tf_op jit(solution)/shard_map/all_gather | solution.py:27
  29.8 0.2 fusion.6
  30.0 0.0 copy-done
  30.0 0.0 copy-done.5
  30.0 0.2 convolution_bitcast_fusion.2
  30.3 27.9 %all-gather.5.cloned.1.call-done = bf16[3,2048,512]{2,1,0:T(8,128)(2,1)} async-done(((bf16[3,256,512]{2,1,0:T(8,128)(2,1)}), bf16[3,2048,512]{2,1,0:T(8,128)(2,1)}) %all-gather.5.cloned.1.call-update) | async-done | bytes 6291472 | tf_op jit(solution)/shard_map/all_gather | solution.py:37
  58.2 0.0 copy-done.4
  58.2 3.8 fusion.3
  62.0 1.4 broadcast_select_fusion
  63.4 2.2 collective-permute-start
  65.6 1.3 collective-permute-start.1
  66.9 0.1 dynamic_slice.3
  67.0 0.1 copy.20
  67.1 163.1 %gather_fusion.1 = f32[49152,8]{1,0:T(8,128)} fusion(f32[8,255]{0,1:T(8,128)S(1)} %copy.20, s32[49152]{0:T(1024)S(1)} %broadcast_clamp_fusion), kind=kCustom, calls=%fused_computation.1 | custom fusion | bytes 3342336 | tf_op jit(solution)/shard_map/jit(_take)/gather | solution.py:64
  230.2 14.5 %copy.23 = f32[128,384,8]{1,0,2:T(8,128)S(1)} copy(f32[128,384,8]{2,1,0:T(8,128)} %bitcast.53) | data formatting | bytes 3145728 | tf_op jit(solution)/shard_map/jit(_take)/gather | solution.py:64
  244.7 0.1 compare_and_fusion
  244.8 0.1 copy.18
  244.9 0.0 collective-permute-done
  245.0 0.0 collective-permute-done.1
  245.0 0.1 pad_maximum_fusion
  245.0 0.1 fusion.52
  245.1 0.2 copy.19
  245.3 0.2 copy.22
  245.5 0.7 fusion.53
  246.3 0.6 fusion.1
  246.8 0.6 fusion.5
  247.4 0.0 all-gather.7.cloned.1.call-done
  247.4 3.0 fusion.54
  250.4 0.0 reduce-scatter.3.cloned.1.call-update
  250.5 0.0 copy-start.3
  250.5 0.0 all-gather.9.cloned.1.call-start
  250.5 0.5 all-gather.9.cloned.1.call-update
  251.1 0.0 all-gather.11.cloned.1.call-start
  251.1 0.5 all-gather.11.cloned.1.call-update
  251.6 0.0 reduce-scatter.5.cloned.1.call-start
  251.7 28.8 %reduce-scatter.3.cloned.1.call-done = f32[128,512]{1,0:T(8,128)} async-done(((f32[128,2048]{1,0:T(8,128)}), f32[128,512]{1,0:T(8,128)}) %reduce-scatter.3.cloned.1.call-update) | async-done | bytes 262160 | tf_op jit(solution)/shard_map/reduce_scatter | solution.py:48
  280.5 1.0 add_convert_fusion.1
  281.5 16.1 %all_gather.21 = bf16[128,2048]{1,0:T(8,128)(2,1)S(1)} all-gather(bf16[128,512]{1,0:T(8,128)(2,1)S(1)} %add_convert_fusion.1), channel_id=1, replica_groups=mesh['row'=8,'col'=4] {'col'}, dimensions={1}, use_global_device_ids=true | all-gather | bytes 655360 | tf_op jit(solution)/shard_map/all_gather | solution.py:27
  297.6 0.2 fusion.9
  297.7 46.6 %all-gather.9.cloned.1.call-done = bf16[2,2048,1280]{2,1,0:T(8,128)(2,1)} async-done(((bf16[2,256,1280]{2,1,0:T(8,128)(2,1)}), bf16[2,2048,1280]{2,1,0:T(8,128)(2,1)}) %all-gather.9.cloned.1.call-update) | async-done | bytes 10485776 | tf_op jit(solution)/shard_map/all_gather | solution.py:37
  344.4 0.0 copy-done.3
  344.4 5.6 %convolution_bitcast_fusion = f32[2,128,1280]{2,1,0:T(8,128)S(1)} fusion(bf16[2,2048,1280]{2,1,0:T(8,128)(2,1)} %all-gather.9.cloned.1.call-done, bf16[128,2048]{1,0:T(8,128)(2,1)S(1)} %all_gather.21, f32[2048]{0:T(1024)S(1)} %copy-done.3, f32[128]{0:T(128)S(1)} %add_rsqrt_fusion), kind=kOutput, calls=%fused_computation.2 | convolution fusion | flops 1343225856 | bytes 12329472 | tf_op jit(solution)/shard_map/td,kdc->ktc/dot_general | solution.py:34
  350.0 38.4 %all-gather.11.cloned.1.call-done = bf16[1280,2048]{1,0:T(8,128)(2,1)} async-done(((bf16[1280,256]{1,0:T(8,128)(2,1)}), bf16[1280,2048]{1,0:T(8,128)(2,1)}) %all-gather.11.cloned.1.call-update) | async-done | bytes 5242896 | tf_op jit(solution)/shard_map/all_gather | solution.py:45
  388.4 4.5 %fusion.33 = f32[128,2048]{1,0:T(8,128)} fusion(bf16[1280,2048]{1,0:T(8,128)(2,1)} %all-gather.11.cloned.1.call-done, f32[2,128,1280]{2,1,0:T(8,128)S(1)} %convolution_bitcast_fusion), kind=kOutput, calls=%fused_computation.48 | convolution fusion | flops 672727040 | bytes 7602176 | tf_op jit(solution)/shard_map/dot_general | solution.py:43
  392.8 0.0 reduce-scatter.5.cloned.1.call-update
  392.8 27.3 %reduce-scatter.5.cloned.1.call-done = f32[128,512]{1,0:T(8,128)} async-done(((f32[128,2048]{1,0:T(8,128)}), f32[128,512]{1,0:T(8,128)}) %reduce-scatter.5.cloned.1.call-update) | async-done | bytes 262160 | tf_op jit(solution)/shard_map/reduce_scatter | solution.py:48
  420.1 1.6 add_convert_fusion
  (11 shorter events, 0.1 us)
Async XLA Ops:
  7.2 22.8 %copy-start = (f32[32,8]{0,1:T(8,128)S(1)}, f32[32,8]{0,1:T(8,128)}, u32[]{:S(2)}) copy-start(f32[32,8]{0,1:T(8,128)} %param.19) | copy-start | bytes 3076
  7.2 1.6 copy-start.1
  7.2 5.2 %copy-start.2 = (bf16[128,512]{1,0:T(8,128)(2,1)S(1)}, bf16[128,512]{1,0:T(8,128)(2,1)}, u32[]{:S(2)}) copy-start(bf16[128,512]{1,0:T(8,128)(2,1)} %param.13) | copy-start | bytes 393220
  7.2 51.0 %all-gather.5.cloned.1.call-start = ((), (), s32[]{:S(2)}) async-start(), calls=%async_computation.2 | async-start | bytes 7077888 | tf_op jit(solution)/shard_map/all_gather | solution.py:37
  7.9 239.5 %all-gather.7.cloned.1.call-start = ((), (), s32[]{:S(2)}) async-start(), calls=%async_computation.3 | async-start | bytes 2359296 | tf_op jit(solution)/shard_map/all_gather | solution.py:45
  8.7 271.8 %reduce-scatter.3.cloned.1.call-start = ((), (), s32[]{:S(2)}) async-start(), calls=%async_computation.4 | async-start | bytes 1310720 | tf_op jit(solution)/shard_map/reduce_scatter | solution.py:48
  8.8 21.2 %copy-start.5 = (s32[255]{0:T(256)S(1)}, s32[255]{0:T(256)}, u32[]{:S(2)}) copy-start(s32[255]{0:T(256)} %param.15) | copy-start | bytes 3064
  10.7 47.5 %copy-start.4 = (f32[2048]{0:T(1024)S(1)}, f32[2048]{0:T(1024)}, u32[]{:S(2)}) copy-start(f32[2048]{0:T(1024)} %param.17) | copy-start | bytes 24580
  63.4 181.6 %collective-permute-start = (bf16[2,128,512]{2,1,0:T(8,128)(2,1)S(1)}, bf16[2,128,512]{2,1,0:T(8,128)(2,1)S(1)}, u32[]{:S(2)}, u32[]{:S(2)}) collective-permute-start(bf16[2,128,512]{2,1,0:T(8,128)(2,1)S(1)} %get-tuple-element.17), channel_id=1, source_target_pairs={{0,4},{4,8},{8,12},{12,16},{16,20},{20,24},{24,28},{1,5},{5,9},{9,... | collective-permute-start | bytes 786440 | tf_op jit(solution)/shard_map/ppermute | solution.py:18
  65.6 179.4 %collective-permute-start.1 = (bf16[2,128,512]{2,1,0:T(8,128)(2,1)S(1)}, bf16[2,128,512]{2,1,0:T(8,128)(2,1)S(1)}, u32[]{:S(2)}, u32[]{:S(2)}) collective-permute-start(bf16[2,128,512]{2,1,0:T(8,128)(2,1)S(1)} %get-tuple-element.17), channel_id=1, source_target_pairs={{4,0},{8,4},{12,8},{16,12},{20,16},{24,20},{28,24},{5,1},{9,5},{13... | collective-permute-start | bytes 786440 | tf_op jit(solution)/shard_map/ppermute | solution.py:21
  250.5 93.9 %copy-start.3 = (f32[2048]{0:T(1024)S(1)}, f32[2048]{0:T(1024)}, u32[]{:S(2)}) copy-start(f32[2048]{0:T(1024)} %param.21) | copy-start | bytes 24580
  250.5 93.9 %all-gather.9.cloned.1.call-start = ((), (), s32[]{:S(2)}) async-start(), calls=%async_computation.5 | async-start | bytes 11796480 | tf_op jit(solution)/shard_map/all_gather | solution.py:37
  251.1 137.3 %all-gather.11.cloned.1.call-start = ((), (), s32[]{:S(2)}) async-start(), calls=%async_computation.6 | async-start | bytes 5898240 | tf_op jit(solution)/shard_map/all_gather | solution.py:45
  251.6 168.5 %reduce-scatter.5.cloned.1.call-start = ((), (), s32[]{:S(2)}) async-start(), calls=%async_computation.7 | async-start | bytes 1310720 | tf_op jit(solution)/shard_map/reduce_scatter | solution.py:48
Sparse Core Ops, SparseCore 0:
  9.9 48.2 all-gather.4
  60.1 29.5 all-gather.6
  250.6 29.8 reduce-scatter.2
  282.4 61.9 all-gather.8
  346.3 42.0 all-gather.10
  393.0 27.1 reduce-scatter.4
where the time goes:
time: 429 us
  local copies, waits for them, and re-layouts  180 us (42%)
  waiting for transfers between devices  172 us (40%)
  blocking collectives  33.4 us (8%)
  matrix products  18.4 us (4%)
  between operations  15.1 us (4%)
  other arithmetic  6.21 us (1%)
    gather x2, local copies, waits for them, and re-layouts, attend_tile(): rel_terms = jnp.take(bias_rows, offset, axis=1)  178 us
    all_gather x2, waiting for transfers between devices, project_rows(): lax.all_gather(stacked, 'row', axis=1, tiled=True)  74.6 us
    reduce_scatter x2, waiting for transfers between devices, project_columns(): lax.psum_scatter(partial_terms, 'col', scatter_dimension=1, tiled=True)  56.1 us
    all_gather x2, waiting for transfers between devices, project_columns(): lax.all_gather(weight, 'row', axis=1, tiled=True)  38.4 us
    all_gather x2, blocking collectives, normed_features(): gathered = lax.all_gather(shard_part, 'col', axis=1, tiled=True)  33.4 us
    dot_general x2, matrix products, project_rows(): jnp.einsum('td,kdc->ktc', normed, lax.all_gather(stacked, 'row', axis=1,...  9.36 us
  transfers between devices with their start and end apart: 8, of which 5 were waited for; matrix products, arithmetic and copies ran while one was open for 46% of the time, Pallas kernels for 0%

commit v1 on v0

v1 whole, which is shorter than its diff:
```python
import functools

import jax
import jax.numpy as jnp
from jax import lax
from jax.experimental import pallas as pl
from jax.experimental.pallas import tpu as pltpu
from jax.sharding import PartitionSpec as P

BLOCK = 128


epsilon = 1e-06
masked_score = -1e30
VMEM = pl.BlockSpec(memory_space=pltpu.VMEM)
SMEM = pl.BlockSpec(memory_space=pltpu.SMEM)


def bias_kernel(row_ref, seg_ref, table_ref, rel_ref, out_ref):
    heads, count, width = out_ref.shape
    rows = seg_ref.shape[0]
    row = row_ref[0]
    table = table_ref[...]
    rel = rel_ref[...]
    by_distance = jnp.zeros((heads, table.shape[1]), jnp.float32)
    for bucket in range(rel.shape[1]):
        by_distance = jnp.where(table == bucket, rel[:, bucket : bucket + 1], by_distance)
    by_distance = jnp.concatenate(
        [by_distance, jnp.zeros((heads, width - table.shape[1]), jnp.float32)], axis=1
    )

    def segment_row(index):
        clipped = jnp.clip(index, 0, rows - 1)
        found = seg_ref[pl.ds(clipped, 1), :].astype(jnp.float32)
        return jnp.where(index == clipped, found, -1.0)

    own = segment_row(row)
    query_seg = jnp.broadcast_to(own, (count, count)).T
    allowed = jnp.concatenate(
        [query_seg == segment_row(row - 1), query_seg == own, query_seg == segment_row(row + 1)],
        axis=1,
    )
    for head in range(heads):
        line = jnp.broadcast_to(by_distance[head : head + 1, :], (count, width))
        shifted = pltpu.roll(line, 1, 1, stride=1, stride_axis=0)
        out_ref[head] = jnp.where(allowed, shifted, masked_score)


def masked_bias(row, segment_ids, bucket_table, rel_bias, count):
    heads = rel_bias.shape[1]
    table = jnp.pad(bucket_table, (0, 1)).reshape(1, 2 * count)
    return pl.pallas_call(
        bias_kernel,
        out_shape=jax.ShapeDtypeStruct((heads, count, 3 * count), jnp.float32),
        in_specs=[SMEM, VMEM, VMEM, VMEM],
        out_specs=VMEM,
        name="masked_bias",
    )(row.reshape(1), segment_ids.reshape(-1, count), table, rel_bias.T)


def attention_kernel(q_ref, low_ref, own_ref, high_ref, bias_ref, out_ref):
    heads, count, _ = bias_ref.shape
    width = q_ref.shape[1] // heads
    contract = (((1,), (1,)), ((), ()))
    for pair in range(0, heads, 2):
        parts = []
        for head in (pair, pair + 1):
            cut = slice(head * width, (head + 1) * width)
            query = q_ref[:, cut]
            scores = jnp.concatenate(
                [
                    lax.dot_general(
                        query, ref[0, :, cut], contract, preferred_element_type=jnp.float32
                    )
                    for ref in (low_ref, own_ref, high_ref)
                ],
                axis=1,
            )
            scores = scores + bias_ref[head]
            top = jnp.max(scores, axis=1, keepdims=True)
            weights = jnp.exp(scores - top)
            denominator = jnp.sum(weights, axis=1, keepdims=True)
            rounded = weights.astype(jnp.bfloat16)
            total = sum(
                jnp.dot(
                    rounded[:, i * count : (i + 1) * count],
                    ref[1, :, cut],
                    preferred_element_type=jnp.float32,
                )
                for i, ref in enumerate((low_ref, own_ref, high_ref))
            )
            parts.append(total / denominator)
        out_ref[:, pair * width : (pair + 2) * width] = jnp.concatenate(parts, axis=1).astype(
            out_ref.dtype
        )


def attention(queries, low, own, high, bias):
    heads, count, span = bias.shape
    return pl.pallas_call(
        attention_kernel,
        out_shape=jax.ShapeDtypeStruct(queries.shape, jnp.bfloat16),
        in_specs=[VMEM] * 5,
        out_specs=VMEM,
        cost_estimate=pl.CostEstimate(
            flops=4 * queries.size * span, bytes_accessed=4 * bias.size, transcendentals=bias.size
        ),
        name="attention",
    )(queries, low, own, high, bias)


def normed_features(shard_part, gain_vector):
    gathered = lax.all_gather(shard_part, "col", axis=1, tiled=True)
    widened = gathered.astype(jnp.float32)
    factor = lax.rsqrt(jnp.mean(widened * widened, axis=1, keepdims=True) + epsilon)
    return (widened * factor * gain_vector).astype(jnp.bfloat16)


def project_rows(normed, stacked):
    return jnp.einsum(
        "td,kdc->ktc",
        normed,
        lax.all_gather(stacked, "row", axis=1, tiled=True),
        preferred_element_type=jnp.float32,
    )


def project_columns(hidden, weight):
    partial_terms = jnp.dot(
        hidden,
        lax.all_gather(weight, "row", axis=1, tiled=True),
        preferred_element_type=jnp.float32,
    )
    return lax.psum_scatter(partial_terms, "col", scatter_dimension=1, tiled=True)


def per_device(
    tokens,
    segment_ids,
    bucket_table,
    slot_index,
    gain_attn,
    w_qkv,
    rel_bias,
    w_out,
    gain_ffn,
    w_in,
    w_down,
):
    row_count = tokens.shape[0]
    normed = normed_features(tokens, gain_attn)
    projected = project_rows(normed, w_qkv).astype(jnp.bfloat16)
    row = lax.axis_index("row")
    bias = masked_bias(row, segment_ids, bucket_table, rel_bias, row_count)
    count = lax.axis_size("row")
    forward = [(i, i + 1) for i in range(count - 1)]
    backward = [(target, source) for source, target in forward]
    low = lax.ppermute(projected[1:], "row", forward)
    high = lax.ppermute(projected[1:], "row", backward)
    context = attention(projected[0], low, projected[1:], high, bias)
    attended = project_columns(context, w_out)
    residual_mid = (tokens.astype(jnp.float32) + attended).astype(jnp.bfloat16)
    normed_two = normed_features(residual_mid, gain_ffn)
    branches = project_rows(normed_two, w_in)
    hidden = (jax.nn.gelu(branches[0], approximate=True) * branches[1]).astype(jnp.bfloat16)
    output = (residual_mid.astype(jnp.float32) + project_columns(hidden, w_down)).astype(
        jnp.bfloat16
    )
    blocks = projected[1:].reshape(2, slot_index.shape[1], BLOCK, projected.shape[2])
    kv_cache = (
        jnp.zeros_like(blocks)
        .at[:, slot_index[0]]
        .set(blocks)
        .reshape(2, row_count, projected.shape[2])
    )
    return (output, kv_cache)


def solution(mesh):
    return jax.shard_map(
        per_device,
        mesh=mesh,
        in_specs=(
            P("row", "col"),
            P(),
            P(),
            P("row", None),
            P(),
            P(None, "row", "col"),
            P(None, "col"),
            P("col", "row"),
            P(),
            P(None, "row", "col"),
            P("col", "row"),
        ),
        out_specs=(P("row", "col"), P(None, "row", "col")),
        check_vma=False,
    )
```

time: 429 us -> 269 us (0.63)
  local copies, waits for them, and re-layouts: 180 us -> 2.65 us
  waiting for transfers between devices: 172 us -> 184 us
  Pallas kernels: 0 us -> 7.57 us
    gather x3 -> x0, local copies, waits for them, and re-layouts: 179 us -> none  [the longest x2 178 us: attend_tile(): rel_terms = jnp.take(bias_rows, offset, axis=1)]
    all_gather x2, waiting for transfers between devices: 38.4 us -> 50.9 us  [project_columns(): lax.all_gather(weight, 'row', axis=1, tiled=True)]
    pallas_call x0 -> x2, Pallas kernels: none -> 7.57 us  [the longest x1 5 us: attention(): pl.pallas_call(attention_kernel, out_shape=jax.ShapeDtypeStruct(queries.s...]
  transfers between devices with their start and end apart: 8 -> 8, of which waited for: 5 -> 6; matrix products, arithmetic and copies ran while one was open for 46% -> 5% of each run, Pallas kernels for 0% -> 3%
where the time goes in v1:
time: 269 us; the launch traced here: 268 us
  waiting for transfers between devices  184 us (68%)
  blocking collectives  33.6 us (12%)
  matrix products  16.9 us (6%)
  between operations  14.8 us (6%)
  Pallas kernels  7.57 us (3%)
  other arithmetic  5.09 us (2%)
  starting transfers between devices  3.69 us (1%)
    all_gather x2, waiting for transfers between devices, project_rows(): lax.all_gather(stacked, 'row', axis=1, tiled=True)  77 us
    reduce_scatter x2, waiting for transfers between devices, project_columns(): lax.psum_scatter(partial_terms, 'col', scatter_dimension=1, tiled=True)  53.4 us
    all_gather x2, waiting for transfers between devices, project_columns(): lax.all_gather(weight, 'row', axis=1, tiled=True)  50.9 us
    all_gather x2, blocking collectives, normed_features(): gathered = lax.all_gather(shard_part, 'col', axis=1, tiled=True)  33.6 us
    dot_general x2, matrix products, project_rows(): jnp.einsum('td,kdc->ktc', normed, lax.all_gather(stacked, 'row', axis=1,...  9.38 us
    dot_general x2, matrix products, project_columns(): jnp.dot(hidden, lax.all_gather(weight, 'row', axis=1, tiled=True), prefer...  7.51 us
  transfers between devices with their start and end apart: 8, of which 6 were waited for; matrix products, arithmetic and copies ran while one was open for 5% of the time, Pallas kernels for 3%

profile of v1, /device:TPU:0, one launch (start us, length us, event | category | flops | bytes accessed | tf_op | source)
XLA Modules:
  0.0 268.1 jit_solution(11379088016669483255)
XLA Ops:
  7.2 0.0 copy-start.5
  7.2 0.0 all-gather.5.cloned.1.call-start
  7.2 0.7 all-gather.5.cloned.1.call-update
  7.9 0.0 all-gather.7.cloned.1.call-start
  8.0 0.7 all-gather.7.cloned.1.call-update
  8.7 0.0 reduce-scatter.3.cloned.1.call-start
  9.4 0.7 and_reduce_fusion
  10.1 17.6 %all_gather.18 = bf16[128,2048]{1,0:T(8,128)(2,1)S(1)} all-gather(bf16[128,512]{1,0:T(8,128)(2,1)} %param.13), channel_id=1, replica_groups=mesh['row'=8,'col'=4] {'col'}, dimensions={1}, use_global_device_ids=true | all-gather | bytes 655360 | tf_op jit(solution)/shard_map/all_gather | solution.py:113
  27.6 0.2 fusion.1
  27.8 30.4 %all-gather.5.cloned.1.call-done = bf16[3,2048,512]{2,1,0:T(8,128)(2,1)} async-done(((bf16[3,256,512]{2,1,0:T(8,128)(2,1)}), bf16[3,2048,512]{2,1,0:T(8,128)(2,1)}) %all-gather.5.cloned.1.call-update) | async-done | bytes 6291472 | tf_op jit(solution)/shard_map/all_gather | solution.py:123
  58.2 3.8 %fusion = bf16[3,128,512]{2,1,0:T(8,128)(2,1)S(1)} fusion(bf16[3,2048,512]{2,1,0:T(8,128)(2,1)} %all-gather.5.cloned.1.call-done, bf16[128,2048]{1,0:T(8,128)(2,1)S(1)} %all_gather.18, f32[2048]{0:T(1024)} %param.17, f32[128]{0:T(128)S(1)} %add_rsqrt_fusion.1), kind=kOutput, calls=%fused_computation.6 | convolution fusion | flops 806551552 | bytes 7217664 | tf_op jit(solution)/shard_map/td,kdc->ktc/dot_general | solution.py:120
  62.0 1.4 broadcast_select_fusion
  63.4 0.0 copy-start
  63.4 2.2 collective-permute-start
  65.6 1.3 collective-permute-start.1
  66.9 0.0 copy-done.5
  66.9 0.6 pad.6
  67.5 0.0 copy-start.1
  67.5 2.6 masked_bias.1.bias_ref
  70.0 0.7 slice_bitcast_fusion.2.q_ref
  70.7 0.0 copy-start.4
  70.7 0.0 collective-permute-done.low_ref
  70.7 0.0 copy-start.2
  70.7 0.0 collective-permute-done.1.high_ref
  70.7 0.0 copy-done
  70.7 0.7 copy-done.2
  71.4 0.0 copy-start.3
  71.4 0.7 copy-done.3
  72.1 5.0 %attention.1 = bf16[128,512]{1,0:T(8,128)(2,1)} custom-call(bf16[128,512]{1,0:T(8,128)(2,1)} %slice_bitcast_fusion.2.q_ref, bf16[2,128,512]{2,1,0:T(8,128)(2,1)} %copy-done.2, bf16[2,128,512]{2,1,0:T(8,128)(2,1)} %copy-done, bf16[2,128,512]{2,1,0:T(8,128)(2,1)} %copy-done.3, f32[8,128,384]{2,1,0:T(8,128)} %masked_bias.1.bias_ref), custom_call_target="tpu_custom_call" | custom-call | flops 100663296 | bytes 1572864 | tf_op jit(solution)/shard_map/attention/pallas_call | solution.py:100
  77.1 12.5 %all-gather.7.cloned.1.call-done = bf16[512,2048]{1,0:T(8,128)(2,1)} async-done(((bf16[512,256]{1,0:T(8,128)(2,1)}), bf16[512,2048]{1,0:T(8,128)(2,1)}) %all-gather.7.cloned.1.call-update) | async-done | bytes 2097168 | tf_op jit(solution)/shard_map/all_gather | solution.py:131
  89.7 3.1 %fusion.34 = f32[128,2048]{1,0:T(8,128)} fusion(bf16[128,512]{1,0:T(8,128)(2,1)} %attention.1, bf16[512,2048]{1,0:T(8,128)(2,1)} %all-gather.7.cloned.1.call-done), kind=kOutput, calls=%fused_computation.47 | convolution fusion | flops 268435456 | bytes 3276800 | tf_op jit(solution)/shard_map/dot_general | solution.py:129
  92.7 0.0 reduce-scatter.3.cloned.1.call-update
  92.8 0.0 all-gather.9.cloned.1.call-start
  92.8 0.5 all-gather.9.cloned.1.call-update
  93.4 0.0 all-gather.11.cloned.1.call-start
  93.4 0.5 all-gather.11.cloned.1.call-update
  93.9 0.0 reduce-scatter.5.cloned.1.call-start
  94.0 26.1 %reduce-scatter.3.cloned.1.call-done = f32[128,512]{1,0:T(8,128)} async-done(((f32[128,2048]{1,0:T(8,128)}), f32[128,512]{1,0:T(8,128)}) %reduce-scatter.3.cloned.1.call-update) | async-done | bytes 262160 | tf_op jit(solution)/shard_map/reduce_scatter | solution.py:134
  120.1 0.0 copy-done.1
  120.1 1.0 add_convert_fusion.1
  121.1 16.0 %all_gather.21 = bf16[128,2048]{1,0:T(8,128)(2,1)S(1)} all-gather(bf16[128,512]{1,0:T(8,128)(2,1)S(1)} %add_convert_fusion.1), channel_id=1, replica_groups=mesh['row'=8,'col'=4] {'col'}, dimensions={1}, use_global_device_ids=true | all-gather | bytes 655360 | tf_op jit(solution)/shard_map/all_gather | solution.py:113
  137.1 0.2 fusion.4
  137.3 46.6 %all-gather.9.cloned.1.call-done = bf16[2,2048,1280]{2,1,0:T(8,128)(2,1)} async-done(((bf16[2,256,1280]{2,1,0:T(8,128)(2,1)}), bf16[2,2048,1280]{2,1,0:T(8,128)(2,1)}) %all-gather.9.cloned.1.call-update) | async-done | bytes 10485776 | tf_op jit(solution)/shard_map/all_gather | solution.py:123
  184.0 0.0 copy-done.4
  184.0 5.5 %convolution_bitcast_fusion = f32[2,128,1280]{2,1,0:T(8,128)S(1)} fusion(bf16[2,2048,1280]{2,1,0:T(8,128)(2,1)} %all-gather.9.cloned.1.call-done, bf16[128,2048]{1,0:T(8,128)(2,1)S(1)} %all_gather.21, f32[2048]{0:T(1024)S(1)} %copy-done.4, f32[128]{0:T(128)S(1)} %add_rsqrt_fusion), kind=kOutput, calls=%fused_computation | convolution fusion | flops 1343225856 | bytes 12329472 | tf_op jit(solution)/shard_map/td,kdc->ktc/dot_general | solution.py:120
  189.5 38.4 %all-gather.11.cloned.1.call-done = bf16[1280,2048]{1,0:T(8,128)(2,1)} async-done(((bf16[1280,256]{1,0:T(8,128)(2,1)}), bf16[1280,2048]{1,0:T(8,128)(2,1)}) %all-gather.11.cloned.1.call-update) | async-done | bytes 5242896 | tf_op jit(solution)/shard_map/all_gather | solution.py:131
  227.9 4.4 %fusion.24 = f32[128,2048]{1,0:T(8,128)} fusion(bf16[1280,2048]{1,0:T(8,128)(2,1)} %all-gather.11.cloned.1.call-done, f32[2,128,1280]{2,1,0:T(8,128)S(1)} %convolution_bitcast_fusion), kind=kOutput, calls=%fused_computation.31 | convolution fusion | flops 672727040 | bytes 7602176 | tf_op jit(solution)/shard_map/dot_general | solution.py:129
  232.3 0.0 reduce-scatter.5.cloned.1.call-update
  232.4 27.3 %reduce-scatter.5.cloned.1.call-done = f32[128,512]{1,0:T(8,128)} async-done(((f32[128,2048]{1,0:T(8,128)}), f32[128,512]{1,0:T(8,128)}) %reduce-scatter.5.cloned.1.call-update) | async-done | bytes 262160 | tf_op jit(solution)/shard_map/reduce_scatter | solution.py:134
  259.7 1.6 add_convert_fusion
  (2 shorter events, 0.0 us)
Async XLA Ops:
  7.2 59.7 %copy-start.5 = (s32[255]{0:T(256)S(1)}, s32[255]{0:T(256)}, u32[]{:S(2)}) copy-start(s32[255]{0:T(256)} %param.15) | copy-start | bytes 3064
  7.2 51.0 %all-gather.5.cloned.1.call-start = ((), (), s32[]{:S(2)}) async-start(), calls=%async_computation.2 | async-start | bytes 7077888 | tf_op jit(solution)/shard_map/all_gather | solution.py:123
  7.9 81.7 %all-gather.7.cloned.1.call-start = ((), (), s32[]{:S(2)}) async-start(), calls=%async_computation.3 | async-start | bytes 2359296 | tf_op jit(solution)/shard_map/all_gather | solution.py:131
  8.7 111.4 %reduce-scatter.3.cloned.1.call-start = ((), (), s32[]{:S(2)}) async-start(), calls=%async_computation.4 | async-start | bytes 1310720 | tf_op jit(solution)/shard_map/reduce_scatter | solution.py:134
  63.4 7.3 %copy-start = (bf16[2,128,512]{2,1,0:T(8,128)(2,1)}, bf16[2,128,512]{2,1,0:T(8,128)(2,1)S(1)}, u32[]{:S(2)}) copy-start(bf16[2,128,512]{2,1,0:T(8,128)(2,1)S(1)} %get-tuple-element.15.own_ref) | copy-start | bytes 786436
  63.4 7.3 %collective-permute-start = (bf16[2,128,512]{2,1,0:T(8,128)(2,1)S(1)}, bf16[2,128,512]{2,1,0:T(8,128)(2,1)S(1)}, u32[]{:S(2)}, u32[]{:S(2)}) collective-permute-start(bf16[2,128,512]{2,1,0:T(8,128)(2,1)S(1)} %get-tuple-element.15.own_ref), channel_id=1, source_target_pairs={{0,4},{4,8},{8,12},{12,16},{16,20},{20,24},{24,28},{1,5},{5,9},{9,... | collective-permute-start | bytes 786440 | tf_op jit(solution)/shard_map/ppermute | solution.py:158
  65.6 5.1 %collective-permute-start.1 = (bf16[2,128,512]{2,1,0:T(8,128)(2,1)S(1)}, bf16[2,128,512]{2,1,0:T(8,128)(2,1)S(1)}, u32[]{:S(2)}, u32[]{:S(2)}) collective-permute-start(bf16[2,128,512]{2,1,0:T(8,128)(2,1)S(1)} %get-tuple-element.15.own_ref), channel_id=1, source_target_pairs={{4,0},{8,4},{12,8},{16,12},{20,16},{24,20},{28,24},{5,1},{9,5},{13... | collective-permute-start | bytes 786440 | tf_op jit(solution)/shard_map/ppermute | solution.py:159
  67.5 52.7 %copy-start.1 = (bf16[128,512]{1,0:T(8,128)(2,1)S(1)}, bf16[128,512]{1,0:T(8,128)(2,1)}, u32[]{:S(2)}) copy-start(bf16[128,512]{1,0:T(8,128)(2,1)} %param.13) | copy-start | bytes 393220
  70.7 113.3 %copy-start.4 = (f32[2048]{0:T(1024)S(1)}, f32[2048]{0:T(1024)}, u32[]{:S(2)}) copy-start(f32[2048]{0:T(1024)} %param.21) | copy-start | bytes 24580
  70.7 0.7 copy-start.2
  71.4 0.7 copy-start.3
  92.8 91.2 %all-gather.9.cloned.1.call-start = ((), (), s32[]{:S(2)}) async-start(), calls=%async_computation.5 | async-start | bytes 11796480 | tf_op jit(solution)/shard_map/all_gather | solution.py:123
  93.4 134.6 %all-gather.11.cloned.1.call-start = ((), (), s32[]{:S(2)}) async-start(), calls=%async_computation.6 | async-start | bytes 5898240 | tf_op jit(solution)/shard_map/all_gather | solution.py:131
  93.9 165.7 %reduce-scatter.5.cloned.1.call-start = ((), (), s32[]{:S(2)}) async-start(), calls=%async_computation.7 | async-start | bytes 1310720 | tf_op jit(solution)/shard_map/reduce_scatter | solution.py:134
Sparse Core Ops, SparseCore 0:
  9.9 48.2 all-gather.4
  60.0 29.5 all-gather.6
  92.9 27.1 reduce-scatter.2
  122.0 61.8 all-gather.8
  185.8 42.0 all-gather.10
  232.5 27.1 reduce-scatter.4

commit v2 on v1

--- a/solution.py
+++ b/solution.py
@@ -109,29 +109,164 @@
     )(queries, low, own, high, bias)
 
 
-def normed_features(shard_part, gain_vector):
-    gathered = lax.all_gather(shard_part, "col", axis=1, tiled=True)
-    widened = gathered.astype(jnp.float32)
-    factor = lax.rsqrt(jnp.mean(widened * widened, axis=1, keepdims=True) + epsilon)
-    return (widened * factor * gain_vector).astype(jnp.bfloat16)
-
-
-def project_rows(normed, stacked):
-    return jnp.einsum(
-        "td,kdc->ktc",
-        normed,
-        lax.all_gather(stacked, "row", axis=1, tiled=True),
-        preferred_element_type=jnp.float32,
-    )
-
-
-def project_columns(hidden, weight):
-    partial_terms = jnp.dot(
-        hidden,
-        lax.all_gather(weight, "row", axis=1, tiled=True),
-        preferred_element_type=jnp.float32,
-    )
-    return lax.psum_scatter(partial_terms, "col", scatter_dimension=1, tiled=True)
+def exchange(value, axis, partner):
+    count = lax.axis_size(axis)
+    return lax.ppermute(value, axis, [(i, partner(i) % count) for i in range(count)])
+
+
+def other_core(value):
+    return exchange(value, "row", lambda i: i ^ 1)
+
+
+def pair_exchange(value, step):
+    return exchange(value, "row", lambda i: i ^ (2 * step))
+
+
+def shifted(value, step):
+    return exchange(value, "col", lambda i: i + step)
+
+
+def after(value, *earlier):
+    return lax.optimization_barrier((value, *earlier))[0]
+
+
+def near_pieces(weight):
+    pairs = lax.axis_size("row") // 2
+    if pairs == 4:
+        return [pair_exchange(weight, 1), pair_exchange(weight, 2)]
+    return [pair_exchange(weight, step) for step in range(1, pairs)]
+
+
+def far_pieces(near, axis):
+    if len(near) != 2:
+        return []
+    first, _ = jnp.split(near[0], 2, axis=axis)
+    _, second = jnp.split(near[1], 2, axis=axis)
+    return [pair_exchange(first, 2), pair_exchange(second, 1)]
+
+
+def project_kernel(split, place_ref, scale_ref, gain_ref, *refs):
+    blocks = lax.axis_size("col")
+    token_refs, refs = refs[:blocks], refs[blocks:]
+    *weight_refs, own_ref, send_ref, held = refs
+    row, col = place_ref[0], place_ref[1]
+    pair, core = row // 2, row % 2
+    scale = scale_ref[...]
+    for step in range(blocks):
+        block = lax.rem(col - step + blocks, blocks)
+        gain = gain_ref[pl.ds(2 * block + core, 1), :]
+        held[block] = (token_refs[step][...].astype(jnp.float32) * scale * gain).astype(
+            jnp.bfloat16
+        )
+    far = len(weight_refs) == blocks + 1
+    direct = blocks - 1 if far else blocks
+    count = own_ref.shape[0]
+    parts, width = weight_refs[0].shape[0], weight_refs[0].shape[2]
+    tile = min(256, width)
+    for part in range(parts):
+        for start in range(0, width, tile):
+            stop = min(start + tile, width)
+            total = None
+            for step in range(blocks):
+                if step < direct:
+                    weight = weight_refs[step][part, :, start:stop]
+                elif split == 0:
+                    weight = weight_refs[direct + part][0, :, start:stop]
+                else:
+                    half = start // (width // 2)
+                    offset = start - half * (width // 2)
+                    weight = weight_refs[direct + half][part, :, offset : offset + stop - start]
+                term = jnp.dot(held[pair ^ step], weight, preferred_element_type=jnp.float32)
+                total = term if total is None else total + term
+            place = slice(part * width + start, part * width + stop)
+            own_ref[:, place] = total[:count]
+            send_ref[:, place] = total[count:].astype(send_ref.dtype)
+
+
+def project(place, scale, gain, token_blocks, pieces, split, name):
+    tokens_two, depth = token_blocks[0].shape
+    columns = pieces[0].shape[0] * pieces[0].shape[2]
+    count = tokens_two // 2
+    return pl.pallas_call(
+        functools.partial(project_kernel, split),
+        out_shape=(
+            jax.ShapeDtypeStruct((count, columns), jnp.float32),
+            jax.ShapeDtypeStruct((count, columns), jnp.bfloat16),
+        ),
+        in_specs=[SMEM] + [VMEM] * (2 + len(token_blocks) + len(pieces)),
+        out_specs=(VMEM, VMEM),
+        scratch_shapes=[pltpu.VMEM((len(token_blocks), tokens_two, depth), jnp.bfloat16)],
+        compiler_params=pltpu.CompilerParams(vmem_limit_bytes=40 << 20),
+        cost_estimate=pl.CostEstimate(
+            flops=2 * tokens_two * depth * len(token_blocks) * columns,
+            bytes_accessed=2 * depth * len(token_blocks) * columns,
+            transcendentals=0,
+        ),
+        name=name,
+    )(place, scale, gain, *token_blocks, *pieces)
+
+
+def columns_kernel(place_ref, own_in_ref, other_in_ref, *refs):
+    blocks = lax.axis_size("col")
+    *weight_refs, own_ref = refs[: len(refs) - blocks]
+    send_refs, held = refs[len(refs) - blocks : -1], refs[-1]
+    row, col = place_ref[0], place_ref[1]
+    pair = row // 2
+    hidden = jnp.concatenate([own_in_ref[...], other_in_ref[...]], axis=0)
+    far = len(weight_refs) == blocks + 1
+    direct = blocks - 1 if far else blocks
+    for step in range(blocks):
+        if step < direct:
+            total = jnp.dot(hidden, weight_refs[step][...], preferred_element_type=jnp.float32)
+        else:
+            half = hidden.shape[1] // 2
+            total = jnp.dot(
+                hidden[:, :half], weight_refs[direct][...], preferred_element_type=jnp.float32
+            ) + jnp.dot(
+                hidden[:, half:], weight_refs[direct + 1][...], preferred_element_type=jnp.float32
+            )
+        held[lax.rem((pair ^ step) - col + blocks, blocks)] = total
+    own_ref[...] = held[0]
+    for step in range(1, blocks):
+        send_refs[step - 1][...] = held[step].astype(jnp.bfloat16)
+
+
+def columns(place, own, other, pieces, name):
+    count, depth = own.shape
+    width = pieces[0].shape[1]
+    blocks = lax.axis_size("col")
+    return pl.pallas_call(
+        columns_kernel,
+        out_shape=(
+            jax.ShapeDtypeStruct((2 * count, width), jnp.float32),
+            *[jax.ShapeDtypeStruct((2 * count, width), jnp.bfloat16)] * (blocks - 1),
+        ),
+        in_specs=[SMEM] + [VMEM] * (2 + len(pieces)),
+        out_specs=tuple([VMEM] * blocks),
+        scratch_shapes=[pltpu.VMEM((blocks, 2 * count, width), jnp.float32)],
+        compiler_params=pltpu.CompilerParams(vmem_limit_bytes=40 << 20),
+        cost_estimate=pl.CostEstimate(
+            flops=4 * count * depth * width * blocks,
+            bytes_accessed=2 * depth * width * blocks,
+            transcendentals=0,
+        ),
+        name=name,
+    )(place, own, other, *pieces)
+
+
+def summed(own, sends, residual):
+    total = own + residual.astype(jnp.float32)
+    for step, send in enumerate(sends, 1):
+        total = total + shifted(send, step).astype(jnp.float32)
+    return total.astype(jnp.bfloat16)
+
+
+def gathered(block):
+    return [block] + [shifted(block, step) for step in range(1, lax.axis_size("col"))]
+
+
+def square_sums(blocks):
+    return sum(jnp.sum(jnp.square(b.astype(jnp.float32)), axis=1) for b in blocks)
 
 
 def per_device(
@@ -147,31 +282,79 @@
     w_in,
     w_down,
 ):
-    row_count = tokens.shape[0]
-    normed = normed_features(tokens, gain_attn)
-    projected = project_rows(normed, w_qkv).astype(jnp.bfloat16)
-    row = lax.axis_index("row")
-    bias = masked_bias(row, segment_ids, bucket_table, rel_bias, row_count)
-    count = lax.axis_size("row")
-    forward = [(i, i + 1) for i in range(count - 1)]
+    rows, cols = lax.axis_size("row"), lax.axis_size("col")
+    count, width = tokens.shape
+    half = width // 2
+    features = width * cols
+    row, col = lax.axis_index("row"), lax.axis_index("col")
+    core = row % 2
+    place = jnp.stack([row, col]).astype(jnp.int32)
+
+    qkv_near = near_pieces(w_qkv)
+
+    kept = jnp.where(core == 0, tokens[:, :half], tokens[:, half:])
+    given = jnp.where(core == 0, tokens[:, half:], tokens[:, :half])
+    token_block = jnp.concatenate([kept, other_core(given)], axis=0)
+    token_blocks = gathered(token_block)
+    squares = square_sums(token_blocks)
+    squares = squares + jnp.roll(other_core(squares), count)
+    scale = lax.rsqrt(squares / features + epsilon)[:, None]
+    bias = masked_bias(row, segment_ids, bucket_table, rel_bias, count)
+
+    out_near = near_pieces(after(w_out, *qkv_near))
+    qkv_far = far_pieces(qkv_near, 2)
+    in_near = near_pieces(after(w_in, *(qkv_far or qkv_near)))
+    own, send = project(
+        place, scale, gain_attn.reshape(rows, -1), token_blocks, [w_qkv, *qkv_near, *qkv_far], 2, "qkv"
+    )
+    projected = (own + other_core(send).astype(jnp.float32)).astype(jnp.bfloat16)
+    projected = projected.reshape(count, 3, width).transpose(1, 0, 2)
+    forward = [(i, i + 1) for i in range(rows - 1)]
     backward = [(target, source) for source, target in forward]
     low = lax.ppermute(projected[1:], "row", forward)
     high = lax.ppermute(projected[1:], "row", backward)
+    out_far = far_pieces(out_near, 0)
     context = attention(projected[0], low, projected[1:], high, bias)
-    attended = project_columns(context, w_out)
-    residual_mid = (tokens.astype(jnp.float32) + attended).astype(jnp.bfloat16)
-    normed_two = normed_features(residual_mid, gain_ffn)
-    branches = project_rows(normed_two, w_in)
-    hidden = (jax.nn.gelu(branches[0], approximate=True) * branches[1]).astype(jnp.bfloat16)
-    output = (residual_mid.astype(jnp.float32) + project_columns(hidden, w_down)).astype(
-        jnp.bfloat16
-    )
-    blocks = projected[1:].reshape(2, slot_index.shape[1], BLOCK, projected.shape[2])
+    own, *sends = columns(
+        place, context, other_core(context), [w_out, *out_near, *out_far], "attention_out"
+    )
+    middle = summed(own, sends, token_block)
+
+    middle_blocks = gathered(middle)
+    squares = square_sums(middle_blocks)
+    squares = squares[:count] + other_core(squares[count:])
+    scale = lax.rsqrt(squares / features + epsilon)[:, None]
+    in_far = far_pieces(in_near, 0)
+    down_near = near_pieces(after(w_down, *in_near))
+    down_far = far_pieces(down_near, 0)
+    own, send = project(
+        place,
+        jnp.ones((2 * count, 1), jnp.float32),
+        gain_ffn.reshape(rows, -1),
+        middle_blocks,
+        [w_in, *in_near, *in_far],
+        0,
+        "ffn_in",
+    )
+    branches = (own + other_core(send).astype(jnp.float32)) * scale
+    inner = branches.shape[1] // 2
+    hidden = (
+        jax.nn.gelu(branches[:, :inner], approximate=True) * branches[:, inner:]
+    ).astype(jnp.bfloat16)
+    own, *sends = columns(
+        place, hidden, other_core(hidden), [w_down, *down_near, *down_far], "ffn_out"
+    )
+    result = summed(own, sends, middle)
+    received = other_core(result[count:])
+    output = jnp.where(
+        core == 0,
+        jnp.concatenate([result[:count], received], axis=1),
+        jnp.concatenate([received, result[:count]], axis=1),
+    )
+
+    blocks = projected[1:].reshape(2, slot_index.shape[1], BLOCK, width)
     kv_cache = (
-        jnp.zeros_like(blocks)
-        .at[:, slot_index[0]]
-        .set(blocks)
-        .reshape(2, row_count, projected.shape[2])
+        jnp.zeros_like(blocks).at[:, slot_index[0]].set(blocks).reshape(2, count, width)
     )
     return (output, kv_cache)
 

time: 269 us -> 168 us (0.62)
  waiting for transfers between devices: 184 us -> 85.9 us
  starting transfers between devices: 3.69 us -> 43 us
  blocking collectives: 33.6 us -> 0 us
  matrix products: 16.9 us -> 0 us
  between operations: 14.8 us -> 1.69 us
  local copies, waits for them, and re-layouts: 2.65 us -> 11.7 us
  Pallas kernels: 7.57 us -> 16.1 us
  other arithmetic: 5.09 us -> 8.92 us
    all_gather x4 -> x0, waiting for transfers between devices: 128 us -> none  [the longest x2 77 us: project_rows(): lax.all_gather(stacked, 'row', axis=1, tiled=True)]
    ppermute x0 -> x36, waiting for transfers between devices: none -> 85.9 us  [exchange(): lax.ppermute(value, axis, [(i, partner(i) % count) for i in range(count)])]
    reduce_scatter x2 -> x0, waiting for transfers between devices: 53.4 us -> none  [project_columns(): lax.psum_scatter(partial_terms, 'col', scatter_dimension=1, tiled=True)]
    ppermute x0 -> x36, starting transfers between devices: none -> 39.7 us  [exchange(): lax.ppermute(value, axis, [(i, partner(i) % count) for i in range(count)])]
    all_gather x2 -> x0, blocking collectives: 33.6 us -> none  [normed_features(): gathered = lax.all_gather(shard_part, 'col', axis=1, tiled=True)]
    dot_general x4 -> x0, matrix products: 16.9 us -> none  [the longest x2 9.38 us: project_rows(): jnp.einsum('td,kdc->ktc', normed, lax.all_gather(stacked, 'row', axis=1,...]
    pallas_call x0 -> x4, Pallas kernels: none -> 8.52 us  [the longest x2 5.45 us: project(): pl.pallas_call(functools.partial(project_kernel, split), out_shape=(jax.S...]
    split x0 -> x8, local copies, waits for them, and re-layouts: none -> 4.07 us  [the longest x4 2.4 us: far_pieces(): _, second = jnp.split(near[1], 2, axis=axis)]
  transfers between devices with their start and end apart: 8 -> 38, of which waited for: 6 -> 17; matrix products, arithmetic and copies ran while one was open for 5% -> 11% of each run, Pallas kernels for 3% -> 7%
where the time goes in v2:
time: 168 us; the launch traced here: 167 us
  waiting for transfers between devices  85.9 us (51%)
  starting transfers between devices  43 us (26%)
  Pallas kernels  16.1 us (10%)
  local copies, waits for them, and re-layouts  11.7 us (7%)
  other arithmetic  8.92 us (5%)
  between operations  1.69 us (1%)
    ppermute x36, waiting for transfers between devices, exchange(): lax.ppermute(value, axis, [(i, partner(i) % count) for i in range(count)])  85.9 us
    ppermute x36, starting transfers between devices, exchange(): lax.ppermute(value, axis, [(i, partner(i) % count) for i in range(count)])  39.7 us
    pallas_call x2, Pallas kernels, project(): pl.pallas_call(functools.partial(project_kernel, split), out_shape=(jax.S...  5.45 us
    pallas_call x1, Pallas kernels, attention(): pl.pallas_call(attention_kernel, out_shape=jax.ShapeDtypeStruct(queries.s...  5.01 us
  transfers between devices with their start and end apart: 38, of which 17 were waited for; matrix products, arithmetic and copies ran while one was open for 11% of the time, Pallas kernels for 7%

profile of v2, /device:TPU:0, one launch (start us, length us, event | category | flops | bytes accessed | tf_op | source)
XLA Modules:
  0.0 167.2 jit_solution(6557943281828629971)
XLA Ops:
  0.6 0.9 broadcast_select_fusion.2
  2.1 0.9 collective-permute-done
  3.0 5.0 %collective-permute-start.3 = (bf16[256,256]{1,0:T(8,128)(2,1)S(1)}, bf16[256,256]{1,0:T(8,128)(2,1)S(1)}, u32[]{:S(2)}, u32[]{:S(2)}) collective-permute-start(bf16[256,256]{1,0:T(8,128)(2,1)S(1)} %pad_maximum_fusion.refs_0_), channel_id=1, source_target_pairs={{0,3},{1,0},{2,1},{3,2},{4,7},{5,4},{6,5},{7,6},{8,11},{9,8},{10,9... | collective-permute-start | bytes 393224 | tf_op jit(solution)/shard_map/ppermute | solution.py:114
  8.0 1.5 collective-permute-start.5
  9.5 1.5 collective-permute-start.6
  11.0 1.0 collective-permute-start.1
  12.3 8.1 %collective-permute-done.2.refs_2_ = bf16[256,256]{1,0:T(8,128)(2,1)S(1)} collective-permute-done((bf16[256,256]{1,0:T(8,128)(2,1)S(1)}, bf16[256,256]{1,0:T(8,128)(2,1)S(1)}, u32[]{:S(2)}, u32[]{:S(2)}) %collective-permute-start.2) | collective-permute-done | bytes 131104 | tf_op jit(solution)/shard_map/ppermute | solution.py:114
  20.8 0.7 reshape.129.gain_ref
  21.5 6.0 %collective-permute-done.5.refs_5_ = bf16[3,256,512]{2,1,0:T(8,128)(2,1)S(1)} collective-permute-done((bf16[3,256,512]{2,1,0:T(8,128)(2,1)}, bf16[3,256,512]{2,1,0:T(8,128)(2,1)S(1)}, u32[]{:S(2)}, u32[]{:S(2)}) %collective-permute-start.5) | collective-permute-done | bytes 786464 | tf_op jit(solution)/shard_map/ppermute | solution.py:114
  27.5 0.8 split.32
  28.3 1.5 collective-permute-start.7
  29.8 0.8 split.33
  30.6 1.5 collective-permute-start.8
  32.3 6.2 %collective-permute-done.7.refs_7_ = bf16[3,256,256]{2,1,0:T(8,128)(2,1)S(1)} collective-permute-done((bf16[3,256,256]{2,1,0:T(8,128)(2,1)}, bf16[3,256,256]{2,1,0:T(8,128)(2,1)S(1)}, u32[]{:S(2)}, u32[]{:S(2)}) %collective-permute-start.7) | collective-permute-done | bytes 393248 | tf_op jit(solution)/shard_map/ppermute | solution.py:114
  38.5 2.1 %collective-permute-done.8.refs_8_ = bf16[3,256,256]{2,1,0:T(8,128)(2,1)} collective-permute-done((bf16[3,256,256]{2,1,0:T(8,128)(2,1)}, bf16[3,256,256]{2,1,0:T(8,128)(2,1)}, u32[]{:S(2)}, u32[]{:S(2)}) %collective-permute-start.8) | collective-permute-done | bytes 393248 | tf_op jit(solution)/shard_map/ppermute | solution.py:114
  40.7 2.1 %qkv.1 = (f32[128,1536]{1,0:T(8,128)S(1)}, bf16[128,1536]{1,0:T(8,128)(2,1)S(1)}) custom-call(s32[2]{0:T(128)S(1)} %pad_add_fusion.place_ref, f32[256,1]{1,0:T(8,128)S(1)} %rsqrt.13.scale_ref, f32[8,256]{1,0:T(8,128)S(1)} %reshape.129.gain_ref, bf16[256,256]{1,0:T(8,128)(2,1)S(1)} %pad_maximum_fusion.refs_0_, ...), custom_call_target="tpu_custom_call" | custom-call | flops 805306368 | bytes 3145728 | tf_op jit(solution)/shard_map/qkv/pallas_call | solution.py:190
  42.9 1.6 collective-permute-start.23
  45.6 0.7 and_reduce_fusion
  46.9 1.5 collective-permute-start.14
  48.4 0.8 add_convert_fusion
  49.2 1.9 %copy.27 = bf16[128,1536]{0,1:T(8,128)(2,1)} copy(bf16[128,1536]{1,0:T(8,128)(2,1)} %add_convert_fusion) | data formatting | bytes 786432 | tf_op jit(solution)/shard_map/convert_element_type | solution.py:310
  51.1 1.9 %copy.28 = bf16[128,3,512]{2,0,1:T(8,128)(2,1)} copy(bf16[128,3,512]{0,2,1:T(8,128)(2,1)} %bitcast.18) | data formatting | bytes 786432 | tf_op jit(solution)/shard_map/reshape | solution.py:311
  53.1 2.4 %broadcast_select_fusion = (bf16[2,128,512]{2,1,0:T(8,128)(2,1)}, bf16[2,128,512]{2,1,0:T(8,128)(2,1)}) fusion(pred[]{:T(512)} %and_reduce_fusion, bf16[3,128,512]{2,1,0:T(8,128)(2,1)} %bitcast.19), kind=kLoop, calls=%fused_computation.32 | loop fusion | flops 131072 | bytes 786433 | tf_op jit(solution)/shard_map/scatter | solution.py:357
  55.5 2.0 %collective-permute-start.10 = (bf16[2,128,512]{2,1,0:T(8,128)(2,1)}, bf16[2,128,512]{2,1,0:T(8,128)(2,1)}, u32[]{:S(2)}, u32[]{:S(2)}) collective-permute-start(bf16[2,128,512]{2,1,0:T(8,128)(2,1)} %get-tuple-element.47.own_ref), channel_id=1, source_target_pairs={{0,4},{4,8},{8,12},{12,16},{16,20},{20,24},{24,28},{1,5},{5,9},{9,... | collective-permute-start | bytes 786440 | tf_op jit(solution)/shard_map/ppermute | solution.py:314
  57.5 22.9 %collective-permute-done.13.refs_1_ = bf16[512,256]{1,0:T(8,128)(2,1)S(1)} collective-permute-done((bf16[512,256]{1,0:T(8,128)(2,1)S(1)}, bf16[512,256]{1,0:T(8,128)(2,1)S(1)}, u32[]{:S(2)}, u32[]{:S(2)}) %collective-permute-start.13) | collective-permute-done | bytes 262176 | tf_op jit(solution)/shard_map/ppermute | solution.py:114
  80.4 1.3 collective-permute-start.11
  81.7 0.6 pad.6
  82.2 2.5 %masked_bias.1.bias_ref = f32[8,128,384]{2,1,0:T(8,128)} custom-call(s32[1]{0:T(128)} %bitcast.row_ref, s32[8,128]{1,0:T(8,128)} %bitcast.21, s32[1,256]{1,0:T(1,128)} %bitcast.23, f32[8,32]{1,0:T(8,128)} %bitcast.22), custom_call_target="tpu_custom_call" | custom-call | tf_op jit(solution)/shard_map/masked_bias/pallas_call | solution.py:52
  84.8 2.5 %collective-permute-start.15 = (bf16[256,256]{1,0:T(8,128)(2,1)S(1)}, bf16[256,256]{1,0:T(8,128)(2,1)S(1)}, u32[]{:S(2)}, u32[]{:S(2)}) collective-permute-start(bf16[256,256]{1,0:T(8,128)(2,1)S(1)} %split.34), channel_id=1, source_target_pairs={{0,16},{4,20},{8,24},{12,28},{16,0},{20,4},{24,8},{28,12},{1,17},{... | collective-permute-start | bytes 393224 | tf_op jit(solution)/shard_map/ppermute | solution.py:114
  87.3 0.7 split.35
  87.9 1.6 slice_bitcast_fusion.q_ref
  89.8 5.0 %attention.1.own_in_ref = bf16[128,512]{1,0:T(8,128)(2,1)} custom-call(bf16[128,512]{1,0:T(8,128)(2,1)} %slice_bitcast_fusion.q_ref, bf16[2,128,512]{2,1,0:T(8,128)(2,1)} %collective-permute-done.10.low_ref, bf16[2,128,512]{2,1,0:T(8,128)(2,1)} %get-tuple-element.47.own_ref, bf16[2,128,512]{2,1,0:T(8,128)(2,1)} %collective-permute-done.11.high_ref, ...), custom_call_target="tpu_custom_call" | custom-call | flops 100663296 | bytes 1572864 | tf_op jit(solution)/shard_map/attention/pallas_call | solution.py:100
  94.8 0.7 collective-permute-start.12
  95.5 0.9 split.36
  96.4 0.9 collective-permute-start.25
  97.3 0.9 split.37
  98.7 1.5 attention_out.1
  100.3 1.0 collective-permute-start.18
  101.3 2.8 %collective-permute-start.19 = (bf16[256,256]{1,0:T(8,128)(2,1)S(1)}, bf16[256,256]{1,0:T(8,128)(2,1)S(1)}, u32[]{:S(2)}, u32[]{:S(2)}) collective-permute-start(bf16[256,256]{1,0:T(8,128)(2,1)S(1)} %get-tuple-element.35), channel_id=1, source_target_pairs={{0,3},{1,0},{2,1},{3,2},{4,7},{5,4},{6,5},{7,6},{8,11},{9,8},{10,9... | collective-permute-start | bytes 393224 | tf_op jit(solution)/shard_map/ppermute | solution.py:114
  104.1 4.5 %collective-permute-done.17 = bf16[256,256]{1,0:T(8,128)(2,1)S(1)} collective-permute-done((bf16[256,256]{1,0:T(8,128)(2,1)S(1)}, bf16[256,256]{1,0:T(8,128)(2,1)S(1)}, u32[]{:S(2)}, u32[]{:S(2)}) %collective-permute-start.17) | collective-permute-done | bytes 131104 | tf_op jit(solution)/shard_map/ppermute | solution.py:114
  108.5 4.7 %collective-permute-done.18 = bf16[256,256]{1,0:T(8,128)(2,1)S(1)} collective-permute-done((bf16[256,256]{1,0:T(8,128)(2,1)S(1)}, bf16[256,256]{1,0:T(8,128)(2,1)S(1)}, u32[]{:S(2)}, u32[]{:S(2)}) %collective-permute-start.18) | collective-permute-done | bytes 131104 | tf_op jit(solution)/shard_map/ppermute | solution.py:114
  113.4 2.5 %collective-permute-start.22 = (bf16[256,256]{1,0:T(8,128)(2,1)S(1)}, bf16[256,256]{1,0:T(8,128)(2,1)}, u32[]{:S(2)}, u32[]{:S(2)}) collective-permute-start(bf16[256,256]{1,0:T(8,128)(2,1)S(1)} %get-tuple-element.45.refs_0_), channel_id=1, source_target_pairs={{0,3},{1,0},{2,1},{3,2},{4,7},{5,4},{6,5},{7,6},{8,11},{9,8},{10,9... | collective-permute-start | bytes 393224 | tf_op jit(solution)/shard_map/ppermute | solution.py:114
  115.9 1.5 collective-permute-start.21
  117.4 0.7 reshape.128.gain_ref
  118.1 1.8 %collective-permute-done.22.refs_3_ = bf16[256,256]{1,0:T(8,128)(2,1)} collective-permute-done((bf16[256,256]{1,0:T(8,128)(2,1)S(1)}, bf16[256,256]{1,0:T(8,128)(2,1)}, u32[]{:S(2)}, u32[]{:S(2)}) %collective-permute-start.22) | collective-permute-done | bytes 131104 | tf_op jit(solution)/shard_map/ppermute | solution.py:114
  119.9 1.0 multiply_reduce_fusion
  120.9 1.5 collective-permute-start.30
  122.4 6.0 %collective-permute-done.21.refs_2_ = bf16[256,256]{1,0:T(8,128)(2,1)S(1)} collective-permute-done((bf16[256,256]{1,0:T(8,128)(2,1)S(1)}, bf16[256,256]{1,0:T(8,128)(2,1)S(1)}, u32[]{:S(2)}, u32[]{:S(2)}) %collective-permute-start.21) | collective-permute-done | bytes 131104 | tf_op jit(solution)/shard_map/ppermute | solution.py:114
  128.4 1.7 %collective-permute-start.31 = (bf16[1280,256]{1,0:T(8,128)(2,1)}, bf16[1280,256]{1,0:T(8,128)(2,1)S(1)}, u32[]{:S(2)}, u32[]{:S(2)}) collective-permute-start(bf16[1280,256]{1,0:T(8,128)(2,1)} %refs_0_.3), channel_id=1, source_target_pairs={{0,16},{4,20},{8,24},{12,28},{16,0},{20,4},{24,8},{28,12},{1,17},{... | collective-permute-start | bytes 1966088 | tf_op jit(solution)/shard_map/ppermute | solution.py:114
  130.1 3.3 %ffn_in.1 = (f32[128,2560]{1,0:T(8,128)S(1)}, bf16[128,2560]{1,0:T(8,128)(2,1)S(1)}) custom-call(s32[2]{0:T(128)S(1)} %pad_add_fusion.place_ref, f32[256,1]{1,0:T(8,128)S(1)} %broadcast_in_dim.2.scale_ref, f32[8,256]{1,0:T(8,128)S(1)} %reshape.128.gain_ref, bf16[256,256]{1,0:T(8,128)(2,1)S(1)} %get-tuple-element.45.refs_0_, ...), custom_call_target="tpu_custom_call" | custom-call | flops 1342177280 | bytes 5242880 | tf_op jit(solution)/shard_map/ffn_in/pallas_call | solution.py:190
  133.7 1.0 multiply_reduce_fusion.2
  135.3 0.8 collective-permute-done.28
  136.1 0.9 collective-permute-start.32
  137.0 9.2 %collective-permute-done.31.refs_2_ = bf16[1280,256]{1,0:T(8,128)(2,1)S(1)} collective-permute-done((bf16[1280,256]{1,0:T(8,128)(2,1)}, bf16[1280,256]{1,0:T(8,128)(2,1)S(1)}, u32[]{:S(2)}, u32[]{:S(2)}) %collective-permute-start.31) | collective-permute-done | bytes 655392 | tf_op jit(solution)/shard_map/ppermute | solution.py:114
  146.3 1.5 collective-permute-start.33
  148.3 2.3 %collective-permute-done.32.refs_3_ = bf16[640,256]{1,0:T(8,128)(2,1)S(1)} collective-permute-done((bf16[640,256]{1,0:T(8,128)(2,1)S(1)}, bf16[640,256]{1,0:T(8,128)(2,1)S(1)}, u32[]{:S(2)}, u32[]{:S(2)}) %collective-permute-start.32) | collective-permute-done | bytes 327712 | tf_op jit(solution)/shard_map/ppermute | solution.py:114
  150.6 2.8 %collective-permute-done.33.refs_4_ = bf16[640,256]{1,0:T(8,128)(2,1)S(1)} collective-permute-done((bf16[640,256]{1,0:T(8,128)(2,1)S(1)}, bf16[640,256]{1,0:T(8,128)(2,1)S(1)}, u32[]{:S(2)}, u32[]{:S(2)}) %collective-permute-start.33) | collective-permute-done | bytes 327712 | tf_op jit(solution)/shard_map/ppermute | solution.py:114
  153.4 1.6 ffn_out.1
  155.1 0.8 collective-permute-start.35
  155.8 3.0 %collective-permute-start.36 = (bf16[256,256]{1,0:T(8,128)(2,1)S(1)}, bf16[256,256]{1,0:T(8,128)(2,1)S(1)}, u32[]{:S(2)}, u32[]{:S(2)}) collective-permute-start(bf16[256,256]{1,0:T(8,128)(2,1)S(1)} %get-tuple-element.43), channel_id=1, source_target_pairs={{0,3},{1,0},{2,1},{3,2},{4,7},{5,4},{6,5},{7,6},{8,11},{9,8},{10,9... | collective-permute-start | bytes 393224 | tf_op jit(solution)/shard_map/ppermute | solution.py:114
  158.9 3.1 %collective-permute-done.34 = bf16[256,256]{1,0:T(8,128)(2,1)S(1)} collective-permute-done((bf16[256,256]{1,0:T(8,128)(2,1)S(1)}, bf16[256,256]{1,0:T(8,128)(2,1)S(1)}, u32[]{:S(2)}, u32[]{:S(2)}) %collective-permute-start.34) | collective-permute-done | bytes 131104 | tf_op jit(solution)/shard_map/ppermute | solution.py:114
  162.0 3.1 %collective-permute-done.35 = bf16[256,256]{1,0:T(8,128)(2,1)S(1)} collective-permute-done((bf16[256,256]{1,0:T(8,128)(2,1)S(1)}, bf16[256,256]{1,0:T(8,128)(2,1)S(1)}, u32[]{:S(2)}, u32[]{:S(2)}) %collective-permute-start.35) | collective-permute-done | bytes 131104 | tf_op jit(solution)/shard_map/ppermute | solution.py:114
  165.3 1.2 collective-permute-done.37
  166.6 0.7 maximum_select_fusion
  (88 shorter events, 5.0 us)
Async XLA Ops:
  1.5 30.7 %copy-start.9 = (bf16[128,256]{1,0:T(8,128)(2,1)}, bf16[128,256]{1,0:T(8,128)(2,1)S(1)}, u32[]{:S(2)}) copy-start(bf16[128,256]{1,0:T(8,128)(2,1)S(1)} %get-tuple-element.50) | copy-start | bytes 196612
  1.5 1.4 collective-permute-start
  3.0 29.3 %copy-start.11 = (bf16[128,256]{1,0:T(8,128)(2,1)}, bf16[128,256]{1,0:T(8,128)(2,1)S(1)}, u32[]{:S(2)}) copy-start(bf16[128,256]{1,0:T(8,128)(2,1)S(1)} %collective-permute-done) | copy-start | bytes 196612
  3.0 37.7 %copy-start = (bf16[3,256,512]{2,1,0:T(8,128)(2,1)S(1)}, bf16[3,256,512]{2,1,0:T(8,128)(2,1)}, u32[]{:S(2)}) copy-start(bf16[3,256,512]{2,1,0:T(8,128)(2,1)} %refs_4_.2) | copy-start | bytes 2359300
  3.0 9.1 %collective-permute-start.3 = (bf16[256,256]{1,0:T(8,128)(2,1)S(1)}, bf16[256,256]{1,0:T(8,128)(2,1)S(1)}, u32[]{:S(2)}, u32[]{:S(2)}) collective-permute-start(bf16[256,256]{1,0:T(8,128)(2,1)S(1)} %pad_maximum_fusion.refs_0_), channel_id=1, source_target_pairs={{0,3},{1,0},{2,1},{3,2},{4,7},{5,4},{6,5},{7,6},{8,11},{9,8},{10,9... | collective-permute-start | bytes 393224 | tf_op jit(solution)/shard_map/ppermute | solution.py:114
  8.0 19.5 %collective-permute-start.5 = (bf16[3,256,512]{2,1,0:T(8,128)(2,1)}, bf16[3,256,512]{2,1,0:T(8,128)(2,1)S(1)}, u32[]{:S(2)}, u32[]{:S(2)}) collective-permute-start(bf16[3,256,512]{2,1,0:T(8,128)(2,1)} %refs_4_.2), channel_id=1, source_target_pairs={{0,8},{4,12},{8,0},{12,4},{16,24},{20,28},{24,16},{28,20},{1,9},{5... | collective-permute-start | bytes 2359304 | tf_op jit(solution)/shard_map/ppermute | solution.py:114
  9.5 20.3 %collective-permute-start.6 = (bf16[3,256,512]{2,1,0:T(8,128)(2,1)}, bf16[3,256,512]{2,1,0:T(8,128)(2,1)S(1)}, u32[]{:S(2)}, u32[]{:S(2)}) collective-permute-start(bf16[3,256,512]{2,1,0:T(8,128)(2,1)} %refs_4_.2), channel_id=1, source_target_pairs={{0,16},{4,20},{8,24},{12,28},{16,0},{20,4},{24,8},{28,12},{1,17},{... | collective-permute-start | bytes 2359304 | tf_op jit(solution)/shard_map/ppermute | solution.py:114
  11.0 9.4 %collective-permute-start.2 = (bf16[256,256]{1,0:T(8,128)(2,1)S(1)}, bf16[256,256]{1,0:T(8,128)(2,1)S(1)}, u32[]{:S(2)}, u32[]{:S(2)}) collective-permute-start(bf16[256,256]{1,0:T(8,128)(2,1)S(1)} %pad_maximum_fusion.refs_0_), channel_id=1, source_target_pairs={{0,2},{1,3},{2,0},{3,1},{4,6},{5,7},{6,4},{7,5},{8,10},{9,11},{10,... | collective-permute-start | bytes 393224 | tf_op jit(solution)/shard_map/ppermute | solution.py:114
  11.0 9.5 %collective-permute-start.1 = (bf16[256,256]{1,0:T(8,128)(2,1)S(1)}, bf16[256,256]{1,0:T(8,128)(2,1)S(1)}, u32[]{:S(2)}, u32[]{:S(2)}) collective-permute-start(bf16[256,256]{1,0:T(8,128)(2,1)S(1)} %pad_maximum_fusion.refs_0_), channel_id=1, source_target_pairs={{0,1},{1,2},{2,3},{3,0},{4,5},{5,6},{6,7},{7,4},{8,9},{9,10},{10,1... | collective-permute-start | bytes 393224 | tf_op jit(solution)/shard_map/ppermute | solution.py:114
  20.7 11.4 %collective-permute-start.4 = (f32[256]{0:T(256)S(1)}, f32[256]{0:T(256)S(1)}, u32[]{:S(2)}, u32[]{:S(2)}) collective-permute-start(f32[256]{0:T(256)S(1)} %add_add_fusion.1), channel_id=1, source_target_pairs={{0,4},{4,0},{8,12},{12,8},{16,20},{20,16},{24,28},{28,24},{1,5},{5... | collective-permute-start | bytes 3080 | tf_op jit(solution)/shard_map/ppermute | solution.py:114
  28.3 10.2 %collective-permute-start.7 = (bf16[3,256,256]{2,1,0:T(8,128)(2,1)}, bf16[3,256,256]{2,1,0:T(8,128)(2,1)S(1)}, u32[]{:S(2)}, u32[]{:S(2)}) collective-permute-start(bf16[3,256,256]{2,1,0:T(8,128)(2,1)} %split.32), channel_id=1, source_target_pairs={{0,16},{4,20},{8,24},{12,28},{16,0},{20,4},{24,8},{28,12},{1,17},{... | collective-permute-start | bytes 1179656 | tf_op jit(solution)/shard_map/ppermute | solution.py:114
  30.6 10.1 %collective-permute-start.8 = (bf16[3,256,256]{2,1,0:T(8,128)(2,1)}, bf16[3,256,256]{2,1,0:T(8,128)(2,1)}, u32[]{:S(2)}, u32[]{:S(2)}) collective-permute-start(bf16[3,256,256]{2,1,0:T(8,128)(2,1)} %split.33), channel_id=1, source_target_pairs={{0,8},{4,12},{8,0},{12,4},{16,24},{20,28},{24,16},{28,20},{1,9},{5... | collective-permute-start | bytes 1179656 | tf_op jit(solution)/shard_map/ppermute | solution.py:114
  32.3 14.0 %copy-start.7 = (bf16[512,256]{1,0:T(8,128)(2,1)S(1)}, bf16[512,256]{1,0:T(8,128)(2,1)}, u32[]{:S(2)}) copy-start(bf16[512,256]{1,0:T(8,128)(2,1)} %refs_0_.2) | copy-start | bytes 786436
  42.8 5.6 %collective-permute-start.9 = (bf16[128,1536]{1,0:T(8,128)(2,1)S(1)}, bf16[128,1536]{1,0:T(8,128)(2,1)S(1)}, u32[]{:S(2)}, u32[]{:S(2)}) collective-permute-start(bf16[128,1536]{1,0:T(8,128)(2,1)S(1)} %get-tuple-element.30), channel_id=1, source_target_pairs={{0,4},{4,0},{8,12},{12,8},{16,20},{20,16},{24,28},{28,24},{1,5},{5... | collective-permute-start | bytes 1179656 | tf_op jit(solution)/shard_map/ppermute | solution.py:114
  42.9 52.6 %collective-permute-start.23 = (bf16[2,256,1280]{2,1,0:T(8,128)(2,1)}, bf16[2,256,1280]{2,1,0:T(8,128)(2,1)S(1)}, u32[]{:S(2)}, u32[]{:S(2)}) collective-permute-start(bf16[2,256,1280]{2,1,0:T(8,128)(2,1)} %refs_4_.3), channel_id=1, source_target_pairs={{0,8},{4,12},{8,0},{12,4},{16,24},{20,28},{24,16},{28,20},{1,9},{5... | collective-permute-start | bytes 3932168 | tf_op jit(solution)/shard_map/ppermute | solution.py:114
  44.5 52.8 %collective-permute-start.24 = (bf16[2,256,1280]{2,1,0:T(8,128)(2,1)}, bf16[2,256,1280]{2,1,0:T(8,128)(2,1)S(1)}, u32[]{:S(2)}, u32[]{:S(2)}) collective-permute-start(bf16[2,256,1280]{2,1,0:T(8,128)(2,1)} %refs_4_.3), channel_id=1, source_target_pairs={{0,16},{4,20},{8,24},{12,28},{16,0},{20,4},{24,8},{28,12},{1,17},{... | collective-permute-start | bytes 3932168 | tf_op jit(solution)/shard_map/ppermute | solution.py:114
  46.3 34.0 %collective-permute-start.13 = (bf16[512,256]{1,0:T(8,128)(2,1)S(1)}, bf16[512,256]{1,0:T(8,128)(2,1)S(1)}, u32[]{:S(2)}, u32[]{:S(2)}) collective-permute-start(bf16[512,256]{1,0:T(8,128)(2,1)S(1)} %copy-done.7), channel_id=1, source_target_pairs={{0,8},{4,12},{8,0},{12,4},{16,24},{20,28},{24,16},{28,20},{1,9},{5... | collective-permute-start | bytes 786440 | tf_op jit(solution)/shard_map/ppermute | solution.py:114
  46.9 37.9 %collective-permute-start.14 = (bf16[512,256]{1,0:T(8,128)(2,1)S(1)}, bf16[512,256]{1,0:T(8,128)(2,1)S(1)}, u32[]{:S(2)}, u32[]{:S(2)}) collective-permute-start(bf16[512,256]{1,0:T(8,128)(2,1)S(1)} %copy-done.7), channel_id=1, source_target_pairs={{0,16},{4,20},{8,24},{12,28},{16,0},{20,4},{24,8},{28,12},{1,17},{... | collective-permute-start | bytes 786440 | tf_op jit(solution)/shard_map/ppermute | solution.py:114
  49.2 32.4 %copy-start.13 = (s32[255]{0:T(256)S(1)}, s32[255]{0:T(256)}, u32[]{:S(2)}) copy-start(s32[255]{0:T(256)} %param.15) | copy-start | bytes 3064
  55.5 34.0 %collective-permute-start.10 = (bf16[2,128,512]{2,1,0:T(8,128)(2,1)}, bf16[2,128,512]{2,1,0:T(8,128)(2,1)}, u32[]{:S(2)}, u32[]{:S(2)}) collective-permute-start(bf16[2,128,512]{2,1,0:T(8,128)(2,1)} %get-tuple-element.47.own_ref), channel_id=1, source_target_pairs={{0,4},{4,8},{8,12},{12,16},{16,20},{20,24},{24,28},{1,5},{5,9},{9,... | collective-permute-start | bytes 786440 | tf_op jit(solution)/shard_map/ppermute | solution.py:314
  80.4 14.4 %copy-start.2 = (bf16[512,256]{1,0:T(8,128)(2,1)}, bf16[512,256]{1,0:T(8,128)(2,1)S(1)}, u32[]{:S(2)}) copy-start(bf16[512,256]{1,0:T(8,128)(2,1)S(1)} %collective-permute-done.13.refs_1_) | copy-start | bytes 786436
  80.4 9.4 %collective-permute-start.11 = (bf16[2,128,512]{2,1,0:T(8,128)(2,1)}, bf16[2,128,512]{2,1,0:T(8,128)(2,1)}, u32[]{:S(2)}, u32[]{:S(2)}) collective-permute-start(bf16[2,128,512]{2,1,0:T(8,128)(2,1)} %get-tuple-element.47.own_ref), channel_id=1, source_target_pairs={{4,0},{8,4},{12,8},{16,12},{20,16},{24,20},{28,24},{5,1},{9,5},{13... | collective-permute-start | bytes 786440 | tf_op jit(solution)/shard_map/ppermute | solution.py:315
  84.8 10.0 %copy-start.4 = (bf16[512,256]{1,0:T(8,128)(2,1)}, bf16[512,256]{1,0:T(8,128)(2,1)S(1)}, u32[]{:S(2)}) copy-start(bf16[512,256]{1,0:T(8,128)(2,1)S(1)} %collective-permute-done.14.refs_2_) | copy-start | bytes 786436
  84.8 13.8 %collective-permute-start.15 = (bf16[256,256]{1,0:T(8,128)(2,1)S(1)}, bf16[256,256]{1,0:T(8,128)(2,1)S(1)}, u32[]{:S(2)}, u32[]{:S(2)}) collective-permute-start(bf16[256,256]{1,0:T(8,128)(2,1)S(1)} %split.34), channel_id=1, source_target_pairs={{0,16},{4,20},{8,24},{12,28},{16,0},{20,4},{24,8},{28,12},{1,17},{... | collective-permute-start | bytes 393224 | tf_op jit(solution)/shard_map/ppermute | solution.py:114
  89.5 9.1 %collective-permute-start.16 = (bf16[256,256]{1,0:T(8,128)(2,1)}, bf16[256,256]{1,0:T(8,128)(2,1)}, u32[]{:S(2)}, u32[]{:S(2)}) collective-permute-start(bf16[256,256]{1,0:T(8,128)(2,1)} %split.35), channel_id=1, source_target_pairs={{0,8},{4,12},{8,0},{12,4},{16,24},{20,28},{24,16},{28,20},{1,9},{5... | collective-permute-start | bytes 393224 | tf_op jit(solution)/shard_map/ppermute | solution.py:114
  94.8 3.9 %copy-start.6 = (bf16[128,512]{1,0:T(8,128)(2,1)S(1)}, bf16[128,512]{1,0:T(8,128)(2,1)}, u32[]{:S(2)}) copy-start(bf16[128,512]{1,0:T(8,128)(2,1)} %attention.1.own_in_ref) | copy-start | bytes 393220
  94.8 3.9 %copy-start.8 = (bf16[512,256]{1,0:T(8,128)(2,1)S(1)}, bf16[512,256]{1,0:T(8,128)(2,1)}, u32[]{:S(2)}) copy-start(bf16[512,256]{1,0:T(8,128)(2,1)} %refs_0_.2) | copy-start | bytes 786436
  94.8 3.9 %collective-permute-start.12 = (bf16[128,512]{1,0:T(8,128)(2,1)}, bf16[128,512]{1,0:T(8,128)(2,1)S(1)}, u32[]{:S(2)}, u32[]{:S(2)}) collective-permute-start(bf16[128,512]{1,0:T(8,128)(2,1)} %attention.1.own_in_ref), channel_id=1, source_target_pairs={{0,4},{4,0},{8,12},{12,8},{16,20},{20,16},{24,28},{28,24},{1,5},{5... | collective-permute-start | bytes 393224 | tf_op jit(solution)/shard_map/ppermute | solution.py:114
  95.5 3.2 %copy-start.3 = (bf16[512,256]{1,0:T(8,128)(2,1)S(1)}, bf16[512,256]{1,0:T(8,128)(2,1)}, u32[]{:S(2)}) copy-start(bf16[512,256]{1,0:T(8,128)(2,1)} %copy-done.2) | copy-start | bytes 786436
  95.5 3.2 %copy-start.5 = (bf16[512,256]{1,0:T(8,128)(2,1)S(1)}, bf16[512,256]{1,0:T(8,128)(2,1)}, u32[]{:S(2)}) copy-start(bf16[512,256]{1,0:T(8,128)(2,1)} %copy-done.4) | copy-start | bytes 786436
  96.4 16.9 %copy-start.10 = (bf16[128,256]{1,0:T(8,128)(2,1)S(1)}, bf16[128,256]{1,0:T(8,128)(2,1)}, u32[]{:S(2)}) copy-start(bf16[128,256]{1,0:T(8,128)(2,1)} %copy-done.9) | copy-start | bytes 196612
  96.4 16.9 %copy-start.12 = (bf16[128,256]{1,0:T(8,128)(2,1)S(1)}, bf16[128,256]{1,0:T(8,128)(2,1)}, u32[]{:S(2)}) copy-start(bf16[128,256]{1,0:T(8,128)(2,1)} %copy-done.11) | copy-start | bytes 196612
  96.4 33.7 %collective-permute-start.25 = (bf16[1,256,1280]{2,1,0:T(8,128)(2,1)}, bf16[1,256,1280]{2,1,0:T(8,128)(2,1)S(1)}, u32[]{:S(2)}, u32[]{:S(2)}) collective-permute-start(bf16[1,256,1280]{2,1,0:T(8,128)(2,1)} %split.36), channel_id=1, source_target_pairs={{0,16},{4,20},{8,24},{12,28},{16,0},{20,4},{24,8},{28,12},{1,17},{... | collective-permute-start | bytes 1966088 | tf_op jit(solution)/shard_map/ppermute | solution.py:114
  98.2 31.9 %collective-permute-start.26 = (bf16[1,256,1280]{2,1,0:T(8,128)(2,1)}, bf16[1,256,1280]{2,1,0:T(8,128)(2,1)}, u32[]{:S(2)}, u32[]{:S(2)}) collective-permute-start(bf16[1,256,1280]{2,1,0:T(8,128)(2,1)} %split.37), channel_id=1, source_target_pairs={{0,8},{4,12},{8,0},{12,4},{16,24},{20,28},{24,16},{28,20},{1,9},{5... | collective-permute-start | bytes 1966088 | tf_op jit(solution)/shard_map/ppermute | solution.py:114
  100.2 8.3 %collective-permute-start.17 = (bf16[256,256]{1,0:T(8,128)(2,1)S(1)}, bf16[256,256]{1,0:T(8,128)(2,1)S(1)}, u32[]{:S(2)}, u32[]{:S(2)}) collective-permute-start(bf16[256,256]{1,0:T(8,128)(2,1)S(1)} %get-tuple-element.33), channel_id=1, source_target_pairs={{0,1},{1,2},{2,3},{3,0},{4,5},{5,6},{6,7},{7,4},{8,9},{9,10},{10,1... | collective-permute-start | bytes 393224 | tf_op jit(solution)/shard_map/ppermute | solution.py:114
  100.3 12.9 %collective-permute-start.18 = (bf16[256,256]{1,0:T(8,128)(2,1)S(1)}, bf16[256,256]{1,0:T(8,128)(2,1)S(1)}, u32[]{:S(2)}, u32[]{:S(2)}) collective-permute-start(bf16[256,256]{1,0:T(8,128)(2,1)S(1)} %get-tuple-element.34), channel_id=1, source_target_pairs={{0,2},{1,3},{2,0},{3,1},{4,6},{5,7},{6,4},{7,5},{8,10},{9,11},{10,... | collective-permute-start | bytes 393224 | tf_op jit(solution)/shard_map/ppermute | solution.py:114
  101.3 11.9 %collective-permute-start.19 = (bf16[256,256]{1,0:T(8,128)(2,1)S(1)}, bf16[256,256]{1,0:T(8,128)(2,1)S(1)}, u32[]{:S(2)}, u32[]{:S(2)}) collective-permute-start(bf16[256,256]{1,0:T(8,128)(2,1)S(1)} %get-tuple-element.35), channel_id=1, source_target_pairs={{0,3},{1,0},{2,1},{3,2},{4,7},{5,4},{6,5},{7,6},{8,11},{9,8},{10,9... | collective-permute-start | bytes 393224 | tf_op jit(solution)/shard_map/ppermute | solution.py:114
  113.4 6.5 %collective-permute-start.22 = (bf16[256,256]{1,0:T(8,128)(2,1)S(1)}, bf16[256,256]{1,0:T(8,128)(2,1)}, u32[]{:S(2)}, u32[]{:S(2)}) collective-permute-start(bf16[256,256]{1,0:T(8,128)(2,1)S(1)} %get-tuple-element.45.refs_0_), channel_id=1, source_target_pairs={{0,3},{1,0},{2,1},{3,2},{4,7},{5,4},{6,5},{7,6},{8,11},{9,8},{10,9... | collective-permute-start | bytes 393224 | tf_op jit(solution)/shard_map/ppermute | solution.py:114
  115.9 12.5 %collective-permute-start.21 = (bf16[256,256]{1,0:T(8,128)(2,1)S(1)}, bf16[256,256]{1,0:T(8,128)(2,1)S(1)}, u32[]{:S(2)}, u32[]{:S(2)}) collective-permute-start(bf16[256,256]{1,0:T(8,128)(2,1)S(1)} %get-tuple-element.45.refs_0_), channel_id=1, source_target_pairs={{0,2},{1,3},{2,0},{3,1},{4,6},{5,7},{6,4},{7,5},{8,10},{9,11},{10,... | collective-permute-start | bytes 393224 | tf_op jit(solution)/shard_map/ppermute | solution.py:114
  117.4 12.7 %collective-permute-start.20 = (bf16[256,256]{1,0:T(8,128)(2,1)S(1)}, bf16[256,256]{1,0:T(8,128)(2,1)}, u32[]{:S(2)}, u32[]{:S(2)}) collective-permute-start(bf16[256,256]{1,0:T(8,128)(2,1)S(1)} %get-tuple-element.45.refs_0_), channel_id=1, source_target_pairs={{0,1},{1,2},{2,3},{3,0},{4,5},{5,6},{6,7},{7,4},{8,9},{9,10},{10,1... | collective-permute-start | bytes 393224 | tf_op jit(solution)/shard_map/ppermute | solution.py:114
  120.9 15.2 %collective-permute-start.30 = (bf16[1280,256]{1,0:T(8,128)(2,1)}, bf16[1280,256]{1,0:T(8,128)(2,1)S(1)}, u32[]{:S(2)}, u32[]{:S(2)}) collective-permute-start(bf16[1280,256]{1,0:T(8,128)(2,1)} %refs_0_.3), channel_id=1, source_target_pairs={{0,8},{4,12},{8,0},{12,4},{16,24},{20,28},{24,16},{28,20},{1,9},{5... | collective-permute-start | bytes 1966088 | tf_op jit(solution)/shard_map/ppermute | solution.py:114
  128.4 17.9 %collective-permute-start.31 = (bf16[1280,256]{1,0:T(8,128)(2,1)}, bf16[1280,256]{1,0:T(8,128)(2,1)S(1)}, u32[]{:S(2)}, u32[]{:S(2)}) collective-permute-start(bf16[1280,256]{1,0:T(8,128)(2,1)} %refs_0_.3), channel_id=1, source_target_pairs={{0,16},{4,20},{8,24},{12,28},{16,0},{20,4},{24,8},{28,12},{1,17},{... | collective-permute-start | bytes 1966088 | tf_op jit(solution)/shard_map/ppermute | solution.py:114
  133.5 14.4 %collective-permute-start.27 = (bf16[128,2560]{1,0:T(8,128)(2,1)S(1)}, bf16[128,2560]{1,0:T(8,128)(2,1)S(1)}, u32[]{:S(2)}, u32[]{:S(2)}) collective-permute-start(bf16[128,2560]{1,0:T(8,128)(2,1)S(1)} %get-tuple-element.38), channel_id=1, source_target_pairs={{0,4},{4,0},{8,12},{12,8},{16,20},{20,16},{24,28},{28,24},{1,5},{5... | collective-permute-start | bytes 1966088 | tf_op jit(solution)/shard_map/ppermute | solution.py:114
  134.7 1.4 collective-permute-start.28
  136.1 14.5 %collective-permute-start.32 = (bf16[640,256]{1,0:T(8,128)(2,1)S(1)}, bf16[640,256]{1,0:T(8,128)(2,1)S(1)}, u32[]{:S(2)}, u32[]{:S(2)}) collective-permute-start(bf16[640,256]{1,0:T(8,128)(2,1)S(1)} %split.38), channel_id=1, source_target_pairs={{0,16},{4,20},{8,24},{12,28},{16,0},{20,4},{24,8},{28,12},{1,17},{... | collective-permute-start | bytes 983048 | tf_op jit(solution)/shard_map/ppermute | solution.py:114
  146.3 7.1 %collective-permute-start.33 = (bf16[640,256]{1,0:T(8,128)(2,1)S(1)}, bf16[640,256]{1,0:T(8,128)(2,1)S(1)}, u32[]{:S(2)}, u32[]{:S(2)}) collective-permute-start(bf16[640,256]{1,0:T(8,128)(2,1)S(1)} %split.39), channel_id=1, source_target_pairs={{0,8},{4,12},{8,0},{12,4},{16,24},{20,28},{24,16},{28,20},{1,9},{5... | collective-permute-start | bytes 983048 | tf_op jit(solution)/shard_map/ppermute | solution.py:114
  148.0 5.4 %copy-start.1 = (bf16[1280,256]{1,0:T(8,128)(2,1)S(1)}, bf16[1280,256]{1,0:T(8,128)(2,1)}, u32[]{:S(2)}) copy-start(bf16[1280,256]{1,0:T(8,128)(2,1)} %refs_0_.3) | copy-start | bytes 1966084
  148.3 5.2 %collective-permute-start.29 = (bf16[128,1280]{1,0:T(8,128)(2,1)S(1)}, bf16[128,1280]{1,0:T(8,128)(2,1)S(1)}, u32[]{:S(2)}, u32[]{:S(2)}) collective-permute-start(bf16[128,1280]{1,0:T(8,128)(2,1)S(1)} %fusion.8.own_in_ref), channel_id=1, source_target_pairs={{0,4},{4,0},{8,12},{12,8},{16,20},{20,16},{24,28},{28,24},{1,5},{5... | collective-permute-start | bytes 983048 | tf_op jit(solution)/shard_map/ppermute | solution.py:114
  155.0 7.0 %collective-permute-start.34 = (bf16[256,256]{1,0:T(8,128)(2,1)S(1)}, bf16[256,256]{1,0:T(8,128)(2,1)S(1)}, u32[]{:S(2)}, u32[]{:S(2)}) collective-permute-start(bf16[256,256]{1,0:T(8,128)(2,1)S(1)} %get-tuple-element.41), channel_id=1, source_target_pairs={{0,1},{1,2},{2,3},{3,0},{4,5},{5,6},{6,7},{7,4},{8,9},{9,10},{10,1... | collective-permute-start | bytes 393224 | tf_op jit(solution)/shard_map/ppermute | solution.py:114
  155.1 10.0 %collective-permute-start.35 = (bf16[256,256]{1,0:T(8,128)(2,1)S(1)}, bf16[256,256]{1,0:T(8,128)(2,1)S(1)}, u32[]{:S(2)}, u32[]{:S(2)}) collective-permute-start(bf16[256,256]{1,0:T(8,128)(2,1)S(1)} %get-tuple-element.42), channel_id=1, source_target_pairs={{0,2},{1,3},{2,0},{3,1},{4,6},{5,7},{6,4},{7,5},{8,10},{9,11},{10,... | collective-permute-start | bytes 393224 | tf_op jit(solution)/shard_map/ppermute | solution.py:114
  155.8 9.3 %collective-permute-start.36 = (bf16[256,256]{1,0:T(8,128)(2,1)S(1)}, bf16[256,256]{1,0:T(8,128)(2,1)S(1)}, u32[]{:S(2)}, u32[]{:S(2)}) collective-permute-start(bf16[256,256]{1,0:T(8,128)(2,1)S(1)} %get-tuple-element.43), channel_id=1, source_target_pairs={{0,3},{1,0},{2,1},{3,2},{4,7},{5,4},{6,5},{7,6},{8,11},{9,8},{10,9... | collective-permute-start | bytes 393224 | tf_op jit(solution)/shard_map/ppermute | solution.py:114
  165.2 1.3 collective-permute-start.37

commit v3 on v2

v3 whole, which is shorter than its diff:
```python
import functools

import jax
import jax.numpy as jnp
from jax import lax
from jax.experimental import pallas as pl
from jax.experimental.pallas import tpu as pltpu
from jax.sharding import PartitionSpec as P

BLOCK = 128


epsilon = 1e-06
masked_score = -1e30
VMEM = pl.BlockSpec(memory_space=pltpu.VMEM)
SMEM = pl.BlockSpec(memory_space=pltpu.SMEM)


def bias_kernel(row_ref, seg_ref, table_ref, rel_ref, out_ref):
    heads, count, width = out_ref.shape
    rows = seg_ref.shape[0]
    row = row_ref[0]
    table = table_ref[...]
    rel = rel_ref[...]
    by_distance = jnp.zeros((heads, table.shape[1]), jnp.float32)
    for bucket in range(rel.shape[1]):
        by_distance = jnp.where(table == bucket, rel[:, bucket : bucket + 1], by_distance)
    by_distance = jnp.concatenate(
        [by_distance, jnp.zeros((heads, width - table.shape[1]), jnp.float32)], axis=1
    )

    def segment_row(index):
        clipped = jnp.clip(index, 0, rows - 1)
        found = seg_ref[pl.ds(clipped, 1), :].astype(jnp.float32)
        return jnp.where(index == clipped, found, -1.0)

    own = segment_row(row)
    query_seg = jnp.broadcast_to(own, (count, count)).T
    allowed = jnp.concatenate(
        [query_seg == segment_row(row - 1), query_seg == own, query_seg == segment_row(row + 1)],
        axis=1,
    )
    for head in range(heads):
        line = jnp.broadcast_to(by_distance[head : head + 1, :], (count, width))
        shifted = pltpu.roll(line, 1, 1, stride=1, stride_axis=0)
        out_ref[head] = jnp.where(allowed, shifted, masked_score)


def masked_bias(row, segment_ids, bucket_table, rel_bias, count):
    heads = rel_bias.shape[1]
    table = jnp.pad(bucket_table, (0, 1)).reshape(1, 2 * count)
    return pl.pallas_call(
        bias_kernel,
        out_shape=jax.ShapeDtypeStruct((heads, count, 3 * count), jnp.float32),
        in_specs=[SMEM, VMEM, VMEM, VMEM],
        out_specs=VMEM,
        name="masked_bias",
    )(row.reshape(1), segment_ids.reshape(-1, count), table, rel_bias.T)


def attention_kernel(q_ref, *refs):
    *key_refs, bias_ref, out_ref = refs
    key_refs, value_refs = key_refs[:3], key_refs[3:]
    heads, count, _ = bias_ref.shape
    width = q_ref.shape[1] // heads
    contract = (((1,), (1,)), ((), ()))
    parts = []
    for head in range(heads):
        cut = slice(head * width, (head + 1) * width)
        query = q_ref[:, cut]
        scores = jnp.concatenate(
            [
                lax.dot_general(query, ref[:, cut], contract, preferred_element_type=jnp.float32)
                for ref in key_refs
            ],
            axis=1,
        )
        scores = scores + bias_ref[head]
        top = jnp.max(scores, axis=1, keepdims=True)
        weights = jnp.exp(scores - top)
        denominator = jnp.sum(weights, axis=1, keepdims=True)
        rounded = weights.astype(jnp.bfloat16)
        total = sum(
            jnp.dot(
                rounded[:, i * count : (i + 1) * count],
                ref[:, cut],
                preferred_element_type=jnp.float32,
            )
            for i, ref in enumerate(value_refs)
        )
        parts.append(total / denominator)
    out_ref[...] = jnp.concatenate(parts, axis=1).astype(out_ref.dtype)


def attention(queries, low, own, high, bias):
    heads, count, span = bias.shape
    width = queries.shape[1]
    steps = heads // 2
    lanes = width // steps
    keys = pl.BlockSpec((count, lanes), lambda i: (0, i))
    values = pl.BlockSpec((count, lanes), lambda i: (0, i + steps))
    return pl.pallas_call(
        attention_kernel,
        out_shape=jax.ShapeDtypeStruct((count, width), jnp.bfloat16),
        grid=(steps,),
        in_specs=[keys] * 4 + [values] * 3 + [pl.BlockSpec((2, count, span), lambda i: (i, 0, 0))],
        out_specs=keys,
        cost_estimate=pl.CostEstimate(
            flops=4 * queries.size * span, bytes_accessed=4 * bias.size, transcendentals=bias.size
        ),
        name="attention",
    )(queries, low, own, high, low, own, high, bias)


def exchange(value, axis, partner):
    count = lax.axis_size(axis)
    return lax.ppermute(value, axis, [(i, partner(i) % count) for i in range(count)])


def other_core(value):
    return exchange(value, "row", lambda i: i ^ 1)


def pair_exchange(value, step):
    return exchange(value, "row", lambda i: i ^ (2 * step))


def shifted(value, step):
    return exchange(value, "col", lambda i: i + step)


def after(value, *earlier):
    return lax.optimization_barrier((value, *earlier))[0]


def near_pieces(weight):
    pairs = lax.axis_size("row") // 2
    if pairs == 4:
        return [pair_exchange(weight, 1), pair_exchange(weight, 2)]
    return [pair_exchange(weight, step) for step in range(1, pairs)]


def after_all(values, *earlier):
    return list(lax.optimization_barrier((*values, *earlier))[: len(values)])


def first_hop(weight, *earlier):
    weight = after(weight, *earlier)
    return weight, near_pieces(weight)


def far_pieces(near, axis):
    if len(near) != 2:
        return []
    first, _ = jnp.split(near[0], 2, axis=axis)
    _, second = jnp.split(near[1], 2, axis=axis)
    return [pair_exchange(first, 2), pair_exchange(second, 1)]


def norm_kernel(place_ref, gain_ref, *refs):
    *block_refs, kept_ref, given_ref = refs
    blocks = len(block_refs)
    core, col = lax.rem(place_ref[0], 2), place_ref[1]
    wide = [ref[...].astype(jnp.float32) for ref in block_refs]
    squares = sum(jnp.sum(block * block, axis=1, keepdims=True) for block in wide)
    half = wide[0].shape[1] // 2
    scale = lax.rsqrt(squares / (2 * half * blocks) + epsilon)
    for step, block in enumerate(wide):
        index = lax.rem(col - step + blocks, blocks)
        normed = (block * scale * gain_ref[pl.ds(index, 1), :]).astype(jnp.bfloat16)
        low, high = normed[:, :half], normed[:, half:]
        kept_ref[index] = jnp.where(core == 0, low, high)
        given_ref[index] = jnp.where(core == 0, high, low)


def norm_tokens(place, gain, token_blocks):
    count, width = token_blocks[0].shape
    shape = jax.ShapeDtypeStruct((len(token_blocks), count, width // 2), jnp.bfloat16)
    return pl.pallas_call(
        norm_kernel,
        out_shape=(shape, shape),
        in_specs=[SMEM] + [VMEM] * (1 + len(token_blocks)),
        out_specs=(VMEM, VMEM),
        name="norm_tokens",
    )(place, gain, *token_blocks)


def multiply_pieces(groups, held, pair, piece, width, own_refs, send_refs):
    blocks, tokens_two, _ = held.shape
    count = tokens_two // 2
    tile = min(256, width, held.shape[2])
    for group, own_ref, send_ref in zip(groups, own_refs, send_refs):
        for place, part in enumerate(group):
            for start in range(0, width, tile):
                stop = min(start + tile, width)
                total = None
                for step in range(blocks):
                    weight = piece(step, part, start, stop)
                    term = jnp.dot(held[pair ^ step], weight, preferred_element_type=jnp.float32)
                    total = term if total is None else total + term
                where = slice(place * width + start, place * width + stop)
                own_ref[:, where] = total[:count]
                send_ref[:, where] = total[count:].astype(send_ref.dtype)


def pack_kernel(qkv_ref, out_ref, packed_ref):
    parts, depth, width = qkv_ref.shape
    row = 0
    for part in range(parts):
        for start in range(0, width, depth):
            packed_ref[row : row + depth, :] = qkv_ref[part, :, start : start + depth]
            row += depth
    packed_ref[row:, :] = out_ref[...]


def packed(w_qkv, w_out):
    parts, depth, width = w_qkv.shape
    count = parts * width // depth
    return pl.pallas_call(
        pack_kernel,
        out_shape=jax.ShapeDtypeStruct((count * depth + width, depth), w_qkv.dtype),
        in_specs=[VMEM, VMEM],
        out_specs=VMEM,
        name="pack",
    )(w_qkv, w_out)


def qkv_kernel(place_ref, own_in_ref, other_in_ref, *refs):
    *weight_refs, own_q, own_kv, send_q, send_kv, held = refs
    count = own_in_ref.shape[1]
    held[:, :count] = own_in_ref[...]
    held[:, count:] = other_in_ref[...]
    blocks, depth = held.shape[0], weight_refs[0].shape[1]
    direct = blocks - 1 if len(weight_refs) == blocks + 1 else blocks
    width = own_q.shape[1]

    def piece(step, part, start, stop):
        row = (part * width // depth + start // depth) * depth
        offset = start % depth
        if step < direct:
            return weight_refs[step][row : row + depth, offset : offset + stop - start]
        half = weight_refs[direct].shape[0]
        row = row - row // half * half
        which = (part * width + start) // (half // depth * depth)
        return weight_refs[direct + which][row : row + depth, offset : offset + stop - start]

    multiply_pieces(
        ((0,), (1, 2)), held, place_ref[0] // 2, piece, width, (own_q, own_kv), (send_q, send_kv)
    )


def project_qkv(place, own, other, pieces):
    blocks, count, depth = own.shape
    width = 2 * depth
    shapes = [jax.ShapeDtypeStruct((count, n * width), jnp.float32) for n in (1, 2)] * 2
    return pl.pallas_call(
        qkv_kernel,
        out_shape=tuple(shapes),
        in_specs=[SMEM] + [VMEM] * (2 + len(pieces)),
        out_specs=tuple([VMEM] * 4),
        scratch_shapes=[pltpu.VMEM((blocks, 2 * count, depth), jnp.bfloat16)],
        compiler_params=pltpu.CompilerParams(vmem_limit_bytes=16 << 20),
        cost_estimate=pl.CostEstimate(
            flops=12 * count * depth * blocks * width,
            bytes_accessed=6 * depth * blocks * width,
            transcendentals=0,
        ),
        name="qkv",
    )(place, own, other, *pieces)


def ffn_in_kernel(place_ref, gain_ref, *refs):
    blocks = lax.axis_size("col")
    block_refs, refs = refs[:blocks], refs[blocks:]
    *weight_refs, own_ref, send_ref, held = refs
    row, col = place_ref[0], place_ref[1]
    for step, ref in enumerate(block_refs):
        index = lax.rem(col - step + blocks, blocks)
        gain = gain_ref[pl.ds(2 * index + lax.rem(row, 2), 1), :]
        held[index] = (ref[...].astype(jnp.float32) * gain).astype(jnp.bfloat16)
    direct = blocks - 1 if len(weight_refs) == blocks + 1 else blocks

    def piece(step, part, start, stop):
        if step < direct:
            return weight_refs[step][part, :, start:stop]
        return weight_refs[direct + part][0, :, start:stop]

    width = weight_refs[0].shape[2]
    multiply_pieces(((0, 1),), held, row // 2, piece, width, (own_ref,), (send_ref,))


def project_ffn(place, gain, token_blocks, pieces):
    tokens_two, depth = token_blocks[0].shape
    blocks, count = len(token_blocks), tokens_two // 2
    columns = 2 * pieces[0].shape[2]
    return pl.pallas_call(
        ffn_in_kernel,
        out_shape=(
            jax.ShapeDtypeStruct((count, columns), jnp.float32),
            jax.ShapeDtypeStruct((count, columns), jnp.bfloat16),
        ),
        in_specs=[SMEM] + [VMEM] * (1 + blocks + len(pieces)),
        out_specs=(VMEM, VMEM),
        scratch_shapes=[pltpu.VMEM((blocks, tokens_two, depth), jnp.bfloat16)],
        compiler_params=pltpu.CompilerParams(vmem_limit_bytes=16 << 20),
        cost_estimate=pl.CostEstimate(
            flops=2 * tokens_two * depth * blocks * columns,
            bytes_accessed=2 * depth * blocks * columns,
            transcendentals=0,
        ),
        name="ffn_in",
    )(place, gain, *token_blocks, *pieces)


def columns_kernel(first, place_ref, own_in_ref, other_in_ref, *refs):
    blocks = lax.axis_size("col")
    *weight_refs, own_ref = refs[: len(refs) - blocks]
    send_refs, held = refs[len(refs) - blocks : -1], refs[-1]
    row, col = place_ref[0], place_ref[1]
    pair = row // 2
    hidden = jnp.concatenate([own_in_ref[...], other_in_ref[...]], axis=0)
    far = len(weight_refs) == blocks + 1
    direct = blocks - 1 if far else blocks
    for step in range(blocks):
        if step < direct:
            total = jnp.dot(hidden, weight_refs[step][first:, :], preferred_element_type=jnp.float32)
        elif first:
            skipped = first - weight_refs[direct].shape[0]
            total = jnp.dot(
                hidden, weight_refs[direct + 1][skipped:, :], preferred_element_type=jnp.float32
            )
        else:
            half = hidden.shape[1] // 2
            total = jnp.dot(
                hidden[:, :half], weight_refs[direct][...], preferred_element_type=jnp.float32
            ) + jnp.dot(
                hidden[:, half:], weight_refs[direct + 1][...], preferred_element_type=jnp.float32
            )
        held[lax.rem((pair ^ step) - col + blocks, blocks)] = total
    own_ref[...] = held[0]
    for step in range(1, blocks):
        send_refs[step - 1][...] = held[step].astype(jnp.bfloat16)


def columns(place, own, other, pieces, name):
    count, depth = own.shape
    width = pieces[0].shape[1]
    blocks = lax.axis_size("col")
    return pl.pallas_call(
        functools.partial(columns_kernel, pieces[0].shape[0] - depth),
        out_shape=(
            jax.ShapeDtypeStruct((2 * count, width), jnp.float32),
            *[jax.ShapeDtypeStruct((2 * count, width), jnp.bfloat16)] * (blocks - 1),
        ),
        in_specs=[SMEM] + [VMEM] * (2 + len(pieces)),
        out_specs=tuple([VMEM] * blocks),
        scratch_shapes=[pltpu.VMEM((blocks, 2 * count, width), jnp.float32)],
        compiler_params=pltpu.CompilerParams(vmem_limit_bytes=16 << 20),
        cost_estimate=pl.CostEstimate(
            flops=4 * count * depth * width * blocks,
            bytes_accessed=2 * depth * width * blocks,
            transcendentals=0,
        ),
        name=name,
    )(place, own, other, *pieces)


def summed(own, sends, residual):
    total = own + residual.astype(jnp.float32)
    for step, send in enumerate(sends, 1):
        total = total + shifted(send, step).astype(jnp.float32)
    return total.astype(jnp.bfloat16)


def gathered(block):
    return [block] + [shifted(block, step) for step in range(1, lax.axis_size("col"))]


def square_sums(blocks):
    return sum(jnp.sum(jnp.square(b.astype(jnp.float32)), axis=1) for b in blocks)


def per_device(
    tokens,
    segment_ids,
    bucket_table,
    slot_index,
    gain_attn,
    w_qkv,
    rel_bias,
    w_out,
    gain_ffn,
    w_in,
    w_down,
):
    rows, cols = lax.axis_size("row"), lax.axis_size("col")
    count, width = tokens.shape
    half = width // 2
    features = width * cols
    row, col = lax.axis_index("row"), lax.axis_index("col")
    core = row % 2
    place = jnp.stack([row, col]).astype(jnp.int32)

    first = packed(w_qkv, w_out)
    first_near = near_pieces(first)
    token_blocks = gathered(tokens)
    kept, given = norm_tokens(place, gain_attn.reshape(cols, width), token_blocks)
    received = other_core(after(given, *first_near))
    token_block = jnp.concatenate(
        [
            jnp.where(core == 0, tokens[:, :half], tokens[:, half:]),
            other_core(jnp.where(core == 0, tokens[:, half:], tokens[:, :half])),
        ],
        axis=0,
    )
    bias = masked_bias(row, segment_ids, bucket_table, rel_bias, count)
    first_far = far_pieces(first_near, 0)
    first_pieces = [first, *first_near, *first_far]
    w_down, down_near = first_hop(w_down, received)
    kept, bias, token_block = lax.optimization_barrier((kept, bias, token_block))
    own_q, own_kv, send_q, send_kv = project_qkv(
        place, kept, received, first_pieces
    )
    key_value = (own_kv + other_core(send_kv)).astype(jnp.bfloat16)
    queries = (own_q + other_core(after(send_q, key_value))).astype(jnp.bfloat16)
    forward = [(i, i + 1) for i in range(rows - 1)]
    backward = [(target, source) for source, target in forward]
    low = lax.ppermute(key_value, "row", forward)
    high = lax.ppermute(key_value, "row", backward)
    low, high, *down_near = lax.optimization_barrier((low, high, *down_near))
    in_near = near_pieces(after(w_in, low, high, *down_near))
    context = attention(queries, low, key_value, high, bias)
    own, *sends = columns(
        place, context, other_core(context), first_pieces, "attention_out"
    )
    middle = summed(own, sends, token_block)
    in_far = far_pieces(after_all(in_near, middle), 0)

    middle_blocks = gathered(middle)
    squares = square_sums(middle_blocks)
    squares = squares[:count] + other_core(squares[count:])
    scale = lax.rsqrt(squares / features + epsilon)[:, None]
    down_far = far_pieces(after_all(down_near, middle_blocks[1]), 0)
    own, send = project_ffn(
        place, gain_ffn.reshape(rows, -1), middle_blocks, [w_in, *in_near, *in_far]
    )
    other_sum, *down_far = lax.optimization_barrier((other_core(send), *down_far))
    branches = (own + other_sum.astype(jnp.float32)) * scale
    inner = branches.shape[1] // 2
    hidden = (
        jax.nn.gelu(branches[:, :inner], approximate=True) * branches[:, inner:]
    ).astype(jnp.bfloat16)
    own, *sends = columns(
        place, hidden, other_core(hidden), [w_down, *down_near, *down_far], "ffn_out"
    )
    result = summed(own, sends, middle)
    received = other_core(result[count:])
    output = jnp.where(
        core == 0,
        jnp.concatenate([result[:count], received], axis=1),
        jnp.concatenate([received, result[:count]], axis=1),
    )

    stacked = jnp.stack([key_value[:, :width], key_value[:, width:]])
    blocks = stacked.reshape(2, slot_index.shape[1], BLOCK, width)
    kv_cache = (
        jnp.zeros_like(blocks).at[:, slot_index[0]].set(blocks).reshape(2, count, width)
    )
    return (output, kv_cache)


def solution(mesh):
    return jax.shard_map(
        per_device,
        mesh=mesh,
        in_specs=(
            P("row", "col"),
            P(),
            P(),
            P("row", None),
            P(),
            P(None, "row", "col"),
            P(None, "col"),
            P("col", "row"),
            P(),
            P(None, "row", "col"),
            P("col", "row"),
        ),
        out_specs=(P("row", "col"), P(None, "row", "col")),
        check_vma=False,
    )
```

time: 168 us -> 152 us (0.905)
  waiting for transfers between devices: 85.9 us -> 65.8 us
  Pallas kernels: 16.1 us -> 22.7 us
  local copies, waits for them, and re-layouts: 11.7 us -> 9.41 us
    ppermute x36 -> x33, waiting for transfers between devices: 85.9 us -> 65.8 us  [exchange(): lax.ppermute(value, axis, [(i, partner(i) % count) for i in range(count)])]
    pallas_call x5 -> x7, Pallas kernels: 13.5 us -> 20.1 us  [the longest x1 5.52 us: attention(): pl.pallas_call(attention_kernel, out_shape=jax.ShapeDtypeStruct((count, w...]
    reduce_sum x8 -> x4, other arithmetic: 2.77 us -> 0.51 us  [square_sums(): jnp.sum(jnp.square(b.astype(jnp.float32)), axis=1)]
    unnamed x28 -> x34, local copies, waits for them, and re-layouts: 0.06 us -> 2.26 us
    reshape x2 -> x1, local copies, waits for them, and re-layouts: 2.61 us -> 0.61 us  [per_device(): gain_attn.reshape(cols, width)]
    convert_element_type x1 -> x0, local copies, waits for them, and re-layouts: 1.92 us -> none  [per_device(): (own + other_core(send).astype(jnp.float32)).astype(jnp.bfloat16)]
    ppermute x36 -> x33, starting transfers between devices: 39.7 us -> 41 us  [exchange(): lax.ppermute(value, axis, [(i, partner(i) % count) for i in range(count)])]
  transfers between devices with their start and end apart: 38 -> 35, of which waited for: 17 -> 16; matrix products, arithmetic and copies ran while one was open for 11% -> 8% of each run, Pallas kernels for 7% -> 10%
where the time goes in v3:
time: 152 us; the launch traced here: 151 us
  waiting for transfers between devices  65.8 us (43%)
  starting transfers between devices  44.1 us (29%)
  Pallas kernels  22.7 us (15%)
  local copies, waits for them, and re-layouts  9.41 us (6%)
  other arithmetic  7.61 us (5%)
  between operations  1.61 us (1%)
    ppermute x33, waiting for transfers between devices, exchange(): lax.ppermute(value, axis, [(i, partner(i) % count) for i in range(count)])  65.8 us
    ppermute x33, starting transfers between devices, exchange(): lax.ppermute(value, axis, [(i, partner(i) % count) for i in range(count)])  41 us
    pallas_call x1, Pallas kernels, attention(): pl.pallas_call(attention_kernel, out_shape=jax.ShapeDtypeStruct((count, w...  5.52 us
    pallas_call x2, Pallas kernels, columns(): pl.pallas_call(functools.partial(columns_kernel, pieces[0].shape[0] - dep...  4.12 us
    pallas_call x1, Pallas kernels, project_ffn(): pl.pallas_call(ffn_in_kernel, out_shape=(jax.ShapeDtypeStruct((count, col...  3.74 us
  transfers between devices with their start and end apart: 35, of which 16 were waited for; matrix products, arithmetic and copies ran while one was open for 8% of the time, Pallas kernels for 10%

profile of v3, /device:TPU:0, one launch (start us, length us, event | category | flops | bytes accessed | tf_op | source)
XLA Modules:
  0.0 151.3 jit_solution(7726847388419672540)
XLA Ops:
  0.6 2.3 %pack.1.refs_0_ = bf16[2048,256]{1,0:T(8,128)(2,1)} custom-call(bf16[3,256,512]{2,1,0:T(8,128)(2,1)} %qkv_ref.1, bf16[512,256]{1,0:T(8,128)(2,1)} %out_ref.1), custom_call_target="tpu_custom_call" | custom-call | tf_op jit(solution)/shard_map/pack/pallas_call | solution.py:219
  2.9 2.9 %collective-permute-start.4 = (bf16[2048,256]{1,0:T(8,128)(2,1)}, bf16[2048,256]{1,0:T(8,128)(2,1)S(1)}, u32[]{:S(2)}, u32[]{:S(2)}) collective-permute-start(bf16[2048,256]{1,0:T(8,128)(2,1)} %pack.1.refs_0_), channel_id=1, source_target_pairs={{0,8},{4,12},{8,0},{12,4},{16,24},{20,28},{24,16},{28,20},{1,9},{5... | collective-permute-start | bytes 3145736 | tf_op jit(solution)/shard_map/ppermute | solution.py:117
  5.8 1.5 %collective-permute-start.5 = (bf16[2048,256]{1,0:T(8,128)(2,1)}, bf16[2048,256]{1,0:T(8,128)(2,1)S(1)}, u32[]{:S(2)}, u32[]{:S(2)}) collective-permute-start(bf16[2048,256]{1,0:T(8,128)(2,1)} %pack.1.refs_0_), channel_id=1, source_target_pairs={{0,16},{4,20},{8,24},{12,28},{16,0},{20,4},{24,8},{28,12},{1,17},{... | collective-permute-start | bytes 3145736 | tf_op jit(solution)/shard_map/ppermute | solution.py:117
  7.4 1.6 %collective-permute-start = (bf16[128,512]{1,0:T(8,128)(2,1)S(1)}, bf16[128,512]{1,0:T(8,128)(2,1)S(1)}, u32[]{:S(2)}, u32[]{:S(2)}) collective-permute-start(bf16[128,512]{1,0:T(8,128)(2,1)S(1)} %copy-done.10), channel_id=1, source_target_pairs={{0,1},{1,2},{2,3},{3,0},{4,5},{5,6},{6,7},{7,4},{8,9},{9,10},{10,1... | collective-permute-start | bytes 393224 | tf_op jit(solution)/shard_map/ppermute | solution.py:117
  8.9 2.6 %collective-permute-start.1 = (bf16[128,512]{1,0:T(8,128)(2,1)S(1)}, bf16[128,512]{1,0:T(8,128)(2,1)S(1)}, u32[]{:S(2)}, u32[]{:S(2)}) collective-permute-start(bf16[128,512]{1,0:T(8,128)(2,1)S(1)} %copy-done.10), channel_id=1, source_target_pairs={{0,2},{1,3},{2,0},{3,1},{4,6},{5,7},{6,4},{7,5},{8,10},{9,11},{10,... | collective-permute-start | bytes 393224 | tf_op jit(solution)/shard_map/ppermute | solution.py:117
  11.5 1.3 collective-permute-start.2
  12.9 16.3 %collective-permute-done.4.refs_1_ = bf16[2048,256]{1,0:T(8,128)(2,1)S(1)} collective-permute-done((bf16[2048,256]{1,0:T(8,128)(2,1)}, bf16[2048,256]{1,0:T(8,128)(2,1)S(1)}, u32[]{:S(2)}, u32[]{:S(2)}) %collective-permute-start.4) | collective-permute-done | bytes 1048608 | tf_op jit(solution)/shard_map/ppermute | solution.py:117
  29.2 0.8 split.24
  30.1 1.8 %collective-permute-start.7 = (bf16[1024,256]{1,0:T(8,128)(2,1)}, bf16[1024,256]{1,0:T(8,128)(2,1)}, u32[]{:S(2)}, u32[]{:S(2)}) collective-permute-start(bf16[1024,256]{1,0:T(8,128)(2,1)} %split.24), channel_id=1, source_target_pairs={{0,16},{4,20},{8,24},{12,28},{16,0},{20,4},{24,8},{28,12},{1,17},{... | collective-permute-start | bytes 1572872 | tf_op jit(solution)/shard_map/ppermute | solution.py:117
  31.8 0.8 split.25
  32.6 1.5 collective-permute-start.8
  34.1 0.6 reshape.60.gain_ref
  34.8 0.6 pad_add_fusion.place_ref
  35.4 0.6 copy-done.11
  36.0 2.2 %norm_tokens.1 = (bf16[4,128,256]{2,1,0:T(8,128)(2,1)}, bf16[4,128,256]{2,1,0:T(8,128)(2,1)}) custom-call(s32[2]{0:T(128)} %pad_add_fusion.place_ref, f32[4,512]{1,0:T(4,128)} %reshape.60.gain_ref, bf16[128,512]{1,0:T(8,128)(2,1)} %refs_0_.1, bf16[128,512]{1,0:T(8,128)(2,1)} %copy-done.11, bf16[128,512]{1,0:T(8,128)(2,1)} %copy-done.12, ...), custom_call_target="tpu_custom_call" | custom-call | tf_op jit(solution)/shard_map/norm_tokens/pallas_call | solution.py:179
  38.3 1.6 %broadcast_select_fusion.1 = (bf16[128,256]{1,0:T(8,128)(2,1)}, bf16[128,256]{1,0:T(8,128)(2,1)S(1)}) fusion(pred[]{:T(512)S(6)} %eq.4, bf16[128,512]{1,0:T(8,128)(2,1)} %refs_0_.1), kind=kLoop, calls=%fused_computation.30 | loop fusion | flops 65536 | bytes 262145 | tf_op jit(solution)/shard_map/jit(_where)/select_n | solution.py:411
  40.3 0.6 pad.6
  40.9 2.5 %masked_bias.1.refs_6_ = f32[8,128,384]{2,1,0:T(8,128)} custom-call(s32[1]{0:T(128)} %bitcast.row_ref, s32[8,128]{1,0:T(8,128)} %bitcast.13, s32[1,256]{1,0:T(1,128)} %bitcast.15, f32[8,32]{1,0:T(8,128)} %bitcast.14), custom_call_target="tpu_custom_call" | custom-call | tf_op jit(solution)/shard_map/masked_bias/pallas_call | solution.py:52
  43.4 0.6 copy-done.13
  44.0 0.9 pad_maximum_fusion
  45.5 2.3 %qkv.1 = (f32[128,512]{1,0:T(8,128)S(1)}, f32[128,1024]{1,0:T(8,128)S(1)}, f32[128,512]{1,0:T(8,128)S(1)}, f32[128,1024]{1,0:T(8,128)S(1)}) custom-call(s32[2]{0:T(128)S(1)} %copy-done.5, bf16[4,128,256]{2,1,0:T(8,128)(2,1)S(1)} %copy-done.4, bf16[4,128,256]{2,1,0:T(8,128)(2,1)} %collective-permute-done.6.other_in_ref, bf16[2048,256]{1,0:T(8,128)(2,1)S(1)} %copy-done, ...), custom_call_target="tpu_custom_call" | custom-call | flops 805306368 | bytes 3145728 | tf_op jit(solution)/shard_map/qkv/pallas_call | solution.py:256
  47.9 1.6 %collective-permute-start.13 = (bf16[1280,256]{1,0:T(8,128)(2,1)S(1)}, bf16[1280,256]{1,0:T(8,128)(2,1)}, u32[]{:S(2)}, u32[]{:S(2)}) collective-permute-start(bf16[1280,256]{1,0:T(8,128)(2,1)S(1)} %copy-done.1), channel_id=1, source_target_pairs={{0,8},{4,12},{8,0},{12,4},{16,24},{20,28},{24,16},{28,20},{1,9},{5... | collective-permute-start | bytes 1966088 | tf_op jit(solution)/shard_map/ppermute | solution.py:117
  50.0 1.9 %collective-permute-start.11 = (bf16[128,1024]{1,0:T(8,128)(2,1)S(1)}, bf16[128,1024]{1,0:T(8,128)(2,1)S(1)}, u32[]{:S(2)}, u32[]{:S(2)}) collective-permute-start(bf16[128,1024]{1,0:T(8,128)(2,1)S(1)} %add_convert_fusion.refs_1_.refs_4_), channel_id=1, source_target_pairs={{0,4},{4,8},{8,12},{12,16},{16,20},{20,24},{24,28},{1,5},{5,9},{9,... | collective-permute-start | bytes 786440 | tf_op jit(solution)/shard_map/ppermute | solution.py:428
  51.9 1.3 collective-permute-start.12
  53.2 12.4 %collective-permute-done.13.refs_1_ = bf16[1280,256]{1,0:T(8,128)(2,1)} collective-permute-done((bf16[1280,256]{1,0:T(8,128)(2,1)S(1)}, bf16[1280,256]{1,0:T(8,128)(2,1)}, u32[]{:S(2)}, u32[]{:S(2)}) %collective-permute-start.13) | collective-permute-done | bytes 655392 | tf_op jit(solution)/shard_map/ppermute | solution.py:117
  65.6 0.8 collective-permute-done.14.refs_2_
  66.3 3.8 %collective-permute-start.22 = (bf16[2,256,1280]{2,1,0:T(8,128)(2,1)}, bf16[2,256,1280]{2,1,0:T(8,128)(2,1)}, u32[]{:S(2)}, u32[]{:S(2)}) collective-permute-start(bf16[2,256,1280]{2,1,0:T(8,128)(2,1)} %refs_4_.1), channel_id=1, source_target_pairs={{0,8},{4,12},{8,0},{12,4},{16,24},{20,28},{24,16},{28,20},{1,9},{5... | collective-permute-start | bytes 3932168 | tf_op jit(solution)/shard_map/ppermute | solution.py:117
  70.2 2.1 %collective-permute-start.23 = (bf16[2,256,1280]{2,1,0:T(8,128)(2,1)}, bf16[2,256,1280]{2,1,0:T(8,128)(2,1)}, u32[]{:S(2)}, u32[]{:S(2)}) collective-permute-start(bf16[2,256,1280]{2,1,0:T(8,128)(2,1)} %refs_4_.1), channel_id=1, source_target_pairs={{0,16},{4,20},{8,24},{12,28},{16,0},{20,4},{24,8},{28,12},{1,17},{... | collective-permute-start | bytes 3932168 | tf_op jit(solution)/shard_map/ppermute | solution.py:117
  72.2 1.5 %collective-permute-done.10 = f32[128,512]{1,0:T(8,128)S(1)} collective-permute-done((f32[128,512]{1,0:T(8,128)S(1)}, f32[128,512]{1,0:T(8,128)S(1)}, u32[]{:S(2)}, u32[]{:S(2)}) %collective-permute-start.10) | collective-permute-done | bytes 262176 | tf_op jit(solution)/shard_map/ppermute | solution.py:117
  73.8 0.7 add_convert_fusion.2.q_ref
  74.5 5.5 %attention.1.own_in_ref = bf16[128,512]{1,0:T(8,128)(2,1)} custom-call(bf16[128,512]{1,0:T(8,128)(2,1)} %add_convert_fusion.2.q_ref, bf16[128,1024]{1,0:T(8,128)(2,1)} %copy-done.8, bf16[128,1024]{1,0:T(8,128)(2,1)} %copy-done.6, bf16[128,1024]{1,0:T(8,128)(2,1)} %copy-done.9, bf16[128,1024]{1,0:T(8,128)(2,1)} %copy-done.8, bf16[128,1024]{1,0:T(8,128)(2,1)} %copy-done.6, ...), custom_call_target="tpu_custom_call" | custom-call | flops 100663296 | bytes 1572864 | tf_op jit(solution)/shard_map/attention/pallas_call | solution.py:102
  80.1 1.4 collective-permute-done.15.other_in_ref
  81.5 0.9 copy-done.3
  82.5 1.8 %attention_out.1 = (f32[256,256]{1,0:T(8,128)S(1)}, bf16[256,256]{1,0:T(8,128)(2,1)S(1)}, bf16[256,256]{1,0:T(8,128)(2,1)S(1)}, bf16[256,256]{1,0:T(8,128)(2,1)S(1)}) custom-call(s32[2]{0:T(128)S(1)} %copy-done.5, bf16[128,512]{1,0:T(8,128)(2,1)S(1)} %copy-done.3, bf16[128,512]{1,0:T(8,128)(2,1)S(1)} %collective-permute-done.15.other_in_ref, ...), custom_call_target="tpu_custom_call" | custom-call | flops 268435456 | bytes 1048576 | tf_op jit(solution)/shard_map/attention_out/pallas_call | solution.py:349
  84.3 3.6 %collective-permute-start.18 = (bf16[256,256]{1,0:T(8,128)(2,1)S(1)}, bf16[256,256]{1,0:T(8,128)(2,1)S(1)}, u32[]{:S(2)}, u32[]{:S(2)}) collective-permute-start(bf16[256,256]{1,0:T(8,128)(2,1)S(1)} %get-tuple-element.65), channel_id=1, source_target_pairs={{0,3},{1,0},{2,1},{3,2},{4,7},{5,4},{6,5},{7,6},{8,11},{9,8},{10,9... | collective-permute-start | bytes 393224 | tf_op jit(solution)/shard_map/ppermute | solution.py:117
  87.9 1.0 collective-permute-start.16
  88.9 2.9 %collective-permute-done.18 = bf16[256,256]{1,0:T(8,128)(2,1)S(1)} collective-permute-done((bf16[256,256]{1,0:T(8,128)(2,1)S(1)}, bf16[256,256]{1,0:T(8,128)(2,1)S(1)}, u32[]{:S(2)}, u32[]{:S(2)}) %collective-permute-start.18) | collective-permute-done | bytes 131104 | tf_op jit(solution)/shard_map/ppermute | solution.py:117
  91.8 7.8 %collective-permute-done.17 = bf16[256,256]{1,0:T(8,128)(2,1)S(1)} collective-permute-done((bf16[256,256]{1,0:T(8,128)(2,1)S(1)}, bf16[256,256]{1,0:T(8,128)(2,1)S(1)}, u32[]{:S(2)}, u32[]{:S(2)}) %collective-permute-start.17) | collective-permute-done | bytes 131104 | tf_op jit(solution)/shard_map/ppermute | solution.py:117
  99.8 2.1 %collective-permute-done.23.refs_6_ = bf16[2,256,1280]{2,1,0:T(8,128)(2,1)} collective-permute-done((bf16[2,256,1280]{2,1,0:T(8,128)(2,1)}, bf16[2,256,1280]{2,1,0:T(8,128)(2,1)}, u32[]{:S(2)}, u32[]{:S(2)}) %collective-permute-start.23) | collective-permute-done | bytes 1310752 | tf_op jit(solution)/shard_map/ppermute | solution.py:117
  101.9 1.1 split.20
  103.0 1.1 collective-permute-start.24
  104.1 1.1 split.21
  105.3 0.7 collective-permute-start.25
  105.9 1.6 %collective-permute-start.19 = (bf16[256,256]{1,0:T(8,128)(2,1)S(1)}, bf16[256,256]{1,0:T(8,128)(2,1)S(1)}, u32[]{:S(2)}, u32[]{:S(2)}) collective-permute-start(bf16[256,256]{1,0:T(8,128)(2,1)S(1)} %get-tuple-element.83.refs_0_), channel_id=1, source_target_pairs={{0,1},{1,2},{2,3},{3,0},{4,5},{5,6},{6,7},{7,4},{8,9},{9,10},{10,1... | collective-permute-start | bytes 393224 | tf_op jit(solution)/shard_map/ppermute | solution.py:117
  107.5 2.2 %collective-permute-start.21 = (bf16[256,256]{1,0:T(8,128)(2,1)S(1)}, bf16[256,256]{1,0:T(8,128)(2,1)S(1)}, u32[]{:S(2)}, u32[]{:S(2)}) collective-permute-start(bf16[256,256]{1,0:T(8,128)(2,1)S(1)} %get-tuple-element.83.refs_0_), channel_id=1, source_target_pairs={{0,3},{1,0},{2,1},{3,2},{4,7},{5,4},{6,5},{7,6},{8,11},{9,8},{10,9... | collective-permute-start | bytes 393224 | tf_op jit(solution)/shard_map/ppermute | solution.py:117
  109.7 0.8 collective-permute-start.20
  110.5 3.6 %collective-permute-done.19.refs_1_ = bf16[256,256]{1,0:T(8,128)(2,1)S(1)} collective-permute-done((bf16[256,256]{1,0:T(8,128)(2,1)S(1)}, bf16[256,256]{1,0:T(8,128)(2,1)S(1)}, u32[]{:S(2)}, u32[]{:S(2)}) %collective-permute-start.19) | collective-permute-done | bytes 131104 | tf_op jit(solution)/shard_map/ppermute | solution.py:117
  114.1 1.0 split.22
  115.1 1.8 %collective-permute-start.27 = (bf16[640,256]{1,0:T(8,128)(2,1)S(1)}, bf16[640,256]{1,0:T(8,128)(2,1)S(1)}, u32[]{:S(2)}, u32[]{:S(2)}) collective-permute-start(bf16[640,256]{1,0:T(8,128)(2,1)S(1)} %split.22), channel_id=1, source_target_pairs={{0,16},{4,20},{8,24},{12,28},{16,0},{20,4},{24,8},{28,12},{1,17},{... | collective-permute-start | bytes 983048 | tf_op jit(solution)/shard_map/ppermute | solution.py:117
  116.9 1.0 split.23
  117.9 0.7 collective-permute-start.28
  118.8 1.9 %collective-permute-done.20.refs_2_ = bf16[256,256]{1,0:T(8,128)(2,1)S(1)} collective-permute-done((bf16[256,256]{1,0:T(8,128)(2,1)S(1)}, bf16[256,256]{1,0:T(8,128)(2,1)S(1)}, u32[]{:S(2)}, u32[]{:S(2)}) %collective-permute-start.20) | collective-permute-done | bytes 131104 | tf_op jit(solution)/shard_map/ppermute | solution.py:117
  120.7 2.3 %collective-permute-done.25.refs_8_ = bf16[1,256,1280]{2,1,0:T(8,128)(2,1)S(1)} collective-permute-done((bf16[1,256,1280]{2,1,0:T(8,128)(2,1)S(1)}, bf16[1,256,1280]{2,1,0:T(8,128)(2,1)S(1)}, u32[]{:S(2)}, u32[]{:S(2)}) %collective-permute-start.25) | collective-permute-done | bytes 655392 | tf_op jit(solution)/shard_map/ppermute | solution.py:117
  123.0 3.7 %ffn_in.1 = (f32[128,2560]{1,0:T(8,128)S(1)}, bf16[128,2560]{1,0:T(8,128)(2,1)S(1)}) custom-call(s32[2]{0:T(128)S(1)} %copy-done.5, f32[8,256]{1,0:T(8,128)S(1)} %reshape.59.gain_ref, bf16[256,256]{1,0:T(8,128)(2,1)S(1)} %get-tuple-element.83.refs_0_, bf16[256,256]{1,0:T(8,128)(2,1)S(1)} %collective-permute-done.19.refs_1_, ...), custom_call_target="tpu_custom_call" | custom-call | flops 1342177280 | bytes 5242880 | tf_op jit(solution)/shard_map/ffn_in/pallas_call | solution.py:296
  127.1 0.6 collective-permute-start.29
  127.6 1.3 collective-permute-done.29
  130.3 0.7 and_reduce_fusion
  131.1 2.3 %ffn_out.1 = (f32[256,256]{1,0:T(8,128)S(1)}, bf16[256,256]{1,0:T(8,128)(2,1)S(1)}, bf16[256,256]{1,0:T(8,128)(2,1)S(1)}, bf16[256,256]{1,0:T(8,128)(2,1)S(1)}) custom-call(s32[2]{0:T(128)S(1)} %copy-done.5, bf16[128,1280]{1,0:T(8,128)(2,1)S(1)} %fusion.8.own_in_ref, bf16[128,1280]{1,0:T(8,128)(2,1)S(1)} %collective-permute-done.30.other_in_ref, ...), custom_call_target="tpu_custom_call" | custom-call | flops 671088640 | bytes 2621440 | tf_op jit(solution)/shard_map/ffn_out/pallas_call | solution.py:349
  133.4 3.7 %collective-permute-start.33 = (bf16[256,256]{1,0:T(8,128)(2,1)S(1)}, bf16[256,256]{1,0:T(8,128)(2,1)S(1)}, u32[]{:S(2)}, u32[]{:S(2)}) collective-permute-start(bf16[256,256]{1,0:T(8,128)(2,1)S(1)} %get-tuple-element.81), channel_id=1, source_target_pairs={{0,3},{1,0},{2,1},{3,2},{4,7},{5,4},{6,5},{7,6},{8,11},{9,8},{10,9... | collective-permute-start | bytes 393224 | tf_op jit(solution)/shard_map/ppermute | solution.py:117
  137.1 1.0 collective-permute-start.31
  138.1 2.9 %collective-permute-done.33 = bf16[256,256]{1,0:T(8,128)(2,1)S(1)} collective-permute-done((bf16[256,256]{1,0:T(8,128)(2,1)S(1)}, bf16[256,256]{1,0:T(8,128)(2,1)S(1)}, u32[]{:S(2)}, u32[]{:S(2)}) %collective-permute-start.33) | collective-permute-done | bytes 131104 | tf_op jit(solution)/shard_map/ppermute | solution.py:117
  141.0 8.0 %collective-permute-done.32 = bf16[256,256]{1,0:T(8,128)(2,1)S(1)} collective-permute-done((bf16[256,256]{1,0:T(8,128)(2,1)S(1)}, bf16[256,256]{1,0:T(8,128)(2,1)S(1)}, u32[]{:S(2)}, u32[]{:S(2)}) %collective-permute-start.32) | collective-permute-done | bytes 131104 | tf_op jit(solution)/shard_map/ppermute | solution.py:117
  149.2 1.4 maximum_select_fusion
  150.6 0.7 maximum_select_fusion.1
  (77 shorter events, 3.5 us)
Async XLA Ops:
  0.6 6.7 %copy-start.10 = (bf16[128,512]{1,0:T(8,128)(2,1)S(1)}, bf16[128,512]{1,0:T(8,128)(2,1)}, u32[]{:S(2)}) copy-start(bf16[128,512]{1,0:T(8,128)(2,1)} %refs_0_.1) | copy-start | bytes 393220
  2.9 31.2 %copy-start.14 = (f32[2048]{0:T(1024)S(1)}, f32[2048]{0:T(1024)}, u32[]{:S(2)}) copy-start(f32[2048]{0:T(1024)} %param.17) | copy-start | bytes 24580
  2.9 37.4 %copy-start.16 = (s32[255]{0:T(256)S(1)}, s32[255]{0:T(256)}, u32[]{:S(2)}) copy-start(s32[255]{0:T(256)} %param.15) | copy-start | bytes 3064
  2.9 26.3 %collective-permute-start.4 = (bf16[2048,256]{1,0:T(8,128)(2,1)}, bf16[2048,256]{1,0:T(8,128)(2,1)S(1)}, u32[]{:S(2)}, u32[]{:S(2)}) collective-permute-start(bf16[2048,256]{1,0:T(8,128)(2,1)} %pack.1.refs_0_), channel_id=1, source_target_pairs={{0,8},{4,12},{8,0},{12,4},{16,24},{20,28},{24,16},{28,20},{1,9},{5... | collective-permute-start | bytes 3145736 | tf_op jit(solution)/shard_map/ppermute | solution.py:117
  5.8 26.0 %collective-permute-start.5 = (bf16[2048,256]{1,0:T(8,128)(2,1)}, bf16[2048,256]{1,0:T(8,128)(2,1)S(1)}, u32[]{:S(2)}, u32[]{:S(2)}) collective-permute-start(bf16[2048,256]{1,0:T(8,128)(2,1)} %pack.1.refs_0_), channel_id=1, source_target_pairs={{0,16},{4,20},{8,24},{12,28},{16,0},{20,4},{24,8},{28,12},{1,17},{... | collective-permute-start | bytes 3145736 | tf_op jit(solution)/shard_map/ppermute | solution.py:117
  7.4 28.0 %collective-permute-start = (bf16[128,512]{1,0:T(8,128)(2,1)S(1)}, bf16[128,512]{1,0:T(8,128)(2,1)S(1)}, u32[]{:S(2)}, u32[]{:S(2)}) collective-permute-start(bf16[128,512]{1,0:T(8,128)(2,1)S(1)} %copy-done.10), channel_id=1, source_target_pairs={{0,1},{1,2},{2,3},{3,0},{4,5},{5,6},{6,7},{7,4},{8,9},{9,10},{10,1... | collective-permute-start | bytes 393224 | tf_op jit(solution)/shard_map/ppermute | solution.py:117
  8.9 26.4 %collective-permute-start.1 = (bf16[128,512]{1,0:T(8,128)(2,1)S(1)}, bf16[128,512]{1,0:T(8,128)(2,1)S(1)}, u32[]{:S(2)}, u32[]{:S(2)}) collective-permute-start(bf16[128,512]{1,0:T(8,128)(2,1)S(1)} %copy-done.10), channel_id=1, source_target_pairs={{0,2},{1,3},{2,0},{3,1},{4,6},{5,7},{6,4},{7,5},{8,10},{9,11},{10,... | collective-permute-start | bytes 393224 | tf_op jit(solution)/shard_map/ppermute | solution.py:117
  11.5 23.8 %collective-permute-start.2 = (bf16[128,512]{1,0:T(8,128)(2,1)S(1)}, bf16[128,512]{1,0:T(8,128)(2,1)}, u32[]{:S(2)}, u32[]{:S(2)}) collective-permute-start(bf16[128,512]{1,0:T(8,128)(2,1)S(1)} %copy-done.10), channel_id=1, source_target_pairs={{0,3},{1,0},{2,1},{3,2},{4,7},{5,4},{6,5},{7,6},{8,11},{9,8},{10,9... | collective-permute-start | bytes 393224 | tf_op jit(solution)/shard_map/ppermute | solution.py:117
  30.1 14.9 %collective-permute-start.7 = (bf16[1024,256]{1,0:T(8,128)(2,1)}, bf16[1024,256]{1,0:T(8,128)(2,1)}, u32[]{:S(2)}, u32[]{:S(2)}) collective-permute-start(bf16[1024,256]{1,0:T(8,128)(2,1)} %split.24), channel_id=1, source_target_pairs={{0,16},{4,20},{8,24},{12,28},{16,0},{20,4},{24,8},{28,12},{1,17},{... | collective-permute-start | bytes 1572872 | tf_op jit(solution)/shard_map/ppermute | solution.py:117
  32.6 12.8 %collective-permute-start.8 = (bf16[1024,256]{1,0:T(8,128)(2,1)}, bf16[1024,256]{1,0:T(8,128)(2,1)}, u32[]{:S(2)}, u32[]{:S(2)}) collective-permute-start(bf16[1024,256]{1,0:T(8,128)(2,1)} %split.25), channel_id=1, source_target_pairs={{0,8},{4,12},{8,0},{12,4},{16,24},{20,28},{24,16},{28,20},{1,9},{5... | collective-permute-start | bytes 1572872 | tf_op jit(solution)/shard_map/ppermute | solution.py:117
  35.3 10.2 %copy-start = (bf16[2048,256]{1,0:T(8,128)(2,1)S(1)}, bf16[2048,256]{1,0:T(8,128)(2,1)}, u32[]{:S(2)}) copy-start(bf16[2048,256]{1,0:T(8,128)(2,1)} %pack.1.refs_0_) | copy-start | bytes 3145732
  35.3 10.2 %copy-start.5 = (s32[2]{0:T(128)S(1)}, s32[2]{0:T(128)}, u32[]{:S(2)}) copy-start(s32[2]{0:T(128)} %pad_add_fusion.place_ref) | copy-start | bytes 28
  35.3 0.7 copy-start.11
  35.4 0.7 copy-start.12
  38.3 7.2 %copy-start.4 = (bf16[4,128,256]{2,1,0:T(8,128)(2,1)S(1)}, bf16[4,128,256]{2,1,0:T(8,128)(2,1)}, u32[]{:S(2)}) copy-start(bf16[4,128,256]{2,1,0:T(8,128)(2,1)} %get-tuple-element.49.own_in_ref) | copy-start | bytes 786436
  38.3 6.7 %collective-permute-start.6 = (bf16[4,128,256]{2,1,0:T(8,128)(2,1)}, bf16[4,128,256]{2,1,0:T(8,128)(2,1)}, u32[]{:S(2)}, u32[]{:S(2)}) collective-permute-start(bf16[4,128,256]{2,1,0:T(8,128)(2,1)} %get-tuple-element.51), channel_id=1, source_target_pairs={{0,4},{4,0},{8,12},{12,8},{16,20},{20,16},{24,28},{28,24},{1,5},{5... | collective-permute-start | bytes 786440 | tf_op jit(solution)/shard_map/ppermute | solution.py:117
  39.8 3.6 %collective-permute-start.3 = (bf16[128,256]{1,0:T(8,128)(2,1)S(1)}, bf16[128,256]{1,0:T(8,128)(2,1)S(1)}, u32[]{:S(2)}, u32[]{:S(2)}) collective-permute-start(bf16[128,256]{1,0:T(8,128)(2,1)S(1)} %get-tuple-element.89), channel_id=1, source_target_pairs={{0,4},{4,0},{8,12},{12,8},{16,20},{20,16},{24,28},{28,24},{1,5},{5... | collective-permute-start | bytes 196616 | tf_op jit(solution)/shard_map/ppermute | solution.py:117
  43.4 0.6 copy-start.13
  44.9 2.9 %copy-start.1 = (bf16[1280,256]{1,0:T(8,128)(2,1)S(1)}, bf16[1280,256]{1,0:T(8,128)(2,1)}, u32[]{:S(2)}) copy-start(bf16[1280,256]{1,0:T(8,128)(2,1)} %refs_0_.2) | copy-start | bytes 1966084
  47.8 2.2 %collective-permute-start.9 = (f32[128,1024]{1,0:T(8,128)S(1)}, f32[128,1024]{1,0:T(8,128)S(1)}, u32[]{:S(2)}, u32[]{:S(2)}) collective-permute-start(f32[128,1024]{1,0:T(8,128)S(1)} %get-tuple-element.55), channel_id=1, source_target_pairs={{0,4},{4,0},{8,12},{12,8},{16,20},{20,16},{24,28},{28,24},{1,5},{5... | collective-permute-start | bytes 1572872 | tf_op jit(solution)/shard_map/ppermute | solution.py:117
  47.9 17.7 %collective-permute-start.13 = (bf16[1280,256]{1,0:T(8,128)(2,1)S(1)}, bf16[1280,256]{1,0:T(8,128)(2,1)}, u32[]{:S(2)}, u32[]{:S(2)}) collective-permute-start(bf16[1280,256]{1,0:T(8,128)(2,1)S(1)} %copy-done.1), channel_id=1, source_target_pairs={{0,8},{4,12},{8,0},{12,4},{16,24},{20,28},{24,16},{28,20},{1,9},{5... | collective-permute-start | bytes 1966088 | tf_op jit(solution)/shard_map/ppermute | solution.py:117
  49.4 16.9 %collective-permute-start.14 = (bf16[1280,256]{1,0:T(8,128)(2,1)S(1)}, bf16[1280,256]{1,0:T(8,128)(2,1)}, u32[]{:S(2)}, u32[]{:S(2)}) collective-permute-start(bf16[1280,256]{1,0:T(8,128)(2,1)S(1)} %copy-done.1), channel_id=1, source_target_pairs={{0,16},{4,20},{8,24},{12,28},{16,0},{20,4},{24,8},{28,12},{1,17},{... | collective-permute-start | bytes 1966088 | tf_op jit(solution)/shard_map/ppermute | solution.py:117
  50.0 24.5 %copy-start.6 = (bf16[128,1024]{1,0:T(8,128)(2,1)}, bf16[128,1024]{1,0:T(8,128)(2,1)S(1)}, u32[]{:S(2)}) copy-start(bf16[128,1024]{1,0:T(8,128)(2,1)S(1)} %add_convert_fusion.refs_1_.refs_4_) | copy-start | bytes 786436
  50.0 16.3 %collective-permute-start.11 = (bf16[128,1024]{1,0:T(8,128)(2,1)S(1)}, bf16[128,1024]{1,0:T(8,128)(2,1)S(1)}, u32[]{:S(2)}, u32[]{:S(2)}) collective-permute-start(bf16[128,1024]{1,0:T(8,128)(2,1)S(1)} %add_convert_fusion.refs_1_.refs_4_), channel_id=1, source_target_pairs={{0,4},{4,8},{8,12},{12,16},{16,20},{20,24},{24,28},{1,5},{5,9},{9,... | collective-permute-start | bytes 786440 | tf_op jit(solution)/shard_map/ppermute | solution.py:428
  51.9 14.4 %collective-permute-start.12 = (bf16[128,1024]{1,0:T(8,128)(2,1)S(1)}, bf16[128,1024]{1,0:T(8,128)(2,1)S(1)}, u32[]{:S(2)}, u32[]{:S(2)}) collective-permute-start(bf16[128,1024]{1,0:T(8,128)(2,1)S(1)} %add_convert_fusion.refs_1_.refs_4_), channel_id=1, source_target_pairs={{4,0},{8,4},{12,8},{16,12},{20,16},{24,20},{28,24},{5,1},{9,5},{13... | collective-permute-start | bytes 786440 | tf_op jit(solution)/shard_map/ppermute | solution.py:429
  66.3 7.4 %copy-start.8 = (bf16[128,1024]{1,0:T(8,128)(2,1)}, bf16[128,1024]{1,0:T(8,128)(2,1)S(1)}, u32[]{:S(2)}) copy-start(bf16[128,1024]{1,0:T(8,128)(2,1)S(1)} %collective-permute-done.11.refs_0_.refs_3_) | copy-start | bytes 786436
  66.3 7.4 %copy-start.9 = (bf16[128,1024]{1,0:T(8,128)(2,1)}, bf16[128,1024]{1,0:T(8,128)(2,1)S(1)}, u32[]{:S(2)}) copy-start(bf16[128,1024]{1,0:T(8,128)(2,1)S(1)} %collective-permute-done.12.refs_2_.refs_5_) | copy-start | bytes 786436
  66.3 33.4 %collective-permute-start.22 = (bf16[2,256,1280]{2,1,0:T(8,128)(2,1)}, bf16[2,256,1280]{2,1,0:T(8,128)(2,1)}, u32[]{:S(2)}, u32[]{:S(2)}) collective-permute-start(bf16[2,256,1280]{2,1,0:T(8,128)(2,1)} %refs_4_.1), channel_id=1, source_target_pairs={{0,8},{4,12},{8,0},{12,4},{16,24},{20,28},{24,16},{28,20},{1,9},{5... | collective-permute-start | bytes 3932168 | tf_op jit(solution)/shard_map/ppermute | solution.py:117
  70.2 31.7 %collective-permute-start.23 = (bf16[2,256,1280]{2,1,0:T(8,128)(2,1)}, bf16[2,256,1280]{2,1,0:T(8,128)(2,1)}, u32[]{:S(2)}, u32[]{:S(2)}) collective-permute-start(bf16[2,256,1280]{2,1,0:T(8,128)(2,1)} %refs_4_.1), channel_id=1, source_target_pairs={{0,16},{4,20},{8,24},{12,28},{16,0},{20,4},{24,8},{28,12},{1,17},{... | collective-permute-start | bytes 3932168 | tf_op jit(solution)/shard_map/ppermute | solution.py:117
  72.2 1.5 %collective-permute-start.10 = (f32[128,512]{1,0:T(8,128)S(1)}, f32[128,512]{1,0:T(8,128)S(1)}, u32[]{:S(2)}, u32[]{:S(2)}) collective-permute-start(f32[128,512]{1,0:T(8,128)S(1)} %get-tuple-element.56), channel_id=1, source_target_pairs={{0,4},{4,0},{8,12},{12,8},{16,20},{20,16},{24,28},{28,24},{1,5},{5... | collective-permute-start | bytes 786440 | tf_op jit(solution)/shard_map/ppermute | solution.py:117
  80.0 1.6 %collective-permute-start.15 = (bf16[128,512]{1,0:T(8,128)(2,1)}, bf16[128,512]{1,0:T(8,128)(2,1)S(1)}, u32[]{:S(2)}, u32[]{:S(2)}) collective-permute-start(bf16[128,512]{1,0:T(8,128)(2,1)} %attention.1.own_in_ref), channel_id=1, source_target_pairs={{0,4},{4,0},{8,12},{12,8},{16,20},{20,16},{24,28},{28,24},{1,5},{5... | collective-permute-start | bytes 393224 | tf_op jit(solution)/shard_map/ppermute | solution.py:117
  81.5 0.9 copy-start.3
  84.3 7.6 %collective-permute-start.18 = (bf16[256,256]{1,0:T(8,128)(2,1)S(1)}, bf16[256,256]{1,0:T(8,128)(2,1)S(1)}, u32[]{:S(2)}, u32[]{:S(2)}) collective-permute-start(bf16[256,256]{1,0:T(8,128)(2,1)S(1)} %get-tuple-element.65), channel_id=1, source_target_pairs={{0,3},{1,0},{2,1},{3,2},{4,7},{5,4},{6,5},{7,6},{8,11},{9,8},{10,9... | collective-permute-start | bytes 393224 | tf_op jit(solution)/shard_map/ppermute | solution.py:117
  87.9 11.7 %collective-permute-start.17 = (bf16[256,256]{1,0:T(8,128)(2,1)S(1)}, bf16[256,256]{1,0:T(8,128)(2,1)S(1)}, u32[]{:S(2)}, u32[]{:S(2)}) collective-permute-start(bf16[256,256]{1,0:T(8,128)(2,1)S(1)} %get-tuple-element.64), channel_id=1, source_target_pairs={{0,2},{1,3},{2,0},{3,1},{4,6},{5,7},{6,4},{7,5},{8,10},{9,11},{10,... | collective-permute-start | bytes 393224 | tf_op jit(solution)/shard_map/ppermute | solution.py:117
  87.9 11.7 %collective-permute-start.16 = (bf16[256,256]{1,0:T(8,128)(2,1)S(1)}, bf16[256,256]{1,0:T(8,128)(2,1)S(1)}, u32[]{:S(2)}, u32[]{:S(2)}) collective-permute-start(bf16[256,256]{1,0:T(8,128)(2,1)S(1)} %get-tuple-element.63), channel_id=1, source_target_pairs={{0,1},{1,2},{2,3},{3,0},{4,5},{5,6},{6,7},{7,4},{8,9},{9,10},{10,1... | collective-permute-start | bytes 393224 | tf_op jit(solution)/shard_map/ppermute | solution.py:117
  101.9 8.6 %copy-start.15 = (f32[2048]{0:T(1024)S(1)}, f32[2048]{0:T(1024)}, u32[]{:S(2)}) copy-start(f32[2048]{0:T(1024)} %param.21) | copy-start | bytes 24580
  103.0 17.7 %collective-permute-start.24 = (bf16[1,256,1280]{2,1,0:T(8,128)(2,1)S(1)}, bf16[1,256,1280]{2,1,0:T(8,128)(2,1)S(1)}, u32[]{:S(2)}, u32[]{:S(2)}) collective-permute-start(bf16[1,256,1280]{2,1,0:T(8,128)(2,1)S(1)} %split.20), channel_id=1, source_target_pairs={{0,16},{4,20},{8,24},{12,28},{16,0},{20,4},{24,8},{28,12},{1,17},{... | collective-permute-start | bytes 1966088 | tf_op jit(solution)/shard_map/ppermute | solution.py:117
  105.3 17.7 %collective-permute-start.25 = (bf16[1,256,1280]{2,1,0:T(8,128)(2,1)S(1)}, bf16[1,256,1280]{2,1,0:T(8,128)(2,1)S(1)}, u32[]{:S(2)}, u32[]{:S(2)}) collective-permute-start(bf16[1,256,1280]{2,1,0:T(8,128)(2,1)S(1)} %split.21), channel_id=1, source_target_pairs={{0,8},{4,12},{8,0},{12,4},{16,24},{20,28},{24,16},{28,20},{1,9},{5... | collective-permute-start | bytes 1966088 | tf_op jit(solution)/shard_map/ppermute | solution.py:117
  105.9 8.2 %collective-permute-start.19 = (bf16[256,256]{1,0:T(8,128)(2,1)S(1)}, bf16[256,256]{1,0:T(8,128)(2,1)S(1)}, u32[]{:S(2)}, u32[]{:S(2)}) collective-permute-start(bf16[256,256]{1,0:T(8,128)(2,1)S(1)} %get-tuple-element.83.refs_0_), channel_id=1, source_target_pairs={{0,1},{1,2},{2,3},{3,0},{4,5},{5,6},{6,7},{7,4},{8,9},{9,10},{10,1... | collective-permute-start | bytes 393224 | tf_op jit(solution)/shard_map/ppermute | solution.py:117
  107.5 10.4 %collective-permute-start.21 = (bf16[256,256]{1,0:T(8,128)(2,1)S(1)}, bf16[256,256]{1,0:T(8,128)(2,1)S(1)}, u32[]{:S(2)}, u32[]{:S(2)}) collective-permute-start(bf16[256,256]{1,0:T(8,128)(2,1)S(1)} %get-tuple-element.83.refs_0_), channel_id=1, source_target_pairs={{0,3},{1,0},{2,1},{3,2},{4,7},{5,4},{6,5},{7,6},{8,11},{9,8},{10,9... | collective-permute-start | bytes 393224 | tf_op jit(solution)/shard_map/ppermute | solution.py:117
  109.7 11.0 %collective-permute-start.20 = (bf16[256,256]{1,0:T(8,128)(2,1)S(1)}, bf16[256,256]{1,0:T(8,128)(2,1)S(1)}, u32[]{:S(2)}, u32[]{:S(2)}) collective-permute-start(bf16[256,256]{1,0:T(8,128)(2,1)S(1)} %get-tuple-element.83.refs_0_), channel_id=1, source_target_pairs={{0,2},{1,3},{2,0},{3,1},{4,6},{5,7},{6,4},{7,5},{8,10},{9,11},{10,... | collective-permute-start | bytes 393224 | tf_op jit(solution)/shard_map/ppermute | solution.py:117
  115.1 13.8 %collective-permute-start.27 = (bf16[640,256]{1,0:T(8,128)(2,1)S(1)}, bf16[640,256]{1,0:T(8,128)(2,1)S(1)}, u32[]{:S(2)}, u32[]{:S(2)}) collective-permute-start(bf16[640,256]{1,0:T(8,128)(2,1)S(1)} %split.22), channel_id=1, source_target_pairs={{0,16},{4,20},{8,24},{12,28},{16,0},{20,4},{24,8},{28,12},{1,17},{... | collective-permute-start | bytes 983048 | tf_op jit(solution)/shard_map/ppermute | solution.py:117
  117.9 11.0 %collective-permute-start.28 = (bf16[640,256]{1,0:T(8,128)(2,1)S(1)}, bf16[640,256]{1,0:T(8,128)(2,1)S(1)}, u32[]{:S(2)}, u32[]{:S(2)}) collective-permute-start(bf16[640,256]{1,0:T(8,128)(2,1)S(1)} %split.23), channel_id=1, source_target_pairs={{0,8},{4,12},{8,0},{12,4},{16,24},{20,28},{24,16},{28,20},{1,9},{5... | collective-permute-start | bytes 983048 | tf_op jit(solution)/shard_map/ppermute | solution.py:117
  126.7 2.2 %collective-permute-start.26 = (bf16[128,2560]{1,0:T(8,128)(2,1)S(1)}, bf16[128,2560]{1,0:T(8,128)(2,1)S(1)}, u32[]{:S(2)}, u32[]{:S(2)}) collective-permute-start(bf16[128,2560]{1,0:T(8,128)(2,1)S(1)} %get-tuple-element.72), channel_id=1, source_target_pairs={{0,4},{4,0},{8,12},{12,8},{16,20},{20,16},{24,28},{28,24},{1,5},{5... | collective-permute-start | bytes 1966088 | tf_op jit(solution)/shard_map/ppermute | solution.py:117
  127.1 1.8 %collective-permute-start.29 = (f32[128]{0:T(128)S(1)}, f32[128]{0:T(128)S(1)}, u32[]{:S(2)}, u32[]{:S(2)}) collective-permute-start(f32[128]{0:T(128)S(1)} %slice.60), channel_id=1, source_target_pairs={{0,4},{4,0},{8,12},{12,8},{16,20},{20,16},{24,28},{28,24},{1,5},{5... | collective-permute-start | bytes 1544 | tf_op jit(solution)/shard_map/ppermute | solution.py:117
  129.2 1.9 %copy-start.2 = (bf16[1280,256]{1,0:T(8,128)(2,1)S(1)}, bf16[1280,256]{1,0:T(8,128)(2,1)}, u32[]{:S(2)}) copy-start(bf16[1280,256]{1,0:T(8,128)(2,1)} %refs_0_.2) | copy-start | bytes 1966084
  129.4 1.7 %collective-permute-start.30 = (bf16[128,1280]{1,0:T(8,128)(2,1)S(1)}, bf16[128,1280]{1,0:T(8,128)(2,1)S(1)}, u32[]{:S(2)}, u32[]{:S(2)}) collective-permute-start(bf16[128,1280]{1,0:T(8,128)(2,1)S(1)} %fusion.8.own_in_ref), channel_id=1, source_target_pairs={{0,4},{4,0},{8,12},{12,8},{16,20},{20,16},{24,28},{28,24},{1,5},{5... | collective-permute-start | bytes 983048 | tf_op jit(solution)/shard_map/ppermute | solution.py:117
  131.0 7.1 %copy-start.7 = (bf16[128,1024]{1,0:T(8,128)(2,1)S(1)}, bf16[128,1024]{1,0:T(8,128)(2,1)}, u32[]{:S(2)}) copy-start(bf16[128,1024]{1,0:T(8,128)(2,1)} %copy-done.6) | copy-start | bytes 786436
  133.4 7.6 %collective-permute-start.33 = (bf16[256,256]{1,0:T(8,128)(2,1)S(1)}, bf16[256,256]{1,0:T(8,128)(2,1)S(1)}, u32[]{:S(2)}, u32[]{:S(2)}) collective-permute-start(bf16[256,256]{1,0:T(8,128)(2,1)S(1)} %get-tuple-element.81), channel_id=1, source_target_pairs={{0,3},{1,0},{2,1},{3,2},{4,7},{5,4},{6,5},{7,6},{8,11},{9,8},{10,9... | collective-permute-start | bytes 393224 | tf_op jit(solution)/shard_map/ppermute | solution.py:117
  137.1 11.9 %collective-permute-start.32 = (bf16[256,256]{1,0:T(8,128)(2,1)S(1)}, bf16[256,256]{1,0:T(8,128)(2,1)S(1)}, u32[]{:S(2)}, u32[]{:S(2)}) collective-permute-start(bf16[256,256]{1,0:T(8,128)(2,1)S(1)} %get-tuple-element.80), channel_id=1, source_target_pairs={{0,2},{1,3},{2,0},{3,1},{4,6},{5,7},{6,4},{7,5},{8,10},{9,11},{10,... | collective-permute-start | bytes 393224 | tf_op jit(solution)/shard_map/ppermute | solution.py:117
  137.1 11.9 %collective-permute-start.31 = (bf16[256,256]{1,0:T(8,128)(2,1)S(1)}, bf16[256,256]{1,0:T(8,128)(2,1)S(1)}, u32[]{:S(2)}, u32[]{:S(2)}) collective-permute-start(bf16[256,256]{1,0:T(8,128)(2,1)S(1)} %get-tuple-element.79), channel_id=1, source_target_pairs={{0,1},{1,2},{2,3},{3,0},{4,5},{5,6},{6,7},{7,4},{8,9},{9,10},{10,1... | collective-permute-start | bytes 393224 | tf_op jit(solution)/shard_map/ppermute | solution.py:117
  149.1 1.5 collective-permute-start.34

commit v4 on v3

--- a/solution.py
+++ b/solution.py
@@ -54,62 +54,66 @@
         out_shape=jax.ShapeDtypeStruct((heads, count, 3 * count), jnp.float32),
         in_specs=[SMEM, VMEM, VMEM, VMEM],
         out_specs=VMEM,
+        compiler_params=pltpu.CompilerParams(vmem_limit_bytes=8 << 20),
         name="masked_bias",
     )(row.reshape(1), segment_ids.reshape(-1, count), table, rel_bias.T)
 
 
-def attention_kernel(q_ref, *refs):
-    *key_refs, bias_ref, out_ref = refs
-    key_refs, value_refs = key_refs[:3], key_refs[3:]
+def attention_kernel(q_ref, low_ref, own_ref, high_ref, bias_ref, out_ref):
     heads, count, _ = bias_ref.shape
-    width = q_ref.shape[1] // heads
-    contract = (((1,), (1,)), ((), ()))
-    parts = []
-    for head in range(heads):
-        cut = slice(head * width, (head + 1) * width)
-        query = q_ref[:, cut]
-        scores = jnp.concatenate(
-            [
-                lax.dot_general(query, ref[:, cut], contract, preferred_element_type=jnp.float32)
-                for ref in key_refs
-            ],
-            axis=1,
+    total_width = q_ref.shape[1]
+    width = total_width // heads
+    sides = (low_ref, own_ref, high_ref)
+    for pair in range(0, heads, 2):
+        parts = []
+        for head in (pair, pair + 1):
+            cut = slice(head * width, (head + 1) * width)
+            after_keys = slice(total_width + head * width, total_width + (head + 1) * width)
+            query = q_ref[:, cut]
+            scores = jnp.concatenate(
+                [
+                    lax.dot_general(
+                        query,
+                        ref[:, cut],
+                        (((1,), (1,)), ((), ())),
+                        preferred_element_type=jnp.float32,
+                    )
+                    for ref in sides
+                ],
+                axis=1,
+            )
+            scores = scores + bias_ref[head]
+            top = jnp.max(scores, axis=1, keepdims=True)
+            weights = jnp.exp(scores - top)
+            denominator = jnp.sum(weights, axis=1, keepdims=True)
+            rounded = weights.astype(jnp.bfloat16)
+            total = sum(
+                jnp.dot(
+                    rounded[:, i * count : (i + 1) * count],
+                    ref[:, after_keys],
+                    preferred_element_type=jnp.float32,
+                )
+                for i, ref in enumerate(sides)
+            )
+            parts.append(total / denominator)
+        out_ref[:, pair * width : (pair + 2) * width] = jnp.concatenate(parts, axis=1).astype(
+            out_ref.dtype
         )
-        scores = scores + bias_ref[head]
-        top = jnp.max(scores, axis=1, keepdims=True)
-        weights = jnp.exp(scores - top)
-        denominator = jnp.sum(weights, axis=1, keepdims=True)
-        rounded = weights.astype(jnp.bfloat16)
-        total = sum(
-            jnp.dot(
-                rounded[:, i * count : (i + 1) * count],
-                ref[:, cut],
-                preferred_element_type=jnp.float32,
-            )
-            for i, ref in enumerate(value_refs)
-        )
-        parts.append(total / denominator)
-    out_ref[...] = jnp.concatenate(parts, axis=1).astype(out_ref.dtype)
 
 
 def attention(queries, low, own, high, bias):
-    heads, count, span = bias.shape
-    width = queries.shape[1]
-    steps = heads // 2
-    lanes = width // steps
-    keys = pl.BlockSpec((count, lanes), lambda i: (0, i))
-    values = pl.BlockSpec((count, lanes), lambda i: (0, i + steps))
+    count, span = bias.shape[1:]
     return pl.pallas_call(
         attention_kernel,
-        out_shape=jax.ShapeDtypeStruct((count, width), jnp.bfloat16),
-        grid=(steps,),
-        in_specs=[keys] * 4 + [values] * 3 + [pl.BlockSpec((2, count, span), lambda i: (i, 0, 0))],
-        out_specs=keys,
+        out_shape=jax.ShapeDtypeStruct(queries.shape, jnp.bfloat16),
+        in_specs=[VMEM] * 5,
+        out_specs=VMEM,
+        compiler_params=pltpu.CompilerParams(vmem_limit_bytes=16 << 20),
         cost_estimate=pl.CostEstimate(
             flops=4 * queries.size * span, bytes_accessed=4 * bias.size, transcendentals=bias.size
         ),
         name="attention",
-    )(queries, low, own, high, low, own, high, bias)
+    )(queries, low, own, high, bias)
 
 
 def exchange(value, axis, partner):
@@ -149,12 +153,46 @@
     return weight, near_pieces(weight)
 
 
-def far_pieces(near, axis):
-    if len(near) != 2:
+def first_phase(low, high):
+    pairs = lax.axis_size("row") // 2
+    if pairs != 4:
+        return [pair_exchange(part, step) for step in range(1, pairs) for part in (low, high)]
+    return [pair_exchange(low, 1), pair_exchange(high, 2)]
+
+
+def packet_kernel(own_ref, low_in, high_in, low_ref, high_ref):
+    size = low_in.shape[0]
+    low_ref[0], high_ref[0] = own_ref[0], own_ref[1]
+    low_ref[1], high_ref[1] = low_in[...], high_in[...]
+
+
+def second_phase(own, first):
+    if len(first) != 2:
         return []
-    first, _ = jnp.split(near[0], 2, axis=axis)
-    _, second = jnp.split(near[1], 2, axis=axis)
-    return [pair_exchange(first, 2), pair_exchange(second, 1)]
+    shape = jax.ShapeDtypeStruct(own.shape, own.dtype)
+    low, high = pl.pallas_call(
+        packet_kernel,
+        out_shape=(shape, shape),
+        in_specs=[VMEM] * 3,
+        out_specs=(VMEM, VMEM),
+        compiler_params=pltpu.CompilerParams(vmem_limit_bytes=8 << 20),
+        name="packet",
+    )(own, *first)
+    return [pair_exchange(high, 1), pair_exchange(low, 2)]
+
+
+def half_ref(refs, step, part):
+    own, *others = refs
+    if step == 0:
+        return own.at[part]
+    if len(others) != 4:
+        return others[2 * (step - 1) + part]
+    near_low, side_high, highs, lows = others
+    if step == 3:
+        return (highs if part else lows).at[1]
+    if part == step - 1:
+        return near_low if part == 0 else side_high
+    return (highs if part else lows).at[0]
 
 
 def norm_kernel(place_ref, gain_ref, *refs):
@@ -181,6 +219,7 @@
         out_shape=(shape, shape),
         in_specs=[SMEM] + [VMEM] * (1 + len(token_blocks)),
         out_specs=(VMEM, VMEM),
+        compiler_params=pltpu.CompilerParams(vmem_limit_bytes=8 << 20),
         name="norm_tokens",
     )(place, gain, *token_blocks)
 
@@ -221,8 +260,30 @@
         out_shape=jax.ShapeDtypeStruct((count * depth + width, depth), w_qkv.dtype),
         in_specs=[VMEM, VMEM],
         out_specs=VMEM,
+        compiler_params=pltpu.CompilerParams(vmem_limit_bytes=8 << 20),
         name="pack",
     )(w_qkv, w_out)
+
+
+def relay_kernel(low_in, high_in, low_ref, high_ref):
+    half = low_ref.shape[0]
+    low_ref[...] = low_in[:half]
+    high_ref[...] = high_in[half:]
+
+
+def relayed(near):
+    if len(near) != 2:
+        return []
+    rows, width = near[0].shape
+    shape = jax.ShapeDtypeStruct((rows // 2, width), near[0].dtype)
+    return pl.pallas_call(
+        relay_kernel,
+        out_shape=(shape, shape),
+        in_specs=[VMEM] * 2,
+        out_specs=(VMEM, VMEM),
+        compiler_params=pltpu.CompilerParams(vmem_limit_bytes=8 << 20),
+        name="relay",
+    )(*near)
 
 
 def qkv_kernel(place_ref, own_in_ref, other_in_ref, *refs):
@@ -278,12 +339,8 @@
         index = lax.rem(col - step + blocks, blocks)
         gain = gain_ref[pl.ds(2 * index + lax.rem(row, 2), 1), :]
         held[index] = (ref[...].astype(jnp.float32) * gain).astype(jnp.bfloat16)
-    direct = blocks - 1 if len(weight_refs) == blocks + 1 else blocks
-
     def piece(step, part, start, stop):
-        if step < direct:
-            return weight_refs[step][part, :, start:stop]
-        return weight_refs[direct + part][0, :, start:stop]
+        return half_ref(weight_refs, step, part)[:, start:stop]
 
     width = weight_refs[0].shape[2]
     multiply_pieces(((0, 1),), held, row // 2, piece, width, (own_ref,), (send_ref,))
@@ -322,19 +379,23 @@
     far = len(weight_refs) == blocks + 1
     direct = blocks - 1 if far else blocks
     for step in range(blocks):
-        if step < direct:
+        if not first:
+            half = hidden.shape[1] // 2
+            total = jnp.dot(
+                hidden[:, :half],
+                half_ref(weight_refs, step, 0)[...],
+                preferred_element_type=jnp.float32,
+            ) + jnp.dot(
+                hidden[:, half:],
+                half_ref(weight_refs, step, 1)[...],
+                preferred_element_type=jnp.float32,
+            )
+        elif step < direct:
             total = jnp.dot(hidden, weight_refs[step][first:, :], preferred_element_type=jnp.float32)
-        elif first:
+        else:
             skipped = first - weight_refs[direct].shape[0]
             total = jnp.dot(
                 hidden, weight_refs[direct + 1][skipped:, :], preferred_element_type=jnp.float32
-            )
-        else:
-            half = hidden.shape[1] // 2
-            total = jnp.dot(
-                hidden[:, :half], weight_refs[direct][...], preferred_element_type=jnp.float32
-            ) + jnp.dot(
-                hidden[:, half:], weight_refs[direct + 1][...], preferred_element_type=jnp.float32
             )
         held[lax.rem((pair ^ step) - col + blocks, blocks)] = total
     own_ref[...] = held[0]
@@ -344,10 +405,10 @@
 
 def columns(place, own, other, pieces, name):
     count, depth = own.shape
-    width = pieces[0].shape[1]
+    width = pieces[0].shape[-1]
     blocks = lax.axis_size("col")
     return pl.pallas_call(
-        functools.partial(columns_kernel, pieces[0].shape[0] - depth),
+        functools.partial(columns_kernel, pieces[0].size // width - depth),
         out_shape=(
             jax.ShapeDtypeStruct((2 * count, width), jnp.float32),
             *[jax.ShapeDtypeStruct((2 * count, width), jnp.bfloat16)] * (blocks - 1),
@@ -414,44 +475,46 @@
         axis=0,
     )
     bias = masked_bias(row, segment_ids, bucket_table, rel_bias, count)
-    first_far = far_pieces(first_near, 0)
+    first_far = [pair_exchange(p, step) for p, step in zip(relayed(first_near), (2, 1))]
     first_pieces = [first, *first_near, *first_far]
-    w_down, down_near = first_hop(w_down, received)
     kept, bias, token_block = lax.optimization_barrier((kept, bias, token_block))
+    w_in, w_down, *_ = lax.optimization_barrier((w_in, w_down.reshape(2, -1, half), received))
+    down_first = first_phase(w_down[0], w_down[1])
+    in_first = first_phase(w_in[0], w_in[1])
     own_q, own_kv, send_q, send_kv = project_qkv(
         place, kept, received, first_pieces
     )
-    key_value = (own_kv + other_core(send_kv)).astype(jnp.bfloat16)
+    other_kv, *down_first = lax.optimization_barrier((other_core(send_kv), *down_first))
+    key_value = (own_kv + other_kv).astype(jnp.bfloat16)
     queries = (own_q + other_core(after(send_q, key_value))).astype(jnp.bfloat16)
     forward = [(i, i + 1) for i in range(rows - 1)]
     backward = [(target, source) for source, target in forward]
     low = lax.ppermute(key_value, "row", forward)
     high = lax.ppermute(key_value, "row", backward)
-    low, high, *down_near = lax.optimization_barrier((low, high, *down_near))
-    in_near = near_pieces(after(w_in, low, high, *down_near))
+    low, high, *in_first = lax.optimization_barrier((low, high, *in_first))
+    in_pieces = [w_in, *in_first, *second_phase(w_in, in_first)]
     context = attention(queries, low, key_value, high, bias)
     own, *sends = columns(
         place, context, other_core(context), first_pieces, "attention_out"
     )
     middle = summed(own, sends, token_block)
-    in_far = far_pieces(after_all(in_near, middle), 0)
 
     middle_blocks = gathered(middle)
     squares = square_sums(middle_blocks)
     squares = squares[:count] + other_core(squares[count:])
     scale = lax.rsqrt(squares / features + epsilon)[:, None]
-    down_far = far_pieces(after_all(down_near, middle_blocks[1]), 0)
+    down_second = second_phase(after(w_down, middle_blocks[-1]), down_first)
     own, send = project_ffn(
-        place, gain_ffn.reshape(rows, -1), middle_blocks, [w_in, *in_near, *in_far]
-    )
-    other_sum, *down_far = lax.optimization_barrier((other_core(send), *down_far))
+        place, gain_ffn.reshape(rows, -1), middle_blocks, in_pieces
+    )
+    other_sum, *down_second = lax.optimization_barrier((other_core(send), *down_second))
     branches = (own + other_sum.astype(jnp.float32)) * scale
     inner = branches.shape[1] // 2
     hidden = (
         jax.nn.gelu(branches[:, :inner], approximate=True) * branches[:, inner:]
     ).astype(jnp.bfloat16)
     own, *sends = columns(
-        place, hidden, other_core(hidden), [w_down, *down_near, *down_far], "ffn_out"
+        place, hidden, other_core(hidden), [w_down, *down_first, *down_second], "ffn_out"
     )
     result = summed(own, sends, middle)
     received = other_core(result[count:])

time: 152 us -> 144 us (0.947)
  waiting for transfers between devices: 65.8 us -> 76.3 us
  Pallas kernels: 22.7 us -> 14.4 us
  local copies, waits for them, and re-layouts: 9.41 us -> 5.01 us
  starting transfers between devices: 44.1 us -> 40.7 us
  other arithmetic: 7.61 us -> 5.86 us
    ppermute x33, waiting for transfers between devices: 65.8 us -> 76.3 us  [exchange(): lax.ppermute(value, axis, [(i, partner(i) % count) for i in range(count)])]
    split x6 -> x0, local copies, waits for them, and re-layouts: 5.92 us -> none  [the longest x3 2.98 us: far_pieces(): first, _ = jnp.split(near[0], 2, axis=axis)]
    ppermute x33, starting transfers between devices: 41 us -> 38.1 us  [exchange(): lax.ppermute(value, axis, [(i, partner(i) % count) for i in range(count)])]
    pallas_call x1, Pallas kernels: 2.26 us -> 0.07 us  [packed(): pl.pallas_call(pack_kernel, out_shape=jax.ShapeDtypeStruct((count * depth...]
    pallas_call x3 -> x6, Pallas kernels: 9.64 us -> 7.47 us  [the longest x2 2.79 us: columns(): pl.pallas_call(functools.partial(columns_kernel, pieces[0].size // width...]
    pallas_call x1, Pallas kernels: 2.54 us -> 0.65 us  [masked_bias(): pl.pallas_call(bias_kernel, out_shape=jax.ShapeDtypeStruct((heads, count,...]
    unnamed x34 -> x48, local copies, waits for them, and re-layouts: 2.26 us -> 4.13 us
    reduce_sum x4, other arithmetic: 0.51 us -> 2.32 us  [square_sums(): jnp.sum(jnp.square(b.astype(jnp.float32)), axis=1)]
  transfers between devices with their start and end apart: 35 -> 35, of which waited for: 16 -> 22; matrix products, arithmetic and copies ran while one was open for 8% -> 4% of each run, Pallas kernels for 10% -> 8%
where the time goes in v4:
time: 144 us
  waiting for transfers between devices  76.3 us (53%)
  starting transfers between devices  40.7 us (28%)
  Pallas kernels  14.4 us (10%)
  other arithmetic  5.86 us (4%)
  local copies, waits for them, and re-layouts  5.01 us (3%)
  between operations  1.72 us (1%)
    ppermute x33, waiting for transfers between devices, exchange(): lax.ppermute(value, axis, [(i, partner(i) % count) for i in range(count)])  76.3 us
    ppermute x33, starting transfers between devices, exchange(): lax.ppermute(value, axis, [(i, partner(i) % count) for i in range(count)])  38.1 us
    unnamed x48, local copies, waits for them, and re-layouts  4.13 us
    pallas_call x1, Pallas kernels, project_ffn(): pl.pallas_call(ffn_in_kernel, out_shape=(jax.ShapeDtypeStruct((count, col...  3.49 us
  transfers between devices with their start and end apart: 35, of which 22 were waited for; matrix products, arithmetic and copies ran while one was open for 4% of the time, Pallas kernels for 8%

profile of v4, /device:TPU:0, one launch (start us, length us, event | category | flops | bytes accessed | tf_op | source)
XLA Modules:
  0.0 144.0 jit_solution(9605660638103940137)
XLA Ops:
  0.6 1.1 copy-done.17
  1.8 0.9 copy-done.19
  2.8 3.0 %collective-permute-start.4 = (bf16[2048,256]{1,0:T(8,128)(2,1)S(1)}, bf16[2048,256]{1,0:T(8,128)(2,1)S(1)}, u32[]{:S(2)}, u32[]{:S(2)}) collective-permute-start(bf16[2048,256]{1,0:T(8,128)(2,1)S(1)} %pack.1.refs_0_), channel_id=1, source_target_pairs={{0,8},{4,12},{8,0},{12,4},{16,24},{20,28},{24,16},{28,20},{1,9},{5... | collective-permute-start | bytes 3145736 | tf_op jit(solution)/shard_map/ppermute | solution.py:121
  5.8 1.5 %collective-permute-start.5 = (bf16[2048,256]{1,0:T(8,128)(2,1)S(1)}, bf16[2048,256]{1,0:T(8,128)(2,1)S(1)}, u32[]{:S(2)}, u32[]{:S(2)}) collective-permute-start(bf16[2048,256]{1,0:T(8,128)(2,1)S(1)} %pack.1.refs_0_), channel_id=1, source_target_pairs={{0,16},{4,20},{8,24},{12,28},{16,0},{20,4},{24,8},{28,12},{1,17},{... | collective-permute-start | bytes 3145736 | tf_op jit(solution)/shard_map/ppermute | solution.py:121
  7.3 1.6 %collective-permute-start = (bf16[128,512]{1,0:T(8,128)(2,1)S(1)}, bf16[128,512]{1,0:T(8,128)(2,1)S(1)}, u32[]{:S(2)}, u32[]{:S(2)}) collective-permute-start(bf16[128,512]{1,0:T(8,128)(2,1)S(1)} %copy-done.18), channel_id=1, source_target_pairs={{0,1},{1,2},{2,3},{3,0},{4,5},{5,6},{6,7},{7,4},{8,9},{9,10},{10,1... | collective-permute-start | bytes 393224 | tf_op jit(solution)/shard_map/ppermute | solution.py:121
  8.9 2.6 %collective-permute-start.1 = (bf16[128,512]{1,0:T(8,128)(2,1)S(1)}, bf16[128,512]{1,0:T(8,128)(2,1)S(1)}, u32[]{:S(2)}, u32[]{:S(2)}) collective-permute-start(bf16[128,512]{1,0:T(8,128)(2,1)S(1)} %copy-done.18), channel_id=1, source_target_pairs={{0,2},{1,3},{2,0},{3,1},{4,6},{5,7},{6,4},{7,5},{8,10},{9,11},{10,... | collective-permute-start | bytes 393224 | tf_op jit(solution)/shard_map/ppermute | solution.py:121
  11.5 1.3 collective-permute-start.2
  12.9 2.8 %collective-permute-done.refs_1_ = bf16[128,512]{1,0:T(8,128)(2,1)S(1)} collective-permute-done((bf16[128,512]{1,0:T(8,128)(2,1)S(1)}, bf16[128,512]{1,0:T(8,128)(2,1)S(1)}, u32[]{:S(2)}, u32[]{:S(2)}) %collective-permute-start) | collective-permute-done | bytes 131104 | tf_op jit(solution)/shard_map/ppermute | solution.py:121
  15.7 3.9 %collective-permute-done.1.refs_2_ = bf16[128,512]{1,0:T(8,128)(2,1)S(1)} collective-permute-done((bf16[128,512]{1,0:T(8,128)(2,1)S(1)}, bf16[128,512]{1,0:T(8,128)(2,1)S(1)}, u32[]{:S(2)}, u32[]{:S(2)}) %collective-permute-start.1) | collective-permute-done | bytes 131104 | tf_op jit(solution)/shard_map/ppermute | solution.py:121
  19.8 1.2 norm_tokens.1
  21.1 7.9 %collective-permute-done.4.low_in.refs_1_ = bf16[2048,256]{1,0:T(8,128)(2,1)S(1)} collective-permute-done((bf16[2048,256]{1,0:T(8,128)(2,1)S(1)}, bf16[2048,256]{1,0:T(8,128)(2,1)S(1)}, u32[]{:S(2)}, u32[]{:S(2)}) %collective-permute-start.4) | collective-permute-done | bytes 1048608 | tf_op jit(solution)/shard_map/ppermute | solution.py:121
  29.0 1.5 %collective-permute-done.5.high_in.refs_2_ = bf16[2048,256]{1,0:T(8,128)(2,1)S(1)} collective-permute-done((bf16[2048,256]{1,0:T(8,128)(2,1)S(1)}, bf16[2048,256]{1,0:T(8,128)(2,1)S(1)}, u32[]{:S(2)}, u32[]{:S(2)}) %collective-permute-start.5) | collective-permute-done | bytes 1048608 | tf_op jit(solution)/shard_map/ppermute | solution.py:121
  30.5 1.6 %collective-permute-start.7 = (bf16[1024,256]{1,0:T(8,128)(2,1)S(1)}, bf16[1024,256]{1,0:T(8,128)(2,1)S(1)}, u32[]{:S(2)}, u32[]{:S(2)}) collective-permute-start(bf16[1024,256]{1,0:T(8,128)(2,1)S(1)} %get-tuple-element.58), channel_id=1, source_target_pairs={{0,16},{4,20},{8,24},{12,28},{16,0},{20,4},{24,8},{28,12},{1,17},{... | collective-permute-start | bytes 1572872 | tf_op jit(solution)/shard_map/ppermute | solution.py:121
  32.1 0.5 collective-permute-start.8
  32.8 0.6 masked_bias.1.bias_ref
  33.4 0.5 collective-permute-done.3
  34.1 1.6 %collective-permute-start.10 = (bf16[640,256]{1,0:T(8,128)(2,1)S(1)}, bf16[640,256]{1,0:T(8,128)(2,1)S(1)}, u32[]{:S(2)}, u32[]{:S(2)}) collective-permute-start(bf16[640,256]{1,0:T(8,128)(2,1)S(1)} %get-tuple-element.99), channel_id=1, source_target_pairs={{0,8},{4,12},{8,0},{12,4},{16,24},{20,28},{24,16},{28,20},{1,9},{5... | collective-permute-start | bytes 983048 | tf_op jit(solution)/shard_map/ppermute | solution.py:121
  35.6 0.5 collective-permute-start.11
  36.1 9.2 %collective-permute-done.7.refs_3_ = bf16[1024,256]{1,0:T(8,128)(2,1)S(1)} collective-permute-done((bf16[1024,256]{1,0:T(8,128)(2,1)S(1)}, bf16[1024,256]{1,0:T(8,128)(2,1)S(1)}, u32[]{:S(2)}, u32[]{:S(2)}) %collective-permute-start.7) | collective-permute-done | bytes 524320 | tf_op jit(solution)/shard_map/ppermute | solution.py:121
  45.3 1.6 %collective-permute-done.8.refs_4_ = bf16[1024,256]{1,0:T(8,128)(2,1)S(1)} collective-permute-done((bf16[1024,256]{1,0:T(8,128)(2,1)S(1)}, bf16[1024,256]{1,0:T(8,128)(2,1)S(1)}, u32[]{:S(2)}, u32[]{:S(2)}) %collective-permute-start.8) | collective-permute-done | bytes 524320 | tf_op jit(solution)/shard_map/ppermute | solution.py:121
  46.9 1.5 %qkv.1 = (f32[128,512]{1,0:T(8,128)S(1)}, f32[128,1024]{1,0:T(8,128)S(1)}, f32[128,512]{1,0:T(8,128)S(1)}, f32[128,1024]{1,0:T(8,128)S(1)}) custom-call(s32[2]{0:T(128)S(1)} %pad_add_fusion.place_ref, bf16[4,128,256]{2,1,0:T(8,128)(2,1)S(1)} %get-tuple-element.55.own_in_ref, bf16[4,128,256]{2,1,0:T(8,128)(2,1)S(1)} %collective-permute-done.6.other_in_ref, ...), custom_call_target="tpu_custom_call" | custom-call | flops 805306368 | bytes 3145728 | tf_op jit(solution)/shard_map/qkv/pallas_call | solution.py:317
  48.6 0.6 collective-permute-start.15
  49.2 0.3 collective-permute-start.16
  49.5 4.4 %collective-permute-done.10.low_in.refs_1_ = bf16[640,256]{1,0:T(8,128)(2,1)S(1)} collective-permute-done((bf16[640,256]{1,0:T(8,128)(2,1)S(1)}, bf16[640,256]{1,0:T(8,128)(2,1)S(1)}, u32[]{:S(2)}, u32[]{:S(2)}) %collective-permute-start.10) | collective-permute-done | bytes 327712 | tf_op jit(solution)/shard_map/ppermute | solution.py:121
  54.0 1.3 collective-permute-start.13
  55.3 1.3 collective-permute-start.14
  56.6 11.3 %collective-permute-done.15.low_in.refs_5_ = bf16[256,1280]{1,0:T(8,128)(2,1)S(1)} collective-permute-done((bf16[256,1280]{1,0:T(8,128)(2,1)S(1)}, bf16[256,1280]{1,0:T(8,128)(2,1)S(1)}, u32[]{:S(2)}, u32[]{:S(2)}) %collective-permute-start.15) | collective-permute-done | bytes 655392 | tf_op jit(solution)/shard_map/ppermute | solution.py:121
  67.9 1.9 %packet.2 = (bf16[2,256,1280]{2,1,0:T(8,128)(2,1)}, bf16[2,256,1280]{2,1,0:T(8,128)(2,1)}) custom-call(bf16[2,256,1280]{2,1,0:T(8,128)(2,1)S(1)} %copy-done, bf16[256,1280]{1,0:T(8,128)(2,1)S(1)} %collective-permute-done.15.low_in.refs_5_, bf16[256,1280]{1,0:T(8,128)(2,1)S(1)} %collective-permute-done.16.high_in.refs_6_), custom_call_target="tpu_custom_call" | custom-call | tf_op jit(solution)/shard_map/packet/pallas_call | solution.py:173
  69.8 4.3 %collective-permute-start.24 = (bf16[2,256,1280]{2,1,0:T(8,128)(2,1)}, bf16[2,256,1280]{2,1,0:T(8,128)(2,1)}, u32[]{:S(2)}, u32[]{:S(2)}) collective-permute-start(bf16[2,256,1280]{2,1,0:T(8,128)(2,1)} %get-tuple-element.78), channel_id=1, source_target_pairs={{0,8},{4,12},{8,0},{12,4},{16,24},{20,28},{24,16},{28,20},{1,9},{5... | collective-permute-start | bytes 3932168 | tf_op jit(solution)/shard_map/ppermute | solution.py:121
  74.1 1.3 collective-permute-start.25
  75.4 1.5 %collective-permute-done.12 = f32[128,512]{1,0:T(8,128)S(1)} collective-permute-done((f32[128,512]{1,0:T(8,128)S(1)}, f32[128,512]{1,0:T(8,128)S(1)}, u32[]{:S(2)}, u32[]{:S(2)}) %collective-permute-start.12) | collective-permute-done | bytes 262176 | tf_op jit(solution)/shard_map/ppermute | solution.py:121
  77.0 2.7 %attention.1.own_in_ref = bf16[128,512]{1,0:T(8,128)(2,1)S(1)} custom-call(bf16[128,512]{1,0:T(8,128)(2,1)S(1)} %add_convert_fusion.2.q_ref, bf16[128,1024]{1,0:T(8,128)(2,1)S(1)} %collective-permute-done.13.low_ref, bf16[128,1024]{1,0:T(8,128)(2,1)S(1)} %add_convert_fusion.own_ref, bf16[128,1024]{1,0:T(8,128)(2,1)S(1)} %collective-permute-done.14.high_ref, ...), custom_call_target="tpu_custom_call" | custom-call | flops 100663296 | bytes 1572864 | tf_op jit(solution)/shard_map/attention/pallas_call | solution.py:106
  79.9 1.2 collective-permute-done.17.other_in_ref
  81.1 1.1 attention_out.1
  82.2 3.6 %collective-permute-start.20 = (bf16[256,256]{1,0:T(8,128)(2,1)S(1)}, bf16[256,256]{1,0:T(8,128)(2,1)S(1)}, u32[]{:S(2)}, u32[]{:S(2)}) collective-permute-start(bf16[256,256]{1,0:T(8,128)(2,1)S(1)} %get-tuple-element.75), channel_id=1, source_target_pairs={{0,3},{1,0},{2,1},{3,2},{4,7},{5,4},{6,5},{7,6},{8,11},{9,8},{10,9... | collective-permute-start | bytes 393224 | tf_op jit(solution)/shard_map/ppermute | solution.py:121
  85.9 1.0 collective-permute-start.18
  86.9 2.9 %collective-permute-done.20 = bf16[256,256]{1,0:T(8,128)(2,1)S(1)} collective-permute-done((bf16[256,256]{1,0:T(8,128)(2,1)S(1)}, bf16[256,256]{1,0:T(8,128)(2,1)S(1)}, u32[]{:S(2)}, u32[]{:S(2)}) %collective-permute-start.20) | collective-permute-done | bytes 131104 | tf_op jit(solution)/shard_map/ppermute | solution.py:121
  89.8 7.8 %collective-permute-done.19 = bf16[256,256]{1,0:T(8,128)(2,1)S(1)} collective-permute-done((bf16[256,256]{1,0:T(8,128)(2,1)S(1)}, bf16[256,256]{1,0:T(8,128)(2,1)S(1)}, u32[]{:S(2)}, u32[]{:S(2)}) %collective-permute-start.19) | collective-permute-done | bytes 131104 | tf_op jit(solution)/shard_map/ppermute | solution.py:121
  97.8 1.5 %collective-permute-start.23 = (bf16[256,256]{1,0:T(8,128)(2,1)S(1)}, bf16[256,256]{1,0:T(8,128)(2,1)}, u32[]{:S(2)}, u32[]{:S(2)}) collective-permute-start(bf16[256,256]{1,0:T(8,128)(2,1)S(1)} %get-tuple-element.95.refs_0_), channel_id=1, source_target_pairs={{0,3},{1,0},{2,1},{3,2},{4,7},{5,4},{6,5},{7,6},{8,11},{9,8},{10,9... | collective-permute-start | bytes 393224 | tf_op jit(solution)/shard_map/ppermute | solution.py:121
  99.2 0.6 collective-permute-start.21
  99.8 2.5 %collective-permute-start.22 = (bf16[256,256]{1,0:T(8,128)(2,1)S(1)}, bf16[256,256]{1,0:T(8,128)(2,1)}, u32[]{:S(2)}, u32[]{:S(2)}) collective-permute-start(bf16[256,256]{1,0:T(8,128)(2,1)S(1)} %get-tuple-element.95.refs_0_), channel_id=1, source_target_pairs={{0,2},{1,3},{2,0},{3,1},{4,6},{5,7},{6,4},{7,5},{8,10},{9,11},{10,... | collective-permute-start | bytes 393224 | tf_op jit(solution)/shard_map/ppermute | solution.py:121
  102.3 0.7 reshape.62.gain_ref
  103.0 0.8 collective-permute-done.23.refs_3_
  103.9 1.0 copy-done.12
  104.8 1.0 copy-done.15
  105.9 2.0 %collective-permute-start.27 = (bf16[2,640,256]{2,1,0:T(8,128)(2,1)S(1)}, bf16[2,640,256]{2,1,0:T(8,128)(2,1)S(1)}, u32[]{:S(2)}, u32[]{:S(2)}) collective-permute-start(bf16[2,640,256]{2,1,0:T(8,128)(2,1)S(1)} %get-tuple-element.85), channel_id=1, source_target_pairs={{0,8},{4,12},{8,0},{12,4},{16,24},{20,28},{24,16},{28,20},{1,9},{5... | collective-permute-start | bytes 1966088 | tf_op jit(solution)/shard_map/ppermute | solution.py:121
  107.9 1.0 multiply_reduce_fusion
  109.0 0.6 collective-permute-start.28
  109.6 2.3 %collective-permute-done.22.refs_2_ = bf16[256,256]{1,0:T(8,128)(2,1)} collective-permute-done((bf16[256,256]{1,0:T(8,128)(2,1)S(1)}, bf16[256,256]{1,0:T(8,128)(2,1)}, u32[]{:S(2)}, u32[]{:S(2)}) %collective-permute-start.22) | collective-permute-done | bytes 131104 | tf_op jit(solution)/shard_map/ppermute | solution.py:121
  111.9 3.5 %ffn_in.1 = (f32[128,2560]{1,0:T(8,128)S(1)}, bf16[128,2560]{1,0:T(8,128)(2,1)S(1)}) custom-call(s32[2]{0:T(128)S(1)} %pad_add_fusion.place_ref, f32[8,256]{1,0:T(8,128)S(1)} %reshape.62.gain_ref, bf16[256,256]{1,0:T(8,128)(2,1)S(1)} %get-tuple-element.95.refs_0_, bf16[256,256]{1,0:T(8,128)(2,1)S(1)} %collective-permute-done.21.refs_1_, ...), custom_call_target="tpu_custom_call" | custom-call | flops 1342177280 | bytes 5242880 | tf_op jit(solution)/shard_map/ffn_in/pallas_call | solution.py:353
  115.5 1.0 multiply_reduce_fusion.1
  116.6 0.6 collective-permute-start.29
  117.2 0.8 collective-permute-done.29
  118.0 2.5 %collective-permute-done.27.refs_3_ = bf16[2,640,256]{2,1,0:T(8,128)(2,1)S(1)} collective-permute-done((bf16[2,640,256]{2,1,0:T(8,128)(2,1)S(1)}, bf16[2,640,256]{2,1,0:T(8,128)(2,1)S(1)}, u32[]{:S(2)}, u32[]{:S(2)}) %collective-permute-start.27) | collective-permute-done | bytes 655392 | tf_op jit(solution)/shard_map/ppermute | solution.py:121
  120.5 2.6 %collective-permute-done.28.refs_4_ = bf16[2,640,256]{2,1,0:T(8,128)(2,1)S(1)} collective-permute-done((bf16[2,640,256]{2,1,0:T(8,128)(2,1)S(1)}, bf16[2,640,256]{2,1,0:T(8,128)(2,1)S(1)}, u32[]{:S(2)}, u32[]{:S(2)}) %collective-permute-start.28) | collective-permute-done | bytes 655392 | tf_op jit(solution)/shard_map/ppermute | solution.py:121
  124.3 0.7 and_reduce_fusion
  125.3 1.7 %ffn_out.1 = (f32[256,256]{1,0:T(8,128)S(1)}, bf16[256,256]{1,0:T(8,128)(2,1)S(1)}, bf16[256,256]{1,0:T(8,128)(2,1)S(1)}, bf16[256,256]{1,0:T(8,128)(2,1)S(1)}) custom-call(s32[2]{0:T(128)S(1)} %pad_add_fusion.place_ref, bf16[128,1280]{1,0:T(8,128)(2,1)S(1)} %fusion.8.own_in_ref, bf16[128,1280]{1,0:T(8,128)(2,1)S(1)} %collective-permute-done.30.other_in_ref, ...), custom_call_target="tpu_custom_call" | custom-call | flops 671088640 | bytes 2621440 | tf_op jit(solution)/shard_map/ffn_out/pallas_call | solution.py:410
  127.0 2.0 %collective-permute-start.33 = (bf16[256,256]{1,0:T(8,128)(2,1)S(1)}, bf16[256,256]{1,0:T(8,128)(2,1)S(1)}, u32[]{:S(2)}, u32[]{:S(2)}) collective-permute-start(bf16[256,256]{1,0:T(8,128)(2,1)S(1)} %get-tuple-element.93), channel_id=1, source_target_pairs={{0,3},{1,0},{2,1},{3,2},{4,7},{5,4},{6,5},{7,6},{8,11},{9,8},{10,9... | collective-permute-start | bytes 393224 | tf_op jit(solution)/shard_map/ppermute | solution.py:121
  128.9 0.7 collective-permute-start.32
  129.7 1.7 %collective-permute-start.31 = (bf16[256,256]{1,0:T(8,128)(2,1)S(1)}, bf16[256,256]{1,0:T(8,128)(2,1)S(1)}, u32[]{:S(2)}, u32[]{:S(2)}) collective-permute-start(bf16[256,256]{1,0:T(8,128)(2,1)S(1)} %get-tuple-element.91), channel_id=1, source_target_pairs={{0,1},{1,2},{2,3},{3,0},{4,5},{5,6},{6,7},{7,4},{8,9},{9,10},{10,1... | collective-permute-start | bytes 393224 | tf_op jit(solution)/shard_map/ppermute | solution.py:121
  131.4 1.5 %collective-permute-done.33 = bf16[256,256]{1,0:T(8,128)(2,1)S(1)} collective-permute-done((bf16[256,256]{1,0:T(8,128)(2,1)S(1)}, bf16[256,256]{1,0:T(8,128)(2,1)S(1)}, u32[]{:S(2)}, u32[]{:S(2)}) %collective-permute-start.33) | collective-permute-done | bytes 131104 | tf_op jit(solution)/shard_map/ppermute | solution.py:121
  132.9 8.8 %collective-permute-done.32 = bf16[256,256]{1,0:T(8,128)(2,1)S(1)} collective-permute-done((bf16[256,256]{1,0:T(8,128)(2,1)S(1)}, bf16[256,256]{1,0:T(8,128)(2,1)S(1)}, u32[]{:S(2)}, u32[]{:S(2)}) %collective-permute-start.32) | collective-permute-done | bytes 131104 | tf_op jit(solution)/shard_map/ppermute | solution.py:121
  141.9 1.4 maximum_select_fusion
  143.3 0.7 maximum_select_fusion.1
  (90 shorter events, 2.6 us)
Async XLA Ops:
  0.6 1.1 copy-start.17
  1.8 0.9 copy-start.19
  2.7 4.6 %copy-start.18 = (bf16[128,512]{1,0:T(8,128)(2,1)S(1)}, bf16[128,512]{1,0:T(8,128)(2,1)}, u32[]{:S(2)}) copy-start(bf16[128,512]{1,0:T(8,128)(2,1)} %refs_0_.1) | copy-start | bytes 393220
  2.7 10.1 %copy-start.22 = (f32[2048]{0:T(1024)S(1)}, f32[2048]{0:T(1024)}, u32[]{:S(2)}) copy-start(f32[2048]{0:T(1024)} %param.17) | copy-start | bytes 24580
  2.8 26.2 %collective-permute-start.4 = (bf16[2048,256]{1,0:T(8,128)(2,1)S(1)}, bf16[2048,256]{1,0:T(8,128)(2,1)S(1)}, u32[]{:S(2)}, u32[]{:S(2)}) collective-permute-start(bf16[2048,256]{1,0:T(8,128)(2,1)S(1)} %pack.1.refs_0_), channel_id=1, source_target_pairs={{0,8},{4,12},{8,0},{12,4},{16,24},{20,28},{24,16},{28,20},{1,9},{5... | collective-permute-start | bytes 3145736 | tf_op jit(solution)/shard_map/ppermute | solution.py:121
  5.8 24.6 %collective-permute-start.5 = (bf16[2048,256]{1,0:T(8,128)(2,1)S(1)}, bf16[2048,256]{1,0:T(8,128)(2,1)S(1)}, u32[]{:S(2)}, u32[]{:S(2)}) collective-permute-start(bf16[2048,256]{1,0:T(8,128)(2,1)S(1)} %pack.1.refs_0_), channel_id=1, source_target_pairs={{0,16},{4,20},{8,24},{12,28},{16,0},{20,4},{24,8},{28,12},{1,17},{... | collective-permute-start | bytes 3145736 | tf_op jit(solution)/shard_map/ppermute | solution.py:121
  7.3 8.4 %collective-permute-start = (bf16[128,512]{1,0:T(8,128)(2,1)S(1)}, bf16[128,512]{1,0:T(8,128)(2,1)S(1)}, u32[]{:S(2)}, u32[]{:S(2)}) collective-permute-start(bf16[128,512]{1,0:T(8,128)(2,1)S(1)} %copy-done.18), channel_id=1, source_target_pairs={{0,1},{1,2},{2,3},{3,0},{4,5},{5,6},{6,7},{7,4},{8,9},{9,10},{10,1... | collective-permute-start | bytes 393224 | tf_op jit(solution)/shard_map/ppermute | solution.py:121
  8.9 10.7 %collective-permute-start.1 = (bf16[128,512]{1,0:T(8,128)(2,1)S(1)}, bf16[128,512]{1,0:T(8,128)(2,1)S(1)}, u32[]{:S(2)}, u32[]{:S(2)}) collective-permute-start(bf16[128,512]{1,0:T(8,128)(2,1)S(1)} %copy-done.18), channel_id=1, source_target_pairs={{0,2},{1,3},{2,0},{3,1},{4,6},{5,7},{6,4},{7,5},{8,10},{9,11},{10,... | collective-permute-start | bytes 393224 | tf_op jit(solution)/shard_map/ppermute | solution.py:121
  11.5 8.3 %collective-permute-start.2 = (bf16[128,512]{1,0:T(8,128)(2,1)S(1)}, bf16[128,512]{1,0:T(8,128)(2,1)}, u32[]{:S(2)}, u32[]{:S(2)}) collective-permute-start(bf16[128,512]{1,0:T(8,128)(2,1)S(1)} %copy-done.18), channel_id=1, source_target_pairs={{0,3},{1,0},{2,1},{3,2},{4,7},{5,4},{6,5},{7,6},{8,11},{9,8},{10,9... | collective-permute-start | bytes 393224 | tf_op jit(solution)/shard_map/ppermute | solution.py:121
  21.0 11.7 %copy-start.23 = (s32[255]{0:T(256)S(1)}, s32[255]{0:T(256)}, u32[]{:S(2)}) copy-start(s32[255]{0:T(256)} %param.15) | copy-start | bytes 3064
  21.0 11.7 %copy-start.20 = (s32[1024]{0:T(1024)S(1)}, s32[1024]{0:T(1024)}, u32[]{:S(2)}) copy-start(s32[1024]{0:T(1024)} %param.14) | copy-start | bytes 12292
  21.1 11.7 %copy-start.21 = (f32[32,8]{0,1:T(8,128)S(1)}, f32[32,8]{0,1:T(8,128)}, u32[]{:S(2)}) copy-start(f32[32,8]{0,1:T(8,128)} %param.19) | copy-start | bytes 3076
  30.4 3.0 %copy-start.1 = (bf16[2048,256]{1,0:T(8,128)(2,1)}, bf16[2048,256]{1,0:T(8,128)(2,1)S(1)}, u32[]{:S(2)}) copy-start(bf16[2048,256]{1,0:T(8,128)(2,1)S(1)} %collective-permute-done.5.high_in.refs_2_) | copy-start | bytes 3145732
  30.4 3.6 %collective-permute-start.6 = (bf16[4,128,256]{2,1,0:T(8,128)(2,1)S(1)}, bf16[4,128,256]{2,1,0:T(8,128)(2,1)S(1)}, u32[]{:S(2)}, u32[]{:S(2)}) collective-permute-start(bf16[4,128,256]{2,1,0:T(8,128)(2,1)S(1)} %get-tuple-element.57), channel_id=1, source_target_pairs={{0,4},{4,0},{8,12},{12,8},{16,20},{20,16},{24,28},{28,24},{1,5},{5... | collective-permute-start | bytes 786440 | tf_op jit(solution)/shard_map/ppermute | solution.py:121
  30.5 3.5 %copy-start.3 = (bf16[1280,256]{1,0:T(8,128)(2,1)S(1)}, bf16[1280,256]{1,0:T(8,128)(2,1)}, u32[]{:S(2)}) copy-start(bf16[1280,256]{1,0:T(8,128)(2,1)} %param.23) | copy-start | bytes 1966084
  30.5 14.8 %collective-permute-start.7 = (bf16[1024,256]{1,0:T(8,128)(2,1)S(1)}, bf16[1024,256]{1,0:T(8,128)(2,1)S(1)}, u32[]{:S(2)}, u32[]{:S(2)}) collective-permute-start(bf16[1024,256]{1,0:T(8,128)(2,1)S(1)} %get-tuple-element.58), channel_id=1, source_target_pairs={{0,16},{4,20},{8,24},{12,28},{16,0},{20,4},{24,8},{28,12},{1,17},{... | collective-permute-start | bytes 1572872 | tf_op jit(solution)/shard_map/ppermute | solution.py:121
  32.1 14.8 %collective-permute-start.8 = (bf16[1024,256]{1,0:T(8,128)(2,1)S(1)}, bf16[1024,256]{1,0:T(8,128)(2,1)S(1)}, u32[]{:S(2)}, u32[]{:S(2)}) collective-permute-start(bf16[1024,256]{1,0:T(8,128)(2,1)S(1)} %get-tuple-element.59), channel_id=1, source_target_pairs={{0,8},{4,12},{8,0},{12,4},{16,24},{20,28},{24,16},{28,20},{1,9},{5... | collective-permute-start | bytes 1572872 | tf_op jit(solution)/shard_map/ppermute | solution.py:121
  32.6 1.3 collective-permute-start.3
  34.0 12.9 %copy-start.2 = (bf16[2048,256]{1,0:T(8,128)(2,1)S(1)}, bf16[2048,256]{1,0:T(8,128)(2,1)}, u32[]{:S(2)}) copy-start(bf16[2048,256]{1,0:T(8,128)(2,1)} %copy-done.1) | copy-start | bytes 3145732
  34.1 19.8 %collective-permute-start.10 = (bf16[640,256]{1,0:T(8,128)(2,1)S(1)}, bf16[640,256]{1,0:T(8,128)(2,1)S(1)}, u32[]{:S(2)}, u32[]{:S(2)}) collective-permute-start(bf16[640,256]{1,0:T(8,128)(2,1)S(1)} %get-tuple-element.99), channel_id=1, source_target_pairs={{0,8},{4,12},{8,0},{12,4},{16,24},{20,28},{24,16},{28,20},{1,9},{5... | collective-permute-start | bytes 983048 | tf_op jit(solution)/shard_map/ppermute | solution.py:121
  35.6 12.9 %copy-start = (bf16[2,256,1280]{2,1,0:T(8,128)(2,1)S(1)}, bf16[2,256,1280]{2,1,0:T(8,128)(2,1)}, u32[]{:S(2)}) copy-start(bf16[2,256,1280]{2,1,0:T(8,128)(2,1)} %refs_4_) | copy-start | bytes 3932164
  35.6 18.3 %collective-permute-start.11 = (bf16[640,256]{1,0:T(8,128)(2,1)S(1)}, bf16[640,256]{1,0:T(8,128)(2,1)S(1)}, u32[]{:S(2)}, u32[]{:S(2)}) collective-permute-start(bf16[640,256]{1,0:T(8,128)(2,1)S(1)} %get-tuple-element.98), channel_id=1, source_target_pairs={{0,16},{4,20},{8,24},{12,28},{16,0},{20,4},{24,8},{28,12},{1,17},{... | collective-permute-start | bytes 983048 | tf_op jit(solution)/shard_map/ppermute | solution.py:121
  48.4 5.5 %collective-permute-start.9 = (f32[128,1024]{1,0:T(8,128)S(1)}, f32[128,1024]{1,0:T(8,128)S(1)}, u32[]{:S(2)}, u32[]{:S(2)}) collective-permute-start(f32[128,1024]{1,0:T(8,128)S(1)} %get-tuple-element.63), channel_id=1, source_target_pairs={{0,4},{4,0},{8,12},{12,8},{16,20},{20,16},{24,28},{28,24},{1,5},{5... | collective-permute-start | bytes 1572872 | tf_op jit(solution)/shard_map/ppermute | solution.py:121
  48.6 19.3 %collective-permute-start.15 = (bf16[256,1280]{1,0:T(8,128)(2,1)S(1)}, bf16[256,1280]{1,0:T(8,128)(2,1)S(1)}, u32[]{:S(2)}, u32[]{:S(2)}) collective-permute-start(bf16[256,1280]{1,0:T(8,128)(2,1)S(1)} %get-tuple-element.97), channel_id=1, source_target_pairs={{0,8},{4,12},{8,0},{12,4},{16,24},{20,28},{24,16},{28,20},{1,9},{5... | collective-permute-start | bytes 1966088 | tf_op jit(solution)/shard_map/ppermute | solution.py:121
  49.2 18.7 %collective-permute-start.16 = (bf16[256,1280]{1,0:T(8,128)(2,1)S(1)}, bf16[256,1280]{1,0:T(8,128)(2,1)S(1)}, u32[]{:S(2)}, u32[]{:S(2)}) collective-permute-start(bf16[256,1280]{1,0:T(8,128)(2,1)S(1)} %get-tuple-element.96), channel_id=1, source_target_pairs={{0,16},{4,20},{8,24},{12,28},{16,0},{20,4},{24,8},{28,12},{1,17},{... | collective-permute-start | bytes 1966088 | tf_op jit(solution)/shard_map/ppermute | solution.py:121
  53.9 15.9 %copy-start.11 = (bf16[640,256]{1,0:T(8,128)(2,1)}, bf16[640,256]{1,0:T(8,128)(2,1)S(1)}, u32[]{:S(2)}) copy-start(bf16[640,256]{1,0:T(8,128)(2,1)S(1)} %collective-permute-done.10.low_in.refs_1_) | copy-start | bytes 983044
  53.9 15.9 %copy-start.14 = (bf16[640,256]{1,0:T(8,128)(2,1)}, bf16[640,256]{1,0:T(8,128)(2,1)S(1)}, u32[]{:S(2)}) copy-start(bf16[640,256]{1,0:T(8,128)(2,1)S(1)} %collective-permute-done.11.high_in.refs_2_) | copy-start | bytes 983044
  54.0 23.1 %copy-start.9 = (bf16[128,1024]{1,0:T(8,128)(2,1)}, bf16[128,1024]{1,0:T(8,128)(2,1)S(1)}, u32[]{:S(2)}) copy-start(bf16[128,1024]{1,0:T(8,128)(2,1)S(1)} %add_convert_fusion.own_ref) | copy-start | bytes 786436
  54.0 14.0 %collective-permute-start.13 = (bf16[128,1024]{1,0:T(8,128)(2,1)S(1)}, bf16[128,1024]{1,0:T(8,128)(2,1)S(1)}, u32[]{:S(2)}, u32[]{:S(2)}) collective-permute-start(bf16[128,1024]{1,0:T(8,128)(2,1)S(1)} %add_convert_fusion.own_ref), channel_id=1, source_target_pairs={{0,4},{4,8},{8,12},{12,16},{16,20},{20,24},{24,28},{1,5},{5,9},{9,... | collective-permute-start | bytes 786440 | tf_op jit(solution)/shard_map/ppermute | solution.py:492
  55.3 12.7 %collective-permute-start.14 = (bf16[128,1024]{1,0:T(8,128)(2,1)S(1)}, bf16[128,1024]{1,0:T(8,128)(2,1)S(1)}, u32[]{:S(2)}, u32[]{:S(2)}) collective-permute-start(bf16[128,1024]{1,0:T(8,128)(2,1)S(1)} %add_convert_fusion.own_ref), channel_id=1, source_target_pairs={{4,0},{8,4},{12,8},{16,12},{20,16},{24,20},{28,24},{5,1},{9,5},{13... | collective-permute-start | bytes 786440 | tf_op jit(solution)/shard_map/ppermute | solution.py:493
  67.9 1.9 %copy-start.5 = (bf16[256,1280]{1,0:T(8,128)(2,1)}, bf16[256,1280]{1,0:T(8,128)(2,1)S(1)}, u32[]{:S(2)}) copy-start(bf16[256,1280]{1,0:T(8,128)(2,1)S(1)} %collective-permute-done.15.low_in.refs_5_) | copy-start | bytes 1966084
  67.9 1.9 %copy-start.7 = (bf16[256,1280]{1,0:T(8,128)(2,1)}, bf16[256,1280]{1,0:T(8,128)(2,1)S(1)}, u32[]{:S(2)}) copy-start(bf16[256,1280]{1,0:T(8,128)(2,1)S(1)} %collective-permute-done.16.high_in.refs_6_) | copy-start | bytes 1966084
  69.8 42.0 %collective-permute-start.24 = (bf16[2,256,1280]{2,1,0:T(8,128)(2,1)}, bf16[2,256,1280]{2,1,0:T(8,128)(2,1)}, u32[]{:S(2)}, u32[]{:S(2)}) collective-permute-start(bf16[2,256,1280]{2,1,0:T(8,128)(2,1)} %get-tuple-element.78), channel_id=1, source_target_pairs={{0,8},{4,12},{8,0},{12,4},{16,24},{20,28},{24,16},{28,20},{1,9},{5... | collective-permute-start | bytes 3932168 | tf_op jit(solution)/shard_map/ppermute | solution.py:121
  74.1 37.7 %collective-permute-start.25 = (bf16[2,256,1280]{2,1,0:T(8,128)(2,1)}, bf16[2,256,1280]{2,1,0:T(8,128)(2,1)}, u32[]{:S(2)}, u32[]{:S(2)}) collective-permute-start(bf16[2,256,1280]{2,1,0:T(8,128)(2,1)} %get-tuple-element.79), channel_id=1, source_target_pairs={{0,16},{4,20},{8,24},{12,28},{16,0},{20,4},{24,8},{28,12},{1,17},{... | collective-permute-start | bytes 3932168 | tf_op jit(solution)/shard_map/ppermute | solution.py:121
  75.4 1.5 %collective-permute-start.12 = (f32[128,512]{1,0:T(8,128)S(1)}, f32[128,512]{1,0:T(8,128)S(1)}, u32[]{:S(2)}, u32[]{:S(2)}) collective-permute-start(f32[128,512]{1,0:T(8,128)S(1)} %get-tuple-element.66), channel_id=1, source_target_pairs={{0,4},{4,0},{8,12},{12,8},{16,20},{20,16},{24,28},{28,24},{1,5},{5... | collective-permute-start | bytes 786440 | tf_op jit(solution)/shard_map/ppermute | solution.py:121
  79.7 1.4 collective-permute-start.17
  82.2 21.7 %copy-start.4 = (bf16[1280,256]{1,0:T(8,128)(2,1)S(1)}, bf16[1280,256]{1,0:T(8,128)(2,1)}, u32[]{:S(2)}) copy-start(bf16[1280,256]{1,0:T(8,128)(2,1)} %param.23) | copy-start | bytes 1966084
  82.2 29.7 %copy-start.6 = (bf16[256,1280]{1,0:T(8,128)(2,1)S(1)}, bf16[256,1280]{1,0:T(8,128)(2,1)}, u32[]{:S(2)}) copy-start(bf16[256,1280]{1,0:T(8,128)(2,1)} %copy-done.5) | copy-start | bytes 1966084
  82.2 29.6 %copy-start.8 = (bf16[256,1280]{1,0:T(8,128)(2,1)S(1)}, bf16[256,1280]{1,0:T(8,128)(2,1)}, u32[]{:S(2)}) copy-start(bf16[256,1280]{1,0:T(8,128)(2,1)} %copy-done.7) | copy-start | bytes 1966084
  82.2 7.6 %collective-permute-start.20 = (bf16[256,256]{1,0:T(8,128)(2,1)S(1)}, bf16[256,256]{1,0:T(8,128)(2,1)S(1)}, u32[]{:S(2)}, u32[]{:S(2)}) collective-permute-start(bf16[256,256]{1,0:T(8,128)(2,1)S(1)} %get-tuple-element.75), channel_id=1, source_target_pairs={{0,3},{1,0},{2,1},{3,2},{4,7},{5,4},{6,5},{7,6},{8,11},{9,8},{10,9... | collective-permute-start | bytes 393224 | tf_op jit(solution)/shard_map/ppermute | solution.py:121
  85.9 11.7 %collective-permute-start.19 = (bf16[256,256]{1,0:T(8,128)(2,1)S(1)}, bf16[256,256]{1,0:T(8,128)(2,1)S(1)}, u32[]{:S(2)}, u32[]{:S(2)}) collective-permute-start(bf16[256,256]{1,0:T(8,128)(2,1)S(1)} %get-tuple-element.74), channel_id=1, source_target_pairs={{0,2},{1,3},{2,0},{3,1},{4,6},{5,7},{6,4},{7,5},{8,10},{9,11},{10,... | collective-permute-start | bytes 393224 | tf_op jit(solution)/shard_map/ppermute | solution.py:121
  85.9 11.7 %collective-permute-start.18 = (bf16[256,256]{1,0:T(8,128)(2,1)S(1)}, bf16[256,256]{1,0:T(8,128)(2,1)S(1)}, u32[]{:S(2)}, u32[]{:S(2)}) collective-permute-start(bf16[256,256]{1,0:T(8,128)(2,1)S(1)} %get-tuple-element.73), channel_id=1, source_target_pairs={{0,1},{1,2},{2,3},{3,0},{4,5},{5,6},{6,7},{7,4},{8,9},{9,10},{10,1... | collective-permute-start | bytes 393224 | tf_op jit(solution)/shard_map/ppermute | solution.py:121
  97.8 6.1 %collective-permute-start.23 = (bf16[256,256]{1,0:T(8,128)(2,1)S(1)}, bf16[256,256]{1,0:T(8,128)(2,1)}, u32[]{:S(2)}, u32[]{:S(2)}) collective-permute-start(bf16[256,256]{1,0:T(8,128)(2,1)S(1)} %get-tuple-element.95.refs_0_), channel_id=1, source_target_pairs={{0,3},{1,0},{2,1},{3,2},{4,7},{5,4},{6,5},{7,6},{8,11},{9,8},{10,9... | collective-permute-start | bytes 393224 | tf_op jit(solution)/shard_map/ppermute | solution.py:121
  99.2 9.7 %collective-permute-start.21 = (bf16[256,256]{1,0:T(8,128)(2,1)S(1)}, bf16[256,256]{1,0:T(8,128)(2,1)S(1)}, u32[]{:S(2)}, u32[]{:S(2)}) collective-permute-start(bf16[256,256]{1,0:T(8,128)(2,1)S(1)} %get-tuple-element.95.refs_0_), channel_id=1, source_target_pairs={{0,1},{1,2},{2,3},{3,0},{4,5},{5,6},{6,7},{7,4},{8,9},{9,10},{10,1... | collective-permute-start | bytes 393224 | tf_op jit(solution)/shard_map/ppermute | solution.py:121
  99.8 12.0 %collective-permute-start.22 = (bf16[256,256]{1,0:T(8,128)(2,1)S(1)}, bf16[256,256]{1,0:T(8,128)(2,1)}, u32[]{:S(2)}, u32[]{:S(2)}) collective-permute-start(bf16[256,256]{1,0:T(8,128)(2,1)S(1)} %get-tuple-element.95.refs_0_), channel_id=1, source_target_pairs={{0,2},{1,3},{2,0},{3,1},{4,6},{5,7},{6,4},{7,5},{8,10},{9,11},{10,... | collective-permute-start | bytes 393224 | tf_op jit(solution)/shard_map/ppermute | solution.py:121
  103.9 1.0 copy-start.12
  104.8 1.0 copy-start.15
  105.9 14.6 %collective-permute-start.27 = (bf16[2,640,256]{2,1,0:T(8,128)(2,1)S(1)}, bf16[2,640,256]{2,1,0:T(8,128)(2,1)S(1)}, u32[]{:S(2)}, u32[]{:S(2)}) collective-permute-start(bf16[2,640,256]{2,1,0:T(8,128)(2,1)S(1)} %get-tuple-element.85), channel_id=1, source_target_pairs={{0,8},{4,12},{8,0},{12,4},{16,24},{20,28},{24,16},{28,20},{1,9},{5... | collective-permute-start | bytes 1966088 | tf_op jit(solution)/shard_map/ppermute | solution.py:121
  109.0 14.1 %collective-permute-start.28 = (bf16[2,640,256]{2,1,0:T(8,128)(2,1)S(1)}, bf16[2,640,256]{2,1,0:T(8,128)(2,1)S(1)}, u32[]{:S(2)}, u32[]{:S(2)}) collective-permute-start(bf16[2,640,256]{2,1,0:T(8,128)(2,1)S(1)} %get-tuple-element.86), channel_id=1, source_target_pairs={{0,16},{4,20},{8,24},{12,28},{16,0},{20,4},{24,8},{28,12},{1,17},{... | collective-permute-start | bytes 1966088 | tf_op jit(solution)/shard_map/ppermute | solution.py:121
  115.4 7.7 %collective-permute-start.26 = (bf16[128,2560]{1,0:T(8,128)(2,1)S(1)}, bf16[128,2560]{1,0:T(8,128)(2,1)S(1)}, u32[]{:S(2)}, u32[]{:S(2)}) collective-permute-start(bf16[128,2560]{1,0:T(8,128)(2,1)S(1)} %get-tuple-element.81), channel_id=1, source_target_pairs={{0,4},{4,0},{8,12},{12,8},{16,20},{20,16},{24,28},{28,24},{1,5},{5... | collective-permute-start | bytes 1966088 | tf_op jit(solution)/shard_map/ppermute | solution.py:121
  116.6 1.4 collective-permute-start.29
  123.3 2.0 %copy-start.13 = (bf16[640,256]{1,0:T(8,128)(2,1)S(1)}, bf16[640,256]{1,0:T(8,128)(2,1)}, u32[]{:S(2)}) copy-start(bf16[640,256]{1,0:T(8,128)(2,1)} %copy-done.11) | copy-start | bytes 983044
  123.3 1.9 %copy-start.16 = (bf16[640,256]{1,0:T(8,128)(2,1)S(1)}, bf16[640,256]{1,0:T(8,128)(2,1)}, u32[]{:S(2)}) copy-start(bf16[640,256]{1,0:T(8,128)(2,1)} %copy-done.14) | copy-start | bytes 983044
  123.6 1.7 %collective-permute-start.30 = (bf16[128,1280]{1,0:T(8,128)(2,1)S(1)}, bf16[128,1280]{1,0:T(8,128)(2,1)S(1)}, u32[]{:S(2)}, u32[]{:S(2)}) collective-permute-start(bf16[128,1280]{1,0:T(8,128)(2,1)S(1)} %fusion.8.own_in_ref), channel_id=1, source_target_pairs={{0,4},{4,0},{8,12},{12,8},{16,20},{20,16},{24,28},{28,24},{1,5},{5... | collective-permute-start | bytes 983048 | tf_op jit(solution)/shard_map/ppermute | solution.py:121
  125.0 6.3 %copy-start.10 = (bf16[128,1024]{1,0:T(8,128)(2,1)S(1)}, bf16[128,1024]{1,0:T(8,128)(2,1)}, u32[]{:S(2)}) copy-start(bf16[128,1024]{1,0:T(8,128)(2,1)} %copy-done.9) | copy-start | bytes 786436
  127.0 5.9 %collective-permute-start.33 = (bf16[256,256]{1,0:T(8,128)(2,1)S(1)}, bf16[256,256]{1,0:T(8,128)(2,1)S(1)}, u32[]{:S(2)}, u32[]{:S(2)}) collective-permute-start(bf16[256,256]{1,0:T(8,128)(2,1)S(1)} %get-tuple-element.93), channel_id=1, source_target_pairs={{0,3},{1,0},{2,1},{3,2},{4,7},{5,4},{6,5},{7,6},{8,11},{9,8},{10,9... | collective-permute-start | bytes 393224 | tf_op jit(solution)/shard_map/ppermute | solution.py:121
  128.9 12.8 %collective-permute-start.32 = (bf16[256,256]{1,0:T(8,128)(2,1)S(1)}, bf16[256,256]{1,0:T(8,128)(2,1)S(1)}, u32[]{:S(2)}, u32[]{:S(2)}) collective-permute-start(bf16[256,256]{1,0:T(8,128)(2,1)S(1)} %get-tuple-element.92), channel_id=1, source_target_pairs={{0,2},{1,3},{2,0},{3,1},{4,6},{5,7},{6,4},{7,5},{8,10},{9,11},{10,... | collective-permute-start | bytes 393224 | tf_op jit(solution)/shard_map/ppermute | solution.py:121
  129.7 12.1 %collective-permute-start.31 = (bf16[256,256]{1,0:T(8,128)(2,1)S(1)}, bf16[256,256]{1,0:T(8,128)(2,1)S(1)}, u32[]{:S(2)}, u32[]{:S(2)}) collective-permute-start(bf16[256,256]{1,0:T(8,128)(2,1)S(1)} %get-tuple-element.91), channel_id=1, source_target_pairs={{0,1},{1,2},{2,3},{3,0},{4,5},{5,6},{6,7},{7,4},{8,9},{9,10},{10,1... | collective-permute-start | bytes 393224 | tf_op jit(solution)/shard_map/ppermute | solution.py:121
  141.8 1.5 %collective-permute-start.34 = (bf16[128,256]{1,0:T(8,128)(2,1)S(1)}, bf16[128,256]{1,0:T(8,128)(2,1)S(1)}, u32[]{:S(2)}, u32[]{:S(2)}) collective-permute-start(bf16[128,256]{1,0:T(8,128)(2,1)S(1)} %get-tuple-element.103), channel_id=1, source_target_pairs={{0,4},{4,0},{8,12},{12,8},{16,20},{20,16},{24,28},{28,24},{1,5},{5... | collective-permute-start | bytes 196616 | tf_op jit(solution)/shard_map/ppermute | solution.py:121

commit v5 on v4

--- a/solution.py
+++ b/solution.py
@@ -108,7 +108,7 @@
         out_shape=jax.ShapeDtypeStruct(queries.shape, jnp.bfloat16),
         in_specs=[VMEM] * 5,
         out_specs=VMEM,
-        compiler_params=pltpu.CompilerParams(vmem_limit_bytes=16 << 20),
+        compiler_params=pltpu.CompilerParams(vmem_limit_bytes=8 << 20),
         cost_estimate=pl.CostEstimate(
             flops=4 * queries.size * span, bytes_accessed=4 * bias.size, transcendentals=bias.size
         ),
@@ -242,48 +242,29 @@
                 send_ref[:, where] = total[count:].astype(send_ref.dtype)
 
 
-def pack_kernel(qkv_ref, out_ref, packed_ref):
-    parts, depth, width = qkv_ref.shape
-    row = 0
-    for part in range(parts):
-        for start in range(0, width, depth):
-            packed_ref[row : row + depth, :] = qkv_ref[part, :, start : start + depth]
-            row += depth
-    packed_ref[row:, :] = out_ref[...]
-
-
-def packed(w_qkv, w_out):
-    parts, depth, width = w_qkv.shape
-    count = parts * width // depth
-    return pl.pallas_call(
-        pack_kernel,
-        out_shape=jax.ShapeDtypeStruct((count * depth + width, depth), w_qkv.dtype),
-        in_specs=[VMEM, VMEM],
-        out_specs=VMEM,
-        compiler_params=pltpu.CompilerParams(vmem_limit_bytes=8 << 20),
-        name="pack",
-    )(w_qkv, w_out)
-
-
-def relay_kernel(low_in, high_in, low_ref, high_ref):
-    half = low_ref.shape[0]
-    low_ref[...] = low_in[:half]
-    high_ref[...] = high_in[half:]
-
-
-def relayed(near):
-    if len(near) != 2:
+def relay_kernel(qkv_low, qkv_high, out_low, out_high, low_ref, high_ref):
+    half = low_ref.shape[2]
+    parts = qkv_low.shape[0]
+    low_ref[:parts] = qkv_low[:, :, :half]
+    low_ref[parts] = out_low[:half]
+    high_ref[:parts] = qkv_high[:, :, half:]
+    high_ref[parts] = out_high[half:]
+
+
+def relayed(qkv_near, out_near):
+    if len(qkv_near) != 2:
         return []
-    rows, width = near[0].shape
-    shape = jax.ShapeDtypeStruct((rows // 2, width), near[0].dtype)
-    return pl.pallas_call(
+    parts, depth, _ = qkv_near[0].shape
+    shape = jax.ShapeDtypeStruct((parts + 1, depth, depth), qkv_near[0].dtype)
+    low, high = pl.pallas_call(
         relay_kernel,
         out_shape=(shape, shape),
-        in_specs=[VMEM] * 2,
+        in_specs=[VMEM] * 4,
         out_specs=(VMEM, VMEM),
         compiler_params=pltpu.CompilerParams(vmem_limit_bytes=8 << 20),
         name="relay",
-    )(*near)
+    )(*qkv_near, *out_near)
+    return [pair_exchange(low, 2), pair_exchange(high, 1)]
 
 
 def qkv_kernel(place_ref, own_in_ref, other_in_ref, *refs):
@@ -291,19 +272,15 @@
     count = own_in_ref.shape[1]
     held[:, :count] = own_in_ref[...]
     held[:, count:] = other_in_ref[...]
-    blocks, depth = held.shape[0], weight_refs[0].shape[1]
+    blocks, width = held.shape[0], own_q.shape[1]
     direct = blocks - 1 if len(weight_refs) == blocks + 1 else blocks
-    width = own_q.shape[1]
 
     def piece(step, part, start, stop):
-        row = (part * width // depth + start // depth) * depth
-        offset = start % depth
         if step < direct:
-            return weight_refs[step][row : row + depth, offset : offset + stop - start]
-        half = weight_refs[direct].shape[0]
-        row = row - row // half * half
-        which = (part * width + start) // (half // depth * depth)
-        return weight_refs[direct + which][row : row + depth, offset : offset + stop - start]
+            return weight_refs[step][part, :, start:stop]
+        half = start // (width // 2)
+        offset = start - half * (width // 2)
+        return weight_refs[direct + half][part, :, offset : offset + stop - start]
 
     multiply_pieces(
         ((0,), (1, 2)), held, place_ref[0] // 2, piece, width, (own_q, own_kv), (send_q, send_kv)
@@ -320,7 +297,7 @@
         in_specs=[SMEM] + [VMEM] * (2 + len(pieces)),
         out_specs=tuple([VMEM] * 4),
         scratch_shapes=[pltpu.VMEM((blocks, 2 * count, depth), jnp.bfloat16)],
-        compiler_params=pltpu.CompilerParams(vmem_limit_bytes=16 << 20),
+        compiler_params=pltpu.CompilerParams(vmem_limit_bytes=8 << 20),
         cost_estimate=pl.CostEstimate(
             flops=12 * count * depth * blocks * width,
             bytes_accessed=6 * depth * blocks * width,
@@ -359,7 +336,7 @@
         in_specs=[SMEM] + [VMEM] * (1 + blocks + len(pieces)),
         out_specs=(VMEM, VMEM),
         scratch_shapes=[pltpu.VMEM((blocks, tokens_two, depth), jnp.bfloat16)],
-        compiler_params=pltpu.CompilerParams(vmem_limit_bytes=16 << 20),
+        compiler_params=pltpu.CompilerParams(vmem_limit_bytes=8 << 20),
         cost_estimate=pl.CostEstimate(
             flops=2 * tokens_two * depth * blocks * columns,
             bytes_accessed=2 * depth * blocks * columns,
@@ -369,7 +346,7 @@
     )(place, gain, *token_blocks, *pieces)
 
 
-def columns_kernel(first, place_ref, own_in_ref, other_in_ref, *refs):
+def columns_kernel(place_ref, own_in_ref, other_in_ref, *refs):
     blocks = lax.axis_size("col")
     *weight_refs, own_ref = refs[: len(refs) - blocks]
     send_refs, held = refs[len(refs) - blocks : -1], refs[-1]
@@ -379,7 +356,7 @@
     far = len(weight_refs) == blocks + 1
     direct = blocks - 1 if far else blocks
     for step in range(blocks):
-        if not first:
+        if len(weight_refs[0].shape) == 3:
             half = hidden.shape[1] // 2
             total = jnp.dot(
                 hidden[:, :half],
@@ -391,12 +368,13 @@
                 preferred_element_type=jnp.float32,
             )
         elif step < direct:
-            total = jnp.dot(hidden, weight_refs[step][first:, :], preferred_element_type=jnp.float32)
+            total = jnp.dot(hidden, weight_refs[step][...], preferred_element_type=jnp.float32)
         else:
-            skipped = first - weight_refs[direct].shape[0]
+            half = hidden.shape[1] // 2
+            low, high = (ref[ref.shape[0] - 1] for ref in weight_refs[direct:])
             total = jnp.dot(
-                hidden, weight_refs[direct + 1][skipped:, :], preferred_element_type=jnp.float32
-            )
+                hidden[:, :half], low, preferred_element_type=jnp.float32
+            ) + jnp.dot(hidden[:, half:], high, preferred_element_type=jnp.float32)
         held[lax.rem((pair ^ step) - col + blocks, blocks)] = total
     own_ref[...] = held[0]
     for step in range(1, blocks):
@@ -408,7 +386,7 @@
     width = pieces[0].shape[-1]
     blocks = lax.axis_size("col")
     return pl.pallas_call(
-        functools.partial(columns_kernel, pieces[0].size // width - depth),
+        columns_kernel,
         out_shape=(
             jax.ShapeDtypeStruct((2 * count, width), jnp.float32),
             *[jax.ShapeDtypeStruct((2 * count, width), jnp.bfloat16)] * (blocks - 1),
@@ -416,7 +394,7 @@
         in_specs=[SMEM] + [VMEM] * (2 + len(pieces)),
         out_specs=tuple([VMEM] * blocks),
         scratch_shapes=[pltpu.VMEM((blocks, 2 * count, width), jnp.float32)],
-        compiler_params=pltpu.CompilerParams(vmem_limit_bytes=16 << 20),
+        compiler_params=pltpu.CompilerParams(vmem_limit_bytes=8 << 20),
         cost_estimate=pl.CostEstimate(
             flops=4 * count * depth * width * blocks,
             bytes_accessed=2 * depth * width * blocks,
@@ -462,11 +440,10 @@
     core = row % 2
     place = jnp.stack([row, col]).astype(jnp.int32)
 
-    first = packed(w_qkv, w_out)
-    first_near = near_pieces(first)
+    qkv_near = near_pieces(w_qkv)
     token_blocks = gathered(tokens)
     kept, given = norm_tokens(place, gain_attn.reshape(cols, width), token_blocks)
-    received = other_core(after(given, *first_near))
+    out_near = near_pieces(after(w_out, token_blocks[1]))
     token_block = jnp.concatenate(
         [
             jnp.where(core == 0, tokens[:, :half], tokens[:, half:]),
@@ -475,18 +452,22 @@
         axis=0,
     )
     bias = masked_bias(row, segment_ids, bucket_table, rel_bias, count)
-    first_far = [pair_exchange(p, step) for p, step in zip(relayed(first_near), (2, 1))]
-    first_pieces = [first, *first_near, *first_far]
-    kept, bias, token_block = lax.optimization_barrier((kept, bias, token_block))
+    ready = lax.optimization_barrier((*qkv_near, *out_near, kept, given, bias, token_block))
+    *near, kept, given, bias, token_block = ready
+    received = other_core(given)
+    qkv_near, out_near = near[: len(near) // 2], near[len(near) // 2 :]
+    far = relayed(qkv_near, out_near)
     w_in, w_down, *_ = lax.optimization_barrier((w_in, w_down.reshape(2, -1, half), received))
     down_first = first_phase(w_down[0], w_down[1])
     in_first = first_phase(w_in[0], w_in[1])
     own_q, own_kv, send_q, send_kv = project_qkv(
-        place, kept, received, first_pieces
-    )
-    other_kv, *down_first = lax.optimization_barrier((other_core(send_kv), *down_first))
+        place, kept, received, [w_qkv, *qkv_near, *far]
+    )
+    other_kv, other_q, *down_first = lax.optimization_barrier(
+        (other_core(send_kv), other_core(send_q), *down_first)
+    )
     key_value = (own_kv + other_kv).astype(jnp.bfloat16)
-    queries = (own_q + other_core(after(send_q, key_value))).astype(jnp.bfloat16)
+    queries = (own_q + other_q).astype(jnp.bfloat16)
     forward = [(i, i + 1) for i in range(rows - 1)]
     backward = [(target, source) for source, target in forward]
     low = lax.ppermute(key_value, "row", forward)
@@ -495,9 +476,14 @@
     in_pieces = [w_in, *in_first, *second_phase(w_in, in_first)]
     context = attention(queries, low, key_value, high, bias)
     own, *sends = columns(
-        place, context, other_core(context), first_pieces, "attention_out"
-    )
-    middle = summed(own, sends, token_block)
+        place, context, other_core(context), [w_out, *out_near, *far], "attention_out"
+    )
+    stacked = jnp.stack([key_value[:, :width], key_value[:, width:]])
+    blocks = stacked.reshape(2, slot_index.shape[1], BLOCK, width)
+    kv_cache = (
+        jnp.zeros_like(blocks).at[:, slot_index[0]].set(blocks).reshape(2, count, width)
+    )
+    middle, kv_cache = lax.optimization_barrier((summed(own, sends, token_block), kv_cache))
 
     middle_blocks = gathered(middle)
     squares = square_sums(middle_blocks)
@@ -524,11 +510,6 @@
         jnp.concatenate([received, result[:count]], axis=1),
     )
 
-    stacked = jnp.stack([key_value[:, :width], key_value[:, width:]])
-    blocks = stacked.reshape(2, slot_index.shape[1], BLOCK, width)
-    kv_cache = (
-        jnp.zeros_like(blocks).at[:, slot_index[0]].set(blocks).reshape(2, count, width)
-    )
     return (output, kv_cache)
 
 

time: 144 us -> 139 us (0.965)
  waiting for transfers between devices: 76.3 us -> 70.3 us
  starting transfers between devices: 40.7 us -> 42.3 us
    ppermute x33 -> x35, waiting for transfers between devices: 76.3 us -> 70.3 us  [exchange(): lax.ppermute(value, axis, [(i, partner(i) % count) for i in range(count)])]
    reduce_sum x4, other arithmetic: 2.32 us -> 0.45 us  [square_sums(): jnp.sum(jnp.square(b.astype(jnp.float32)), axis=1)]
    ppermute x33 -> x35, starting transfers between devices: 38.1 us -> 39.7 us  [exchange(): lax.ppermute(value, axis, [(i, partner(i) % count) for i in range(count)])]
    unnamed x48 -> x34, local copies, waits for them, and re-layouts: 4.13 us -> 3.37 us
  transfers between devices with their start and end apart: 35 -> 37, of which waited for: 22 -> 21; matrix products, arithmetic and copies ran while one was open for 4% -> 4% of each run, Pallas kernels for 8% -> 7%
where the time goes in v5:
time: 139 us; the launch traced here: 138 us
  waiting for transfers between devices  70.3 us (51%)
  starting transfers between devices  42.3 us (30%)
  Pallas kernels  13.6 us (10%)
  local copies, waits for them, and re-layouts  5.62 us (4%)
  other arithmetic  4.92 us (4%)
  between operations  1.66 us (1%)
    ppermute x35, waiting for transfers between devices, exchange(): lax.ppermute(value, axis, [(i, partner(i) % count) for i in range(count)])  70.3 us
    ppermute x35, starting transfers between devices, exchange(): lax.ppermute(value, axis, [(i, partner(i) % count) for i in range(count)])  39.7 us
    unnamed x34, local copies, waits for them, and re-layouts  3.37 us
    pallas_call x1, Pallas kernels, project_ffn(): pl.pallas_call(ffn_in_kernel, out_shape=(jax.ShapeDtypeStruct((count, col...  3.34 us
    pallas_call x2, Pallas kernels, columns(): pl.pallas_call(columns_kernel, out_shape=(jax.ShapeDtypeStruct((2 * count...  2.79 us
  transfers between devices with their start and end apart: 37, of which 21 were waited for; matrix products, arithmetic and copies ran while one was open for 4% of the time, Pallas kernels for 7%

profile of v5, /device:TPU:0, one launch (start us, length us, event | category | flops | bytes accessed | tf_op | source)
XLA Modules:
  0.0 138.4 jit_solution(9587935977505826629)
XLA Ops:
  0.6 3.0 %collective-permute-start = (bf16[3,256,512]{2,1,0:T(8,128)(2,1)}, bf16[3,256,512]{2,1,0:T(8,128)(2,1)S(1)}, u32[]{:S(2)}, u32[]{:S(2)}) collective-permute-start(bf16[3,256,512]{2,1,0:T(8,128)(2,1)} %refs_0_.4), channel_id=1, source_target_pairs={{0,8},{4,12},{8,0},{12,4},{16,24},{20,28},{24,16},{28,20},{1,9},{5... | collective-permute-start | bytes 2359304 | tf_op jit(solution)/shard_map/ppermute | solution.py:121
  3.6 1.5 %collective-permute-start.1 = (bf16[3,256,512]{2,1,0:T(8,128)(2,1)}, bf16[3,256,512]{2,1,0:T(8,128)(2,1)S(1)}, u32[]{:S(2)}, u32[]{:S(2)}) collective-permute-start(bf16[3,256,512]{2,1,0:T(8,128)(2,1)} %refs_0_.4), channel_id=1, source_target_pairs={{0,16},{4,20},{8,24},{12,28},{16,0},{20,4},{24,8},{28,12},{1,17},{... | collective-permute-start | bytes 2359304 | tf_op jit(solution)/shard_map/ppermute | solution.py:121
  5.2 1.6 %collective-permute-start.2 = (bf16[128,512]{1,0:T(8,128)(2,1)}, bf16[128,512]{1,0:T(8,128)(2,1)S(1)}, u32[]{:S(2)}, u32[]{:S(2)}) collective-permute-start(bf16[128,512]{1,0:T(8,128)(2,1)} %refs_0_.3), channel_id=1, source_target_pairs={{0,1},{1,2},{2,3},{3,0},{4,5},{5,6},{6,7},{7,4},{8,9},{9,10},{10,1... | collective-permute-start | bytes 393224 | tf_op jit(solution)/shard_map/ppermute | solution.py:121
  6.7 2.6 %collective-permute-start.5 = (bf16[128,512]{1,0:T(8,128)(2,1)}, bf16[128,512]{1,0:T(8,128)(2,1)S(1)}, u32[]{:S(2)}, u32[]{:S(2)}) collective-permute-start(bf16[128,512]{1,0:T(8,128)(2,1)} %refs_0_.3), channel_id=1, source_target_pairs={{0,2},{1,3},{2,0},{3,1},{4,6},{5,7},{6,4},{7,5},{8,10},{9,11},{10,... | collective-permute-start | bytes 393224 | tf_op jit(solution)/shard_map/ppermute | solution.py:121
  9.3 0.9 broadcast_select_fusion.1
  10.3 3.1 %collective-permute-done.2.refs_1_ = bf16[128,512]{1,0:T(8,128)(2,1)S(1)} collective-permute-done((bf16[128,512]{1,0:T(8,128)(2,1)}, bf16[128,512]{1,0:T(8,128)(2,1)S(1)}, u32[]{:S(2)}, u32[]{:S(2)}) %collective-permute-start.2) | collective-permute-done | bytes 131104 | tf_op jit(solution)/shard_map/ppermute | solution.py:121
  13.4 0.5 collective-permute-start.3
  14.5 3.1 %collective-permute-done.5.refs_2_ = bf16[128,512]{1,0:T(8,128)(2,1)S(1)} collective-permute-done((bf16[128,512]{1,0:T(8,128)(2,1)}, bf16[128,512]{1,0:T(8,128)(2,1)S(1)}, u32[]{:S(2)}, u32[]{:S(2)}) %collective-permute-start.5) | collective-permute-done | bytes 131104 | tf_op jit(solution)/shard_map/ppermute | solution.py:121
  17.5 1.6 %collective-permute-start.6 = (bf16[128,512]{1,0:T(8,128)(2,1)}, bf16[128,512]{1,0:T(8,128)(2,1)S(1)}, u32[]{:S(2)}, u32[]{:S(2)}) collective-permute-start(bf16[128,512]{1,0:T(8,128)(2,1)} %refs_0_.3), channel_id=1, source_target_pairs={{0,3},{1,0},{2,1},{3,2},{4,7},{5,4},{6,5},{7,6},{8,11},{9,8},{10,9... | collective-permute-start | bytes 393224 | tf_op jit(solution)/shard_map/ppermute | solution.py:121
  19.2 0.7 reshape.63.gain_ref
  19.9 0.7 pad.6
  20.6 0.7 copy-done.15
  21.3 0.7 copy-done.16
  22.0 0.6 masked_bias.1.bias_ref
  23.2 0.8 norm_tokens.1
  24.0 3.0 %collective-permute-done.3.out_low.refs_1_ = bf16[512,256]{1,0:T(8,128)(2,1)S(1)} collective-permute-done((bf16[512,256]{1,0:T(8,128)(2,1)}, bf16[512,256]{1,0:T(8,128)(2,1)S(1)}, u32[]{:S(2)}, u32[]{:S(2)}) %collective-permute-start.3) | collective-permute-done | bytes 262176 | tf_op jit(solution)/shard_map/ppermute | solution.py:121
  27.0 1.5 %collective-permute-done.4.out_high.refs_2_ = bf16[512,256]{1,0:T(8,128)(2,1)S(1)} collective-permute-done((bf16[512,256]{1,0:T(8,128)(2,1)}, bf16[512,256]{1,0:T(8,128)(2,1)S(1)}, u32[]{:S(2)}, u32[]{:S(2)}) %collective-permute-start.4) | collective-permute-done | bytes 262176 | tf_op jit(solution)/shard_map/ppermute | solution.py:121
  28.6 1.6 %collective-permute-start.9 = (bf16[4,256,256]{2,1,0:T(8,128)(2,1)S(1)}, bf16[4,256,256]{2,1,0:T(8,128)(2,1)S(1)}, u32[]{:S(2)}, u32[]{:S(2)}) collective-permute-start(bf16[4,256,256]{2,1,0:T(8,128)(2,1)S(1)} %get-tuple-element.70), channel_id=1, source_target_pairs={{0,16},{4,20},{8,24},{12,28},{16,0},{20,4},{24,8},{28,12},{1,17},{... | collective-permute-start | bytes 1572872 | tf_op jit(solution)/shard_map/ppermute | solution.py:121
  30.2 0.5 collective-permute-start.10
  30.7 1.5 %collective-permute-done.8.other_in_ref = bf16[4,128,256]{2,1,0:T(8,128)(2,1)S(1)} collective-permute-done((bf16[4,128,256]{2,1,0:T(8,128)(2,1)S(1)}, bf16[4,128,256]{2,1,0:T(8,128)(2,1)S(1)}, u32[]{:S(2)}, u32[]{:S(2)}) %collective-permute-start.8) | collective-permute-done | bytes 262176 | tf_op jit(solution)/shard_map/ppermute | solution.py:121
  32.3 1.6 %collective-permute-start.13 = (bf16[640,256]{1,0:T(8,128)(2,1)S(1)}, bf16[640,256]{1,0:T(8,128)(2,1)S(1)}, u32[]{:S(2)}, u32[]{:S(2)}) collective-permute-start(bf16[640,256]{1,0:T(8,128)(2,1)S(1)} %get-tuple-element.111), channel_id=1, source_target_pairs={{0,8},{4,12},{8,0},{12,4},{16,24},{20,28},{24,16},{28,20},{1,9},{5... | collective-permute-start | bytes 983048 | tf_op jit(solution)/shard_map/ppermute | solution.py:121
  34.4 9.1 %collective-permute-done.9.refs_3_ = bf16[4,256,256]{2,1,0:T(8,128)(2,1)S(1)} collective-permute-done((bf16[4,256,256]{2,1,0:T(8,128)(2,1)S(1)}, bf16[4,256,256]{2,1,0:T(8,128)(2,1)S(1)}, u32[]{:S(2)}, u32[]{:S(2)}) %collective-permute-start.9) | collective-permute-done | bytes 524320 | tf_op jit(solution)/shard_map/ppermute | solution.py:121
  43.5 1.5 %collective-permute-done.10.refs_4_ = bf16[4,256,256]{2,1,0:T(8,128)(2,1)S(1)} collective-permute-done((bf16[4,256,256]{2,1,0:T(8,128)(2,1)S(1)}, bf16[4,256,256]{2,1,0:T(8,128)(2,1)S(1)}, u32[]{:S(2)}, u32[]{:S(2)}) %collective-permute-start.10) | collective-permute-done | bytes 524320 | tf_op jit(solution)/shard_map/ppermute | solution.py:121
  45.0 1.5 %qkv.1 = (f32[128,512]{1,0:T(8,128)S(1)}, f32[128,1024]{1,0:T(8,128)S(1)}, f32[128,512]{1,0:T(8,128)S(1)}, f32[128,1024]{1,0:T(8,128)S(1)}) custom-call(s32[2]{0:T(128)S(1)} %pad_add_fusion.place_ref, bf16[4,128,256]{2,1,0:T(8,128)(2,1)S(1)} %get-tuple-element.64.own_in_ref, bf16[4,128,256]{2,1,0:T(8,128)(2,1)S(1)} %collective-permute-done.8.other_in_ref, ...), custom_call_target="tpu_custom_call" | custom-call | flops 805306368 | bytes 3145728 | tf_op jit(solution)/shard_map/qkv/pallas_call | solution.py:294
  47.2 0.6 collective-permute-start.17
  47.8 1.5 %collective-permute-done.13.low_in.refs_1_ = bf16[640,256]{1,0:T(8,128)(2,1)S(1)} collective-permute-done((bf16[640,256]{1,0:T(8,128)(2,1)S(1)}, bf16[640,256]{1,0:T(8,128)(2,1)S(1)}, u32[]{:S(2)}, u32[]{:S(2)}) %collective-permute-start.13) | collective-permute-done | bytes 327712 | tf_op jit(solution)/shard_map/ppermute | solution.py:121
  50.0 1.3 collective-permute-start.15
  51.3 1.3 collective-permute-start.16
  52.6 12.3 %collective-permute-done.17.low_in.refs_5_ = bf16[256,1280]{1,0:T(8,128)(2,1)S(1)} collective-permute-done((bf16[256,1280]{1,0:T(8,128)(2,1)S(1)}, bf16[256,1280]{1,0:T(8,128)(2,1)S(1)}, u32[]{:S(2)}, u32[]{:S(2)}) %collective-permute-start.17) | collective-permute-done | bytes 655392 | tf_op jit(solution)/shard_map/ppermute | solution.py:121
  64.9 1.7 %packet.2 = (bf16[2,256,1280]{2,1,0:T(8,128)(2,1)}, bf16[2,256,1280]{2,1,0:T(8,128)(2,1)}) custom-call(bf16[2,256,1280]{2,1,0:T(8,128)(2,1)S(1)} %copy-done, bf16[256,1280]{1,0:T(8,128)(2,1)S(1)} %collective-permute-done.17.low_in.refs_5_, bf16[256,1280]{1,0:T(8,128)(2,1)S(1)} %collective-permute-done.18.high_in.refs_6_), custom_call_target="tpu_custom_call" | custom-call | tf_op jit(solution)/shard_map/packet/pallas_call | solution.py:173
  66.6 4.3 %collective-permute-start.26 = (bf16[2,256,1280]{2,1,0:T(8,128)(2,1)}, bf16[2,256,1280]{2,1,0:T(8,128)(2,1)}, u32[]{:S(2)}, u32[]{:S(2)}) collective-permute-start(bf16[2,256,1280]{2,1,0:T(8,128)(2,1)} %get-tuple-element.91), channel_id=1, source_target_pairs={{0,8},{4,12},{8,0},{12,4},{16,24},{20,28},{24,16},{28,20},{1,9},{5... | collective-permute-start | bytes 3932168 | tf_op jit(solution)/shard_map/ppermute | solution.py:121
  70.8 1.1 collective-permute-start.27
  72.0 2.7 %attention.1.own_in_ref = bf16[128,512]{1,0:T(8,128)(2,1)S(1)} custom-call(bf16[128,512]{1,0:T(8,128)(2,1)S(1)} %add_convert_fusion.2.q_ref, bf16[128,1024]{1,0:T(8,128)(2,1)S(1)} %collective-permute-done.15.low_ref, bf16[128,1024]{1,0:T(8,128)(2,1)S(1)} %add_convert_fusion.own_ref, bf16[128,1024]{1,0:T(8,128)(2,1)S(1)} %collective-permute-done.16.high_ref, ...), custom_call_target="tpu_custom_call" | custom-call | flops 100663296 | bytes 1572864 | tf_op jit(solution)/shard_map/attention/pallas_call | solution.py:106
  75.4 0.7 and_reduce_fusion
  76.1 1.1 attention_out.1
  77.3 3.7 %collective-permute-start.22 = (bf16[256,256]{1,0:T(8,128)(2,1)S(1)}, bf16[256,256]{1,0:T(8,128)(2,1)S(1)}, u32[]{:S(2)}, u32[]{:S(2)}) collective-permute-start(bf16[256,256]{1,0:T(8,128)(2,1)S(1)} %get-tuple-element.87), channel_id=1, source_target_pairs={{0,3},{1,0},{2,1},{3,2},{4,7},{5,4},{6,5},{7,6},{8,11},{9,8},{10,9... | collective-permute-start | bytes 393224 | tf_op jit(solution)/shard_map/ppermute | solution.py:121
  80.9 1.0 collective-permute-start.20
  82.0 1.4 maximum_select_fusion
  83.3 1.5 %collective-permute-done.22 = bf16[256,256]{1,0:T(8,128)(2,1)S(1)} collective-permute-done((bf16[256,256]{1,0:T(8,128)(2,1)S(1)}, bf16[256,256]{1,0:T(8,128)(2,1)S(1)}, u32[]{:S(2)}, u32[]{:S(2)}) %collective-permute-start.22) | collective-permute-done | bytes 131104 | tf_op jit(solution)/shard_map/ppermute | solution.py:121
  84.8 8.2 %collective-permute-done.21 = bf16[256,256]{1,0:T(8,128)(2,1)S(1)} collective-permute-done((bf16[256,256]{1,0:T(8,128)(2,1)S(1)}, bf16[256,256]{1,0:T(8,128)(2,1)S(1)}, u32[]{:S(2)}, u32[]{:S(2)}) %collective-permute-start.21) | collective-permute-done | bytes 131104 | tf_op jit(solution)/shard_map/ppermute | solution.py:121
  93.2 1.2 collective-permute-start.25
  94.4 0.7 reshape.62.gain_ref
  95.1 0.8 collective-permute-start.23
  96.0 2.4 %collective-permute-start.24 = (bf16[256,256]{1,0:T(8,128)(2,1)S(1)}, bf16[256,256]{1,0:T(8,128)(2,1)S(1)}, u32[]{:S(2)}, u32[]{:S(2)}) collective-permute-start(bf16[256,256]{1,0:T(8,128)(2,1)S(1)} %add_convert_fusion.1.refs_0_), channel_id=1, source_target_pairs={{0,2},{1,3},{2,0},{3,1},{4,6},{5,7},{6,4},{7,5},{8,10},{9,11},{10,... | collective-permute-start | bytes 393224 | tf_op jit(solution)/shard_map/ppermute | solution.py:121
  98.5 1.0 copy-done.3
  99.5 1.0 copy-done.6
  100.5 2.0 %collective-permute-start.29 = (bf16[2,640,256]{2,1,0:T(8,128)(2,1)S(1)}, bf16[2,640,256]{2,1,0:T(8,128)(2,1)S(1)}, u32[]{:S(2)}, u32[]{:S(2)}) collective-permute-start(bf16[2,640,256]{2,1,0:T(8,128)(2,1)S(1)} %get-tuple-element.98), channel_id=1, source_target_pairs={{0,8},{4,12},{8,0},{12,4},{16,24},{20,28},{24,16},{28,20},{1,9},{5... | collective-permute-start | bytes 1966088 | tf_op jit(solution)/shard_map/ppermute | solution.py:121
  102.7 1.5 %collective-permute-done.23.refs_1_ = bf16[256,256]{1,0:T(8,128)(2,1)S(1)} collective-permute-done((bf16[256,256]{1,0:T(8,128)(2,1)S(1)}, bf16[256,256]{1,0:T(8,128)(2,1)S(1)}, u32[]{:S(2)}, u32[]{:S(2)}) %collective-permute-start.23) | collective-permute-done | bytes 131104 | tf_op jit(solution)/shard_map/ppermute | solution.py:121
  104.2 0.8 collective-permute-start.30
  105.0 2.2 %collective-permute-done.24.refs_2_ = bf16[256,256]{1,0:T(8,128)(2,1)S(1)} collective-permute-done((bf16[256,256]{1,0:T(8,128)(2,1)S(1)}, bf16[256,256]{1,0:T(8,128)(2,1)S(1)}, u32[]{:S(2)}, u32[]{:S(2)}) %collective-permute-start.24) | collective-permute-done | bytes 131104 | tf_op jit(solution)/shard_map/ppermute | solution.py:121
  107.2 3.3 %ffn_in.1 = (f32[128,2560]{1,0:T(8,128)S(1)}, bf16[128,2560]{1,0:T(8,128)(2,1)S(1)}) custom-call(s32[2]{0:T(128)S(1)} %pad_add_fusion.place_ref, f32[8,256]{1,0:T(8,128)S(1)} %reshape.62.gain_ref, bf16[256,256]{1,0:T(8,128)(2,1)S(1)} %add_convert_fusion.1.refs_0_, bf16[256,256]{1,0:T(8,128)(2,1)S(1)} %collective-permute-done.23.refs_1_, ...), custom_call_target="tpu_custom_call" | custom-call | flops 1342177280 | bytes 5242880 | tf_op jit(solution)/shard_map/ffn_in/pallas_call | solution.py:330
  110.9 0.6 collective-permute-start.31
  111.5 1.3 collective-permute-done.31
  112.8 3.4 %collective-permute-done.29.refs_3_ = bf16[2,640,256]{2,1,0:T(8,128)(2,1)S(1)} collective-permute-done((bf16[2,640,256]{2,1,0:T(8,128)(2,1)S(1)}, bf16[2,640,256]{2,1,0:T(8,128)(2,1)S(1)}, u32[]{:S(2)}, u32[]{:S(2)}) %collective-permute-start.29) | collective-permute-done | bytes 655392 | tf_op jit(solution)/shard_map/ppermute | solution.py:121
  116.1 1.7 %collective-permute-done.30.refs_4_ = bf16[2,640,256]{2,1,0:T(8,128)(2,1)S(1)} collective-permute-done((bf16[2,640,256]{2,1,0:T(8,128)(2,1)S(1)}, bf16[2,640,256]{2,1,0:T(8,128)(2,1)S(1)}, u32[]{:S(2)}, u32[]{:S(2)}) %collective-permute-start.30) | collective-permute-done | bytes 655392 | tf_op jit(solution)/shard_map/ppermute | solution.py:121
  118.3 1.6 %collective-permute-done.32.other_in_ref = bf16[128,1280]{1,0:T(8,128)(2,1)S(1)} collective-permute-done((bf16[128,1280]{1,0:T(8,128)(2,1)S(1)}, bf16[128,1280]{1,0:T(8,128)(2,1)S(1)}, u32[]{:S(2)}, u32[]{:S(2)}) %collective-permute-start.32) | collective-permute-done | bytes 327712 | tf_op jit(solution)/shard_map/ppermute | solution.py:121
  119.9 1.7 %ffn_out.1 = (f32[256,256]{1,0:T(8,128)S(1)}, bf16[256,256]{1,0:T(8,128)(2,1)S(1)}, bf16[256,256]{1,0:T(8,128)(2,1)S(1)}, bf16[256,256]{1,0:T(8,128)(2,1)S(1)}) custom-call(s32[2]{0:T(128)S(1)} %pad_add_fusion.place_ref, bf16[128,1280]{1,0:T(8,128)(2,1)S(1)} %fusion.8.own_in_ref, bf16[128,1280]{1,0:T(8,128)(2,1)S(1)} %collective-permute-done.32.other_in_ref, ...), custom_call_target="tpu_custom_call" | custom-call | flops 671088640 | bytes 2621440 | tf_op jit(solution)/shard_map/ffn_out/pallas_call | solution.py:388
  121.6 2.1 %collective-permute-start.35 = (bf16[256,256]{1,0:T(8,128)(2,1)S(1)}, bf16[256,256]{1,0:T(8,128)(2,1)S(1)}, u32[]{:S(2)}, u32[]{:S(2)}) collective-permute-start(bf16[256,256]{1,0:T(8,128)(2,1)S(1)} %get-tuple-element.106), channel_id=1, source_target_pairs={{0,3},{1,0},{2,1},{3,2},{4,7},{5,4},{6,5},{7,6},{8,11},{9,8},{10,9... | collective-permute-start | bytes 393224 | tf_op jit(solution)/shard_map/ppermute | solution.py:121
  123.8 0.6 collective-permute-start.34
  124.4 1.5 %collective-permute-start.33 = (bf16[256,256]{1,0:T(8,128)(2,1)S(1)}, bf16[256,256]{1,0:T(8,128)(2,1)S(1)}, u32[]{:S(2)}, u32[]{:S(2)}) collective-permute-start(bf16[256,256]{1,0:T(8,128)(2,1)S(1)} %get-tuple-element.104), channel_id=1, source_target_pairs={{0,1},{1,2},{2,3},{3,0},{4,5},{5,6},{6,7},{7,4},{8,9},{9,10},{10,1... | collective-permute-start | bytes 393224 | tf_op jit(solution)/shard_map/ppermute | solution.py:121
  125.9 1.8 %collective-permute-done.35 = bf16[256,256]{1,0:T(8,128)(2,1)S(1)} collective-permute-done((bf16[256,256]{1,0:T(8,128)(2,1)S(1)}, bf16[256,256]{1,0:T(8,128)(2,1)S(1)}, u32[]{:S(2)}, u32[]{:S(2)}) %collective-permute-start.35) | collective-permute-done | bytes 131104 | tf_op jit(solution)/shard_map/ppermute | solution.py:121
  127.7 8.6 %collective-permute-done.34 = bf16[256,256]{1,0:T(8,128)(2,1)S(1)} collective-permute-done((bf16[256,256]{1,0:T(8,128)(2,1)S(1)}, bf16[256,256]{1,0:T(8,128)(2,1)S(1)}, u32[]{:S(2)}, u32[]{:S(2)}) %collective-permute-start.34) | collective-permute-done | bytes 131104 | tf_op jit(solution)/shard_map/ppermute | solution.py:121
  136.5 1.2 collective-permute-done.36
  137.7 0.7 maximum_select_fusion.1
  (80 shorter events, 4.6 us)
Async XLA Ops:
  0.6 22.5 %copy-start.13 = (bf16[128,512]{1,0:T(8,128)(2,1)S(1)}, bf16[128,512]{1,0:T(8,128)(2,1)}, u32[]{:S(2)}) copy-start(bf16[128,512]{1,0:T(8,128)(2,1)} %refs_0_.3) | copy-start | bytes 393220
  0.6 27.8 %collective-permute-start = (bf16[3,256,512]{2,1,0:T(8,128)(2,1)}, bf16[3,256,512]{2,1,0:T(8,128)(2,1)S(1)}, u32[]{:S(2)}, u32[]{:S(2)}) collective-permute-start(bf16[3,256,512]{2,1,0:T(8,128)(2,1)} %refs_0_.4), channel_id=1, source_target_pairs={{0,8},{4,12},{8,0},{12,4},{16,24},{20,28},{24,16},{28,20},{1,9},{5... | collective-permute-start | bytes 2359304 | tf_op jit(solution)/shard_map/ppermute | solution.py:121
  3.6 24.8 %collective-permute-start.1 = (bf16[3,256,512]{2,1,0:T(8,128)(2,1)}, bf16[3,256,512]{2,1,0:T(8,128)(2,1)S(1)}, u32[]{:S(2)}, u32[]{:S(2)}) collective-permute-start(bf16[3,256,512]{2,1,0:T(8,128)(2,1)} %refs_0_.4), channel_id=1, source_target_pairs={{0,16},{4,20},{8,24},{12,28},{16,0},{20,4},{24,8},{28,12},{1,17},{... | collective-permute-start | bytes 2359304 | tf_op jit(solution)/shard_map/ppermute | solution.py:121
  5.2 8.2 %collective-permute-start.2 = (bf16[128,512]{1,0:T(8,128)(2,1)}, bf16[128,512]{1,0:T(8,128)(2,1)S(1)}, u32[]{:S(2)}, u32[]{:S(2)}) collective-permute-start(bf16[128,512]{1,0:T(8,128)(2,1)} %refs_0_.3), channel_id=1, source_target_pairs={{0,1},{1,2},{2,3},{3,0},{4,5},{5,6},{6,7},{7,4},{8,9},{9,10},{10,1... | collective-permute-start | bytes 393224 | tf_op jit(solution)/shard_map/ppermute | solution.py:121
  6.7 10.8 %collective-permute-start.5 = (bf16[128,512]{1,0:T(8,128)(2,1)}, bf16[128,512]{1,0:T(8,128)(2,1)S(1)}, u32[]{:S(2)}, u32[]{:S(2)}) collective-permute-start(bf16[128,512]{1,0:T(8,128)(2,1)} %refs_0_.3), channel_id=1, source_target_pairs={{0,2},{1,3},{2,0},{3,1},{4,6},{5,7},{6,4},{7,5},{8,10},{9,11},{10,... | collective-permute-start | bytes 393224 | tf_op jit(solution)/shard_map/ppermute | solution.py:121
  10.2 3.7 %collective-permute-start.7 = (bf16[128,256]{1,0:T(8,128)(2,1)S(1)}, bf16[128,256]{1,0:T(8,128)(2,1)S(1)}, u32[]{:S(2)}, u32[]{:S(2)}) collective-permute-start(bf16[128,256]{1,0:T(8,128)(2,1)S(1)} %get-tuple-element.117), channel_id=1, source_target_pairs={{0,4},{4,0},{8,12},{12,8},{16,20},{20,16},{24,28},{28,24},{1,5},{5... | collective-permute-start | bytes 196616 | tf_op jit(solution)/shard_map/ppermute | solution.py:121
  13.4 13.6 %collective-permute-start.3 = (bf16[512,256]{1,0:T(8,128)(2,1)}, bf16[512,256]{1,0:T(8,128)(2,1)S(1)}, u32[]{:S(2)}, u32[]{:S(2)}) collective-permute-start(bf16[512,256]{1,0:T(8,128)(2,1)} %refs_0_.5), channel_id=1, source_target_pairs={{0,8},{4,12},{8,0},{12,4},{16,24},{20,28},{24,16},{28,20},{1,9},{5... | collective-permute-start | bytes 786440 | tf_op jit(solution)/shard_map/ppermute | solution.py:121
  14.0 14.5 %collective-permute-start.4 = (bf16[512,256]{1,0:T(8,128)(2,1)}, bf16[512,256]{1,0:T(8,128)(2,1)S(1)}, u32[]{:S(2)}, u32[]{:S(2)}) collective-permute-start(bf16[512,256]{1,0:T(8,128)(2,1)} %refs_0_.5), channel_id=1, source_target_pairs={{0,16},{4,20},{8,24},{12,28},{16,0},{20,4},{24,8},{28,12},{1,17},{... | collective-permute-start | bytes 786440 | tf_op jit(solution)/shard_map/ppermute | solution.py:121
  17.5 5.6 %collective-permute-start.6 = (bf16[128,512]{1,0:T(8,128)(2,1)}, bf16[128,512]{1,0:T(8,128)(2,1)S(1)}, u32[]{:S(2)}, u32[]{:S(2)}) collective-permute-start(bf16[128,512]{1,0:T(8,128)(2,1)} %refs_0_.3), channel_id=1, source_target_pairs={{0,3},{1,0},{2,1},{3,2},{4,7},{5,4},{6,5},{7,6},{8,11},{9,8},{10,9... | collective-permute-start | bytes 393224 | tf_op jit(solution)/shard_map/ppermute | solution.py:121
  20.6 0.7 copy-start.15
  21.3 0.7 copy-start.16
  22.7 9.6 %copy-start.1 = (bf16[1280,256]{1,0:T(8,128)(2,1)S(1)}, bf16[1280,256]{1,0:T(8,128)(2,1)}, u32[]{:S(2)}) copy-start(bf16[1280,256]{1,0:T(8,128)(2,1)} %param.23) | copy-start | bytes 1966084
  27.0 5.3 %copy-start.8 = (bf16[512,256]{1,0:T(8,128)(2,1)}, bf16[512,256]{1,0:T(8,128)(2,1)S(1)}, u32[]{:S(2)}) copy-start(bf16[512,256]{1,0:T(8,128)(2,1)S(1)} %collective-permute-done.3.out_low.refs_1_) | copy-start | bytes 786436
  28.5 3.8 %copy-start.10 = (bf16[512,256]{1,0:T(8,128)(2,1)}, bf16[512,256]{1,0:T(8,128)(2,1)S(1)}, u32[]{:S(2)}) copy-start(bf16[512,256]{1,0:T(8,128)(2,1)S(1)} %collective-permute-done.4.out_high.refs_2_) | copy-start | bytes 786436
  28.5 16.5 %copy-start.12 = (bf16[3,256,512]{2,1,0:T(8,128)(2,1)S(1)}, bf16[3,256,512]{2,1,0:T(8,128)(2,1)}, u32[]{:S(2)}) copy-start(bf16[3,256,512]{2,1,0:T(8,128)(2,1)} %refs_0_.4) | copy-start | bytes 2359300
  28.6 14.9 %collective-permute-start.9 = (bf16[4,256,256]{2,1,0:T(8,128)(2,1)S(1)}, bf16[4,256,256]{2,1,0:T(8,128)(2,1)S(1)}, u32[]{:S(2)}, u32[]{:S(2)}) collective-permute-start(bf16[4,256,256]{2,1,0:T(8,128)(2,1)S(1)} %get-tuple-element.70), channel_id=1, source_target_pairs={{0,16},{4,20},{8,24},{12,28},{16,0},{20,4},{24,8},{28,12},{1,17},{... | collective-permute-start | bytes 1572872 | tf_op jit(solution)/shard_map/ppermute | solution.py:121
  30.2 14.9 %collective-permute-start.10 = (bf16[4,256,256]{2,1,0:T(8,128)(2,1)S(1)}, bf16[4,256,256]{2,1,0:T(8,128)(2,1)S(1)}, u32[]{:S(2)}, u32[]{:S(2)}) collective-permute-start(bf16[4,256,256]{2,1,0:T(8,128)(2,1)S(1)} %get-tuple-element.71), channel_id=1, source_target_pairs={{0,8},{4,12},{8,0},{12,4},{16,24},{20,28},{24,16},{28,20},{1,9},{5... | collective-permute-start | bytes 1572872 | tf_op jit(solution)/shard_map/ppermute | solution.py:121
  30.7 1.5 %collective-permute-start.8 = (bf16[4,128,256]{2,1,0:T(8,128)(2,1)S(1)}, bf16[4,128,256]{2,1,0:T(8,128)(2,1)S(1)}, u32[]{:S(2)}, u32[]{:S(2)}) collective-permute-start(bf16[4,128,256]{2,1,0:T(8,128)(2,1)S(1)} %get-tuple-element.65), channel_id=1, source_target_pairs={{0,4},{4,0},{8,12},{12,8},{16,20},{20,16},{24,28},{28,24},{1,5},{5... | collective-permute-start | bytes 786440 | tf_op jit(solution)/shard_map/ppermute | solution.py:121
  32.3 17.1 %collective-permute-start.13 = (bf16[640,256]{1,0:T(8,128)(2,1)S(1)}, bf16[640,256]{1,0:T(8,128)(2,1)S(1)}, u32[]{:S(2)}, u32[]{:S(2)}) collective-permute-start(bf16[640,256]{1,0:T(8,128)(2,1)S(1)} %get-tuple-element.111), channel_id=1, source_target_pairs={{0,8},{4,12},{8,0},{12,4},{16,24},{20,28},{24,16},{28,20},{1,9},{5... | collective-permute-start | bytes 983048 | tf_op jit(solution)/shard_map/ppermute | solution.py:121
  33.9 13.3 %copy-start = (bf16[2,256,1280]{2,1,0:T(8,128)(2,1)S(1)}, bf16[2,256,1280]{2,1,0:T(8,128)(2,1)}, u32[]{:S(2)}) copy-start(bf16[2,256,1280]{2,1,0:T(8,128)(2,1)} %refs_4_) | copy-start | bytes 3932164
  33.9 16.0 %collective-permute-start.14 = (bf16[640,256]{1,0:T(8,128)(2,1)S(1)}, bf16[640,256]{1,0:T(8,128)(2,1)S(1)}, u32[]{:S(2)}, u32[]{:S(2)}) collective-permute-start(bf16[640,256]{1,0:T(8,128)(2,1)S(1)} %get-tuple-element.110), channel_id=1, source_target_pairs={{0,16},{4,20},{8,24},{12,28},{16,0},{20,4},{24,8},{28,12},{1,17},{... | collective-permute-start | bytes 983048 | tf_op jit(solution)/shard_map/ppermute | solution.py:121
  46.6 3.3 %collective-permute-start.11 = (f32[128,1024]{1,0:T(8,128)S(1)}, f32[128,1024]{1,0:T(8,128)S(1)}, u32[]{:S(2)}, u32[]{:S(2)}) collective-permute-start(f32[128,1024]{1,0:T(8,128)S(1)} %get-tuple-element.73), channel_id=1, source_target_pairs={{0,4},{4,0},{8,12},{12,8},{16,20},{20,16},{24,28},{28,24},{1,5},{5... | collective-permute-start | bytes 1572872 | tf_op jit(solution)/shard_map/ppermute | solution.py:121
  46.6 3.3 %collective-permute-start.12 = (f32[128,512]{1,0:T(8,128)S(1)}, f32[128,512]{1,0:T(8,128)S(1)}, u32[]{:S(2)}, u32[]{:S(2)}) collective-permute-start(f32[128,512]{1,0:T(8,128)S(1)} %get-tuple-element.74), channel_id=1, source_target_pairs={{0,4},{4,0},{8,12},{12,8},{16,20},{20,16},{24,28},{28,24},{1,5},{5... | collective-permute-start | bytes 786440 | tf_op jit(solution)/shard_map/ppermute | solution.py:121
  47.2 17.7 %collective-permute-start.17 = (bf16[256,1280]{1,0:T(8,128)(2,1)S(1)}, bf16[256,1280]{1,0:T(8,128)(2,1)S(1)}, u32[]{:S(2)}, u32[]{:S(2)}) collective-permute-start(bf16[256,1280]{1,0:T(8,128)(2,1)S(1)} %get-tuple-element.109), channel_id=1, source_target_pairs={{0,8},{4,12},{8,0},{12,4},{16,24},{20,28},{24,16},{28,20},{1,9},{5... | collective-permute-start | bytes 1966088 | tf_op jit(solution)/shard_map/ppermute | solution.py:121
  49.4 17.2 %copy-start.2 = (bf16[640,256]{1,0:T(8,128)(2,1)}, bf16[640,256]{1,0:T(8,128)(2,1)S(1)}, u32[]{:S(2)}) copy-start(bf16[640,256]{1,0:T(8,128)(2,1)S(1)} %collective-permute-done.13.low_in.refs_1_) | copy-start | bytes 983044
  49.4 15.5 %collective-permute-start.18 = (bf16[256,1280]{1,0:T(8,128)(2,1)S(1)}, bf16[256,1280]{1,0:T(8,128)(2,1)S(1)}, u32[]{:S(2)}, u32[]{:S(2)}) collective-permute-start(bf16[256,1280]{1,0:T(8,128)(2,1)S(1)} %get-tuple-element.108), channel_id=1, source_target_pairs={{0,16},{4,20},{8,24},{12,28},{16,0},{20,4},{24,8},{28,12},{1,17},{... | collective-permute-start | bytes 1966088 | tf_op jit(solution)/shard_map/ppermute | solution.py:121
  49.9 16.7 %copy-start.5 = (bf16[640,256]{1,0:T(8,128)(2,1)}, bf16[640,256]{1,0:T(8,128)(2,1)S(1)}, u32[]{:S(2)}) copy-start(bf16[640,256]{1,0:T(8,128)(2,1)S(1)} %collective-permute-done.14.high_in.refs_2_) | copy-start | bytes 983044
  50.0 14.9 %collective-permute-start.15 = (bf16[128,1024]{1,0:T(8,128)(2,1)S(1)}, bf16[128,1024]{1,0:T(8,128)(2,1)S(1)}, u32[]{:S(2)}, u32[]{:S(2)}) collective-permute-start(bf16[128,1024]{1,0:T(8,128)(2,1)S(1)} %add_convert_fusion.own_ref), channel_id=1, source_target_pairs={{0,4},{4,8},{8,12},{12,16},{16,20},{20,24},{24,28},{1,5},{5,9},{9,... | collective-permute-start | bytes 786440 | tf_op jit(solution)/shard_map/ppermute | solution.py:473
  51.3 13.6 %collective-permute-start.16 = (bf16[128,1024]{1,0:T(8,128)(2,1)S(1)}, bf16[128,1024]{1,0:T(8,128)(2,1)S(1)}, u32[]{:S(2)}, u32[]{:S(2)}) collective-permute-start(bf16[128,1024]{1,0:T(8,128)(2,1)S(1)} %add_convert_fusion.own_ref), channel_id=1, source_target_pairs={{4,0},{8,4},{12,8},{16,12},{20,16},{24,20},{28,24},{5,1},{9,5},{13... | collective-permute-start | bytes 786440 | tf_op jit(solution)/shard_map/ppermute | solution.py:474
  66.6 40.7 %collective-permute-start.26 = (bf16[2,256,1280]{2,1,0:T(8,128)(2,1)}, bf16[2,256,1280]{2,1,0:T(8,128)(2,1)}, u32[]{:S(2)}, u32[]{:S(2)}) collective-permute-start(bf16[2,256,1280]{2,1,0:T(8,128)(2,1)} %get-tuple-element.91), channel_id=1, source_target_pairs={{0,8},{4,12},{8,0},{12,4},{16,24},{20,28},{24,16},{28,20},{1,9},{5... | collective-permute-start | bytes 3932168 | tf_op jit(solution)/shard_map/ppermute | solution.py:121
  70.8 36.4 %collective-permute-start.27 = (bf16[2,256,1280]{2,1,0:T(8,128)(2,1)}, bf16[2,256,1280]{2,1,0:T(8,128)(2,1)}, u32[]{:S(2)}, u32[]{:S(2)}) collective-permute-start(bf16[2,256,1280]{2,1,0:T(8,128)(2,1)} %get-tuple-element.92), channel_id=1, source_target_pairs={{0,16},{4,20},{8,24},{12,28},{16,0},{20,4},{24,8},{28,12},{1,17},{... | collective-permute-start | bytes 3932168 | tf_op jit(solution)/shard_map/ppermute | solution.py:121
  72.0 4.1 %copy-start.9 = (bf16[512,256]{1,0:T(8,128)(2,1)S(1)}, bf16[512,256]{1,0:T(8,128)(2,1)}, u32[]{:S(2)}) copy-start(bf16[512,256]{1,0:T(8,128)(2,1)} %copy-done.8) | copy-start | bytes 786436
  72.0 4.1 %copy-start.11 = (bf16[512,256]{1,0:T(8,128)(2,1)S(1)}, bf16[512,256]{1,0:T(8,128)(2,1)}, u32[]{:S(2)}) copy-start(bf16[512,256]{1,0:T(8,128)(2,1)} %copy-done.10) | copy-start | bytes 786436
  72.0 4.1 %copy-start.14 = (bf16[512,256]{1,0:T(8,128)(2,1)S(1)}, bf16[512,256]{1,0:T(8,128)(2,1)}, u32[]{:S(2)}) copy-start(bf16[512,256]{1,0:T(8,128)(2,1)} %refs_0_.5) | copy-start | bytes 786436
  74.7 1.4 %collective-permute-start.19 = (bf16[128,512]{1,0:T(8,128)(2,1)S(1)}, bf16[128,512]{1,0:T(8,128)(2,1)S(1)}, u32[]{:S(2)}, u32[]{:S(2)}) collective-permute-start(bf16[128,512]{1,0:T(8,128)(2,1)S(1)} %attention.1.own_in_ref), channel_id=1, source_target_pairs={{0,4},{4,0},{8,12},{12,8},{16,20},{20,16},{24,28},{28,24},{1,5},{5... | collective-permute-start | bytes 393224 | tf_op jit(solution)/shard_map/ppermute | solution.py:121
  77.3 7.6 %collective-permute-start.22 = (bf16[256,256]{1,0:T(8,128)(2,1)S(1)}, bf16[256,256]{1,0:T(8,128)(2,1)S(1)}, u32[]{:S(2)}, u32[]{:S(2)}) collective-permute-start(bf16[256,256]{1,0:T(8,128)(2,1)S(1)} %get-tuple-element.87), channel_id=1, source_target_pairs={{0,3},{1,0},{2,1},{3,2},{4,7},{5,4},{6,5},{7,6},{8,11},{9,8},{10,9... | collective-permute-start | bytes 393224 | tf_op jit(solution)/shard_map/ppermute | solution.py:121
  80.9 12.1 %collective-permute-start.21 = (bf16[256,256]{1,0:T(8,128)(2,1)S(1)}, bf16[256,256]{1,0:T(8,128)(2,1)S(1)}, u32[]{:S(2)}, u32[]{:S(2)}) collective-permute-start(bf16[256,256]{1,0:T(8,128)(2,1)S(1)} %get-tuple-element.86), channel_id=1, source_target_pairs={{0,2},{1,3},{2,0},{3,1},{4,6},{5,7},{6,4},{7,5},{8,10},{9,11},{10,... | collective-permute-start | bytes 393224 | tf_op jit(solution)/shard_map/ppermute | solution.py:121
  80.9 12.1 %collective-permute-start.20 = (bf16[256,256]{1,0:T(8,128)(2,1)S(1)}, bf16[256,256]{1,0:T(8,128)(2,1)S(1)}, u32[]{:S(2)}, u32[]{:S(2)}) collective-permute-start(bf16[256,256]{1,0:T(8,128)(2,1)S(1)} %get-tuple-element.85), channel_id=1, source_target_pairs={{0,1},{1,2},{2,3},{3,0},{4,5},{5,6},{6,7},{7,4},{8,9},{9,10},{10,1... | collective-permute-start | bytes 393224 | tf_op jit(solution)/shard_map/ppermute | solution.py:121
  93.2 5.3 %collective-permute-start.25 = (bf16[256,256]{1,0:T(8,128)(2,1)S(1)}, bf16[256,256]{1,0:T(8,128)(2,1)S(1)}, u32[]{:S(2)}, u32[]{:S(2)}) collective-permute-start(bf16[256,256]{1,0:T(8,128)(2,1)S(1)} %add_convert_fusion.1.refs_0_), channel_id=1, source_target_pairs={{0,3},{1,0},{2,1},{3,2},{4,7},{5,4},{6,5},{7,6},{8,11},{9,8},{10,9... | collective-permute-start | bytes 393224 | tf_op jit(solution)/shard_map/ppermute | solution.py:121
  95.1 9.1 %collective-permute-start.23 = (bf16[256,256]{1,0:T(8,128)(2,1)S(1)}, bf16[256,256]{1,0:T(8,128)(2,1)S(1)}, u32[]{:S(2)}, u32[]{:S(2)}) collective-permute-start(bf16[256,256]{1,0:T(8,128)(2,1)S(1)} %add_convert_fusion.1.refs_0_), channel_id=1, source_target_pairs={{0,1},{1,2},{2,3},{3,0},{4,5},{5,6},{6,7},{7,4},{8,9},{9,10},{10,1... | collective-permute-start | bytes 393224 | tf_op jit(solution)/shard_map/ppermute | solution.py:121
  96.0 11.3 %collective-permute-start.24 = (bf16[256,256]{1,0:T(8,128)(2,1)S(1)}, bf16[256,256]{1,0:T(8,128)(2,1)S(1)}, u32[]{:S(2)}, u32[]{:S(2)}) collective-permute-start(bf16[256,256]{1,0:T(8,128)(2,1)S(1)} %add_convert_fusion.1.refs_0_), channel_id=1, source_target_pairs={{0,2},{1,3},{2,0},{3,1},{4,6},{5,7},{6,4},{7,5},{8,10},{9,11},{10,... | collective-permute-start | bytes 393224 | tf_op jit(solution)/shard_map/ppermute | solution.py:121
  98.5 1.0 copy-start.3
  99.5 1.0 copy-start.6
  100.5 15.6 %collective-permute-start.29 = (bf16[2,640,256]{2,1,0:T(8,128)(2,1)S(1)}, bf16[2,640,256]{2,1,0:T(8,128)(2,1)S(1)}, u32[]{:S(2)}, u32[]{:S(2)}) collective-permute-start(bf16[2,640,256]{2,1,0:T(8,128)(2,1)S(1)} %get-tuple-element.98), channel_id=1, source_target_pairs={{0,8},{4,12},{8,0},{12,4},{16,24},{20,28},{24,16},{28,20},{1,9},{5... | collective-permute-start | bytes 1966088 | tf_op jit(solution)/shard_map/ppermute | solution.py:121
  104.2 13.6 %collective-permute-start.30 = (bf16[2,640,256]{2,1,0:T(8,128)(2,1)S(1)}, bf16[2,640,256]{2,1,0:T(8,128)(2,1)S(1)}, u32[]{:S(2)}, u32[]{:S(2)}) collective-permute-start(bf16[2,640,256]{2,1,0:T(8,128)(2,1)S(1)} %get-tuple-element.99), channel_id=1, source_target_pairs={{0,16},{4,20},{8,24},{12,28},{16,0},{20,4},{24,8},{28,12},{1,17},{... | collective-permute-start | bytes 1966088 | tf_op jit(solution)/shard_map/ppermute | solution.py:121
  110.6 7.2 %collective-permute-start.28 = (bf16[128,2560]{1,0:T(8,128)(2,1)S(1)}, bf16[128,2560]{1,0:T(8,128)(2,1)S(1)}, u32[]{:S(2)}, u32[]{:S(2)}) collective-permute-start(bf16[128,2560]{1,0:T(8,128)(2,1)S(1)} %get-tuple-element.94), channel_id=1, source_target_pairs={{0,4},{4,0},{8,12},{12,8},{16,20},{20,16},{24,28},{28,24},{1,5},{5... | collective-permute-start | bytes 1966088 | tf_op jit(solution)/shard_map/ppermute | solution.py:121
  110.9 1.8 %collective-permute-start.31 = (f32[128]{0:T(128)S(1)}, f32[128]{0:T(128)S(1)}, u32[]{:S(2)}, u32[]{:S(2)}) collective-permute-start(f32[128]{0:T(128)S(1)} %slice.78), channel_id=1, source_target_pairs={{0,4},{4,0},{8,12},{12,8},{16,20},{20,16},{24,28},{28,24},{1,5},{5... | collective-permute-start | bytes 1544 | tf_op jit(solution)/shard_map/ppermute | solution.py:121
  118.0 2.0 %copy-start.4 = (bf16[640,256]{1,0:T(8,128)(2,1)S(1)}, bf16[640,256]{1,0:T(8,128)(2,1)}, u32[]{:S(2)}) copy-start(bf16[640,256]{1,0:T(8,128)(2,1)} %copy-done.2) | copy-start | bytes 983044
  118.0 1.9 %copy-start.7 = (bf16[640,256]{1,0:T(8,128)(2,1)S(1)}, bf16[640,256]{1,0:T(8,128)(2,1)}, u32[]{:S(2)}) copy-start(bf16[640,256]{1,0:T(8,128)(2,1)} %copy-done.5) | copy-start | bytes 983044
  118.2 1.7 %collective-permute-start.32 = (bf16[128,1280]{1,0:T(8,128)(2,1)S(1)}, bf16[128,1280]{1,0:T(8,128)(2,1)S(1)}, u32[]{:S(2)}, u32[]{:S(2)}) collective-permute-start(bf16[128,1280]{1,0:T(8,128)(2,1)S(1)} %fusion.8.own_in_ref), channel_id=1, source_target_pairs={{0,4},{4,0},{8,12},{12,8},{16,20},{20,16},{24,28},{28,24},{1,5},{5... | collective-permute-start | bytes 983048 | tf_op jit(solution)/shard_map/ppermute | solution.py:121
  121.6 6.1 %collective-permute-start.35 = (bf16[256,256]{1,0:T(8,128)(2,1)S(1)}, bf16[256,256]{1,0:T(8,128)(2,1)S(1)}, u32[]{:S(2)}, u32[]{:S(2)}) collective-permute-start(bf16[256,256]{1,0:T(8,128)(2,1)S(1)} %get-tuple-element.106), channel_id=1, source_target_pairs={{0,3},{1,0},{2,1},{3,2},{4,7},{5,4},{6,5},{7,6},{8,11},{9,8},{10,9... | collective-permute-start | bytes 393224 | tf_op jit(solution)/shard_map/ppermute | solution.py:121
  123.8 12.5 %collective-permute-start.34 = (bf16[256,256]{1,0:T(8,128)(2,1)S(1)}, bf16[256,256]{1,0:T(8,128)(2,1)S(1)}, u32[]{:S(2)}, u32[]{:S(2)}) collective-permute-start(bf16[256,256]{1,0:T(8,128)(2,1)S(1)} %get-tuple-element.105), channel_id=1, source_target_pairs={{0,2},{1,3},{2,0},{3,1},{4,6},{5,7},{6,4},{7,5},{8,10},{9,11},{10,... | collective-permute-start | bytes 393224 | tf_op jit(solution)/shard_map/ppermute | solution.py:121
  124.4 11.9 %collective-permute-start.33 = (bf16[256,256]{1,0:T(8,128)(2,1)S(1)}, bf16[256,256]{1,0:T(8,128)(2,1)S(1)}, u32[]{:S(2)}, u32[]{:S(2)}) collective-permute-start(bf16[256,256]{1,0:T(8,128)(2,1)S(1)} %get-tuple-element.104), channel_id=1, source_target_pairs={{0,1},{1,2},{2,3},{3,0},{4,5},{5,6},{6,7},{7,4},{8,9},{9,10},{10,1... | collective-permute-start | bytes 393224 | tf_op jit(solution)/shard_map/ppermute | solution.py:121
  136.4 1.3 collective-permute-start.36

commit v6 on v5

--- a/solution.py
+++ b/solution.py
@@ -178,7 +178,11 @@
         compiler_params=pltpu.CompilerParams(vmem_limit_bytes=8 << 20),
         name="packet",
     )(own, *first)
-    return [pair_exchange(high, 1), pair_exchange(low, 2)]
+    return [low, high]
+
+
+def exchanged(packets):
+    return [pair_exchange(packet, step) for packet, step in zip(packets[::-1], (1, 2))]
 
 
 def half_ref(refs, step, part):
@@ -467,34 +471,39 @@
         (other_core(send_kv), other_core(send_q), *down_first)
     )
     key_value = (own_kv + other_kv).astype(jnp.bfloat16)
+    packets = second_phase(w_down, down_first)
     queries = (own_q + other_q).astype(jnp.bfloat16)
     forward = [(i, i + 1) for i in range(rows - 1)]
     backward = [(target, source) for source, target in forward]
     low = lax.ppermute(key_value, "row", forward)
     high = lax.ppermute(key_value, "row", backward)
-    low, high, *in_first = lax.optimization_barrier((low, high, *in_first))
-    in_pieces = [w_in, *in_first, *second_phase(w_in, in_first)]
+    low, high, *waited = lax.optimization_barrier((low, high, *in_first, *packets))
+    in_first, packets = waited[: len(in_first)], waited[len(in_first) :]
+    in_pieces = [w_in, *in_first, *exchanged(second_phase(w_in, in_first))]
     context = attention(queries, low, key_value, high, bias)
     own, *sends = columns(
         place, context, other_core(context), [w_out, *out_near, *far], "attention_out"
     )
     stacked = jnp.stack([key_value[:, :width], key_value[:, width:]])
     blocks = stacked.reshape(2, slot_index.shape[1], BLOCK, width)
-    kv_cache = (
-        jnp.zeros_like(blocks).at[:, slot_index[0]].set(blocks).reshape(2, count, width)
-    )
+    kv_cache = jnp.zeros_like(blocks)
+    for index in range(slot_index.shape[1]):
+        kv_cache = lax.dynamic_update_slice_in_dim(
+            kv_cache, blocks[:, index : index + 1], slot_index[0, index], axis=1
+        )
+    kv_cache = kv_cache.reshape(2, count, width)
     middle, kv_cache = lax.optimization_barrier((summed(own, sends, token_block), kv_cache))
 
     middle_blocks = gathered(middle)
     squares = square_sums(middle_blocks)
     squares = squares[:count] + other_core(squares[count:])
     scale = lax.rsqrt(squares / features + epsilon)[:, None]
-    down_second = second_phase(after(w_down, middle_blocks[-1]), down_first)
+    down_second = exchanged(after_all(packets, middle_blocks[-1]))
     own, send = project_ffn(
         place, gain_ffn.reshape(rows, -1), middle_blocks, in_pieces
     )
-    other_sum, *down_second = lax.optimization_barrier((other_core(send), *down_second))
-    branches = (own + other_sum.astype(jnp.float32)) * scale
+    scale, *down_second = lax.optimization_barrier((scale, *down_second))
+    branches = (own + other_core(send).astype(jnp.float32)) * scale
     inner = branches.shape[1] // 2
     hidden = (
         jax.nn.gelu(branches[:, :inner], approximate=True) * branches[:, inner:]

time: 139 us -> 138 us (level)
  waiting for transfers between devices: 70.3 us -> 71.8 us
    ppermute x35, waiting for transfers between devices: 70.3 us -> 71.8 us  [exchange(): lax.ppermute(value, axis, [(i, partner(i) % count) for i in range(count)])]
  transfers between devices with their start and end apart: 37 -> 37, of which waited for: 21 -> 22; matrix products, arithmetic and copies ran while one was open for 4% -> 3% of each run, Pallas kernels for 7% -> 7%
where the time goes in v6:
time: 138 us
  waiting for transfers between devices  71.8 us (52%)
  starting transfers between devices  42.1 us (31%)
  Pallas kernels  13.6 us (10%)
  local copies, waits for them, and re-layouts  5.37 us (4%)
  other arithmetic  3.56 us (3%)
    ppermute x35, waiting for transfers between devices, exchange(): lax.ppermute(value, axis, [(i, partner(i) % count) for i in range(count)])  71.8 us
    ppermute x35, starting transfers between devices, exchange(): lax.ppermute(value, axis, [(i, partner(i) % count) for i in range(count)])  39.5 us
    pallas_call x1, Pallas kernels, project_ffn(): pl.pallas_call(ffn_in_kernel, out_shape=(jax.ShapeDtypeStruct((count, col...  3.34 us
    unnamed x34, local copies, waits for them, and re-layouts  3.12 us
    pallas_call x2, Pallas kernels, columns(): pl.pallas_call(columns_kernel, out_shape=(jax.ShapeDtypeStruct((2 * count...  2.8 us
  transfers between devices with their start and end apart: 37, of which 22 were waited for; matrix products, arithmetic and copies ran while one was open for 3% of the time, Pallas kernels for 7%

profile of v6, /device:TPU:0, one launch (start us, length us, event | category | flops | bytes accessed | tf_op | source)
XLA Modules:
  0.0 137.6 jit_solution(2339203296456097859)
XLA Ops:
  0.6 3.0 %collective-permute-start = (bf16[3,256,512]{2,1,0:T(8,128)(2,1)}, bf16[3,256,512]{2,1,0:T(8,128)(2,1)S(1)}, u32[]{:S(2)}, u32[]{:S(2)}) collective-permute-start(bf16[3,256,512]{2,1,0:T(8,128)(2,1)} %refs_0_.4), channel_id=1, source_target_pairs={{0,8},{4,12},{8,0},{12,4},{16,24},{20,28},{24,16},{28,20},{1,9},{5... | collective-permute-start | bytes 2359304 | tf_op jit(solution)/shard_map/ppermute | solution.py:121
  3.6 1.5 %collective-permute-start.1 = (bf16[3,256,512]{2,1,0:T(8,128)(2,1)}, bf16[3,256,512]{2,1,0:T(8,128)(2,1)S(1)}, u32[]{:S(2)}, u32[]{:S(2)}) collective-permute-start(bf16[3,256,512]{2,1,0:T(8,128)(2,1)} %refs_0_.4), channel_id=1, source_target_pairs={{0,16},{4,20},{8,24},{12,28},{16,0},{20,4},{24,8},{28,12},{1,17},{... | collective-permute-start | bytes 2359304 | tf_op jit(solution)/shard_map/ppermute | solution.py:121
  5.2 1.6 %collective-permute-start.2 = (bf16[128,512]{1,0:T(8,128)(2,1)}, bf16[128,512]{1,0:T(8,128)(2,1)S(1)}, u32[]{:S(2)}, u32[]{:S(2)}) collective-permute-start(bf16[128,512]{1,0:T(8,128)(2,1)} %refs_0_.3), channel_id=1, source_target_pairs={{0,1},{1,2},{2,3},{3,0},{4,5},{5,6},{6,7},{7,4},{8,9},{9,10},{10,1... | collective-permute-start | bytes 393224 | tf_op jit(solution)/shard_map/ppermute | solution.py:121
  6.7 2.6 %collective-permute-start.5 = (bf16[128,512]{1,0:T(8,128)(2,1)}, bf16[128,512]{1,0:T(8,128)(2,1)S(1)}, u32[]{:S(2)}, u32[]{:S(2)}) collective-permute-start(bf16[128,512]{1,0:T(8,128)(2,1)} %refs_0_.3), channel_id=1, source_target_pairs={{0,2},{1,3},{2,0},{3,1},{4,6},{5,7},{6,4},{7,5},{8,10},{9,11},{10,... | collective-permute-start | bytes 393224 | tf_op jit(solution)/shard_map/ppermute | solution.py:121
  9.3 0.9 broadcast_select_fusion.1
  10.3 3.1 %collective-permute-done.2.refs_1_ = bf16[128,512]{1,0:T(8,128)(2,1)S(1)} collective-permute-done((bf16[128,512]{1,0:T(8,128)(2,1)}, bf16[128,512]{1,0:T(8,128)(2,1)S(1)}, u32[]{:S(2)}, u32[]{:S(2)}) %collective-permute-start.2) | collective-permute-done | bytes 131104 | tf_op jit(solution)/shard_map/ppermute | solution.py:121
  13.4 0.5 collective-permute-start.3
  14.0 0.5 collective-permute-start.4
  14.5 3.1 %collective-permute-done.5.refs_2_ = bf16[128,512]{1,0:T(8,128)(2,1)S(1)} collective-permute-done((bf16[128,512]{1,0:T(8,128)(2,1)}, bf16[128,512]{1,0:T(8,128)(2,1)S(1)}, u32[]{:S(2)}, u32[]{:S(2)}) %collective-permute-start.5) | collective-permute-done | bytes 131104 | tf_op jit(solution)/shard_map/ppermute | solution.py:121
  17.5 1.6 %collective-permute-start.6 = (bf16[128,512]{1,0:T(8,128)(2,1)}, bf16[128,512]{1,0:T(8,128)(2,1)S(1)}, u32[]{:S(2)}, u32[]{:S(2)}) collective-permute-start(bf16[128,512]{1,0:T(8,128)(2,1)} %refs_0_.3), channel_id=1, source_target_pairs={{0,3},{1,0},{2,1},{3,2},{4,7},{5,4},{6,5},{7,6},{8,11},{9,8},{10,9... | collective-permute-start | bytes 393224 | tf_op jit(solution)/shard_map/ppermute | solution.py:121
  19.2 0.7 reshape.24.gain_ref
  19.9 0.7 pad.4
  20.6 0.7 copy-done.13
  21.3 0.7 copy-done.14
  22.0 0.6 masked_bias.1.bias_ref
  23.2 0.8 norm_tokens.1
  24.0 3.0 %collective-permute-done.3.out_low.refs_1_ = bf16[512,256]{1,0:T(8,128)(2,1)S(1)} collective-permute-done((bf16[512,256]{1,0:T(8,128)(2,1)}, bf16[512,256]{1,0:T(8,128)(2,1)S(1)}, u32[]{:S(2)}, u32[]{:S(2)}) %collective-permute-start.3) | collective-permute-done | bytes 262176 | tf_op jit(solution)/shard_map/ppermute | solution.py:121
  27.0 1.5 %collective-permute-done.4.out_high.refs_2_ = bf16[512,256]{1,0:T(8,128)(2,1)S(1)} collective-permute-done((bf16[512,256]{1,0:T(8,128)(2,1)}, bf16[512,256]{1,0:T(8,128)(2,1)S(1)}, u32[]{:S(2)}, u32[]{:S(2)}) %collective-permute-start.4) | collective-permute-done | bytes 262176 | tf_op jit(solution)/shard_map/ppermute | solution.py:121
  28.6 1.6 %collective-permute-start.9 = (bf16[4,256,256]{2,1,0:T(8,128)(2,1)S(1)}, bf16[4,256,256]{2,1,0:T(8,128)(2,1)S(1)}, u32[]{:S(2)}, u32[]{:S(2)}) collective-permute-start(bf16[4,256,256]{2,1,0:T(8,128)(2,1)S(1)} %get-tuple-element.61), channel_id=1, source_target_pairs={{0,16},{4,20},{8,24},{12,28},{16,0},{20,4},{24,8},{28,12},{1,17},{... | collective-permute-start | bytes 1572872 | tf_op jit(solution)/shard_map/ppermute | solution.py:121
  30.2 0.5 collective-permute-start.10
  30.7 1.5 %collective-permute-done.8.other_in_ref = bf16[4,128,256]{2,1,0:T(8,128)(2,1)S(1)} collective-permute-done((bf16[4,128,256]{2,1,0:T(8,128)(2,1)S(1)}, bf16[4,128,256]{2,1,0:T(8,128)(2,1)S(1)}, u32[]{:S(2)}, u32[]{:S(2)}) %collective-permute-start.8) | collective-permute-done | bytes 262176 | tf_op jit(solution)/shard_map/ppermute | solution.py:121
  32.3 1.6 %collective-permute-start.13 = (bf16[640,256]{1,0:T(8,128)(2,1)S(1)}, bf16[640,256]{1,0:T(8,128)(2,1)S(1)}, u32[]{:S(2)}, u32[]{:S(2)}) collective-permute-start(bf16[640,256]{1,0:T(8,128)(2,1)S(1)} %get-tuple-element.105), channel_id=1, source_target_pairs={{0,8},{4,12},{8,0},{12,4},{16,24},{20,28},{24,16},{28,20},{1,9},{5... | collective-permute-start | bytes 983048 | tf_op jit(solution)/shard_map/ppermute | solution.py:121
  34.4 9.1 %collective-permute-done.9.refs_3_ = bf16[4,256,256]{2,1,0:T(8,128)(2,1)S(1)} collective-permute-done((bf16[4,256,256]{2,1,0:T(8,128)(2,1)S(1)}, bf16[4,256,256]{2,1,0:T(8,128)(2,1)S(1)}, u32[]{:S(2)}, u32[]{:S(2)}) %collective-permute-start.9) | collective-permute-done | bytes 524320 | tf_op jit(solution)/shard_map/ppermute | solution.py:121
  43.5 1.5 %collective-permute-done.10.refs_4_ = bf16[4,256,256]{2,1,0:T(8,128)(2,1)S(1)} collective-permute-done((bf16[4,256,256]{2,1,0:T(8,128)(2,1)S(1)}, bf16[4,256,256]{2,1,0:T(8,128)(2,1)S(1)}, u32[]{:S(2)}, u32[]{:S(2)}) %collective-permute-start.10) | collective-permute-done | bytes 524320 | tf_op jit(solution)/shard_map/ppermute | solution.py:121
  45.0 1.5 %qkv.1 = (f32[128,512]{1,0:T(8,128)S(1)}, f32[128,1024]{1,0:T(8,128)S(1)}, f32[128,512]{1,0:T(8,128)S(1)}, f32[128,1024]{1,0:T(8,128)S(1)}) custom-call(s32[2]{0:T(128)S(1)} %pad_add_fusion.place_ref, bf16[4,128,256]{2,1,0:T(8,128)(2,1)S(1)} %get-tuple-element.55.own_in_ref, bf16[4,128,256]{2,1,0:T(8,128)(2,1)S(1)} %collective-permute-done.8.other_in_ref, ...), custom_call_target="tpu_custom_call" | custom-call | flops 805306368 | bytes 3145728 | tf_op jit(solution)/shard_map/qkv/pallas_call | solution.py:298
  47.2 0.6 collective-permute-start.17
  47.8 1.5 %collective-permute-done.13.low_in.refs_1_ = bf16[640,256]{1,0:T(8,128)(2,1)S(1)} collective-permute-done((bf16[640,256]{1,0:T(8,128)(2,1)S(1)}, bf16[640,256]{1,0:T(8,128)(2,1)S(1)}, u32[]{:S(2)}, u32[]{:S(2)}) %collective-permute-start.13) | collective-permute-done | bytes 327712 | tf_op jit(solution)/shard_map/ppermute | solution.py:121
  50.0 1.3 collective-permute-start.15
  51.3 1.3 collective-permute-start.16
  52.7 0.8 copy-done.15
  53.6 0.8 copy-done.16
  54.4 10.5 %collective-permute-done.17.low_in.refs_5_ = bf16[256,1280]{1,0:T(8,128)(2,1)S(1)} collective-permute-done((bf16[256,1280]{1,0:T(8,128)(2,1)S(1)}, bf16[256,1280]{1,0:T(8,128)(2,1)S(1)}, u32[]{:S(2)}, u32[]{:S(2)}) %collective-permute-start.17) | collective-permute-done | bytes 655392 | tf_op jit(solution)/shard_map/ppermute | solution.py:121
  64.9 1.7 %packet.3 = (bf16[2,256,1280]{2,1,0:T(8,128)(2,1)}, bf16[2,256,1280]{2,1,0:T(8,128)(2,1)}) custom-call(bf16[2,256,1280]{2,1,0:T(8,128)(2,1)S(1)} %copy-done, bf16[256,1280]{1,0:T(8,128)(2,1)S(1)} %collective-permute-done.17.low_in.refs_5_, bf16[256,1280]{1,0:T(8,128)(2,1)S(1)} %collective-permute-done.18.high_in.refs_6_), custom_call_target="tpu_custom_call" | custom-call | tf_op jit(solution)/shard_map/packet/pallas_call | solution.py:173
  66.6 4.3 %collective-permute-start.26 = (bf16[2,256,1280]{2,1,0:T(8,128)(2,1)}, bf16[2,256,1280]{2,1,0:T(8,128)(2,1)}, u32[]{:S(2)}, u32[]{:S(2)}) collective-permute-start(bf16[2,256,1280]{2,1,0:T(8,128)(2,1)} %get-tuple-element.86), channel_id=1, source_target_pairs={{0,8},{4,12},{8,0},{12,4},{16,24},{20,28},{24,16},{28,20},{1,9},{5... | collective-permute-start | bytes 3932168 | tf_op jit(solution)/shard_map/ppermute | solution.py:121
  70.8 1.0 collective-permute-start.27
  72.0 2.7 %attention.1.own_in_ref = bf16[128,512]{1,0:T(8,128)(2,1)S(1)} custom-call(bf16[128,512]{1,0:T(8,128)(2,1)S(1)} %add_convert_fusion.2.q_ref, bf16[128,1024]{1,0:T(8,128)(2,1)S(1)} %collective-permute-done.15.low_ref, bf16[128,1024]{1,0:T(8,128)(2,1)S(1)} %add_convert_fusion.own_ref, bf16[128,1024]{1,0:T(8,128)(2,1)S(1)} %collective-permute-done.16.high_ref, ...), custom_call_target="tpu_custom_call" | custom-call | flops 100663296 | bytes 1572864 | tf_op jit(solution)/shard_map/attention/pallas_call | solution.py:106
  74.7 1.3 collective-permute-done.19.other_in_ref
  76.0 1.1 attention_out.1
  77.2 3.7 %collective-permute-start.22 = (bf16[256,256]{1,0:T(8,128)(2,1)S(1)}, bf16[256,256]{1,0:T(8,128)(2,1)S(1)}, u32[]{:S(2)}, u32[]{:S(2)}) collective-permute-start(bf16[256,256]{1,0:T(8,128)(2,1)S(1)} %get-tuple-element.82), channel_id=1, source_target_pairs={{0,3},{1,0},{2,1},{3,2},{4,7},{5,4},{6,5},{7,6},{8,11},{9,8},{10,9... | collective-permute-start | bytes 393224 | tf_op jit(solution)/shard_map/ppermute | solution.py:121
  80.8 1.0 collective-permute-start.20
  81.9 0.7 pad_maximum_fusion
  82.6 2.2 %collective-permute-done.22 = bf16[256,256]{1,0:T(8,128)(2,1)S(1)} collective-permute-done((bf16[256,256]{1,0:T(8,128)(2,1)S(1)}, bf16[256,256]{1,0:T(8,128)(2,1)S(1)}, u32[]{:S(2)}, u32[]{:S(2)}) %collective-permute-start.22) | collective-permute-done | bytes 131104 | tf_op jit(solution)/shard_map/ppermute | solution.py:121
  84.8 7.7 %collective-permute-done.21 = bf16[256,256]{1,0:T(8,128)(2,1)S(1)} collective-permute-done((bf16[256,256]{1,0:T(8,128)(2,1)S(1)}, bf16[256,256]{1,0:T(8,128)(2,1)S(1)}, u32[]{:S(2)}, u32[]{:S(2)}) %collective-permute-start.21) | collective-permute-done | bytes 131104 | tf_op jit(solution)/shard_map/ppermute | solution.py:121
  92.6 1.5 %collective-permute-start.25 = (bf16[256,256]{1,0:T(8,128)(2,1)S(1)}, bf16[256,256]{1,0:T(8,128)(2,1)S(1)}, u32[]{:S(2)}, u32[]{:S(2)}) collective-permute-start(bf16[256,256]{1,0:T(8,128)(2,1)S(1)} %add_convert_fusion.1.refs_0_), channel_id=1, source_target_pairs={{0,3},{1,0},{2,1},{3,2},{4,7},{5,4},{6,5},{7,6},{8,11},{9,8},{10,9... | collective-permute-start | bytes 393224 | tf_op jit(solution)/shard_map/ppermute | solution.py:121
  94.1 0.7 reshape.23.gain_ref
  94.8 0.6 collective-permute-start.23
  95.4 2.5 %collective-permute-start.24 = (bf16[256,256]{1,0:T(8,128)(2,1)S(1)}, bf16[256,256]{1,0:T(8,128)(2,1)S(1)}, u32[]{:S(2)}, u32[]{:S(2)}) collective-permute-start(bf16[256,256]{1,0:T(8,128)(2,1)S(1)} %add_convert_fusion.1.refs_0_), channel_id=1, source_target_pairs={{0,2},{1,3},{2,0},{3,1},{4,6},{5,7},{6,4},{7,5},{8,10},{9,11},{10,... | collective-permute-start | bytes 393224 | tf_op jit(solution)/shard_map/ppermute | solution.py:121
  98.0 2.1 %collective-permute-start.30 = (bf16[2,640,256]{2,1,0:T(8,128)(2,1)}, bf16[2,640,256]{2,1,0:T(8,128)(2,1)S(1)}, u32[]{:S(2)}, u32[]{:S(2)}) collective-permute-start(bf16[2,640,256]{2,1,0:T(8,128)(2,1)} %copy-done.16), channel_id=1, source_target_pairs={{0,8},{4,12},{8,0},{12,4},{16,24},{20,28},{24,16},{28,20},{1,9},{5... | collective-permute-start | bytes 1966088 | tf_op jit(solution)/shard_map/ppermute | solution.py:121
  100.2 3.4 %collective-permute-done.23.refs_1_ = bf16[256,256]{1,0:T(8,128)(2,1)S(1)} collective-permute-done((bf16[256,256]{1,0:T(8,128)(2,1)S(1)}, bf16[256,256]{1,0:T(8,128)(2,1)S(1)}, u32[]{:S(2)}, u32[]{:S(2)}) %collective-permute-start.23) | collective-permute-done | bytes 131104 | tf_op jit(solution)/shard_map/ppermute | solution.py:121
  103.6 1.0 collective-permute-start.31
  104.6 2.0 %collective-permute-done.24.refs_2_ = bf16[256,256]{1,0:T(8,128)(2,1)S(1)} collective-permute-done((bf16[256,256]{1,0:T(8,128)(2,1)S(1)}, bf16[256,256]{1,0:T(8,128)(2,1)S(1)}, u32[]{:S(2)}, u32[]{:S(2)}) %collective-permute-start.24) | collective-permute-done | bytes 131104 | tf_op jit(solution)/shard_map/ppermute | solution.py:121
  106.6 3.3 %ffn_in.1 = (f32[128,2560]{1,0:T(8,128)S(1)}, bf16[128,2560]{1,0:T(8,128)(2,1)S(1)}) custom-call(s32[2]{0:T(128)S(1)} %pad_add_fusion.place_ref, f32[8,256]{1,0:T(8,128)S(1)} %reshape.23.gain_ref, bf16[256,256]{1,0:T(8,128)(2,1)S(1)} %add_convert_fusion.1.refs_0_, bf16[256,256]{1,0:T(8,128)(2,1)S(1)} %collective-permute-done.23.refs_1_, ...), custom_call_target="tpu_custom_call" | custom-call | flops 1342177280 | bytes 5242880 | tf_op jit(solution)/shard_map/ffn_in/pallas_call | solution.py:334
  110.3 0.6 collective-permute-start.29
  110.9 1.3 collective-permute-done.29
  112.1 2.6 %collective-permute-done.30.refs_3_ = bf16[2,640,256]{2,1,0:T(8,128)(2,1)S(1)} collective-permute-done((bf16[2,640,256]{2,1,0:T(8,128)(2,1)}, bf16[2,640,256]{2,1,0:T(8,128)(2,1)S(1)}, u32[]{:S(2)}, u32[]{:S(2)}) %collective-permute-start.30) | collective-permute-done | bytes 655392 | tf_op jit(solution)/shard_map/ppermute | solution.py:121
  114.7 2.5 %collective-permute-done.31.refs_4_ = bf16[2,640,256]{2,1,0:T(8,128)(2,1)S(1)} collective-permute-done((bf16[2,640,256]{2,1,0:T(8,128)(2,1)}, bf16[2,640,256]{2,1,0:T(8,128)(2,1)S(1)}, u32[]{:S(2)}, u32[]{:S(2)}) %collective-permute-start.31) | collective-permute-done | bytes 655392 | tf_op jit(solution)/shard_map/ppermute | solution.py:121
  117.7 1.6 %collective-permute-done.32.other_in_ref = bf16[128,1280]{1,0:T(8,128)(2,1)S(1)} collective-permute-done((bf16[128,1280]{1,0:T(8,128)(2,1)S(1)}, bf16[128,1280]{1,0:T(8,128)(2,1)S(1)}, u32[]{:S(2)}, u32[]{:S(2)}) %collective-permute-start.32) | collective-permute-done | bytes 327712 | tf_op jit(solution)/shard_map/ppermute | solution.py:121
  119.3 1.7 %ffn_out.1 = (f32[256,256]{1,0:T(8,128)S(1)}, bf16[256,256]{1,0:T(8,128)(2,1)S(1)}, bf16[256,256]{1,0:T(8,128)(2,1)S(1)}, bf16[256,256]{1,0:T(8,128)(2,1)S(1)}) custom-call(s32[2]{0:T(128)S(1)} %pad_add_fusion.place_ref, bf16[128,1280]{1,0:T(8,128)(2,1)S(1)} %fusion.8.own_in_ref, bf16[128,1280]{1,0:T(8,128)(2,1)S(1)} %collective-permute-done.32.other_in_ref, ...), custom_call_target="tpu_custom_call" | custom-call | flops 671088640 | bytes 2621440 | tf_op jit(solution)/shard_map/ffn_out/pallas_call | solution.py:392
  121.0 2.7 %collective-permute-start.35 = (bf16[256,256]{1,0:T(8,128)(2,1)S(1)}, bf16[256,256]{1,0:T(8,128)(2,1)S(1)}, u32[]{:S(2)}, u32[]{:S(2)}) collective-permute-start(bf16[256,256]{1,0:T(8,128)(2,1)S(1)} %get-tuple-element.100), channel_id=1, source_target_pairs={{0,3},{1,0},{2,1},{3,2},{4,7},{5,4},{6,5},{7,6},{8,11},{9,8},{10,9... | collective-permute-start | bytes 393224 | tf_op jit(solution)/shard_map/ppermute | solution.py:121
  123.7 1.0 collective-permute-start.33
  124.8 2.9 %collective-permute-done.35 = bf16[256,256]{1,0:T(8,128)(2,1)S(1)} collective-permute-done((bf16[256,256]{1,0:T(8,128)(2,1)S(1)}, bf16[256,256]{1,0:T(8,128)(2,1)S(1)}, u32[]{:S(2)}, u32[]{:S(2)}) %collective-permute-start.35) | collective-permute-done | bytes 131104 | tf_op jit(solution)/shard_map/ppermute | solution.py:121
  127.7 7.7 %collective-permute-done.34 = bf16[256,256]{1,0:T(8,128)(2,1)S(1)} collective-permute-done((bf16[256,256]{1,0:T(8,128)(2,1)S(1)}, bf16[256,256]{1,0:T(8,128)(2,1)S(1)}, u32[]{:S(2)}, u32[]{:S(2)}) %collective-permute-start.34) | collective-permute-done | bytes 131104 | tf_op jit(solution)/shard_map/ppermute | solution.py:121
  135.6 1.2 collective-permute-done.36
  136.9 0.7 maximum_select_fusion
  (79 shorter events, 4.1 us)
Async XLA Ops:
  0.6 22.5 %copy-start.11 = (bf16[128,512]{1,0:T(8,128)(2,1)S(1)}, bf16[128,512]{1,0:T(8,128)(2,1)}, u32[]{:S(2)}) copy-start(bf16[128,512]{1,0:T(8,128)(2,1)} %refs_0_.3) | copy-start | bytes 393220
  0.6 27.8 %collective-permute-start = (bf16[3,256,512]{2,1,0:T(8,128)(2,1)}, bf16[3,256,512]{2,1,0:T(8,128)(2,1)S(1)}, u32[]{:S(2)}, u32[]{:S(2)}) collective-permute-start(bf16[3,256,512]{2,1,0:T(8,128)(2,1)} %refs_0_.4), channel_id=1, source_target_pairs={{0,8},{4,12},{8,0},{12,4},{16,24},{20,28},{24,16},{28,20},{1,9},{5... | collective-permute-start | bytes 2359304 | tf_op jit(solution)/shard_map/ppermute | solution.py:121
  3.6 24.8 %collective-permute-start.1 = (bf16[3,256,512]{2,1,0:T(8,128)(2,1)}, bf16[3,256,512]{2,1,0:T(8,128)(2,1)S(1)}, u32[]{:S(2)}, u32[]{:S(2)}) collective-permute-start(bf16[3,256,512]{2,1,0:T(8,128)(2,1)} %refs_0_.4), channel_id=1, source_target_pairs={{0,16},{4,20},{8,24},{12,28},{16,0},{20,4},{24,8},{28,12},{1,17},{... | collective-permute-start | bytes 2359304 | tf_op jit(solution)/shard_map/ppermute | solution.py:121
  5.2 8.2 %collective-permute-start.2 = (bf16[128,512]{1,0:T(8,128)(2,1)}, bf16[128,512]{1,0:T(8,128)(2,1)S(1)}, u32[]{:S(2)}, u32[]{:S(2)}) collective-permute-start(bf16[128,512]{1,0:T(8,128)(2,1)} %refs_0_.3), channel_id=1, source_target_pairs={{0,1},{1,2},{2,3},{3,0},{4,5},{5,6},{6,7},{7,4},{8,9},{9,10},{10,1... | collective-permute-start | bytes 393224 | tf_op jit(solution)/shard_map/ppermute | solution.py:121
  6.7 10.8 %collective-permute-start.5 = (bf16[128,512]{1,0:T(8,128)(2,1)}, bf16[128,512]{1,0:T(8,128)(2,1)S(1)}, u32[]{:S(2)}, u32[]{:S(2)}) collective-permute-start(bf16[128,512]{1,0:T(8,128)(2,1)} %refs_0_.3), channel_id=1, source_target_pairs={{0,2},{1,3},{2,0},{3,1},{4,6},{5,7},{6,4},{7,5},{8,10},{9,11},{10,... | collective-permute-start | bytes 393224 | tf_op jit(solution)/shard_map/ppermute | solution.py:121
  10.2 3.7 %collective-permute-start.7 = (bf16[128,256]{1,0:T(8,128)(2,1)S(1)}, bf16[128,256]{1,0:T(8,128)(2,1)S(1)}, u32[]{:S(2)}, u32[]{:S(2)}) collective-permute-start(bf16[128,256]{1,0:T(8,128)(2,1)S(1)} %get-tuple-element.111), channel_id=1, source_target_pairs={{0,4},{4,0},{8,12},{12,8},{16,20},{20,16},{24,28},{28,24},{1,5},{5... | collective-permute-start | bytes 196616 | tf_op jit(solution)/shard_map/ppermute | solution.py:121
  13.4 13.6 %collective-permute-start.3 = (bf16[512,256]{1,0:T(8,128)(2,1)}, bf16[512,256]{1,0:T(8,128)(2,1)S(1)}, u32[]{:S(2)}, u32[]{:S(2)}) collective-permute-start(bf16[512,256]{1,0:T(8,128)(2,1)} %refs_0_.5), channel_id=1, source_target_pairs={{0,8},{4,12},{8,0},{12,4},{16,24},{20,28},{24,16},{28,20},{1,9},{5... | collective-permute-start | bytes 786440 | tf_op jit(solution)/shard_map/ppermute | solution.py:121
  14.0 14.5 %collective-permute-start.4 = (bf16[512,256]{1,0:T(8,128)(2,1)}, bf16[512,256]{1,0:T(8,128)(2,1)S(1)}, u32[]{:S(2)}, u32[]{:S(2)}) collective-permute-start(bf16[512,256]{1,0:T(8,128)(2,1)} %refs_0_.5), channel_id=1, source_target_pairs={{0,16},{4,20},{8,24},{12,28},{16,0},{20,4},{24,8},{28,12},{1,17},{... | collective-permute-start | bytes 786440 | tf_op jit(solution)/shard_map/ppermute | solution.py:121
  17.5 5.6 %collective-permute-start.6 = (bf16[128,512]{1,0:T(8,128)(2,1)}, bf16[128,512]{1,0:T(8,128)(2,1)S(1)}, u32[]{:S(2)}, u32[]{:S(2)}) collective-permute-start(bf16[128,512]{1,0:T(8,128)(2,1)} %refs_0_.3), channel_id=1, source_target_pairs={{0,3},{1,0},{2,1},{3,2},{4,7},{5,4},{6,5},{7,6},{8,11},{9,8},{10,9... | collective-permute-start | bytes 393224 | tf_op jit(solution)/shard_map/ppermute | solution.py:121
  20.6 0.7 copy-start.13
  21.3 0.7 copy-start.14
  22.7 9.6 %copy-start.1 = (bf16[1280,256]{1,0:T(8,128)(2,1)S(1)}, bf16[1280,256]{1,0:T(8,128)(2,1)}, u32[]{:S(2)}) copy-start(bf16[1280,256]{1,0:T(8,128)(2,1)} %param.20) | copy-start | bytes 1966084
  27.0 5.3 %copy-start.6 = (bf16[512,256]{1,0:T(8,128)(2,1)}, bf16[512,256]{1,0:T(8,128)(2,1)S(1)}, u32[]{:S(2)}) copy-start(bf16[512,256]{1,0:T(8,128)(2,1)S(1)} %collective-permute-done.3.out_low.refs_1_) | copy-start | bytes 786436
  28.5 3.8 %copy-start.8 = (bf16[512,256]{1,0:T(8,128)(2,1)}, bf16[512,256]{1,0:T(8,128)(2,1)S(1)}, u32[]{:S(2)}) copy-start(bf16[512,256]{1,0:T(8,128)(2,1)S(1)} %collective-permute-done.4.out_high.refs_2_) | copy-start | bytes 786436
  28.5 16.5 %copy-start.10 = (bf16[3,256,512]{2,1,0:T(8,128)(2,1)S(1)}, bf16[3,256,512]{2,1,0:T(8,128)(2,1)}, u32[]{:S(2)}) copy-start(bf16[3,256,512]{2,1,0:T(8,128)(2,1)} %refs_0_.4) | copy-start | bytes 2359300
  28.6 14.9 %collective-permute-start.9 = (bf16[4,256,256]{2,1,0:T(8,128)(2,1)S(1)}, bf16[4,256,256]{2,1,0:T(8,128)(2,1)S(1)}, u32[]{:S(2)}, u32[]{:S(2)}) collective-permute-start(bf16[4,256,256]{2,1,0:T(8,128)(2,1)S(1)} %get-tuple-element.61), channel_id=1, source_target_pairs={{0,16},{4,20},{8,24},{12,28},{16,0},{20,4},{24,8},{28,12},{1,17},{... | collective-permute-start | bytes 1572872 | tf_op jit(solution)/shard_map/ppermute | solution.py:121
  30.2 14.9 %collective-permute-start.10 = (bf16[4,256,256]{2,1,0:T(8,128)(2,1)S(1)}, bf16[4,256,256]{2,1,0:T(8,128)(2,1)S(1)}, u32[]{:S(2)}, u32[]{:S(2)}) collective-permute-start(bf16[4,256,256]{2,1,0:T(8,128)(2,1)S(1)} %get-tuple-element.62), channel_id=1, source_target_pairs={{0,8},{4,12},{8,0},{12,4},{16,24},{20,28},{24,16},{28,20},{1,9},{5... | collective-permute-start | bytes 1572872 | tf_op jit(solution)/shard_map/ppermute | solution.py:121
  30.7 1.5 %collective-permute-start.8 = (bf16[4,128,256]{2,1,0:T(8,128)(2,1)S(1)}, bf16[4,128,256]{2,1,0:T(8,128)(2,1)S(1)}, u32[]{:S(2)}, u32[]{:S(2)}) collective-permute-start(bf16[4,128,256]{2,1,0:T(8,128)(2,1)S(1)} %get-tuple-element.56), channel_id=1, source_target_pairs={{0,4},{4,0},{8,12},{12,8},{16,20},{20,16},{24,28},{28,24},{1,5},{5... | collective-permute-start | bytes 786440 | tf_op jit(solution)/shard_map/ppermute | solution.py:121
  32.3 17.1 %collective-permute-start.13 = (bf16[640,256]{1,0:T(8,128)(2,1)S(1)}, bf16[640,256]{1,0:T(8,128)(2,1)S(1)}, u32[]{:S(2)}, u32[]{:S(2)}) collective-permute-start(bf16[640,256]{1,0:T(8,128)(2,1)S(1)} %get-tuple-element.105), channel_id=1, source_target_pairs={{0,8},{4,12},{8,0},{12,4},{16,24},{20,28},{24,16},{28,20},{1,9},{5... | collective-permute-start | bytes 983048 | tf_op jit(solution)/shard_map/ppermute | solution.py:121
  33.9 13.3 %copy-start = (bf16[2,256,1280]{2,1,0:T(8,128)(2,1)S(1)}, bf16[2,256,1280]{2,1,0:T(8,128)(2,1)}, u32[]{:S(2)}) copy-start(bf16[2,256,1280]{2,1,0:T(8,128)(2,1)} %refs_4_) | copy-start | bytes 3932164
  33.9 16.0 %collective-permute-start.14 = (bf16[640,256]{1,0:T(8,128)(2,1)S(1)}, bf16[640,256]{1,0:T(8,128)(2,1)S(1)}, u32[]{:S(2)}, u32[]{:S(2)}) collective-permute-start(bf16[640,256]{1,0:T(8,128)(2,1)S(1)} %get-tuple-element.104), channel_id=1, source_target_pairs={{0,16},{4,20},{8,24},{12,28},{16,0},{20,4},{24,8},{28,12},{1,17},{... | collective-permute-start | bytes 983048 | tf_op jit(solution)/shard_map/ppermute | solution.py:121
  46.6 3.3 %collective-permute-start.11 = (f32[128,1024]{1,0:T(8,128)S(1)}, f32[128,1024]{1,0:T(8,128)S(1)}, u32[]{:S(2)}, u32[]{:S(2)}) collective-permute-start(f32[128,1024]{1,0:T(8,128)S(1)} %get-tuple-element.64), channel_id=1, source_target_pairs={{0,4},{4,0},{8,12},{12,8},{16,20},{20,16},{24,28},{28,24},{1,5},{5... | collective-permute-start | bytes 1572872 | tf_op jit(solution)/shard_map/ppermute | solution.py:121
  46.6 3.2 %collective-permute-start.12 = (f32[128,512]{1,0:T(8,128)S(1)}, f32[128,512]{1,0:T(8,128)S(1)}, u32[]{:S(2)}, u32[]{:S(2)}) collective-permute-start(f32[128,512]{1,0:T(8,128)S(1)} %get-tuple-element.65), channel_id=1, source_target_pairs={{0,4},{4,0},{8,12},{12,8},{16,20},{20,16},{24,28},{28,24},{1,5},{5... | collective-permute-start | bytes 786440 | tf_op jit(solution)/shard_map/ppermute | solution.py:121
  47.2 17.7 %collective-permute-start.17 = (bf16[256,1280]{1,0:T(8,128)(2,1)S(1)}, bf16[256,1280]{1,0:T(8,128)(2,1)S(1)}, u32[]{:S(2)}, u32[]{:S(2)}) collective-permute-start(bf16[256,1280]{1,0:T(8,128)(2,1)S(1)} %get-tuple-element.103), channel_id=1, source_target_pairs={{0,8},{4,12},{8,0},{12,4},{16,24},{20,28},{24,16},{28,20},{1,9},{5... | collective-permute-start | bytes 1966088 | tf_op jit(solution)/shard_map/ppermute | solution.py:121
  49.4 3.3 %copy-start.2 = (bf16[640,256]{1,0:T(8,128)(2,1)}, bf16[640,256]{1,0:T(8,128)(2,1)S(1)}, u32[]{:S(2)}) copy-start(bf16[640,256]{1,0:T(8,128)(2,1)S(1)} %collective-permute-done.13.low_in.refs_1_) | copy-start | bytes 983044
  49.4 15.5 %collective-permute-start.18 = (bf16[256,1280]{1,0:T(8,128)(2,1)S(1)}, bf16[256,1280]{1,0:T(8,128)(2,1)S(1)}, u32[]{:S(2)}, u32[]{:S(2)}) collective-permute-start(bf16[256,1280]{1,0:T(8,128)(2,1)S(1)} %get-tuple-element.102), channel_id=1, source_target_pairs={{0,16},{4,20},{8,24},{12,28},{16,0},{20,4},{24,8},{28,12},{1,17},{... | collective-permute-start | bytes 1966088 | tf_op jit(solution)/shard_map/ppermute | solution.py:121
  49.9 2.8 %copy-start.4 = (bf16[640,256]{1,0:T(8,128)(2,1)}, bf16[640,256]{1,0:T(8,128)(2,1)S(1)}, u32[]{:S(2)}) copy-start(bf16[640,256]{1,0:T(8,128)(2,1)S(1)} %collective-permute-done.14.high_in.refs_2_) | copy-start | bytes 983044
  50.0 14.9 %collective-permute-start.15 = (bf16[128,1024]{1,0:T(8,128)(2,1)S(1)}, bf16[128,1024]{1,0:T(8,128)(2,1)S(1)}, u32[]{:S(2)}, u32[]{:S(2)}) collective-permute-start(bf16[128,1024]{1,0:T(8,128)(2,1)S(1)} %add_convert_fusion.own_ref), channel_id=1, source_target_pairs={{0,4},{4,8},{8,12},{12,16},{16,20},{20,24},{24,28},{1,5},{5,9},{9,... | collective-permute-start | bytes 786440 | tf_op jit(solution)/shard_map/ppermute | solution.py:478
  51.3 13.6 %collective-permute-start.16 = (bf16[128,1024]{1,0:T(8,128)(2,1)S(1)}, bf16[128,1024]{1,0:T(8,128)(2,1)S(1)}, u32[]{:S(2)}, u32[]{:S(2)}) collective-permute-start(bf16[128,1024]{1,0:T(8,128)(2,1)S(1)} %add_convert_fusion.own_ref), channel_id=1, source_target_pairs={{4,0},{8,4},{12,8},{16,12},{20,16},{24,20},{28,24},{5,1},{9,5},{13... | collective-permute-start | bytes 786440 | tf_op jit(solution)/shard_map/ppermute | solution.py:479
  52.7 0.9 copy-start.15
  53.6 0.8 copy-start.16
  66.6 40.1 %collective-permute-start.26 = (bf16[2,256,1280]{2,1,0:T(8,128)(2,1)}, bf16[2,256,1280]{2,1,0:T(8,128)(2,1)}, u32[]{:S(2)}, u32[]{:S(2)}) collective-permute-start(bf16[2,256,1280]{2,1,0:T(8,128)(2,1)} %get-tuple-element.86), channel_id=1, source_target_pairs={{0,8},{4,12},{8,0},{12,4},{16,24},{20,28},{24,16},{28,20},{1,9},{5... | collective-permute-start | bytes 3932168 | tf_op jit(solution)/shard_map/ppermute | solution.py:121
  70.8 35.8 %collective-permute-start.27 = (bf16[2,256,1280]{2,1,0:T(8,128)(2,1)}, bf16[2,256,1280]{2,1,0:T(8,128)(2,1)}, u32[]{:S(2)}, u32[]{:S(2)}) collective-permute-start(bf16[2,256,1280]{2,1,0:T(8,128)(2,1)} %get-tuple-element.87), channel_id=1, source_target_pairs={{0,16},{4,20},{8,24},{12,28},{16,0},{20,4},{24,8},{28,12},{1,17},{... | collective-permute-start | bytes 3932168 | tf_op jit(solution)/shard_map/ppermute | solution.py:121
  71.9 4.1 %copy-start.7 = (bf16[512,256]{1,0:T(8,128)(2,1)S(1)}, bf16[512,256]{1,0:T(8,128)(2,1)}, u32[]{:S(2)}) copy-start(bf16[512,256]{1,0:T(8,128)(2,1)} %copy-done.6) | copy-start | bytes 786436
  71.9 4.1 %copy-start.9 = (bf16[512,256]{1,0:T(8,128)(2,1)S(1)}, bf16[512,256]{1,0:T(8,128)(2,1)}, u32[]{:S(2)}) copy-start(bf16[512,256]{1,0:T(8,128)(2,1)} %copy-done.8) | copy-start | bytes 786436
  71.9 4.1 %copy-start.12 = (bf16[512,256]{1,0:T(8,128)(2,1)S(1)}, bf16[512,256]{1,0:T(8,128)(2,1)}, u32[]{:S(2)}) copy-start(bf16[512,256]{1,0:T(8,128)(2,1)} %refs_0_.5) | copy-start | bytes 786436
  74.6 1.4 %collective-permute-start.19 = (bf16[128,512]{1,0:T(8,128)(2,1)S(1)}, bf16[128,512]{1,0:T(8,128)(2,1)S(1)}, u32[]{:S(2)}, u32[]{:S(2)}) collective-permute-start(bf16[128,512]{1,0:T(8,128)(2,1)S(1)} %attention.1.own_in_ref), channel_id=1, source_target_pairs={{0,4},{4,0},{8,12},{12,8},{16,20},{20,16},{24,28},{28,24},{1,5},{5... | collective-permute-start | bytes 393224 | tf_op jit(solution)/shard_map/ppermute | solution.py:121
  77.2 7.6 %collective-permute-start.22 = (bf16[256,256]{1,0:T(8,128)(2,1)S(1)}, bf16[256,256]{1,0:T(8,128)(2,1)S(1)}, u32[]{:S(2)}, u32[]{:S(2)}) collective-permute-start(bf16[256,256]{1,0:T(8,128)(2,1)S(1)} %get-tuple-element.82), channel_id=1, source_target_pairs={{0,3},{1,0},{2,1},{3,2},{4,7},{5,4},{6,5},{7,6},{8,11},{9,8},{10,9... | collective-permute-start | bytes 393224 | tf_op jit(solution)/shard_map/ppermute | solution.py:121
  80.8 11.7 %collective-permute-start.21 = (bf16[256,256]{1,0:T(8,128)(2,1)S(1)}, bf16[256,256]{1,0:T(8,128)(2,1)S(1)}, u32[]{:S(2)}, u32[]{:S(2)}) collective-permute-start(bf16[256,256]{1,0:T(8,128)(2,1)S(1)} %get-tuple-element.81), channel_id=1, source_target_pairs={{0,2},{1,3},{2,0},{3,1},{4,6},{5,7},{6,4},{7,5},{8,10},{9,11},{10,... | collective-permute-start | bytes 393224 | tf_op jit(solution)/shard_map/ppermute | solution.py:121
  80.8 11.7 %collective-permute-start.20 = (bf16[256,256]{1,0:T(8,128)(2,1)S(1)}, bf16[256,256]{1,0:T(8,128)(2,1)S(1)}, u32[]{:S(2)}, u32[]{:S(2)}) collective-permute-start(bf16[256,256]{1,0:T(8,128)(2,1)S(1)} %get-tuple-element.80), channel_id=1, source_target_pairs={{0,1},{1,2},{2,3},{3,0},{4,5},{5,6},{6,7},{7,4},{8,9},{9,10},{10,1... | collective-permute-start | bytes 393224 | tf_op jit(solution)/shard_map/ppermute | solution.py:121
  92.6 5.4 %collective-permute-start.25 = (bf16[256,256]{1,0:T(8,128)(2,1)S(1)}, bf16[256,256]{1,0:T(8,128)(2,1)S(1)}, u32[]{:S(2)}, u32[]{:S(2)}) collective-permute-start(bf16[256,256]{1,0:T(8,128)(2,1)S(1)} %add_convert_fusion.1.refs_0_), channel_id=1, source_target_pairs={{0,3},{1,0},{2,1},{3,2},{4,7},{5,4},{6,5},{7,6},{8,11},{9,8},{10,9... | collective-permute-start | bytes 393224 | tf_op jit(solution)/shard_map/ppermute | solution.py:121
  94.8 8.8 %collective-permute-start.23 = (bf16[256,256]{1,0:T(8,128)(2,1)S(1)}, bf16[256,256]{1,0:T(8,128)(2,1)S(1)}, u32[]{:S(2)}, u32[]{:S(2)}) collective-permute-start(bf16[256,256]{1,0:T(8,128)(2,1)S(1)} %add_convert_fusion.1.refs_0_), channel_id=1, source_target_pairs={{0,1},{1,2},{2,3},{3,0},{4,5},{5,6},{6,7},{7,4},{8,9},{9,10},{10,1... | collective-permute-start | bytes 393224 | tf_op jit(solution)/shard_map/ppermute | solution.py:121
  95.4 11.2 %collective-permute-start.24 = (bf16[256,256]{1,0:T(8,128)(2,1)S(1)}, bf16[256,256]{1,0:T(8,128)(2,1)S(1)}, u32[]{:S(2)}, u32[]{:S(2)}) collective-permute-start(bf16[256,256]{1,0:T(8,128)(2,1)S(1)} %add_convert_fusion.1.refs_0_), channel_id=1, source_target_pairs={{0,2},{1,3},{2,0},{3,1},{4,6},{5,7},{6,4},{7,5},{8,10},{9,11},{10,... | collective-permute-start | bytes 393224 | tf_op jit(solution)/shard_map/ppermute | solution.py:121
  98.0 16.7 %collective-permute-start.30 = (bf16[2,640,256]{2,1,0:T(8,128)(2,1)}, bf16[2,640,256]{2,1,0:T(8,128)(2,1)S(1)}, u32[]{:S(2)}, u32[]{:S(2)}) collective-permute-start(bf16[2,640,256]{2,1,0:T(8,128)(2,1)} %copy-done.16), channel_id=1, source_target_pairs={{0,8},{4,12},{8,0},{12,4},{16,24},{20,28},{24,16},{28,20},{1,9},{5... | collective-permute-start | bytes 1966088 | tf_op jit(solution)/shard_map/ppermute | solution.py:121
  103.6 13.6 %collective-permute-start.31 = (bf16[2,640,256]{2,1,0:T(8,128)(2,1)}, bf16[2,640,256]{2,1,0:T(8,128)(2,1)S(1)}, u32[]{:S(2)}, u32[]{:S(2)}) collective-permute-start(bf16[2,640,256]{2,1,0:T(8,128)(2,1)} %copy-done.15), channel_id=1, source_target_pairs={{0,16},{4,20},{8,24},{12,28},{16,0},{20,4},{24,8},{28,12},{1,17},{... | collective-permute-start | bytes 1966088 | tf_op jit(solution)/shard_map/ppermute | solution.py:121
  110.0 7.2 %collective-permute-start.28 = (bf16[128,2560]{1,0:T(8,128)(2,1)S(1)}, bf16[128,2560]{1,0:T(8,128)(2,1)S(1)}, u32[]{:S(2)}, u32[]{:S(2)}) collective-permute-start(bf16[128,2560]{1,0:T(8,128)(2,1)S(1)} %get-tuple-element.89), channel_id=1, source_target_pairs={{0,4},{4,0},{8,12},{12,8},{16,20},{20,16},{24,28},{28,24},{1,5},{5... | collective-permute-start | bytes 1966088 | tf_op jit(solution)/shard_map/ppermute | solution.py:121
  110.3 1.8 %collective-permute-start.29 = (f32[128]{0:T(128)S(1)}, f32[128]{0:T(128)S(1)}, u32[]{:S(2)}, u32[]{:S(2)}) collective-permute-start(f32[128]{0:T(128)S(1)} %slice.54), channel_id=1, source_target_pairs={{0,4},{4,0},{8,12},{12,8},{16,20},{20,16},{24,28},{28,24},{1,5},{5... | collective-permute-start | bytes 1544 | tf_op jit(solution)/shard_map/ppermute | solution.py:121
  117.4 2.0 %copy-start.3 = (bf16[640,256]{1,0:T(8,128)(2,1)S(1)}, bf16[640,256]{1,0:T(8,128)(2,1)}, u32[]{:S(2)}) copy-start(bf16[640,256]{1,0:T(8,128)(2,1)} %copy-done.2) | copy-start | bytes 983044
  117.4 1.9 %copy-start.5 = (bf16[640,256]{1,0:T(8,128)(2,1)S(1)}, bf16[640,256]{1,0:T(8,128)(2,1)}, u32[]{:S(2)}) copy-start(bf16[640,256]{1,0:T(8,128)(2,1)} %copy-done.4) | copy-start | bytes 983044
  117.6 1.7 %collective-permute-start.32 = (bf16[128,1280]{1,0:T(8,128)(2,1)S(1)}, bf16[128,1280]{1,0:T(8,128)(2,1)S(1)}, u32[]{:S(2)}, u32[]{:S(2)}) collective-permute-start(bf16[128,1280]{1,0:T(8,128)(2,1)S(1)} %fusion.8.own_in_ref), channel_id=1, source_target_pairs={{0,4},{4,0},{8,12},{12,8},{16,20},{20,16},{24,28},{28,24},{1,5},{5... | collective-permute-start | bytes 983048 | tf_op jit(solution)/shard_map/ppermute | solution.py:121
  121.0 6.7 %collective-permute-start.35 = (bf16[256,256]{1,0:T(8,128)(2,1)S(1)}, bf16[256,256]{1,0:T(8,128)(2,1)S(1)}, u32[]{:S(2)}, u32[]{:S(2)}) collective-permute-start(bf16[256,256]{1,0:T(8,128)(2,1)S(1)} %get-tuple-element.100), channel_id=1, source_target_pairs={{0,3},{1,0},{2,1},{3,2},{4,7},{5,4},{6,5},{7,6},{8,11},{9,8},{10,9... | collective-permute-start | bytes 393224 | tf_op jit(solution)/shard_map/ppermute | solution.py:121
  123.7 11.7 %collective-permute-start.34 = (bf16[256,256]{1,0:T(8,128)(2,1)S(1)}, bf16[256,256]{1,0:T(8,128)(2,1)S(1)}, u32[]{:S(2)}, u32[]{:S(2)}) collective-permute-start(bf16[256,256]{1,0:T(8,128)(2,1)S(1)} %get-tuple-element.99), channel_id=1, source_target_pairs={{0,2},{1,3},{2,0},{3,1},{4,6},{5,7},{6,4},{7,5},{8,10},{9,11},{10,... | collective-permute-start | bytes 393224 | tf_op jit(solution)/shard_map/ppermute | solution.py:121
  123.7 11.7 %collective-permute-start.33 = (bf16[256,256]{1,0:T(8,128)(2,1)S(1)}, bf16[256,256]{1,0:T(8,128)(2,1)S(1)}, u32[]{:S(2)}, u32[]{:S(2)}) collective-permute-start(bf16[256,256]{1,0:T(8,128)(2,1)S(1)} %get-tuple-element.98), channel_id=1, source_target_pairs={{0,1},{1,2},{2,3},{3,0},{4,5},{5,6},{6,7},{7,4},{8,9},{9,10},{10,1... | collective-permute-start | bytes 393224 | tf_op jit(solution)/shard_map/ppermute | solution.py:121
  135.5 1.3 collective-permute-start.36

commit v7 on v6

--- a/solution.py
+++ b/solution.py
@@ -246,28 +246,26 @@
                 send_ref[:, where] = total[count:].astype(send_ref.dtype)
 
 
-def relay_kernel(qkv_low, qkv_high, out_low, out_high, low_ref, high_ref):
-    half = low_ref.shape[2]
-    parts = qkv_low.shape[0]
-    low_ref[:parts] = qkv_low[:, :, :half]
-    low_ref[parts] = out_low[:half]
-    high_ref[:parts] = qkv_high[:, :, half:]
-    high_ref[parts] = out_high[half:]
-
-
-def relayed(qkv_near, out_near):
-    if len(qkv_near) != 2:
+def relay_kernel(axis, low_in, high_in, low_ref, high_ref):
+    half = low_ref.shape[axis]
+    low_ref[...] = low_in[:half] if axis == 0 else low_in[:, :, :half]
+    high_ref[...] = high_in[half:] if axis == 0 else high_in[:, :, half:]
+
+
+def relayed(near, axis, name):
+    if len(near) != 2:
         return []
-    parts, depth, _ = qkv_near[0].shape
-    shape = jax.ShapeDtypeStruct((parts + 1, depth, depth), qkv_near[0].dtype)
+    dims = list(near[0].shape)
+    dims[axis] //= 2
+    shape = jax.ShapeDtypeStruct(tuple(dims), near[0].dtype)
     low, high = pl.pallas_call(
-        relay_kernel,
+        functools.partial(relay_kernel, axis),
         out_shape=(shape, shape),
-        in_specs=[VMEM] * 4,
+        in_specs=[VMEM] * 2,
         out_specs=(VMEM, VMEM),
         compiler_params=pltpu.CompilerParams(vmem_limit_bytes=8 << 20),
-        name="relay",
-    )(*qkv_near, *out_near)
+        name=name,
+    )(*near)
     return [pair_exchange(low, 2), pair_exchange(high, 1)]
 
 
@@ -375,7 +373,7 @@
             total = jnp.dot(hidden, weight_refs[step][...], preferred_element_type=jnp.float32)
         else:
             half = hidden.shape[1] // 2
-            low, high = (ref[ref.shape[0] - 1] for ref in weight_refs[direct:])
+            low, high = (ref[...] for ref in weight_refs[direct:])
             total = jnp.dot(
                 hidden[:, :half], low, preferred_element_type=jnp.float32
             ) + jnp.dot(hidden[:, half:], high, preferred_element_type=jnp.float32)
@@ -456,16 +454,19 @@
         axis=0,
     )
     bias = masked_bias(row, segment_ids, bucket_table, rel_bias, count)
-    ready = lax.optimization_barrier((*qkv_near, *out_near, kept, given, bias, token_block))
-    *near, kept, given, bias, token_block = ready
+    *qkv_near, kept, given, token_block = lax.optimization_barrier(
+        (*qkv_near, kept, given, token_block)
+    )
     received = other_core(given)
-    qkv_near, out_near = near[: len(near) // 2], near[len(near) // 2 :]
-    far = relayed(qkv_near, out_near)
+    qkv_far = relayed(qkv_near, 2, "relay_qkv")
+    *out_near, received, bias = lax.optimization_barrier((*out_near, received, bias))
+    out_far = relayed(out_near, 0, "relay_out")
     w_in, w_down, *_ = lax.optimization_barrier((w_in, w_down.reshape(2, -1, half), received))
     down_first = first_phase(w_down[0], w_down[1])
     in_first = first_phase(w_in[0], w_in[1])
+    kept, *out_far = lax.optimization_barrier((kept, *out_far))
     own_q, own_kv, send_q, send_kv = project_qkv(
-        place, kept, received, [w_qkv, *qkv_near, *far]
+        place, kept, received, [w_qkv, *qkv_near, *qkv_far]
     )
     other_kv, other_q, *down_first = lax.optimization_barrier(
         (other_core(send_kv), other_core(send_q), *down_first)
@@ -482,7 +483,7 @@
     in_pieces = [w_in, *in_first, *exchanged(second_phase(w_in, in_first))]
     context = attention(queries, low, key_value, high, bias)
     own, *sends = columns(
-        place, context, other_core(context), [w_out, *out_near, *far], "attention_out"
+        place, context, other_core(context), [w_out, *out_near, *out_far], "attention_out"
     )
     stacked = jnp.stack([key_value[:, :width], key_value[:, width:]])
     blocks = stacked.reshape(2, slot_index.shape[1], BLOCK, width)

time: 138 us -> 136 us (0.986)
  local copies, waits for them, and re-layouts: 5.37 us -> 2.53 us
  starting transfers between devices: 42.1 us -> 44.6 us
    ppermute x35 -> x37, starting transfers between devices: 39.5 us -> 42 us  [exchange(): lax.ppermute(value, axis, [(i, partner(i) % count) for i in range(count)])]
    unnamed x34 -> x28, local copies, waits for them, and re-layouts: 3.12 us -> 0.96 us
    ppermute x35 -> x37, waiting for transfers between devices: 71.8 us -> 70.6 us  [exchange(): lax.ppermute(value, axis, [(i, partner(i) % count) for i in range(count)])]
  transfers between devices with their start and end apart: 37 -> 39, of which waited for: 22 -> 23; matrix products, arithmetic and copies ran while one was open for 3% -> 3% of each run, Pallas kernels for 7% -> 8%
where the time goes in v7:
time: 136 us
  waiting for transfers between devices  70.6 us (52%)
  starting transfers between devices  44.6 us (33%)
  Pallas kernels  13.6 us (10%)
  other arithmetic  3.63 us (3%)
  local copies, waits for them, and re-layouts  2.53 us (2%)
    ppermute x37, waiting for transfers between devices, exchange(): lax.ppermute(value, axis, [(i, partner(i) % count) for i in range(count)])  70.6 us
    ppermute x37, starting transfers between devices, exchange(): lax.ppermute(value, axis, [(i, partner(i) % count) for i in range(count)])  42 us
    pallas_call x1, Pallas kernels, project_ffn(): pl.pallas_call(ffn_in_kernel, out_shape=(jax.ShapeDtypeStruct((count, col...  3.34 us
    pallas_call x2, Pallas kernels, columns(): pl.pallas_call(columns_kernel, out_shape=(jax.ShapeDtypeStruct((2 * count...  2.79 us
  transfers between devices with their start and end apart: 39, of which 23 were waited for; matrix products, arithmetic and copies ran while one was open for 3% of the time, Pallas kernels for 8%

profile of v7, /device:TPU:0, one launch (start us, length us, event | category | flops | bytes accessed | tf_op | source)
XLA Modules:
  0.0 136.0 jit_solution(17182942800160196304)
XLA Ops:
  0.6 3.0 %collective-permute-start = (bf16[3,256,512]{2,1,0:T(8,128)(2,1)}, bf16[3,256,512]{2,1,0:T(8,128)(2,1)S(1)}, u32[]{:S(2)}, u32[]{:S(2)}) collective-permute-start(bf16[3,256,512]{2,1,0:T(8,128)(2,1)} %refs_0_.4), channel_id=1, source_target_pairs={{0,8},{4,12},{8,0},{12,4},{16,24},{20,28},{24,16},{28,20},{1,9},{5... | collective-permute-start | bytes 2359304 | tf_op jit(solution)/shard_map/ppermute | solution.py:121
  3.6 1.5 %collective-permute-start.1 = (bf16[3,256,512]{2,1,0:T(8,128)(2,1)}, bf16[3,256,512]{2,1,0:T(8,128)(2,1)S(1)}, u32[]{:S(2)}, u32[]{:S(2)}) collective-permute-start(bf16[3,256,512]{2,1,0:T(8,128)(2,1)} %refs_0_.4), channel_id=1, source_target_pairs={{0,16},{4,20},{8,24},{12,28},{16,0},{20,4},{24,8},{28,12},{1,17},{... | collective-permute-start | bytes 2359304 | tf_op jit(solution)/shard_map/ppermute | solution.py:121
  5.2 0.9 broadcast_select_fusion.1
  6.2 1.6 %collective-permute-start.2 = (bf16[128,512]{1,0:T(8,128)(2,1)}, bf16[128,512]{1,0:T(8,128)(2,1)S(1)}, u32[]{:S(2)}, u32[]{:S(2)}) collective-permute-start(bf16[128,512]{1,0:T(8,128)(2,1)} %refs_0_.3), channel_id=1, source_target_pairs={{0,1},{1,2},{2,3},{3,0},{4,5},{5,6},{6,7},{7,4},{8,9},{9,10},{10,1... | collective-permute-start | bytes 393224 | tf_op jit(solution)/shard_map/ppermute | solution.py:121
  7.8 2.6 %collective-permute-start.3 = (bf16[128,512]{1,0:T(8,128)(2,1)}, bf16[128,512]{1,0:T(8,128)(2,1)S(1)}, u32[]{:S(2)}, u32[]{:S(2)}) collective-permute-start(bf16[128,512]{1,0:T(8,128)(2,1)} %refs_0_.3), channel_id=1, source_target_pairs={{0,2},{1,3},{2,0},{3,1},{4,6},{5,7},{6,4},{7,5},{8,10},{9,11},{10,... | collective-permute-start | bytes 393224 | tf_op jit(solution)/shard_map/ppermute | solution.py:121
  10.4 1.3 collective-permute-start.4
  11.8 0.7 reshape.24.gain_ref
  12.5 2.1 %collective-permute-done.2.refs_1_ = bf16[128,512]{1,0:T(8,128)(2,1)S(1)} collective-permute-done((bf16[128,512]{1,0:T(8,128)(2,1)}, bf16[128,512]{1,0:T(8,128)(2,1)S(1)}, u32[]{:S(2)}, u32[]{:S(2)}) %collective-permute-start.2) | collective-permute-done | bytes 131104 | tf_op jit(solution)/shard_map/ppermute | solution.py:121
  14.6 0.5 collective-permute-start.6
  15.2 4.7 %collective-permute-done.3.refs_2_ = bf16[128,512]{1,0:T(8,128)(2,1)S(1)} collective-permute-done((bf16[128,512]{1,0:T(8,128)(2,1)}, bf16[128,512]{1,0:T(8,128)(2,1)S(1)}, u32[]{:S(2)}, u32[]{:S(2)}) %collective-permute-start.3) | collective-permute-done | bytes 131104 | tf_op jit(solution)/shard_map/ppermute | solution.py:121
  19.8 0.5 collective-permute-start.7
  20.3 0.9 copy-done.7
  21.2 0.8 norm_tokens.1
  22.2 1.0 collective-permute-done.1.high_in.refs_2_
  23.3 2.4 %collective-permute-start.11 = (bf16[3,256,256]{2,1,0:T(8,128)(2,1)S(1)}, bf16[3,256,256]{2,1,0:T(8,128)(2,1)S(1)}, u32[]{:S(2)}, u32[]{:S(2)}) collective-permute-start(bf16[3,256,256]{2,1,0:T(8,128)(2,1)S(1)} %get-tuple-element.71), channel_id=1, source_target_pairs={{0,16},{4,20},{8,24},{12,28},{16,0},{20,4},{24,8},{28,12},{1,17},{... | collective-permute-start | bytes 1179656 | tf_op jit(solution)/shard_map/ppermute | solution.py:121
  25.7 0.5 collective-permute-start.12
  26.3 0.6 masked_bias.1.bias_ref
  27.0 2.2 %collective-permute-done.7.high_in.refs_2_ = bf16[512,256]{1,0:T(8,128)(2,1)S(1)} collective-permute-done((bf16[512,256]{1,0:T(8,128)(2,1)}, bf16[512,256]{1,0:T(8,128)(2,1)S(1)}, u32[]{:S(2)}, u32[]{:S(2)}) %collective-permute-start.7) | collective-permute-done | bytes 262176 | tf_op jit(solution)/shard_map/ppermute | solution.py:121
  29.2 2.0 %collective-permute-start.9 = (bf16[256,256]{1,0:T(8,128)(2,1)S(1)}, bf16[256,256]{1,0:T(8,128)(2,1)S(1)}, u32[]{:S(2)}, u32[]{:S(2)}) collective-permute-start(bf16[256,256]{1,0:T(8,128)(2,1)S(1)} %get-tuple-element.65), channel_id=1, source_target_pairs={{0,16},{4,20},{8,24},{12,28},{16,0},{20,4},{24,8},{28,12},{1,17},{... | collective-permute-start | bytes 393224 | tf_op jit(solution)/shard_map/ppermute | solution.py:121
  31.2 0.5 collective-permute-start.10
  31.8 1.6 %collective-permute-start.15 = (bf16[640,256]{1,0:T(8,128)(2,1)S(1)}, bf16[640,256]{1,0:T(8,128)(2,1)S(1)}, u32[]{:S(2)}, u32[]{:S(2)}) collective-permute-start(bf16[640,256]{1,0:T(8,128)(2,1)S(1)} %get-tuple-element.117), channel_id=1, source_target_pairs={{0,8},{4,12},{8,0},{12,4},{16,24},{20,28},{24,16},{28,20},{1,9},{5... | collective-permute-start | bytes 983048 | tf_op jit(solution)/shard_map/ppermute | solution.py:121
  33.3 6.4 %collective-permute-done.9.refs_3_ = bf16[256,256]{1,0:T(8,128)(2,1)S(1)} collective-permute-done((bf16[256,256]{1,0:T(8,128)(2,1)S(1)}, bf16[256,256]{1,0:T(8,128)(2,1)S(1)}, u32[]{:S(2)}, u32[]{:S(2)}) %collective-permute-start.9) | collective-permute-done | bytes 131104 | tf_op jit(solution)/shard_map/ppermute | solution.py:121
  39.7 1.5 %collective-permute-start.16 = (bf16[640,256]{1,0:T(8,128)(2,1)S(1)}, bf16[640,256]{1,0:T(8,128)(2,1)S(1)}, u32[]{:S(2)}, u32[]{:S(2)}) collective-permute-start(bf16[640,256]{1,0:T(8,128)(2,1)S(1)} %get-tuple-element.116), channel_id=1, source_target_pairs={{0,16},{4,20},{8,24},{12,28},{16,0},{20,4},{24,8},{28,12},{1,17},{... | collective-permute-start | bytes 983048 | tf_op jit(solution)/shard_map/ppermute | solution.py:121
  41.2 1.5 %qkv.1 = (f32[128,512]{1,0:T(8,128)S(1)}, f32[128,1024]{1,0:T(8,128)S(1)}, f32[128,512]{1,0:T(8,128)S(1)}, f32[128,1024]{1,0:T(8,128)S(1)}) custom-call(s32[2]{0:T(128)S(1)} %pad_add_fusion.place_ref, bf16[4,128,256]{2,1,0:T(8,128)(2,1)S(1)} %get-tuple-element.67.own_in_ref, bf16[4,128,256]{2,1,0:T(8,128)(2,1)S(1)} %collective-permute-done.8.other_in_ref, ...), custom_call_target="tpu_custom_call" | custom-call | flops 805306368 | bytes 3145728 | tf_op jit(solution)/shard_map/qkv/pallas_call | solution.py:296
  42.9 0.5 collective-permute-start.14
  43.4 0.6 collective-permute-start.19
  44.0 3.2 %collective-permute-done.15.low_in.refs_1_ = bf16[640,256]{1,0:T(8,128)(2,1)S(1)} collective-permute-done((bf16[640,256]{1,0:T(8,128)(2,1)S(1)}, bf16[640,256]{1,0:T(8,128)(2,1)S(1)}, u32[]{:S(2)}, u32[]{:S(2)}) %collective-permute-start.15) | collective-permute-done | bytes 327712 | tf_op jit(solution)/shard_map/ppermute | solution.py:121
  47.5 1.2 collective-permute-done.16.high_in.refs_2_
  48.8 1.3 collective-permute-start.17
  50.1 1.3 collective-permute-start.18
  51.5 9.8 %collective-permute-done.19.low_in.refs_5_ = bf16[256,1280]{1,0:T(8,128)(2,1)S(1)} collective-permute-done((bf16[256,1280]{1,0:T(8,128)(2,1)S(1)}, bf16[256,1280]{1,0:T(8,128)(2,1)S(1)}, u32[]{:S(2)}, u32[]{:S(2)}) %collective-permute-start.19) | collective-permute-done | bytes 655392 | tf_op jit(solution)/shard_map/ppermute | solution.py:121
  61.3 2.0 %collective-permute-done.20.high_in.refs_6_ = bf16[256,1280]{1,0:T(8,128)(2,1)S(1)} collective-permute-done((bf16[256,1280]{1,0:T(8,128)(2,1)S(1)}, bf16[256,1280]{1,0:T(8,128)(2,1)S(1)}, u32[]{:S(2)}, u32[]{:S(2)}) %collective-permute-start.20) | collective-permute-done | bytes 655392 | tf_op jit(solution)/shard_map/ppermute | solution.py:121
  63.4 1.7 %packet.3 = (bf16[2,256,1280]{2,1,0:T(8,128)(2,1)}, bf16[2,256,1280]{2,1,0:T(8,128)(2,1)}) custom-call(bf16[2,256,1280]{2,1,0:T(8,128)(2,1)S(1)} %copy-done, bf16[256,1280]{1,0:T(8,128)(2,1)S(1)} %collective-permute-done.19.low_in.refs_5_, bf16[256,1280]{1,0:T(8,128)(2,1)S(1)} %collective-permute-done.20.high_in.refs_6_), custom_call_target="tpu_custom_call" | custom-call | tf_op jit(solution)/shard_map/packet/pallas_call | solution.py:173
  65.0 2.6 %collective-permute-start.28 = (bf16[2,256,1280]{2,1,0:T(8,128)(2,1)}, bf16[2,256,1280]{2,1,0:T(8,128)(2,1)}, u32[]{:S(2)}, u32[]{:S(2)}) collective-permute-start(bf16[2,256,1280]{2,1,0:T(8,128)(2,1)} %get-tuple-element.98), channel_id=1, source_target_pairs={{0,8},{4,12},{8,0},{12,4},{16,24},{20,28},{24,16},{28,20},{1,9},{5... | collective-permute-start | bytes 3932168 | tf_op jit(solution)/shard_map/ppermute | solution.py:121
  67.6 1.4 %collective-permute-start.29 = (bf16[2,256,1280]{2,1,0:T(8,128)(2,1)}, bf16[2,256,1280]{2,1,0:T(8,128)(2,1)}, u32[]{:S(2)}, u32[]{:S(2)}) collective-permute-start(bf16[2,256,1280]{2,1,0:T(8,128)(2,1)} %get-tuple-element.99), channel_id=1, source_target_pairs={{0,16},{4,20},{8,24},{12,28},{16,0},{20,4},{24,8},{28,12},{1,17},{... | collective-permute-start | bytes 3932168 | tf_op jit(solution)/shard_map/ppermute | solution.py:121
  69.1 2.7 %attention.1.own_in_ref = bf16[128,512]{1,0:T(8,128)(2,1)S(1)} custom-call(bf16[128,512]{1,0:T(8,128)(2,1)S(1)} %add_convert_fusion.2.q_ref, bf16[128,1024]{1,0:T(8,128)(2,1)S(1)} %collective-permute-done.17.low_ref, bf16[128,1024]{1,0:T(8,128)(2,1)S(1)} %add_convert_fusion.own_ref, bf16[128,1024]{1,0:T(8,128)(2,1)S(1)} %collective-permute-done.18.high_ref, ...), custom_call_target="tpu_custom_call" | custom-call | flops 100663296 | bytes 1572864 | tf_op jit(solution)/shard_map/attention/pallas_call | solution.py:106
  71.8 1.3 collective-permute-done.21.other_in_ref
  73.2 1.1 attention_out.1
  74.3 3.5 %collective-permute-start.24 = (bf16[256,256]{1,0:T(8,128)(2,1)S(1)}, bf16[256,256]{1,0:T(8,128)(2,1)S(1)}, u32[]{:S(2)}, u32[]{:S(2)}) collective-permute-start(bf16[256,256]{1,0:T(8,128)(2,1)S(1)} %get-tuple-element.94), channel_id=1, source_target_pairs={{0,3},{1,0},{2,1},{3,2},{4,7},{5,4},{6,5},{7,6},{8,11},{9,8},{10,9... | collective-permute-start | bytes 393224 | tf_op jit(solution)/shard_map/ppermute | solution.py:121
  77.8 1.6 %collective-permute-start.22 = (bf16[256,256]{1,0:T(8,128)(2,1)S(1)}, bf16[256,256]{1,0:T(8,128)(2,1)S(1)}, u32[]{:S(2)}, u32[]{:S(2)}) collective-permute-start(bf16[256,256]{1,0:T(8,128)(2,1)S(1)} %get-tuple-element.92), channel_id=1, source_target_pairs={{0,1},{1,2},{2,3},{3,0},{4,5},{5,6},{6,7},{7,4},{8,9},{9,10},{10,1... | collective-permute-start | bytes 393224 | tf_op jit(solution)/shard_map/ppermute | solution.py:121
  79.4 0.7 pad_maximum_fusion
  80.1 1.6 %collective-permute-done.24 = bf16[256,256]{1,0:T(8,128)(2,1)S(1)} collective-permute-done((bf16[256,256]{1,0:T(8,128)(2,1)S(1)}, bf16[256,256]{1,0:T(8,128)(2,1)S(1)}, u32[]{:S(2)}, u32[]{:S(2)}) %collective-permute-start.24) | collective-permute-done | bytes 131104 | tf_op jit(solution)/shard_map/ppermute | solution.py:121
  81.8 7.9 %collective-permute-done.23 = bf16[256,256]{1,0:T(8,128)(2,1)S(1)} collective-permute-done((bf16[256,256]{1,0:T(8,128)(2,1)S(1)}, bf16[256,256]{1,0:T(8,128)(2,1)S(1)}, u32[]{:S(2)}, u32[]{:S(2)}) %collective-permute-start.23) | collective-permute-done | bytes 131104 | tf_op jit(solution)/shard_map/ppermute | solution.py:121
  89.7 1.3 collective-permute-start.27
  91.1 0.7 reshape.23.gain_ref
  91.8 0.7 collective-permute-start.25
  92.5 2.9 %collective-permute-start.26 = (bf16[256,256]{1,0:T(8,128)(2,1)S(1)}, bf16[256,256]{1,0:T(8,128)(2,1)S(1)}, u32[]{:S(2)}, u32[]{:S(2)}) collective-permute-start(bf16[256,256]{1,0:T(8,128)(2,1)S(1)} %add_convert_fusion.1.refs_0_), channel_id=1, source_target_pairs={{0,2},{1,3},{2,0},{3,1},{4,6},{5,7},{6,4},{7,5},{8,10},{9,11},{10,... | collective-permute-start | bytes 393224 | tf_op jit(solution)/shard_map/ppermute | solution.py:121
  95.6 1.7 %collective-permute-start.32 = (bf16[2,640,256]{2,1,0:T(8,128)(2,1)}, bf16[2,640,256]{2,1,0:T(8,128)(2,1)S(1)}, u32[]{:S(2)}, u32[]{:S(2)}) collective-permute-start(bf16[2,640,256]{2,1,0:T(8,128)(2,1)} %copy-done.12), channel_id=1, source_target_pairs={{0,8},{4,12},{8,0},{12,4},{16,24},{20,28},{24,16},{28,20},{1,9},{5... | collective-permute-start | bytes 1966088 | tf_op jit(solution)/shard_map/ppermute | solution.py:121
  97.4 4.0 %collective-permute-done.25.refs_1_ = bf16[256,256]{1,0:T(8,128)(2,1)S(1)} collective-permute-done((bf16[256,256]{1,0:T(8,128)(2,1)S(1)}, bf16[256,256]{1,0:T(8,128)(2,1)S(1)}, u32[]{:S(2)}, u32[]{:S(2)}) %collective-permute-start.25) | collective-permute-done | bytes 131104 | tf_op jit(solution)/shard_map/ppermute | solution.py:121
  101.4 0.7 collective-permute-start.33
  102.1 2.6 %collective-permute-done.26.refs_2_ = bf16[256,256]{1,0:T(8,128)(2,1)S(1)} collective-permute-done((bf16[256,256]{1,0:T(8,128)(2,1)S(1)}, bf16[256,256]{1,0:T(8,128)(2,1)S(1)}, u32[]{:S(2)}, u32[]{:S(2)}) %collective-permute-start.26) | collective-permute-done | bytes 131104 | tf_op jit(solution)/shard_map/ppermute | solution.py:121
  104.8 3.3 %ffn_in.1 = (f32[128,2560]{1,0:T(8,128)S(1)}, bf16[128,2560]{1,0:T(8,128)(2,1)S(1)}) custom-call(s32[2]{0:T(128)S(1)} %pad_add_fusion.place_ref, f32[8,256]{1,0:T(8,128)S(1)} %reshape.23.gain_ref, bf16[256,256]{1,0:T(8,128)(2,1)S(1)} %add_convert_fusion.1.refs_0_, bf16[256,256]{1,0:T(8,128)(2,1)S(1)} %collective-permute-done.25.refs_1_, ...), custom_call_target="tpu_custom_call" | custom-call | flops 1342177280 | bytes 5242880 | tf_op jit(solution)/shard_map/ffn_in/pallas_call | solution.py:332
  108.5 0.6 collective-permute-start.31
  109.0 1.3 collective-permute-done.31
  110.3 1.3 collective-permute-done.32.refs_3_
  111.6 4.7 %collective-permute-done.33.refs_4_ = bf16[2,640,256]{2,1,0:T(8,128)(2,1)S(1)} collective-permute-done((bf16[2,640,256]{2,1,0:T(8,128)(2,1)}, bf16[2,640,256]{2,1,0:T(8,128)(2,1)S(1)}, u32[]{:S(2)}, u32[]{:S(2)}) %collective-permute-start.33) | collective-permute-done | bytes 655392 | tf_op jit(solution)/shard_map/ppermute | solution.py:121
  116.8 1.6 %collective-permute-done.34.other_in_ref = bf16[128,1280]{1,0:T(8,128)(2,1)S(1)} collective-permute-done((bf16[128,1280]{1,0:T(8,128)(2,1)S(1)}, bf16[128,1280]{1,0:T(8,128)(2,1)S(1)}, u32[]{:S(2)}, u32[]{:S(2)}) %collective-permute-start.34) | collective-permute-done | bytes 327712 | tf_op jit(solution)/shard_map/ppermute | solution.py:121
  118.5 1.7 %ffn_out.1 = (f32[256,256]{1,0:T(8,128)S(1)}, bf16[256,256]{1,0:T(8,128)(2,1)S(1)}, bf16[256,256]{1,0:T(8,128)(2,1)S(1)}, bf16[256,256]{1,0:T(8,128)(2,1)S(1)}) custom-call(s32[2]{0:T(128)S(1)} %pad_add_fusion.place_ref, bf16[128,1280]{1,0:T(8,128)(2,1)S(1)} %fusion.8.own_in_ref, bf16[128,1280]{1,0:T(8,128)(2,1)S(1)} %collective-permute-done.34.other_in_ref, ...), custom_call_target="tpu_custom_call" | custom-call | flops 671088640 | bytes 2621440 | tf_op jit(solution)/shard_map/ffn_out/pallas_call | solution.py:390
  120.1 1.2 collective-permute-start.37
  121.7 1.9 %collective-permute-start.35 = (bf16[256,256]{1,0:T(8,128)(2,1)S(1)}, bf16[256,256]{1,0:T(8,128)(2,1)S(1)}, u32[]{:S(2)}, u32[]{:S(2)}) collective-permute-start(bf16[256,256]{1,0:T(8,128)(2,1)S(1)} %get-tuple-element.110), channel_id=1, source_target_pairs={{0,1},{1,2},{2,3},{3,0},{4,5},{5,6},{6,7},{7,4},{8,9},{9,10},{10,1... | collective-permute-start | bytes 393224 | tf_op jit(solution)/shard_map/ppermute | solution.py:121
  123.6 2.8 %collective-permute-done.37 = bf16[256,256]{1,0:T(8,128)(2,1)S(1)} collective-permute-done((bf16[256,256]{1,0:T(8,128)(2,1)S(1)}, bf16[256,256]{1,0:T(8,128)(2,1)S(1)}, u32[]{:S(2)}, u32[]{:S(2)}) %collective-permute-start.37) | collective-permute-done | bytes 131104 | tf_op jit(solution)/shard_map/ppermute | solution.py:121
  126.4 7.4 %collective-permute-done.36 = bf16[256,256]{1,0:T(8,128)(2,1)S(1)} collective-permute-done((bf16[256,256]{1,0:T(8,128)(2,1)S(1)}, bf16[256,256]{1,0:T(8,128)(2,1)S(1)}, u32[]{:S(2)}, u32[]{:S(2)}) %collective-permute-start.36) | collective-permute-done | bytes 131104 | tf_op jit(solution)/shard_map/ppermute | solution.py:121
  134.0 1.2 collective-permute-done.38
  135.3 0.7 maximum_select_fusion
  (78 shorter events, 2.9 us)
Async XLA Ops:
  0.6 21.6 %collective-permute-start = (bf16[3,256,512]{2,1,0:T(8,128)(2,1)}, bf16[3,256,512]{2,1,0:T(8,128)(2,1)S(1)}, u32[]{:S(2)}, u32[]{:S(2)}) collective-permute-start(bf16[3,256,512]{2,1,0:T(8,128)(2,1)} %refs_0_.4), channel_id=1, source_target_pairs={{0,8},{4,12},{8,0},{12,4},{16,24},{20,28},{24,16},{28,20},{1,9},{5... | collective-permute-start | bytes 2359304 | tf_op jit(solution)/shard_map/ppermute | solution.py:121
  3.6 19.6 %collective-permute-start.1 = (bf16[3,256,512]{2,1,0:T(8,128)(2,1)}, bf16[3,256,512]{2,1,0:T(8,128)(2,1)S(1)}, u32[]{:S(2)}, u32[]{:S(2)}) collective-permute-start(bf16[3,256,512]{2,1,0:T(8,128)(2,1)} %refs_0_.4), channel_id=1, source_target_pairs={{0,16},{4,20},{8,24},{12,28},{16,0},{20,4},{24,8},{28,12},{1,17},{... | collective-permute-start | bytes 2359304 | tf_op jit(solution)/shard_map/ppermute | solution.py:121
  5.2 21.1 %copy-start.13 = (s32[255]{0:T(256)S(1)}, s32[255]{0:T(256)}, u32[]{:S(2)}) copy-start(s32[255]{0:T(256)} %param.13) | copy-start | bytes 3064
  5.2 21.1 %copy-start.9 = (s32[1024]{0:T(1024)S(1)}, s32[1024]{0:T(1024)}, u32[]{:S(2)}) copy-start(s32[1024]{0:T(1024)} %param.12) | copy-start | bytes 12292
  5.2 21.1 %copy-start.10 = (f32[32,8]{0,1:T(8,128)S(1)}, f32[32,8]{0,1:T(8,128)}, u32[]{:S(2)}) copy-start(f32[32,8]{0,1:T(8,128)} %param.16) | copy-start | bytes 3076
  6.1 4.3 %collective-permute-start.5 = (bf16[128,256]{1,0:T(8,128)(2,1)S(1)}, bf16[128,256]{1,0:T(8,128)(2,1)S(1)}, u32[]{:S(2)}, u32[]{:S(2)}) collective-permute-start(bf16[128,256]{1,0:T(8,128)(2,1)S(1)} %get-tuple-element.123), channel_id=1, source_target_pairs={{0,4},{4,0},{8,12},{12,8},{16,20},{20,16},{24,28},{28,24},{1,5},{5... | collective-permute-start | bytes 196616 | tf_op jit(solution)/shard_map/ppermute | solution.py:121
  6.2 8.5 %collective-permute-start.2 = (bf16[128,512]{1,0:T(8,128)(2,1)}, bf16[128,512]{1,0:T(8,128)(2,1)S(1)}, u32[]{:S(2)}, u32[]{:S(2)}) collective-permute-start(bf16[128,512]{1,0:T(8,128)(2,1)} %refs_0_.3), channel_id=1, source_target_pairs={{0,1},{1,2},{2,3},{3,0},{4,5},{5,6},{6,7},{7,4},{8,9},{9,10},{10,1... | collective-permute-start | bytes 393224 | tf_op jit(solution)/shard_map/ppermute | solution.py:121
  7.8 12.0 %collective-permute-start.3 = (bf16[128,512]{1,0:T(8,128)(2,1)}, bf16[128,512]{1,0:T(8,128)(2,1)S(1)}, u32[]{:S(2)}, u32[]{:S(2)}) collective-permute-start(bf16[128,512]{1,0:T(8,128)(2,1)} %refs_0_.3), channel_id=1, source_target_pairs={{0,2},{1,3},{2,0},{3,1},{4,6},{5,7},{6,4},{7,5},{8,10},{9,11},{10,... | collective-permute-start | bytes 393224 | tf_op jit(solution)/shard_map/ppermute | solution.py:121
  10.4 9.9 %collective-permute-start.4 = (bf16[128,512]{1,0:T(8,128)(2,1)}, bf16[128,512]{1,0:T(8,128)(2,1)S(1)}, u32[]{:S(2)}, u32[]{:S(2)}) collective-permute-start(bf16[128,512]{1,0:T(8,128)(2,1)} %refs_0_.3), channel_id=1, source_target_pairs={{0,3},{1,0},{2,1},{3,2},{4,7},{5,4},{6,5},{7,6},{8,11},{9,8},{10,9... | collective-permute-start | bytes 393224 | tf_op jit(solution)/shard_map/ppermute | solution.py:121
  14.6 12.4 %collective-permute-start.6 = (bf16[512,256]{1,0:T(8,128)(2,1)}, bf16[512,256]{1,0:T(8,128)(2,1)S(1)}, u32[]{:S(2)}, u32[]{:S(2)}) collective-permute-start(bf16[512,256]{1,0:T(8,128)(2,1)} %refs_0_.5), channel_id=1, source_target_pairs={{0,8},{4,12},{8,0},{12,4},{16,24},{20,28},{24,16},{28,20},{1,9},{5... | collective-permute-start | bytes 786440 | tf_op jit(solution)/shard_map/ppermute | solution.py:121
  19.8 9.4 %collective-permute-start.7 = (bf16[512,256]{1,0:T(8,128)(2,1)}, bf16[512,256]{1,0:T(8,128)(2,1)S(1)}, u32[]{:S(2)}, u32[]{:S(2)}) collective-permute-start(bf16[512,256]{1,0:T(8,128)(2,1)} %refs_0_.5), channel_id=1, source_target_pairs={{0,16},{4,20},{8,24},{12,28},{16,0},{20,4},{24,8},{28,12},{1,17},{... | collective-permute-start | bytes 786440 | tf_op jit(solution)/shard_map/ppermute | solution.py:121
  20.3 0.9 copy-start.7
  23.2 6.0 %collective-permute-start.8 = (bf16[4,128,256]{2,1,0:T(8,128)(2,1)S(1)}, bf16[4,128,256]{2,1,0:T(8,128)(2,1)S(1)}, u32[]{:S(2)}, u32[]{:S(2)}) collective-permute-start(bf16[4,128,256]{2,1,0:T(8,128)(2,1)S(1)} %get-tuple-element.62), channel_id=1, source_target_pairs={{0,4},{4,0},{8,12},{12,8},{16,20},{20,16},{24,28},{28,24},{1,5},{5... | collective-permute-start | bytes 786440 | tf_op jit(solution)/shard_map/ppermute | solution.py:121
  23.2 8.5 %copy-start.1 = (bf16[1280,256]{1,0:T(8,128)(2,1)S(1)}, bf16[1280,256]{1,0:T(8,128)(2,1)}, u32[]{:S(2)}) copy-start(bf16[1280,256]{1,0:T(8,128)(2,1)} %param.20) | copy-start | bytes 1966084
  23.3 18.0 %collective-permute-start.11 = (bf16[3,256,256]{2,1,0:T(8,128)(2,1)S(1)}, bf16[3,256,256]{2,1,0:T(8,128)(2,1)S(1)}, u32[]{:S(2)}, u32[]{:S(2)}) collective-permute-start(bf16[3,256,256]{2,1,0:T(8,128)(2,1)S(1)} %get-tuple-element.71), channel_id=1, source_target_pairs={{0,16},{4,20},{8,24},{12,28},{16,0},{20,4},{24,8},{28,12},{1,17},{... | collective-permute-start | bytes 1179656 | tf_op jit(solution)/shard_map/ppermute | solution.py:121
  25.7 15.5 %collective-permute-start.12 = (bf16[3,256,256]{2,1,0:T(8,128)(2,1)S(1)}, bf16[3,256,256]{2,1,0:T(8,128)(2,1)S(1)}, u32[]{:S(2)}, u32[]{:S(2)}) collective-permute-start(bf16[3,256,256]{2,1,0:T(8,128)(2,1)S(1)} %get-tuple-element.72), channel_id=1, source_target_pairs={{0,8},{4,12},{8,0},{12,4},{16,24},{20,28},{24,16},{28,20},{1,9},{5... | collective-permute-start | bytes 1179656 | tf_op jit(solution)/shard_map/ppermute | solution.py:121
  26.9 14.3 %copy-start.6 = (bf16[3,256,512]{2,1,0:T(8,128)(2,1)S(1)}, bf16[3,256,512]{2,1,0:T(8,128)(2,1)}, u32[]{:S(2)}) copy-start(bf16[3,256,512]{2,1,0:T(8,128)(2,1)} %refs_0_.4) | copy-start | bytes 2359300
  29.2 10.5 %collective-permute-start.9 = (bf16[256,256]{1,0:T(8,128)(2,1)S(1)}, bf16[256,256]{1,0:T(8,128)(2,1)S(1)}, u32[]{:S(2)}, u32[]{:S(2)}) collective-permute-start(bf16[256,256]{1,0:T(8,128)(2,1)S(1)} %get-tuple-element.65), channel_id=1, source_target_pairs={{0,16},{4,20},{8,24},{12,28},{16,0},{20,4},{24,8},{28,12},{1,17},{... | collective-permute-start | bytes 393224 | tf_op jit(solution)/shard_map/ppermute | solution.py:121
  31.2 10.0 %collective-permute-start.10 = (bf16[256,256]{1,0:T(8,128)(2,1)S(1)}, bf16[256,256]{1,0:T(8,128)(2,1)S(1)}, u32[]{:S(2)}, u32[]{:S(2)}) collective-permute-start(bf16[256,256]{1,0:T(8,128)(2,1)S(1)} %get-tuple-element.66), channel_id=1, source_target_pairs={{0,8},{4,12},{8,0},{12,4},{16,24},{20,28},{24,16},{28,20},{1,9},{5... | collective-permute-start | bytes 393224 | tf_op jit(solution)/shard_map/ppermute | solution.py:121
  31.8 15.5 %collective-permute-start.15 = (bf16[640,256]{1,0:T(8,128)(2,1)S(1)}, bf16[640,256]{1,0:T(8,128)(2,1)S(1)}, u32[]{:S(2)}, u32[]{:S(2)}) collective-permute-start(bf16[640,256]{1,0:T(8,128)(2,1)S(1)} %get-tuple-element.117), channel_id=1, source_target_pairs={{0,8},{4,12},{8,0},{12,4},{16,24},{20,28},{24,16},{28,20},{1,9},{5... | collective-permute-start | bytes 983048 | tf_op jit(solution)/shard_map/ppermute | solution.py:121
  39.7 3.7 %copy-start = (bf16[2,256,1280]{2,1,0:T(8,128)(2,1)S(1)}, bf16[2,256,1280]{2,1,0:T(8,128)(2,1)}, u32[]{:S(2)}) copy-start(bf16[2,256,1280]{2,1,0:T(8,128)(2,1)} %refs_4_) | copy-start | bytes 3932164
  39.7 9.0 %collective-permute-start.16 = (bf16[640,256]{1,0:T(8,128)(2,1)S(1)}, bf16[640,256]{1,0:T(8,128)(2,1)S(1)}, u32[]{:S(2)}, u32[]{:S(2)}) collective-permute-start(bf16[640,256]{1,0:T(8,128)(2,1)S(1)} %get-tuple-element.116), channel_id=1, source_target_pairs={{0,16},{4,20},{8,24},{12,28},{16,0},{20,4},{24,8},{28,12},{1,17},{... | collective-permute-start | bytes 983048 | tf_op jit(solution)/shard_map/ppermute | solution.py:121
  42.8 5.9 %collective-permute-start.13 = (f32[128,1024]{1,0:T(8,128)S(1)}, f32[128,1024]{1,0:T(8,128)S(1)}, u32[]{:S(2)}, u32[]{:S(2)}) collective-permute-start(f32[128,1024]{1,0:T(8,128)S(1)} %get-tuple-element.74), channel_id=1, source_target_pairs={{0,4},{4,0},{8,12},{12,8},{16,20},{20,16},{24,28},{28,24},{1,5},{5... | collective-permute-start | bytes 1572872 | tf_op jit(solution)/shard_map/ppermute | solution.py:121
  42.9 5.8 %collective-permute-start.14 = (f32[128,512]{1,0:T(8,128)S(1)}, f32[128,512]{1,0:T(8,128)S(1)}, u32[]{:S(2)}, u32[]{:S(2)}) collective-permute-start(f32[128,512]{1,0:T(8,128)S(1)} %get-tuple-element.75), channel_id=1, source_target_pairs={{0,4},{4,0},{8,12},{12,8},{16,20},{20,16},{24,28},{28,24},{1,5},{5... | collective-permute-start | bytes 786440 | tf_op jit(solution)/shard_map/ppermute | solution.py:121
  43.4 17.9 %collective-permute-start.19 = (bf16[256,1280]{1,0:T(8,128)(2,1)S(1)}, bf16[256,1280]{1,0:T(8,128)(2,1)S(1)}, u32[]{:S(2)}, u32[]{:S(2)}) collective-permute-start(bf16[256,1280]{1,0:T(8,128)(2,1)S(1)} %get-tuple-element.115), channel_id=1, source_target_pairs={{0,8},{4,12},{8,0},{12,4},{16,24},{20,28},{24,16},{28,20},{1,9},{5... | collective-permute-start | bytes 1966088 | tf_op jit(solution)/shard_map/ppermute | solution.py:121
  47.3 4.2 %copy-start.2 = (bf16[640,256]{1,0:T(8,128)(2,1)}, bf16[640,256]{1,0:T(8,128)(2,1)S(1)}, u32[]{:S(2)}) copy-start(bf16[640,256]{1,0:T(8,128)(2,1)S(1)} %collective-permute-done.15.low_in.refs_1_) | copy-start | bytes 983044
  47.3 16.1 %collective-permute-start.20 = (bf16[256,1280]{1,0:T(8,128)(2,1)S(1)}, bf16[256,1280]{1,0:T(8,128)(2,1)S(1)}, u32[]{:S(2)}, u32[]{:S(2)}) collective-permute-start(bf16[256,1280]{1,0:T(8,128)(2,1)S(1)} %get-tuple-element.114), channel_id=1, source_target_pairs={{0,16},{4,20},{8,24},{12,28},{16,0},{20,4},{24,8},{28,12},{1,17},{... | collective-permute-start | bytes 1966088 | tf_op jit(solution)/shard_map/ppermute | solution.py:121
  48.7 2.8 %copy-start.4 = (bf16[640,256]{1,0:T(8,128)(2,1)}, bf16[640,256]{1,0:T(8,128)(2,1)S(1)}, u32[]{:S(2)}) copy-start(bf16[640,256]{1,0:T(8,128)(2,1)S(1)} %collective-permute-done.16.high_in.refs_2_) | copy-start | bytes 983044
  48.8 14.6 %collective-permute-start.17 = (bf16[128,1024]{1,0:T(8,128)(2,1)S(1)}, bf16[128,1024]{1,0:T(8,128)(2,1)S(1)}, u32[]{:S(2)}, u32[]{:S(2)}) collective-permute-start(bf16[128,1024]{1,0:T(8,128)(2,1)S(1)} %add_convert_fusion.own_ref), channel_id=1, source_target_pairs={{0,4},{4,8},{8,12},{12,16},{16,20},{20,24},{24,28},{1,5},{5,9},{9,... | collective-permute-start | bytes 786440 | tf_op jit(solution)/shard_map/ppermute | solution.py:479
  50.1 13.3 %collective-permute-start.18 = (bf16[128,1024]{1,0:T(8,128)(2,1)S(1)}, bf16[128,1024]{1,0:T(8,128)(2,1)S(1)}, u32[]{:S(2)}, u32[]{:S(2)}) collective-permute-start(bf16[128,1024]{1,0:T(8,128)(2,1)S(1)} %add_convert_fusion.own_ref), channel_id=1, source_target_pairs={{4,0},{8,4},{12,8},{16,12},{20,16},{24,20},{28,24},{5,1},{9,5},{13... | collective-permute-start | bytes 786440 | tf_op jit(solution)/shard_map/ppermute | solution.py:480
  51.5 17.6 %copy-start.11 = (bf16[2,640,256]{2,1,0:T(8,128)(2,1)}, bf16[2,640,256]{2,1,0:T(8,128)(2,1)S(1)}, u32[]{:S(2)}) copy-start(bf16[2,640,256]{2,1,0:T(8,128)(2,1)S(1)} %get-tuple-element.105) | copy-start | bytes 1966084
  51.5 28.6 %copy-start.12 = (bf16[2,640,256]{2,1,0:T(8,128)(2,1)}, bf16[2,640,256]{2,1,0:T(8,128)(2,1)S(1)}, u32[]{:S(2)}) copy-start(bf16[2,640,256]{2,1,0:T(8,128)(2,1)S(1)} %get-tuple-element.104) | copy-start | bytes 1966084
  65.0 39.7 %collective-permute-start.28 = (bf16[2,256,1280]{2,1,0:T(8,128)(2,1)}, bf16[2,256,1280]{2,1,0:T(8,128)(2,1)}, u32[]{:S(2)}, u32[]{:S(2)}) collective-permute-start(bf16[2,256,1280]{2,1,0:T(8,128)(2,1)} %get-tuple-element.98), channel_id=1, source_target_pairs={{0,8},{4,12},{8,0},{12,4},{16,24},{20,28},{24,16},{28,20},{1,9},{5... | collective-permute-start | bytes 3932168 | tf_op jit(solution)/shard_map/ppermute | solution.py:121
  67.6 37.1 %collective-permute-start.29 = (bf16[2,256,1280]{2,1,0:T(8,128)(2,1)}, bf16[2,256,1280]{2,1,0:T(8,128)(2,1)}, u32[]{:S(2)}, u32[]{:S(2)}) collective-permute-start(bf16[2,256,1280]{2,1,0:T(8,128)(2,1)} %get-tuple-element.99), channel_id=1, source_target_pairs={{0,16},{4,20},{8,24},{12,28},{16,0},{20,4},{24,8},{28,12},{1,17},{... | collective-permute-start | bytes 3932168 | tf_op jit(solution)/shard_map/ppermute | solution.py:121
  69.1 4.1 %copy-start.8 = (bf16[512,256]{1,0:T(8,128)(2,1)S(1)}, bf16[512,256]{1,0:T(8,128)(2,1)}, u32[]{:S(2)}) copy-start(bf16[512,256]{1,0:T(8,128)(2,1)} %refs_0_.5) | copy-start | bytes 786436
  71.8 1.4 %collective-permute-start.21 = (bf16[128,512]{1,0:T(8,128)(2,1)S(1)}, bf16[128,512]{1,0:T(8,128)(2,1)S(1)}, u32[]{:S(2)}, u32[]{:S(2)}) collective-permute-start(bf16[128,512]{1,0:T(8,128)(2,1)S(1)} %attention.1.own_in_ref), channel_id=1, source_target_pairs={{0,4},{4,0},{8,12},{12,8},{16,20},{20,16},{24,28},{28,24},{1,5},{5... | collective-permute-start | bytes 393224 | tf_op jit(solution)/shard_map/ppermute | solution.py:121
  74.3 7.4 %collective-permute-start.24 = (bf16[256,256]{1,0:T(8,128)(2,1)S(1)}, bf16[256,256]{1,0:T(8,128)(2,1)S(1)}, u32[]{:S(2)}, u32[]{:S(2)}) collective-permute-start(bf16[256,256]{1,0:T(8,128)(2,1)S(1)} %get-tuple-element.94), channel_id=1, source_target_pairs={{0,3},{1,0},{2,1},{3,2},{4,7},{5,4},{6,5},{7,6},{8,11},{9,8},{10,9... | collective-permute-start | bytes 393224 | tf_op jit(solution)/shard_map/ppermute | solution.py:121
  77.8 11.8 %collective-permute-start.23 = (bf16[256,256]{1,0:T(8,128)(2,1)S(1)}, bf16[256,256]{1,0:T(8,128)(2,1)S(1)}, u32[]{:S(2)}, u32[]{:S(2)}) collective-permute-start(bf16[256,256]{1,0:T(8,128)(2,1)S(1)} %get-tuple-element.93), channel_id=1, source_target_pairs={{0,2},{1,3},{2,0},{3,1},{4,6},{5,7},{6,4},{7,5},{8,10},{9,11},{10,... | collective-permute-start | bytes 393224 | tf_op jit(solution)/shard_map/ppermute | solution.py:121
  77.8 11.8 %collective-permute-start.22 = (bf16[256,256]{1,0:T(8,128)(2,1)S(1)}, bf16[256,256]{1,0:T(8,128)(2,1)S(1)}, u32[]{:S(2)}, u32[]{:S(2)}) collective-permute-start(bf16[256,256]{1,0:T(8,128)(2,1)S(1)} %get-tuple-element.92), channel_id=1, source_target_pairs={{0,1},{1,2},{2,3},{3,0},{4,5},{5,6},{6,7},{7,4},{8,9},{9,10},{10,1... | collective-permute-start | bytes 393224 | tf_op jit(solution)/shard_map/ppermute | solution.py:121
  89.7 5.8 %collective-permute-start.27 = (bf16[256,256]{1,0:T(8,128)(2,1)S(1)}, bf16[256,256]{1,0:T(8,128)(2,1)S(1)}, u32[]{:S(2)}, u32[]{:S(2)}) collective-permute-start(bf16[256,256]{1,0:T(8,128)(2,1)S(1)} %add_convert_fusion.1.refs_0_), channel_id=1, source_target_pairs={{0,3},{1,0},{2,1},{3,2},{4,7},{5,4},{6,5},{7,6},{8,11},{9,8},{10,9... | collective-permute-start | bytes 393224 | tf_op jit(solution)/shard_map/ppermute | solution.py:121
  91.8 9.7 %collective-permute-start.25 = (bf16[256,256]{1,0:T(8,128)(2,1)S(1)}, bf16[256,256]{1,0:T(8,128)(2,1)S(1)}, u32[]{:S(2)}, u32[]{:S(2)}) collective-permute-start(bf16[256,256]{1,0:T(8,128)(2,1)S(1)} %add_convert_fusion.1.refs_0_), channel_id=1, source_target_pairs={{0,1},{1,2},{2,3},{3,0},{4,5},{5,6},{6,7},{7,4},{8,9},{9,10},{10,1... | collective-permute-start | bytes 393224 | tf_op jit(solution)/shard_map/ppermute | solution.py:121
  92.5 12.3 %collective-permute-start.26 = (bf16[256,256]{1,0:T(8,128)(2,1)S(1)}, bf16[256,256]{1,0:T(8,128)(2,1)S(1)}, u32[]{:S(2)}, u32[]{:S(2)}) collective-permute-start(bf16[256,256]{1,0:T(8,128)(2,1)S(1)} %add_convert_fusion.1.refs_0_), channel_id=1, source_target_pairs={{0,2},{1,3},{2,0},{3,1},{4,6},{5,7},{6,4},{7,5},{8,10},{9,11},{10,... | collective-permute-start | bytes 393224 | tf_op jit(solution)/shard_map/ppermute | solution.py:121
  95.6 16.0 %collective-permute-start.32 = (bf16[2,640,256]{2,1,0:T(8,128)(2,1)}, bf16[2,640,256]{2,1,0:T(8,128)(2,1)S(1)}, u32[]{:S(2)}, u32[]{:S(2)}) collective-permute-start(bf16[2,640,256]{2,1,0:T(8,128)(2,1)} %copy-done.12), channel_id=1, source_target_pairs={{0,8},{4,12},{8,0},{12,4},{16,24},{20,28},{24,16},{28,20},{1,9},{5... | collective-permute-start | bytes 1966088 | tf_op jit(solution)/shard_map/ppermute | solution.py:121
  101.4 14.8 %collective-permute-start.33 = (bf16[2,640,256]{2,1,0:T(8,128)(2,1)}, bf16[2,640,256]{2,1,0:T(8,128)(2,1)S(1)}, u32[]{:S(2)}, u32[]{:S(2)}) collective-permute-start(bf16[2,640,256]{2,1,0:T(8,128)(2,1)} %copy-done.11), channel_id=1, source_target_pairs={{0,16},{4,20},{8,24},{12,28},{16,0},{20,4},{24,8},{28,12},{1,17},{... | collective-permute-start | bytes 1966088 | tf_op jit(solution)/shard_map/ppermute | solution.py:121
  108.1 8.2 %collective-permute-start.30 = (bf16[128,2560]{1,0:T(8,128)(2,1)S(1)}, bf16[128,2560]{1,0:T(8,128)(2,1)S(1)}, u32[]{:S(2)}, u32[]{:S(2)}) collective-permute-start(bf16[128,2560]{1,0:T(8,128)(2,1)S(1)} %get-tuple-element.101), channel_id=1, source_target_pairs={{0,4},{4,0},{8,12},{12,8},{16,20},{20,16},{24,28},{28,24},{1,5},{5... | collective-permute-start | bytes 1966088 | tf_op jit(solution)/shard_map/ppermute | solution.py:121
  108.5 1.8 %collective-permute-start.31 = (f32[128]{0:T(128)S(1)}, f32[128]{0:T(128)S(1)}, u32[]{:S(2)}, u32[]{:S(2)}) collective-permute-start(f32[128]{0:T(128)S(1)} %slice.54), channel_id=1, source_target_pairs={{0,4},{4,0},{8,12},{12,8},{16,20},{20,16},{24,28},{28,24},{1,5},{5... | collective-permute-start | bytes 1544 | tf_op jit(solution)/shard_map/ppermute | solution.py:121
  116.5 2.0 %copy-start.3 = (bf16[640,256]{1,0:T(8,128)(2,1)S(1)}, bf16[640,256]{1,0:T(8,128)(2,1)}, u32[]{:S(2)}) copy-start(bf16[640,256]{1,0:T(8,128)(2,1)} %copy-done.2) | copy-start | bytes 983044
  116.5 1.9 %copy-start.5 = (bf16[640,256]{1,0:T(8,128)(2,1)S(1)}, bf16[640,256]{1,0:T(8,128)(2,1)}, u32[]{:S(2)}) copy-start(bf16[640,256]{1,0:T(8,128)(2,1)} %copy-done.4) | copy-start | bytes 983044
  116.8 1.7 %collective-permute-start.34 = (bf16[128,1280]{1,0:T(8,128)(2,1)S(1)}, bf16[128,1280]{1,0:T(8,128)(2,1)S(1)}, u32[]{:S(2)}, u32[]{:S(2)}) collective-permute-start(bf16[128,1280]{1,0:T(8,128)(2,1)S(1)} %fusion.8.own_in_ref), channel_id=1, source_target_pairs={{0,4},{4,0},{8,12},{12,8},{16,20},{20,16},{24,28},{28,24},{1,5},{5... | collective-permute-start | bytes 983048 | tf_op jit(solution)/shard_map/ppermute | solution.py:121
  120.1 6.3 %collective-permute-start.37 = (bf16[256,256]{1,0:T(8,128)(2,1)S(1)}, bf16[256,256]{1,0:T(8,128)(2,1)S(1)}, u32[]{:S(2)}, u32[]{:S(2)}) collective-permute-start(bf16[256,256]{1,0:T(8,128)(2,1)S(1)} %get-tuple-element.112), channel_id=1, source_target_pairs={{0,3},{1,0},{2,1},{3,2},{4,7},{5,4},{6,5},{7,6},{8,11},{9,8},{10,9... | collective-permute-start | bytes 393224 | tf_op jit(solution)/shard_map/ppermute | solution.py:121
  121.3 12.5 %collective-permute-start.36 = (bf16[256,256]{1,0:T(8,128)(2,1)S(1)}, bf16[256,256]{1,0:T(8,128)(2,1)S(1)}, u32[]{:S(2)}, u32[]{:S(2)}) collective-permute-start(bf16[256,256]{1,0:T(8,128)(2,1)S(1)} %get-tuple-element.111), channel_id=1, source_target_pairs={{0,2},{1,3},{2,0},{3,1},{4,6},{5,7},{6,4},{7,5},{8,10},{9,11},{10,... | collective-permute-start | bytes 393224 | tf_op jit(solution)/shard_map/ppermute | solution.py:121
  121.7 12.1 %collective-permute-start.35 = (bf16[256,256]{1,0:T(8,128)(2,1)S(1)}, bf16[256,256]{1,0:T(8,128)(2,1)S(1)}, u32[]{:S(2)}, u32[]{:S(2)}) collective-permute-start(bf16[256,256]{1,0:T(8,128)(2,1)S(1)} %get-tuple-element.110), channel_id=1, source_target_pairs={{0,1},{1,2},{2,3},{3,0},{4,5},{5,6},{6,7},{7,4},{8,9},{9,10},{10,1... | collective-permute-start | bytes 393224 | tf_op jit(solution)/shard_map/ppermute | solution.py:121
  133.9 1.3 collective-permute-start.38

commit v8 on v7

--- a/solution.py
+++ b/solution.py
@@ -161,18 +161,19 @@
 
 
 def packet_kernel(own_ref, low_in, high_in, low_ref, high_ref):
-    size = low_in.shape[0]
-    low_ref[0], high_ref[0] = own_ref[0], own_ref[1]
+    cut = low_in.shape[0]
+    stacked = len(own_ref.shape) == 3
+    low_ref[0] = own_ref[0] if stacked else own_ref[:cut]
+    high_ref[0] = own_ref[1] if stacked else own_ref[cut:]
     low_ref[1], high_ref[1] = low_in[...], high_in[...]
 
 
 def second_phase(own, first):
     if len(first) != 2:
         return []
-    shape = jax.ShapeDtypeStruct(own.shape, own.dtype)
     low, high = pl.pallas_call(
         packet_kernel,
-        out_shape=(shape, shape),
+        out_shape=tuple(jax.ShapeDtypeStruct((2, *part.shape), part.dtype) for part in first),
         in_specs=[VMEM] * 3,
         out_specs=(VMEM, VMEM),
         compiler_params=pltpu.CompilerParams(vmem_limit_bytes=8 << 20),
@@ -348,7 +349,7 @@
     )(place, gain, *token_blocks, *pieces)
 
 
-def columns_kernel(place_ref, own_in_ref, other_in_ref, *refs):
+def columns_kernel(cut, place_ref, own_in_ref, other_in_ref, *refs):
     blocks = lax.axis_size("col")
     *weight_refs, own_ref = refs[: len(refs) - blocks]
     send_refs, held = refs[len(refs) - blocks : -1], refs[-1]
@@ -358,17 +359,14 @@
     far = len(weight_refs) == blocks + 1
     direct = blocks - 1 if far else blocks
     for step in range(blocks):
-        if len(weight_refs[0].shape) == 3:
-            half = hidden.shape[1] // 2
+        if cut:
+            low, high = (
+                weight_refs[0][:cut] if step == 0 else half_ref(weight_refs, step, 0)[...],
+                weight_refs[0][cut:] if step == 0 else half_ref(weight_refs, step, 1)[...],
+            )
             total = jnp.dot(
-                hidden[:, :half],
-                half_ref(weight_refs, step, 0)[...],
-                preferred_element_type=jnp.float32,
-            ) + jnp.dot(
-                hidden[:, half:],
-                half_ref(weight_refs, step, 1)[...],
-                preferred_element_type=jnp.float32,
-            )
+                hidden[:, :cut], low, preferred_element_type=jnp.float32
+            ) + jnp.dot(hidden[:, cut:], high, preferred_element_type=jnp.float32)
         elif step < direct:
             total = jnp.dot(hidden, weight_refs[step][...], preferred_element_type=jnp.float32)
         else:
@@ -383,12 +381,12 @@
         send_refs[step - 1][...] = held[step].astype(jnp.bfloat16)
 
 
-def columns(place, own, other, pieces, name):
+def columns(place, own, other, pieces, name, cut=0):
     count, depth = own.shape
     width = pieces[0].shape[-1]
     blocks = lax.axis_size("col")
     return pl.pallas_call(
-        columns_kernel,
+        functools.partial(columns_kernel, cut),
         out_shape=(
             jax.ShapeDtypeStruct((2 * count, width), jnp.float32),
             *[jax.ShapeDtypeStruct((2 * count, width), jnp.bfloat16)] * (blocks - 1),
@@ -461,8 +459,9 @@
     qkv_far = relayed(qkv_near, 2, "relay_qkv")
     *out_near, received, bias = lax.optimization_barrier((*out_near, received, bias))
     out_far = relayed(out_near, 0, "relay_out")
-    w_in, w_down, *_ = lax.optimization_barrier((w_in, w_down.reshape(2, -1, half), received))
-    down_first = first_phase(w_down[0], w_down[1])
+    w_in, w_down, *_ = lax.optimization_barrier((w_in, w_down, received))
+    cut = w_down.shape[0] * 9 // 20 // 16 * 16
+    down_first = first_phase(w_down[:cut], w_down[cut:])
     in_first = first_phase(w_in[0], w_in[1])
     kept, *out_far = lax.optimization_barrier((kept, *out_far))
     own_q, own_kv, send_q, send_kv = project_qkv(
@@ -510,7 +509,7 @@
         jax.nn.gelu(branches[:, :inner], approximate=True) * branches[:, inner:]
     ).astype(jnp.bfloat16)
     own, *sends = columns(
-        place, hidden, other_core(hidden), [w_down, *down_first, *down_second], "ffn_out"
+        place, hidden, other_core(hidden), [w_down, *down_first, *down_second], "ffn_out", cut
     )
     result = summed(own, sends, middle)
     received = other_core(result[count:])

time: 136 us -> 135 us (level)
  no operation moved by 1% of the time
where the time goes in v8:
time: 135 us
  waiting for transfers between devices  69.5 us (51%)
  starting transfers between devices  44 us (33%)
  Pallas kernels  13.7 us (10%)
  other arithmetic  3.58 us (3%)
  local copies, waits for them, and re-layouts  3.35 us (2%)
    ppermute x37, waiting for transfers between devices, exchange(): lax.ppermute(value, axis, [(i, partner(i) % count) for i in range(count)])  69.5 us
    ppermute x37, starting transfers between devices, exchange(): lax.ppermute(value, axis, [(i, partner(i) % count) for i in range(count)])  41.4 us
    pallas_call x1, Pallas kernels, project_ffn(): pl.pallas_call(ffn_in_kernel, out_shape=(jax.ShapeDtypeStruct((count, col...  3.34 us
    pallas_call x2, Pallas kernels, columns(): pl.pallas_call(functools.partial(columns_kernel, cut), out_shape=(jax.Sha...  2.83 us
  transfers between devices with their start and end apart: 39, of which 23 were waited for; matrix products, arithmetic and copies ran while one was open for 3% of the time, Pallas kernels for 8%

profile of v8, /device:TPU:0, one launch (start us, length us, event | category | flops | bytes accessed | tf_op | source)
XLA Modules:
  0.0 135.1 jit_solution(16524924624447195602)
XLA Ops:
  0.6 3.0 %collective-permute-start = (bf16[3,256,512]{2,1,0:T(8,128)(2,1)}, bf16[3,256,512]{2,1,0:T(8,128)(2,1)S(1)}, u32[]{:S(2)}, u32[]{:S(2)}) collective-permute-start(bf16[3,256,512]{2,1,0:T(8,128)(2,1)} %refs_0_.4), channel_id=1, source_target_pairs={{0,8},{4,12},{8,0},{12,4},{16,24},{20,28},{24,16},{28,20},{1,9},{5... | collective-permute-start | bytes 2359304 | tf_op jit(solution)/shard_map/ppermute | solution.py:121
  3.6 1.5 %collective-permute-start.1 = (bf16[3,256,512]{2,1,0:T(8,128)(2,1)}, bf16[3,256,512]{2,1,0:T(8,128)(2,1)S(1)}, u32[]{:S(2)}, u32[]{:S(2)}) collective-permute-start(bf16[3,256,512]{2,1,0:T(8,128)(2,1)} %refs_0_.4), channel_id=1, source_target_pairs={{0,16},{4,20},{8,24},{12,28},{16,0},{20,4},{24,8},{28,12},{1,17},{... | collective-permute-start | bytes 2359304 | tf_op jit(solution)/shard_map/ppermute | solution.py:121
  5.2 0.9 broadcast_select_fusion.1
  6.2 1.6 %collective-permute-start.2 = (bf16[128,512]{1,0:T(8,128)(2,1)}, bf16[128,512]{1,0:T(8,128)(2,1)S(1)}, u32[]{:S(2)}, u32[]{:S(2)}) collective-permute-start(bf16[128,512]{1,0:T(8,128)(2,1)} %refs_0_.3), channel_id=1, source_target_pairs={{0,1},{1,2},{2,3},{3,0},{4,5},{5,6},{6,7},{7,4},{8,9},{9,10},{10,1... | collective-permute-start | bytes 393224 | tf_op jit(solution)/shard_map/ppermute | solution.py:121
  7.8 2.6 %collective-permute-start.3 = (bf16[128,512]{1,0:T(8,128)(2,1)}, bf16[128,512]{1,0:T(8,128)(2,1)S(1)}, u32[]{:S(2)}, u32[]{:S(2)}) collective-permute-start(bf16[128,512]{1,0:T(8,128)(2,1)} %refs_0_.3), channel_id=1, source_target_pairs={{0,2},{1,3},{2,0},{3,1},{4,6},{5,7},{6,4},{7,5},{8,10},{9,11},{10,... | collective-permute-start | bytes 393224 | tf_op jit(solution)/shard_map/ppermute | solution.py:121
  10.4 1.3 collective-permute-start.4
  11.8 0.7 reshape.21.gain_ref
  12.5 2.1 %collective-permute-done.2.refs_1_ = bf16[128,512]{1,0:T(8,128)(2,1)S(1)} collective-permute-done((bf16[128,512]{1,0:T(8,128)(2,1)}, bf16[128,512]{1,0:T(8,128)(2,1)S(1)}, u32[]{:S(2)}, u32[]{:S(2)}) %collective-permute-start.2) | collective-permute-done | bytes 131104 | tf_op jit(solution)/shard_map/ppermute | solution.py:121
  14.6 0.5 collective-permute-start.6
  15.2 4.7 %collective-permute-done.3.refs_2_ = bf16[128,512]{1,0:T(8,128)(2,1)S(1)} collective-permute-done((bf16[128,512]{1,0:T(8,128)(2,1)}, bf16[128,512]{1,0:T(8,128)(2,1)S(1)}, u32[]{:S(2)}, u32[]{:S(2)}) %collective-permute-start.3) | collective-permute-done | bytes 131104 | tf_op jit(solution)/shard_map/ppermute | solution.py:121
  19.8 0.5 collective-permute-start.7
  20.3 0.9 copy-done.7
  21.2 0.8 norm_tokens.1
  22.2 1.0 collective-permute-done.1.high_in.refs_2_
  23.3 2.4 %collective-permute-start.11 = (bf16[3,256,256]{2,1,0:T(8,128)(2,1)S(1)}, bf16[3,256,256]{2,1,0:T(8,128)(2,1)S(1)}, u32[]{:S(2)}, u32[]{:S(2)}) collective-permute-start(bf16[3,256,256]{2,1,0:T(8,128)(2,1)S(1)} %get-tuple-element.71), channel_id=1, source_target_pairs={{0,16},{4,20},{8,24},{12,28},{16,0},{20,4},{24,8},{28,12},{1,17},{... | collective-permute-start | bytes 1179656 | tf_op jit(solution)/shard_map/ppermute | solution.py:121
  25.7 0.5 collective-permute-start.12
  26.3 0.6 masked_bias.1.bias_ref
  27.0 2.2 %collective-permute-done.7.high_in.refs_2_ = bf16[512,256]{1,0:T(8,128)(2,1)S(1)} collective-permute-done((bf16[512,256]{1,0:T(8,128)(2,1)}, bf16[512,256]{1,0:T(8,128)(2,1)S(1)}, u32[]{:S(2)}, u32[]{:S(2)}) %collective-permute-start.7) | collective-permute-done | bytes 262176 | tf_op jit(solution)/shard_map/ppermute | solution.py:121
  29.2 2.0 %collective-permute-start.9 = (bf16[256,256]{1,0:T(8,128)(2,1)S(1)}, bf16[256,256]{1,0:T(8,128)(2,1)S(1)}, u32[]{:S(2)}, u32[]{:S(2)}) collective-permute-start(bf16[256,256]{1,0:T(8,128)(2,1)S(1)} %get-tuple-element.65), channel_id=1, source_target_pairs={{0,16},{4,20},{8,24},{12,28},{16,0},{20,4},{24,8},{28,12},{1,17},{... | collective-permute-start | bytes 393224 | tf_op jit(solution)/shard_map/ppermute | solution.py:121
  31.2 0.5 collective-permute-start.10
  31.8 1.6 %collective-permute-start.15 = (bf16[576,256]{1,0:T(8,128)(2,1)S(1)}, bf16[576,256]{1,0:T(8,128)(2,1)S(1)}, u32[]{:S(2)}, u32[]{:S(2)}) collective-permute-start(bf16[576,256]{1,0:T(8,128)(2,1)S(1)} %slice.47), channel_id=1, source_target_pairs={{0,8},{4,12},{8,0},{12,4},{16,24},{20,28},{24,16},{28,20},{1,9},{5... | collective-permute-start | bytes 884744 | tf_op jit(solution)/shard_map/ppermute | solution.py:121
  33.4 6.3 %collective-permute-done.9.refs_3_ = bf16[256,256]{1,0:T(8,128)(2,1)S(1)} collective-permute-done((bf16[256,256]{1,0:T(8,128)(2,1)S(1)}, bf16[256,256]{1,0:T(8,128)(2,1)S(1)}, u32[]{:S(2)}, u32[]{:S(2)}) %collective-permute-start.9) | collective-permute-done | bytes 131104 | tf_op jit(solution)/shard_map/ppermute | solution.py:121
  39.7 1.5 %collective-permute-start.16 = (bf16[704,256]{1,0:T(8,128)(2,1)S(1)}, bf16[704,256]{1,0:T(8,128)(2,1)S(1)}, u32[]{:S(2)}, u32[]{:S(2)}) collective-permute-start(bf16[704,256]{1,0:T(8,128)(2,1)S(1)} %slice.48), channel_id=1, source_target_pairs={{0,16},{4,20},{8,24},{12,28},{16,0},{20,4},{24,8},{28,12},{1,17},{... | collective-permute-start | bytes 1081352 | tf_op jit(solution)/shard_map/ppermute | solution.py:121
  41.2 1.5 %qkv.1 = (f32[128,512]{1,0:T(8,128)S(1)}, f32[128,1024]{1,0:T(8,128)S(1)}, f32[128,512]{1,0:T(8,128)S(1)}, f32[128,1024]{1,0:T(8,128)S(1)}) custom-call(s32[2]{0:T(128)S(1)} %pad_add_fusion.place_ref, bf16[4,128,256]{2,1,0:T(8,128)(2,1)S(1)} %get-tuple-element.67.own_in_ref, bf16[4,128,256]{2,1,0:T(8,128)(2,1)S(1)} %collective-permute-done.8.other_in_ref, ...), custom_call_target="tpu_custom_call" | custom-call | flops 805306368 | bytes 3145728 | tf_op jit(solution)/shard_map/qkv/pallas_call | solution.py:297
  42.9 0.5 collective-permute-start.14
  43.5 0.6 collective-permute-start.19
  44.1 2.0 %collective-permute-done.15.low_in.refs_1_ = bf16[576,256]{1,0:T(8,128)(2,1)S(1)} collective-permute-done((bf16[576,256]{1,0:T(8,128)(2,1)S(1)}, bf16[576,256]{1,0:T(8,128)(2,1)S(1)}, u32[]{:S(2)}, u32[]{:S(2)}) %collective-permute-start.15) | collective-permute-done | bytes 294944 | tf_op jit(solution)/shard_map/ppermute | solution.py:121
  46.4 4.2 %collective-permute-done.16.high_in.refs_2_ = bf16[704,256]{1,0:T(8,128)(2,1)S(1)} collective-permute-done((bf16[704,256]{1,0:T(8,128)(2,1)S(1)}, bf16[704,256]{1,0:T(8,128)(2,1)S(1)}, u32[]{:S(2)}, u32[]{:S(2)}) %collective-permute-start.16) | collective-permute-done | bytes 360480 | tf_op jit(solution)/shard_map/ppermute | solution.py:121
  50.7 1.3 collective-permute-start.17
  52.0 1.3 collective-permute-start.18
  53.4 0.8 copy-done.12
  54.3 6.9 %collective-permute-done.19.low_in.refs_5_ = bf16[256,1280]{1,0:T(8,128)(2,1)S(1)} collective-permute-done((bf16[256,1280]{1,0:T(8,128)(2,1)S(1)}, bf16[256,1280]{1,0:T(8,128)(2,1)S(1)}, u32[]{:S(2)}, u32[]{:S(2)}) %collective-permute-start.19) | collective-permute-done | bytes 655392 | tf_op jit(solution)/shard_map/ppermute | solution.py:121
  61.1 3.8 %collective-permute-done.20.high_in.refs_6_ = bf16[256,1280]{1,0:T(8,128)(2,1)S(1)} collective-permute-done((bf16[256,1280]{1,0:T(8,128)(2,1)S(1)}, bf16[256,1280]{1,0:T(8,128)(2,1)S(1)}, u32[]{:S(2)}, u32[]{:S(2)}) %collective-permute-start.20) | collective-permute-done | bytes 655392 | tf_op jit(solution)/shard_map/ppermute | solution.py:121
  64.9 1.7 %packet.3 = (bf16[2,256,1280]{2,1,0:T(8,128)(2,1)}, bf16[2,256,1280]{2,1,0:T(8,128)(2,1)}) custom-call(bf16[2,256,1280]{2,1,0:T(8,128)(2,1)S(1)} %copy-done, bf16[256,1280]{1,0:T(8,128)(2,1)S(1)} %collective-permute-done.19.low_in.refs_5_, bf16[256,1280]{1,0:T(8,128)(2,1)S(1)} %collective-permute-done.20.high_in.refs_6_), custom_call_target="tpu_custom_call" | custom-call | tf_op jit(solution)/shard_map/packet/pallas_call | solution.py:174
  66.6 0.6 collective-permute-start.28
  67.2 1.9 %collective-permute-start.29 = (bf16[2,256,1280]{2,1,0:T(8,128)(2,1)}, bf16[2,256,1280]{2,1,0:T(8,128)(2,1)}, u32[]{:S(2)}, u32[]{:S(2)}) collective-permute-start(bf16[2,256,1280]{2,1,0:T(8,128)(2,1)} %get-tuple-element.99), channel_id=1, source_target_pairs={{0,16},{4,20},{8,24},{12,28},{16,0},{20,4},{24,8},{28,12},{1,17},{... | collective-permute-start | bytes 3932168 | tf_op jit(solution)/shard_map/ppermute | solution.py:121
  69.1 2.7 %attention.1.own_in_ref = bf16[128,512]{1,0:T(8,128)(2,1)S(1)} custom-call(bf16[128,512]{1,0:T(8,128)(2,1)S(1)} %add_convert_fusion.2.q_ref, bf16[128,1024]{1,0:T(8,128)(2,1)S(1)} %collective-permute-done.17.low_ref, bf16[128,1024]{1,0:T(8,128)(2,1)S(1)} %add_convert_fusion.own_ref, bf16[128,1024]{1,0:T(8,128)(2,1)S(1)} %collective-permute-done.18.high_ref, ...), custom_call_target="tpu_custom_call" | custom-call | flops 100663296 | bytes 1572864 | tf_op jit(solution)/shard_map/attention/pallas_call | solution.py:106
  71.8 1.3 collective-permute-done.21.other_in_ref
  73.2 1.1 attention_out.1
  74.3 4.0 %collective-permute-start.24 = (bf16[256,256]{1,0:T(8,128)(2,1)S(1)}, bf16[256,256]{1,0:T(8,128)(2,1)S(1)}, u32[]{:S(2)}, u32[]{:S(2)}) collective-permute-start(bf16[256,256]{1,0:T(8,128)(2,1)S(1)} %get-tuple-element.94), channel_id=1, source_target_pairs={{0,3},{1,0},{2,1},{3,2},{4,7},{5,4},{6,5},{7,6},{8,11},{9,8},{10,9... | collective-permute-start | bytes 393224 | tf_op jit(solution)/shard_map/ppermute | solution.py:121
  78.4 0.9 collective-permute-start.22
  79.3 0.7 pad_maximum_fusion
  80.0 2.3 %collective-permute-done.24 = bf16[256,256]{1,0:T(8,128)(2,1)S(1)} collective-permute-done((bf16[256,256]{1,0:T(8,128)(2,1)S(1)}, bf16[256,256]{1,0:T(8,128)(2,1)S(1)}, u32[]{:S(2)}, u32[]{:S(2)}) %collective-permute-start.24) | collective-permute-done | bytes 131104 | tf_op jit(solution)/shard_map/ppermute | solution.py:121
  82.3 7.7 %collective-permute-done.23 = bf16[256,256]{1,0:T(8,128)(2,1)S(1)} collective-permute-done((bf16[256,256]{1,0:T(8,128)(2,1)S(1)}, bf16[256,256]{1,0:T(8,128)(2,1)S(1)}, u32[]{:S(2)}, u32[]{:S(2)}) %collective-permute-start.23) | collective-permute-done | bytes 131104 | tf_op jit(solution)/shard_map/ppermute | solution.py:121
  90.1 1.5 %collective-permute-start.27 = (bf16[256,256]{1,0:T(8,128)(2,1)S(1)}, bf16[256,256]{1,0:T(8,128)(2,1)S(1)}, u32[]{:S(2)}, u32[]{:S(2)}) collective-permute-start(bf16[256,256]{1,0:T(8,128)(2,1)S(1)} %add_convert_fusion.1.refs_0_), channel_id=1, source_target_pairs={{0,3},{1,0},{2,1},{3,2},{4,7},{5,4},{6,5},{7,6},{8,11},{9,8},{10,9... | collective-permute-start | bytes 393224 | tf_op jit(solution)/shard_map/ppermute | solution.py:121
  91.6 0.7 reshape.20.gain_ref
  92.3 0.6 collective-permute-start.25
  92.8 2.5 %collective-permute-start.26 = (bf16[256,256]{1,0:T(8,128)(2,1)S(1)}, bf16[256,256]{1,0:T(8,128)(2,1)S(1)}, u32[]{:S(2)}, u32[]{:S(2)}) collective-permute-start(bf16[256,256]{1,0:T(8,128)(2,1)S(1)} %add_convert_fusion.1.refs_0_), channel_id=1, source_target_pairs={{0,2},{1,3},{2,0},{3,1},{4,6},{5,7},{6,4},{7,5},{8,10},{9,11},{10,... | collective-permute-start | bytes 393224 | tf_op jit(solution)/shard_map/ppermute | solution.py:121
  95.4 2.1 %collective-permute-start.32 = (bf16[2,704,256]{2,1,0:T(8,128)(2,1)}, bf16[2,704,256]{2,1,0:T(8,128)(2,1)S(1)}, u32[]{:S(2)}, u32[]{:S(2)}) collective-permute-start(bf16[2,704,256]{2,1,0:T(8,128)(2,1)} %copy-done.11), channel_id=1, source_target_pairs={{0,8},{4,12},{8,0},{12,4},{16,24},{20,28},{24,16},{28,20},{1,9},{5... | collective-permute-start | bytes 2162696 | tf_op jit(solution)/shard_map/ppermute | solution.py:121
  97.6 3.3 %collective-permute-done.25.refs_1_ = bf16[256,256]{1,0:T(8,128)(2,1)S(1)} collective-permute-done((bf16[256,256]{1,0:T(8,128)(2,1)S(1)}, bf16[256,256]{1,0:T(8,128)(2,1)S(1)}, u32[]{:S(2)}, u32[]{:S(2)}) %collective-permute-start.25) | collective-permute-done | bytes 131104 | tf_op jit(solution)/shard_map/ppermute | solution.py:121
  101.4 2.5 %collective-permute-done.26.refs_2_ = bf16[256,256]{1,0:T(8,128)(2,1)S(1)} collective-permute-done((bf16[256,256]{1,0:T(8,128)(2,1)S(1)}, bf16[256,256]{1,0:T(8,128)(2,1)S(1)}, u32[]{:S(2)}, u32[]{:S(2)}) %collective-permute-start.26) | collective-permute-done | bytes 131104 | tf_op jit(solution)/shard_map/ppermute | solution.py:121
  104.0 3.3 %ffn_in.1 = (f32[128,2560]{1,0:T(8,128)S(1)}, bf16[128,2560]{1,0:T(8,128)(2,1)S(1)}) custom-call(s32[2]{0:T(128)S(1)} %pad_add_fusion.place_ref, f32[8,256]{1,0:T(8,128)S(1)} %reshape.20.gain_ref, bf16[256,256]{1,0:T(8,128)(2,1)S(1)} %add_convert_fusion.1.refs_0_, bf16[256,256]{1,0:T(8,128)(2,1)S(1)} %collective-permute-done.25.refs_1_, ...), custom_call_target="tpu_custom_call" | custom-call | flops 1342177280 | bytes 5242880 | tf_op jit(solution)/shard_map/ffn_in/pallas_call | solution.py:333
  107.7 0.6 collective-permute-start.31
  108.2 1.3 collective-permute-done.31
  109.5 3.6 %collective-permute-done.33.refs_4_ = bf16[2,576,256]{2,1,0:T(8,128)(2,1)S(1)} collective-permute-done((bf16[2,576,256]{2,1,0:T(8,128)(2,1)}, bf16[2,576,256]{2,1,0:T(8,128)(2,1)S(1)}, u32[]{:S(2)}, u32[]{:S(2)}) %collective-permute-start.33) | collective-permute-done | bytes 589856 | tf_op jit(solution)/shard_map/ppermute | solution.py:121
  113.0 0.6 collective-permute-done.32.refs_3_
  114.2 1.6 %collective-permute-done.34.other_in_ref = bf16[128,1280]{1,0:T(8,128)(2,1)S(1)} collective-permute-done((bf16[128,1280]{1,0:T(8,128)(2,1)S(1)}, bf16[128,1280]{1,0:T(8,128)(2,1)S(1)}, u32[]{:S(2)}, u32[]{:S(2)}) %collective-permute-start.34) | collective-permute-done | bytes 327712 | tf_op jit(solution)/shard_map/ppermute | solution.py:121
  115.8 1.7 %ffn_out.1 = (f32[256,256]{1,0:T(8,128)S(1)}, bf16[256,256]{1,0:T(8,128)(2,1)S(1)}, bf16[256,256]{1,0:T(8,128)(2,1)S(1)}, bf16[256,256]{1,0:T(8,128)(2,1)S(1)}) custom-call(s32[2]{0:T(128)S(1)} %pad_add_fusion.place_ref, bf16[128,1280]{1,0:T(8,128)(2,1)S(1)} %fusion.8.own_in_ref, bf16[128,1280]{1,0:T(8,128)(2,1)S(1)} %collective-permute-done.34.other_in_ref, ...), custom_call_target="tpu_custom_call" | custom-call | flops 671088640 | bytes 2621440 | tf_op jit(solution)/shard_map/ffn_out/pallas_call | solution.py:388
  117.6 3.7 %collective-permute-start.37 = (bf16[256,256]{1,0:T(8,128)(2,1)S(1)}, bf16[256,256]{1,0:T(8,128)(2,1)S(1)}, u32[]{:S(2)}, u32[]{:S(2)}) collective-permute-start(bf16[256,256]{1,0:T(8,128)(2,1)S(1)} %get-tuple-element.112), channel_id=1, source_target_pairs={{0,3},{1,0},{2,1},{3,2},{4,7},{5,4},{6,5},{7,6},{8,11},{9,8},{10,9... | collective-permute-start | bytes 393224 | tf_op jit(solution)/shard_map/ppermute | solution.py:121
  121.2 1.2 collective-permute-start.35
  122.4 2.8 %collective-permute-done.37 = bf16[256,256]{1,0:T(8,128)(2,1)S(1)} collective-permute-done((bf16[256,256]{1,0:T(8,128)(2,1)S(1)}, bf16[256,256]{1,0:T(8,128)(2,1)S(1)}, u32[]{:S(2)}, u32[]{:S(2)}) %collective-permute-start.37) | collective-permute-done | bytes 131104 | tf_op jit(solution)/shard_map/ppermute | solution.py:121
  125.2 7.8 %collective-permute-done.36 = bf16[256,256]{1,0:T(8,128)(2,1)S(1)} collective-permute-done((bf16[256,256]{1,0:T(8,128)(2,1)S(1)}, bf16[256,256]{1,0:T(8,128)(2,1)S(1)}, u32[]{:S(2)}, u32[]{:S(2)}) %collective-permute-start.36) | collective-permute-done | bytes 131104 | tf_op jit(solution)/shard_map/ppermute | solution.py:121
  133.2 1.2 collective-permute-done.38
  134.4 0.7 maximum_select_fusion
  (79 shorter events, 3.2 us)
Async XLA Ops:
  0.6 21.6 %collective-permute-start = (bf16[3,256,512]{2,1,0:T(8,128)(2,1)}, bf16[3,256,512]{2,1,0:T(8,128)(2,1)S(1)}, u32[]{:S(2)}, u32[]{:S(2)}) collective-permute-start(bf16[3,256,512]{2,1,0:T(8,128)(2,1)} %refs_0_.4), channel_id=1, source_target_pairs={{0,8},{4,12},{8,0},{12,4},{16,24},{20,28},{24,16},{28,20},{1,9},{5... | collective-permute-start | bytes 2359304 | tf_op jit(solution)/shard_map/ppermute | solution.py:121
  3.6 19.6 %collective-permute-start.1 = (bf16[3,256,512]{2,1,0:T(8,128)(2,1)}, bf16[3,256,512]{2,1,0:T(8,128)(2,1)S(1)}, u32[]{:S(2)}, u32[]{:S(2)}) collective-permute-start(bf16[3,256,512]{2,1,0:T(8,128)(2,1)} %refs_0_.4), channel_id=1, source_target_pairs={{0,16},{4,20},{8,24},{12,28},{16,0},{20,4},{24,8},{28,12},{1,17},{... | collective-permute-start | bytes 2359304 | tf_op jit(solution)/shard_map/ppermute | solution.py:121
  5.2 21.1 %copy-start.13 = (s32[255]{0:T(256)S(1)}, s32[255]{0:T(256)}, u32[]{:S(2)}) copy-start(s32[255]{0:T(256)} %param.13) | copy-start | bytes 3064
  5.2 21.1 %copy-start.9 = (s32[1024]{0:T(1024)S(1)}, s32[1024]{0:T(1024)}, u32[]{:S(2)}) copy-start(s32[1024]{0:T(1024)} %param.12) | copy-start | bytes 12292
  5.2 21.1 %copy-start.10 = (f32[32,8]{0,1:T(8,128)S(1)}, f32[32,8]{0,1:T(8,128)}, u32[]{:S(2)}) copy-start(f32[32,8]{0,1:T(8,128)} %param.16) | copy-start | bytes 3076
  6.1 4.3 %collective-permute-start.5 = (bf16[128,256]{1,0:T(8,128)(2,1)S(1)}, bf16[128,256]{1,0:T(8,128)(2,1)S(1)}, u32[]{:S(2)}, u32[]{:S(2)}) collective-permute-start(bf16[128,256]{1,0:T(8,128)(2,1)S(1)} %get-tuple-element.121), channel_id=1, source_target_pairs={{0,4},{4,0},{8,12},{12,8},{16,20},{20,16},{24,28},{28,24},{1,5},{5... | collective-permute-start | bytes 196616 | tf_op jit(solution)/shard_map/ppermute | solution.py:121
  6.2 8.5 %collective-permute-start.2 = (bf16[128,512]{1,0:T(8,128)(2,1)}, bf16[128,512]{1,0:T(8,128)(2,1)S(1)}, u32[]{:S(2)}, u32[]{:S(2)}) collective-permute-start(bf16[128,512]{1,0:T(8,128)(2,1)} %refs_0_.3), channel_id=1, source_target_pairs={{0,1},{1,2},{2,3},{3,0},{4,5},{5,6},{6,7},{7,4},{8,9},{9,10},{10,1... | collective-permute-start | bytes 393224 | tf_op jit(solution)/shard_map/ppermute | solution.py:121
  7.8 12.0 %collective-permute-start.3 = (bf16[128,512]{1,0:T(8,128)(2,1)}, bf16[128,512]{1,0:T(8,128)(2,1)S(1)}, u32[]{:S(2)}, u32[]{:S(2)}) collective-permute-start(bf16[128,512]{1,0:T(8,128)(2,1)} %refs_0_.3), channel_id=1, source_target_pairs={{0,2},{1,3},{2,0},{3,1},{4,6},{5,7},{6,4},{7,5},{8,10},{9,11},{10,... | collective-permute-start | bytes 393224 | tf_op jit(solution)/shard_map/ppermute | solution.py:121
  10.4 9.9 %collective-permute-start.4 = (bf16[128,512]{1,0:T(8,128)(2,1)}, bf16[128,512]{1,0:T(8,128)(2,1)S(1)}, u32[]{:S(2)}, u32[]{:S(2)}) collective-permute-start(bf16[128,512]{1,0:T(8,128)(2,1)} %refs_0_.3), channel_id=1, source_target_pairs={{0,3},{1,0},{2,1},{3,2},{4,7},{5,4},{6,5},{7,6},{8,11},{9,8},{10,9... | collective-permute-start | bytes 393224 | tf_op jit(solution)/shard_map/ppermute | solution.py:121
  14.6 12.4 %collective-permute-start.6 = (bf16[512,256]{1,0:T(8,128)(2,1)}, bf16[512,256]{1,0:T(8,128)(2,1)S(1)}, u32[]{:S(2)}, u32[]{:S(2)}) collective-permute-start(bf16[512,256]{1,0:T(8,128)(2,1)} %refs_0_.5), channel_id=1, source_target_pairs={{0,8},{4,12},{8,0},{12,4},{16,24},{20,28},{24,16},{28,20},{1,9},{5... | collective-permute-start | bytes 786440 | tf_op jit(solution)/shard_map/ppermute | solution.py:121
  19.8 9.4 %collective-permute-start.7 = (bf16[512,256]{1,0:T(8,128)(2,1)}, bf16[512,256]{1,0:T(8,128)(2,1)S(1)}, u32[]{:S(2)}, u32[]{:S(2)}) collective-permute-start(bf16[512,256]{1,0:T(8,128)(2,1)} %refs_0_.5), channel_id=1, source_target_pairs={{0,16},{4,20},{8,24},{12,28},{16,0},{20,4},{24,8},{28,12},{1,17},{... | collective-permute-start | bytes 786440 | tf_op jit(solution)/shard_map/ppermute | solution.py:121
  20.3 0.9 copy-start.7
  23.2 6.0 %collective-permute-start.8 = (bf16[4,128,256]{2,1,0:T(8,128)(2,1)S(1)}, bf16[4,128,256]{2,1,0:T(8,128)(2,1)S(1)}, u32[]{:S(2)}, u32[]{:S(2)}) collective-permute-start(bf16[4,128,256]{2,1,0:T(8,128)(2,1)S(1)} %get-tuple-element.62), channel_id=1, source_target_pairs={{0,4},{4,0},{8,12},{12,8},{16,20},{20,16},{24,28},{28,24},{1,5},{5... | collective-permute-start | bytes 786440 | tf_op jit(solution)/shard_map/ppermute | solution.py:121
  23.2 8.5 %copy-start.1 = (bf16[1280,256]{1,0:T(8,128)(2,1)S(1)}, bf16[1280,256]{1,0:T(8,128)(2,1)}, u32[]{:S(2)}) copy-start(bf16[1280,256]{1,0:T(8,128)(2,1)} %refs_0_.6) | copy-start | bytes 1966084
  23.3 18.0 %collective-permute-start.11 = (bf16[3,256,256]{2,1,0:T(8,128)(2,1)S(1)}, bf16[3,256,256]{2,1,0:T(8,128)(2,1)S(1)}, u32[]{:S(2)}, u32[]{:S(2)}) collective-permute-start(bf16[3,256,256]{2,1,0:T(8,128)(2,1)S(1)} %get-tuple-element.71), channel_id=1, source_target_pairs={{0,16},{4,20},{8,24},{12,28},{16,0},{20,4},{24,8},{28,12},{1,17},{... | collective-permute-start | bytes 1179656 | tf_op jit(solution)/shard_map/ppermute | solution.py:121
  25.7 15.5 %collective-permute-start.12 = (bf16[3,256,256]{2,1,0:T(8,128)(2,1)S(1)}, bf16[3,256,256]{2,1,0:T(8,128)(2,1)S(1)}, u32[]{:S(2)}, u32[]{:S(2)}) collective-permute-start(bf16[3,256,256]{2,1,0:T(8,128)(2,1)S(1)} %get-tuple-element.72), channel_id=1, source_target_pairs={{0,8},{4,12},{8,0},{12,4},{16,24},{20,28},{24,16},{28,20},{1,9},{5... | collective-permute-start | bytes 1179656 | tf_op jit(solution)/shard_map/ppermute | solution.py:121
  26.9 14.3 %copy-start.6 = (bf16[3,256,512]{2,1,0:T(8,128)(2,1)S(1)}, bf16[3,256,512]{2,1,0:T(8,128)(2,1)}, u32[]{:S(2)}) copy-start(bf16[3,256,512]{2,1,0:T(8,128)(2,1)} %refs_0_.4) | copy-start | bytes 2359300
  29.2 10.5 %collective-permute-start.9 = (bf16[256,256]{1,0:T(8,128)(2,1)S(1)}, bf16[256,256]{1,0:T(8,128)(2,1)S(1)}, u32[]{:S(2)}, u32[]{:S(2)}) collective-permute-start(bf16[256,256]{1,0:T(8,128)(2,1)S(1)} %get-tuple-element.65), channel_id=1, source_target_pairs={{0,16},{4,20},{8,24},{12,28},{16,0},{20,4},{24,8},{28,12},{1,17},{... | collective-permute-start | bytes 393224 | tf_op jit(solution)/shard_map/ppermute | solution.py:121
  31.2 10.0 %collective-permute-start.10 = (bf16[256,256]{1,0:T(8,128)(2,1)S(1)}, bf16[256,256]{1,0:T(8,128)(2,1)S(1)}, u32[]{:S(2)}, u32[]{:S(2)}) collective-permute-start(bf16[256,256]{1,0:T(8,128)(2,1)S(1)} %get-tuple-element.66), channel_id=1, source_target_pairs={{0,8},{4,12},{8,0},{12,4},{16,24},{20,28},{24,16},{28,20},{1,9},{5... | collective-permute-start | bytes 393224 | tf_op jit(solution)/shard_map/ppermute | solution.py:121
  31.8 11.6 %copy-start = (bf16[2,256,1280]{2,1,0:T(8,128)(2,1)S(1)}, bf16[2,256,1280]{2,1,0:T(8,128)(2,1)}, u32[]{:S(2)}) copy-start(bf16[2,256,1280]{2,1,0:T(8,128)(2,1)} %refs_4_) | copy-start | bytes 3932164
  31.8 14.3 %collective-permute-start.15 = (bf16[576,256]{1,0:T(8,128)(2,1)S(1)}, bf16[576,256]{1,0:T(8,128)(2,1)S(1)}, u32[]{:S(2)}, u32[]{:S(2)}) collective-permute-start(bf16[576,256]{1,0:T(8,128)(2,1)S(1)} %slice.47), channel_id=1, source_target_pairs={{0,8},{4,12},{8,0},{12,4},{16,24},{20,28},{24,16},{28,20},{1,9},{5... | collective-permute-start | bytes 884744 | tf_op jit(solution)/shard_map/ppermute | solution.py:121
  39.7 10.9 %collective-permute-start.16 = (bf16[704,256]{1,0:T(8,128)(2,1)S(1)}, bf16[704,256]{1,0:T(8,128)(2,1)S(1)}, u32[]{:S(2)}, u32[]{:S(2)}) collective-permute-start(bf16[704,256]{1,0:T(8,128)(2,1)S(1)} %slice.48), channel_id=1, source_target_pairs={{0,16},{4,20},{8,24},{12,28},{16,0},{20,4},{24,8},{28,12},{1,17},{... | collective-permute-start | bytes 1081352 | tf_op jit(solution)/shard_map/ppermute | solution.py:121
  42.8 7.8 %collective-permute-start.13 = (f32[128,1024]{1,0:T(8,128)S(1)}, f32[128,1024]{1,0:T(8,128)S(1)}, u32[]{:S(2)}, u32[]{:S(2)}) collective-permute-start(f32[128,1024]{1,0:T(8,128)S(1)} %get-tuple-element.74), channel_id=1, source_target_pairs={{0,4},{4,0},{8,12},{12,8},{16,20},{20,16},{24,28},{28,24},{1,5},{5... | collective-permute-start | bytes 1572872 | tf_op jit(solution)/shard_map/ppermute | solution.py:121
  42.9 7.8 %collective-permute-start.14 = (f32[128,512]{1,0:T(8,128)S(1)}, f32[128,512]{1,0:T(8,128)S(1)}, u32[]{:S(2)}, u32[]{:S(2)}) collective-permute-start(f32[128,512]{1,0:T(8,128)S(1)} %get-tuple-element.75), channel_id=1, source_target_pairs={{0,4},{4,0},{8,12},{12,8},{16,20},{20,16},{24,28},{28,24},{1,5},{5... | collective-permute-start | bytes 786440 | tf_op jit(solution)/shard_map/ppermute | solution.py:121
  43.5 17.7 %collective-permute-start.19 = (bf16[256,1280]{1,0:T(8,128)(2,1)S(1)}, bf16[256,1280]{1,0:T(8,128)(2,1)S(1)}, u32[]{:S(2)}, u32[]{:S(2)}) collective-permute-start(bf16[256,1280]{1,0:T(8,128)(2,1)S(1)} %get-tuple-element.115), channel_id=1, source_target_pairs={{0,8},{4,12},{8,0},{12,4},{16,24},{20,28},{24,16},{28,20},{1,9},{5... | collective-permute-start | bytes 1966088 | tf_op jit(solution)/shard_map/ppermute | solution.py:121
  46.1 7.3 %copy-start.4 = (bf16[576,256]{1,0:T(8,128)(2,1)}, bf16[576,256]{1,0:T(8,128)(2,1)S(1)}, u32[]{:S(2)}) copy-start(bf16[576,256]{1,0:T(8,128)(2,1)S(1)} %collective-permute-done.15.low_in.refs_1_) | copy-start | bytes 884740
  46.1 18.8 %collective-permute-start.20 = (bf16[256,1280]{1,0:T(8,128)(2,1)S(1)}, bf16[256,1280]{1,0:T(8,128)(2,1)S(1)}, u32[]{:S(2)}, u32[]{:S(2)}) collective-permute-start(bf16[256,1280]{1,0:T(8,128)(2,1)S(1)} %get-tuple-element.114), channel_id=1, source_target_pairs={{0,16},{4,20},{8,24},{12,28},{16,0},{20,4},{24,8},{28,12},{1,17},{... | collective-permute-start | bytes 1966088 | tf_op jit(solution)/shard_map/ppermute | solution.py:121
  50.6 2.8 %copy-start.2 = (bf16[704,256]{1,0:T(8,128)(2,1)}, bf16[704,256]{1,0:T(8,128)(2,1)S(1)}, u32[]{:S(2)}) copy-start(bf16[704,256]{1,0:T(8,128)(2,1)S(1)} %collective-permute-done.16.high_in.refs_2_) | copy-start | bytes 1081348
  50.7 14.2 %collective-permute-start.17 = (bf16[128,1024]{1,0:T(8,128)(2,1)S(1)}, bf16[128,1024]{1,0:T(8,128)(2,1)S(1)}, u32[]{:S(2)}, u32[]{:S(2)}) collective-permute-start(bf16[128,1024]{1,0:T(8,128)(2,1)S(1)} %add_convert_fusion.own_ref), channel_id=1, source_target_pairs={{0,4},{4,8},{8,12},{12,16},{16,20},{20,24},{24,28},{1,5},{5,9},{9,... | collective-permute-start | bytes 786440 | tf_op jit(solution)/shard_map/ppermute | solution.py:478
  52.0 12.9 %collective-permute-start.18 = (bf16[128,1024]{1,0:T(8,128)(2,1)S(1)}, bf16[128,1024]{1,0:T(8,128)(2,1)S(1)}, u32[]{:S(2)}, u32[]{:S(2)}) collective-permute-start(bf16[128,1024]{1,0:T(8,128)(2,1)S(1)} %add_convert_fusion.own_ref), channel_id=1, source_target_pairs={{4,0},{8,4},{12,8},{16,12},{20,16},{24,20},{28,24},{5,1},{9,5},{13... | collective-permute-start | bytes 786440 | tf_op jit(solution)/shard_map/ppermute | solution.py:479
  53.4 0.8 copy-start.12
  54.3 12.3 %copy-start.11 = (bf16[2,704,256]{2,1,0:T(8,128)(2,1)}, bf16[2,704,256]{2,1,0:T(8,128)(2,1)S(1)}, u32[]{:S(2)}) copy-start(bf16[2,704,256]{2,1,0:T(8,128)(2,1)S(1)} %get-tuple-element.104) | copy-start | bytes 2162692
  66.6 37.4 %collective-permute-start.28 = (bf16[2,256,1280]{2,1,0:T(8,128)(2,1)}, bf16[2,256,1280]{2,1,0:T(8,128)(2,1)}, u32[]{:S(2)}, u32[]{:S(2)}) collective-permute-start(bf16[2,256,1280]{2,1,0:T(8,128)(2,1)} %get-tuple-element.98), channel_id=1, source_target_pairs={{0,8},{4,12},{8,0},{12,4},{16,24},{20,28},{24,16},{28,20},{1,9},{5... | collective-permute-start | bytes 3932168 | tf_op jit(solution)/shard_map/ppermute | solution.py:121
  67.2 36.8 %collective-permute-start.29 = (bf16[2,256,1280]{2,1,0:T(8,128)(2,1)}, bf16[2,256,1280]{2,1,0:T(8,128)(2,1)}, u32[]{:S(2)}, u32[]{:S(2)}) collective-permute-start(bf16[2,256,1280]{2,1,0:T(8,128)(2,1)} %get-tuple-element.99), channel_id=1, source_target_pairs={{0,16},{4,20},{8,24},{12,28},{16,0},{20,4},{24,8},{28,12},{1,17},{... | collective-permute-start | bytes 3932168 | tf_op jit(solution)/shard_map/ppermute | solution.py:121
  69.1 4.1 %copy-start.8 = (bf16[512,256]{1,0:T(8,128)(2,1)S(1)}, bf16[512,256]{1,0:T(8,128)(2,1)}, u32[]{:S(2)}) copy-start(bf16[512,256]{1,0:T(8,128)(2,1)} %refs_0_.5) | copy-start | bytes 786436
  71.8 1.4 %collective-permute-start.21 = (bf16[128,512]{1,0:T(8,128)(2,1)S(1)}, bf16[128,512]{1,0:T(8,128)(2,1)S(1)}, u32[]{:S(2)}, u32[]{:S(2)}) collective-permute-start(bf16[128,512]{1,0:T(8,128)(2,1)S(1)} %attention.1.own_in_ref), channel_id=1, source_target_pairs={{0,4},{4,0},{8,12},{12,8},{16,20},{20,16},{24,28},{28,24},{1,5},{5... | collective-permute-start | bytes 393224 | tf_op jit(solution)/shard_map/ppermute | solution.py:121
  74.3 8.0 %collective-permute-start.24 = (bf16[256,256]{1,0:T(8,128)(2,1)S(1)}, bf16[256,256]{1,0:T(8,128)(2,1)S(1)}, u32[]{:S(2)}, u32[]{:S(2)}) collective-permute-start(bf16[256,256]{1,0:T(8,128)(2,1)S(1)} %get-tuple-element.94), channel_id=1, source_target_pairs={{0,3},{1,0},{2,1},{3,2},{4,7},{5,4},{6,5},{7,6},{8,11},{9,8},{10,9... | collective-permute-start | bytes 393224 | tf_op jit(solution)/shard_map/ppermute | solution.py:121
  78.3 11.6 %collective-permute-start.23 = (bf16[256,256]{1,0:T(8,128)(2,1)S(1)}, bf16[256,256]{1,0:T(8,128)(2,1)S(1)}, u32[]{:S(2)}, u32[]{:S(2)}) collective-permute-start(bf16[256,256]{1,0:T(8,128)(2,1)S(1)} %get-tuple-element.93), channel_id=1, source_target_pairs={{0,2},{1,3},{2,0},{3,1},{4,6},{5,7},{6,4},{7,5},{8,10},{9,11},{10,... | collective-permute-start | bytes 393224 | tf_op jit(solution)/shard_map/ppermute | solution.py:121
  78.4 11.6 %collective-permute-start.22 = (bf16[256,256]{1,0:T(8,128)(2,1)S(1)}, bf16[256,256]{1,0:T(8,128)(2,1)S(1)}, u32[]{:S(2)}, u32[]{:S(2)}) collective-permute-start(bf16[256,256]{1,0:T(8,128)(2,1)S(1)} %get-tuple-element.92), channel_id=1, source_target_pairs={{0,1},{1,2},{2,3},{3,0},{4,5},{5,6},{6,7},{7,4},{8,9},{9,10},{10,1... | collective-permute-start | bytes 393224 | tf_op jit(solution)/shard_map/ppermute | solution.py:121
  90.1 5.4 %collective-permute-start.27 = (bf16[256,256]{1,0:T(8,128)(2,1)S(1)}, bf16[256,256]{1,0:T(8,128)(2,1)S(1)}, u32[]{:S(2)}, u32[]{:S(2)}) collective-permute-start(bf16[256,256]{1,0:T(8,128)(2,1)S(1)} %add_convert_fusion.1.refs_0_), channel_id=1, source_target_pairs={{0,3},{1,0},{2,1},{3,2},{4,7},{5,4},{6,5},{7,6},{8,11},{9,8},{10,9... | collective-permute-start | bytes 393224 | tf_op jit(solution)/shard_map/ppermute | solution.py:121
  92.3 8.6 %collective-permute-start.25 = (bf16[256,256]{1,0:T(8,128)(2,1)S(1)}, bf16[256,256]{1,0:T(8,128)(2,1)S(1)}, u32[]{:S(2)}, u32[]{:S(2)}) collective-permute-start(bf16[256,256]{1,0:T(8,128)(2,1)S(1)} %add_convert_fusion.1.refs_0_), channel_id=1, source_target_pairs={{0,1},{1,2},{2,3},{3,0},{4,5},{5,6},{6,7},{7,4},{8,9},{9,10},{10,1... | collective-permute-start | bytes 393224 | tf_op jit(solution)/shard_map/ppermute | solution.py:121
  92.8 11.1 %collective-permute-start.26 = (bf16[256,256]{1,0:T(8,128)(2,1)S(1)}, bf16[256,256]{1,0:T(8,128)(2,1)S(1)}, u32[]{:S(2)}, u32[]{:S(2)}) collective-permute-start(bf16[256,256]{1,0:T(8,128)(2,1)S(1)} %add_convert_fusion.1.refs_0_), channel_id=1, source_target_pairs={{0,2},{1,3},{2,0},{3,1},{4,6},{5,7},{6,4},{7,5},{8,10},{9,11},{10,... | collective-permute-start | bytes 393224 | tf_op jit(solution)/shard_map/ppermute | solution.py:121
  95.4 18.3 %collective-permute-start.32 = (bf16[2,704,256]{2,1,0:T(8,128)(2,1)}, bf16[2,704,256]{2,1,0:T(8,128)(2,1)S(1)}, u32[]{:S(2)}, u32[]{:S(2)}) collective-permute-start(bf16[2,704,256]{2,1,0:T(8,128)(2,1)} %copy-done.11), channel_id=1, source_target_pairs={{0,8},{4,12},{8,0},{12,4},{16,24},{20,28},{24,16},{28,20},{1,9},{5... | collective-permute-start | bytes 2162696 | tf_op jit(solution)/shard_map/ppermute | solution.py:121
  100.9 12.1 %collective-permute-start.33 = (bf16[2,576,256]{2,1,0:T(8,128)(2,1)}, bf16[2,576,256]{2,1,0:T(8,128)(2,1)S(1)}, u32[]{:S(2)}, u32[]{:S(2)}) collective-permute-start(bf16[2,576,256]{2,1,0:T(8,128)(2,1)} %copy-done.12), channel_id=1, source_target_pairs={{0,16},{4,20},{8,24},{12,28},{16,0},{20,4},{24,8},{28,12},{1,17},{... | collective-permute-start | bytes 1769480 | tf_op jit(solution)/shard_map/ppermute | solution.py:121
  107.3 6.4 %collective-permute-start.30 = (bf16[128,2560]{1,0:T(8,128)(2,1)S(1)}, bf16[128,2560]{1,0:T(8,128)(2,1)S(1)}, u32[]{:S(2)}, u32[]{:S(2)}) collective-permute-start(bf16[128,2560]{1,0:T(8,128)(2,1)S(1)} %get-tuple-element.101), channel_id=1, source_target_pairs={{0,4},{4,0},{8,12},{12,8},{16,20},{20,16},{24,28},{28,24},{1,5},{5... | collective-permute-start | bytes 1966088 | tf_op jit(solution)/shard_map/ppermute | solution.py:121
  107.7 1.8 %collective-permute-start.31 = (f32[128]{0:T(128)S(1)}, f32[128]{0:T(128)S(1)}, u32[]{:S(2)}, u32[]{:S(2)}) collective-permute-start(f32[128]{0:T(128)S(1)} %slice.54), channel_id=1, source_target_pairs={{0,4},{4,0},{8,12},{12,8},{16,20},{20,16},{24,28},{28,24},{1,5},{5... | collective-permute-start | bytes 1544 | tf_op jit(solution)/shard_map/ppermute | solution.py:121
  113.9 2.0 %copy-start.3 = (bf16[704,256]{1,0:T(8,128)(2,1)S(1)}, bf16[704,256]{1,0:T(8,128)(2,1)}, u32[]{:S(2)}) copy-start(bf16[704,256]{1,0:T(8,128)(2,1)} %copy-done.2) | copy-start | bytes 1081348
  113.9 1.9 %copy-start.5 = (bf16[576,256]{1,0:T(8,128)(2,1)S(1)}, bf16[576,256]{1,0:T(8,128)(2,1)}, u32[]{:S(2)}) copy-start(bf16[576,256]{1,0:T(8,128)(2,1)} %copy-done.4) | copy-start | bytes 884740
  114.1 1.7 %collective-permute-start.34 = (bf16[128,1280]{1,0:T(8,128)(2,1)S(1)}, bf16[128,1280]{1,0:T(8,128)(2,1)S(1)}, u32[]{:S(2)}, u32[]{:S(2)}) collective-permute-start(bf16[128,1280]{1,0:T(8,128)(2,1)S(1)} %fusion.8.own_in_ref), channel_id=1, source_target_pairs={{0,4},{4,0},{8,12},{12,8},{16,20},{20,16},{24,28},{28,24},{1,5},{5... | collective-permute-start | bytes 983048 | tf_op jit(solution)/shard_map/ppermute | solution.py:121
  117.6 7.6 %collective-permute-start.37 = (bf16[256,256]{1,0:T(8,128)(2,1)S(1)}, bf16[256,256]{1,0:T(8,128)(2,1)S(1)}, u32[]{:S(2)}, u32[]{:S(2)}) collective-permute-start(bf16[256,256]{1,0:T(8,128)(2,1)S(1)} %get-tuple-element.112), channel_id=1, source_target_pairs={{0,3},{1,0},{2,1},{3,2},{4,7},{5,4},{6,5},{7,6},{8,11},{9,8},{10,9... | collective-permute-start | bytes 393224 | tf_op jit(solution)/shard_map/ppermute | solution.py:121
  121.2 11.8 %collective-permute-start.36 = (bf16[256,256]{1,0:T(8,128)(2,1)S(1)}, bf16[256,256]{1,0:T(8,128)(2,1)S(1)}, u32[]{:S(2)}, u32[]{:S(2)}) collective-permute-start(bf16[256,256]{1,0:T(8,128)(2,1)S(1)} %get-tuple-element.111), channel_id=1, source_target_pairs={{0,2},{1,3},{2,0},{3,1},{4,6},{5,7},{6,4},{7,5},{8,10},{9,11},{10,... | collective-permute-start | bytes 393224 | tf_op jit(solution)/shard_map/ppermute | solution.py:121
  121.2 11.8 %collective-permute-start.35 = (bf16[256,256]{1,0:T(8,128)(2,1)S(1)}, bf16[256,256]{1,0:T(8,128)(2,1)S(1)}, u32[]{:S(2)}, u32[]{:S(2)}) collective-permute-start(bf16[256,256]{1,0:T(8,128)(2,1)S(1)} %get-tuple-element.110), channel_id=1, source_target_pairs={{0,1},{1,2},{2,3},{3,0},{4,5},{5,6},{6,7},{7,4},{8,9},{9,10},{10,1... | collective-permute-start | bytes 393224 | tf_op jit(solution)/shard_map/ppermute | solution.py:121
  133.1 1.3 collective-permute-start.38

commit v9 on v8

--- a/solution.py
+++ b/solution.py
@@ -463,7 +463,8 @@
     cut = w_down.shape[0] * 9 // 20 // 16 * 16
     down_first = first_phase(w_down[:cut], w_down[cut:])
     in_first = first_phase(w_in[0], w_in[1])
-    kept, *out_far = lax.optimization_barrier((kept, *out_far))
+    gain_rows = gain_ffn.reshape(rows, -1)
+    kept, gain_rows, *out_far = lax.optimization_barrier((kept, gain_rows, *out_far))
     own_q, own_kv, send_q, send_kv = project_qkv(
         place, kept, received, [w_qkv, *qkv_near, *qkv_far]
     )
@@ -500,7 +501,7 @@
     scale = lax.rsqrt(squares / features + epsilon)[:, None]
     down_second = exchanged(after_all(packets, middle_blocks[-1]))
     own, send = project_ffn(
-        place, gain_ffn.reshape(rows, -1), middle_blocks, in_pieces
+        place, gain_rows, middle_blocks, in_pieces
     )
     scale, *down_second = lax.optimization_barrier((scale, *down_second))
     branches = (own + other_core(send).astype(jnp.float32)) * scale

time: 135 us -> 135 us (level)
  waiting for transfers between devices: 69.5 us -> 66.9 us
  local copies, waits for them, and re-layouts: 3.35 us -> 5.05 us
    ppermute x37, waiting for transfers between devices: 69.5 us -> 66.9 us  [exchange(): lax.ppermute(value, axis, [(i, partner(i) % count) for i in range(count)])]
    unnamed x28 -> x30, local copies, waits for them, and re-layouts: 1.78 us -> 3.48 us
    pallas_call x2, Pallas kernels: 0.07 us -> 1.71 us  [relayed(): pl.pallas_call(functools.partial(relay_kernel, axis), out_shape=(shape, s...]
    pallas_call x2, Pallas kernels: 1.75 us -> 0.26 us  [second_phase(): pl.pallas_call(packet_kernel, out_shape=tuple((jax.ShapeDtypeStruct((2, *...]
  transfers between devices with their start and end apart: 39 -> 39, of which waited for: 23 -> 22; matrix products, arithmetic and copies ran while one was open for 3% -> 3% of each run, Pallas kernels for 8% -> 9%
where the time goes in v9:
time: 135 us; the launch traced here: 134 us
  waiting for transfers between devices  66.9 us (50%)
  starting transfers between devices  43.4 us (32%)
  Pallas kernels  13.7 us (10%)
  local copies, waits for them, and re-layouts  5.05 us (4%)
  other arithmetic  4.24 us (3%)
    ppermute x37, waiting for transfers between devices, exchange(): lax.ppermute(value, axis, [(i, partner(i) % count) for i in range(count)])  66.9 us
    ppermute x37, starting transfers between devices, exchange(): lax.ppermute(value, axis, [(i, partner(i) % count) for i in range(count)])  40.8 us
    unnamed x30, local copies, waits for them, and re-layouts  3.48 us
    pallas_call x2, Pallas kernels, columns(): pl.pallas_call(functools.partial(columns_kernel, cut), out_shape=(jax.Sha...  3.27 us
  transfers between devices with their start and end apart: 39, of which 22 were waited for; matrix products, arithmetic and copies ran while one was open for 3% of the time, Pallas kernels for 9%

profile of v9, /device:TPU:0, one launch (start us, length us, event | category | flops | bytes accessed | tf_op | source)
XLA Modules:
  0.0 134.2 jit_solution(16636898818888892721)
XLA Ops:
  0.6 3.0 %collective-permute-start = (bf16[3,256,512]{2,1,0:T(8,128)(2,1)}, bf16[3,256,512]{2,1,0:T(8,128)(2,1)S(1)}, u32[]{:S(2)}, u32[]{:S(2)}) collective-permute-start(bf16[3,256,512]{2,1,0:T(8,128)(2,1)} %refs_0_.4), channel_id=1, source_target_pairs={{0,8},{4,12},{8,0},{12,4},{16,24},{20,28},{24,16},{28,20},{1,9},{5... | collective-permute-start | bytes 2359304 | tf_op jit(solution)/shard_map/ppermute | solution.py:121
  3.6 1.5 %collective-permute-start.1 = (bf16[3,256,512]{2,1,0:T(8,128)(2,1)}, bf16[3,256,512]{2,1,0:T(8,128)(2,1)S(1)}, u32[]{:S(2)}, u32[]{:S(2)}) collective-permute-start(bf16[3,256,512]{2,1,0:T(8,128)(2,1)} %refs_0_.4), channel_id=1, source_target_pairs={{0,16},{4,20},{8,24},{12,28},{16,0},{20,4},{24,8},{28,12},{1,17},{... | collective-permute-start | bytes 2359304 | tf_op jit(solution)/shard_map/ppermute | solution.py:121
  5.2 0.9 broadcast_select_fusion.1
  6.2 1.6 %collective-permute-start.2 = (bf16[128,512]{1,0:T(8,128)(2,1)}, bf16[128,512]{1,0:T(8,128)(2,1)S(1)}, u32[]{:S(2)}, u32[]{:S(2)}) collective-permute-start(bf16[128,512]{1,0:T(8,128)(2,1)} %refs_0_.3), channel_id=1, source_target_pairs={{0,1},{1,2},{2,3},{3,0},{4,5},{5,6},{6,7},{7,4},{8,9},{9,10},{10,1... | collective-permute-start | bytes 393224 | tf_op jit(solution)/shard_map/ppermute | solution.py:121
  7.8 2.6 %collective-permute-start.3 = (bf16[128,512]{1,0:T(8,128)(2,1)}, bf16[128,512]{1,0:T(8,128)(2,1)S(1)}, u32[]{:S(2)}, u32[]{:S(2)}) collective-permute-start(bf16[128,512]{1,0:T(8,128)(2,1)} %refs_0_.3), channel_id=1, source_target_pairs={{0,2},{1,3},{2,0},{3,1},{4,6},{5,7},{6,4},{7,5},{8,10},{9,11},{10,... | collective-permute-start | bytes 393224 | tf_op jit(solution)/shard_map/ppermute | solution.py:121
  10.4 1.3 %collective-permute-start.4 = (bf16[128,512]{1,0:T(8,128)(2,1)}, bf16[128,512]{1,0:T(8,128)(2,1)S(1)}, u32[]{:S(2)}, u32[]{:S(2)}) collective-permute-start(bf16[128,512]{1,0:T(8,128)(2,1)} %refs_0_.3), channel_id=1, source_target_pairs={{0,3},{1,0},{2,1},{3,2},{4,7},{5,4},{6,5},{7,6},{8,11},{9,8},{10,9... | collective-permute-start | bytes 393224 | tf_op jit(solution)/shard_map/ppermute | solution.py:121
  11.8 0.7 reshape.20.gain_ref
  12.5 0.7 pad_maximum_fusion.1
  13.2 1.4 %collective-permute-done.2.refs_1_ = bf16[128,512]{1,0:T(8,128)(2,1)S(1)} collective-permute-done((bf16[128,512]{1,0:T(8,128)(2,1)}, bf16[128,512]{1,0:T(8,128)(2,1)S(1)}, u32[]{:S(2)}, u32[]{:S(2)}) %collective-permute-start.2) | collective-permute-done | bytes 131104 | tf_op jit(solution)/shard_map/ppermute | solution.py:121
  14.6 0.5 collective-permute-start.6
  15.2 4.7 %collective-permute-done.3.refs_2_ = bf16[128,512]{1,0:T(8,128)(2,1)S(1)} collective-permute-done((bf16[128,512]{1,0:T(8,128)(2,1)}, bf16[128,512]{1,0:T(8,128)(2,1)S(1)}, u32[]{:S(2)}, u32[]{:S(2)}) %collective-permute-start.3) | collective-permute-done | bytes 131104 | tf_op jit(solution)/shard_map/ppermute | solution.py:121
  20.3 0.9 copy-done.5
  21.2 0.8 norm_tokens.1
  22.1 0.7 copy-done.7
  23.2 1.0 relay_qkv.1
  24.2 2.4 %collective-permute-start.11 = (bf16[3,256,256]{2,1,0:T(8,128)(2,1)}, bf16[3,256,256]{2,1,0:T(8,128)(2,1)}, u32[]{:S(2)}, u32[]{:S(2)}) collective-permute-start(bf16[3,256,256]{2,1,0:T(8,128)(2,1)} %get-tuple-element.73), channel_id=1, source_target_pairs={{0,16},{4,20},{8,24},{12,28},{16,0},{20,4},{24,8},{28,12},{1,17},{... | collective-permute-start | bytes 1179656 | tf_op jit(solution)/shard_map/ppermute | solution.py:121
  26.6 0.5 collective-permute-start.12
  27.2 0.6 masked_bias.1.bias_ref
  27.8 1.0 collective-permute-done.7.high_in.refs_2_
  28.8 0.7 copy-done.9
  29.5 0.7 relay_out.1
  30.2 1.3 collective-permute-start.9
  32.0 0.7 reshape.21.gain_ref
  32.8 1.6 %collective-permute-start.15 = (bf16[576,256]{1,0:T(8,128)(2,1)S(1)}, bf16[576,256]{1,0:T(8,128)(2,1)S(1)}, u32[]{:S(2)}, u32[]{:S(2)}) collective-permute-start(bf16[576,256]{1,0:T(8,128)(2,1)S(1)} %slice.47), channel_id=1, source_target_pairs={{0,8},{4,12},{8,0},{12,4},{16,24},{20,28},{24,16},{28,20},{1,9},{5... | collective-permute-start | bytes 884744 | tf_op jit(solution)/shard_map/ppermute | solution.py:121
  34.4 5.4 %collective-permute-done.9.refs_3_ = bf16[256,256]{1,0:T(8,128)(2,1)} collective-permute-done((bf16[256,256]{1,0:T(8,128)(2,1)}, bf16[256,256]{1,0:T(8,128)(2,1)}, u32[]{:S(2)}, u32[]{:S(2)}) %collective-permute-start.9) | collective-permute-done | bytes 131104 | tf_op jit(solution)/shard_map/ppermute | solution.py:121
  39.8 1.5 %collective-permute-start.16 = (bf16[704,256]{1,0:T(8,128)(2,1)S(1)}, bf16[704,256]{1,0:T(8,128)(2,1)S(1)}, u32[]{:S(2)}, u32[]{:S(2)}) collective-permute-start(bf16[704,256]{1,0:T(8,128)(2,1)S(1)} %slice.48), channel_id=1, source_target_pairs={{0,16},{4,20},{8,24},{12,28},{16,0},{20,4},{24,8},{28,12},{1,17},{... | collective-permute-start | bytes 1081352 | tf_op jit(solution)/shard_map/ppermute | solution.py:121
  41.7 1.1 copy-done.4
  42.8 2.1 %qkv.1 = (f32[128,512]{1,0:T(8,128)S(1)}, f32[128,1024]{1,0:T(8,128)S(1)}, f32[128,512]{1,0:T(8,128)S(1)}, f32[128,1024]{1,0:T(8,128)S(1)}) custom-call(s32[2]{0:T(128)S(1)} %pad_add_fusion.place_ref, bf16[4,128,256]{2,1,0:T(8,128)(2,1)S(1)} %copy-done.8, bf16[4,128,256]{2,1,0:T(8,128)(2,1)S(1)} %copy-done.10, bf16[3,256,512]{2,1,0:T(8,128)(2,1)S(1)} %copy-done.4, ...), custom_call_target="tpu_custom_call" | custom-call | flops 805306368 | bytes 3145728 | tf_op jit(solution)/shard_map/qkv/pallas_call | solution.py:297
  45.6 0.6 collective-permute-start.19
  46.2 0.9 collective-permute-done.15.low_in.refs_1_
  47.4 3.3 %collective-permute-done.16.high_in.refs_2_ = bf16[704,256]{1,0:T(8,128)(2,1)S(1)} collective-permute-done((bf16[704,256]{1,0:T(8,128)(2,1)S(1)}, bf16[704,256]{1,0:T(8,128)(2,1)S(1)}, u32[]{:S(2)}, u32[]{:S(2)}) %collective-permute-start.16) | collective-permute-done | bytes 360480 | tf_op jit(solution)/shard_map/ppermute | solution.py:121
  50.8 1.3 collective-permute-start.17
  52.1 1.3 collective-permute-start.18
  53.5 9.8 %collective-permute-done.19.low_in.refs_5_ = bf16[256,1280]{1,0:T(8,128)(2,1)S(1)} collective-permute-done((bf16[256,1280]{1,0:T(8,128)(2,1)S(1)}, bf16[256,1280]{1,0:T(8,128)(2,1)S(1)}, u32[]{:S(2)}, u32[]{:S(2)}) %collective-permute-start.19) | collective-permute-done | bytes 655392 | tf_op jit(solution)/shard_map/ppermute | solution.py:121
  63.3 2.1 %collective-permute-done.20.high_in.refs_6_ = bf16[256,1280]{1,0:T(8,128)(2,1)S(1)} collective-permute-done((bf16[256,1280]{1,0:T(8,128)(2,1)S(1)}, bf16[256,1280]{1,0:T(8,128)(2,1)S(1)}, u32[]{:S(2)}, u32[]{:S(2)}) %collective-permute-start.20) | collective-permute-done | bytes 655392 | tf_op jit(solution)/shard_map/ppermute | solution.py:121
  65.5 2.3 %collective-permute-start.28 = (bf16[2,256,1280]{2,1,0:T(8,128)(2,1)S(1)}, bf16[2,256,1280]{2,1,0:T(8,128)(2,1)S(1)}, u32[]{:S(2)}, u32[]{:S(2)}) collective-permute-start(bf16[2,256,1280]{2,1,0:T(8,128)(2,1)S(1)} %get-tuple-element.100), channel_id=1, source_target_pairs={{0,8},{4,12},{8,0},{12,4},{16,24},{20,28},{24,16},{28,20},{1,9},{5... | collective-permute-start | bytes 3932168 | tf_op jit(solution)/shard_map/ppermute | solution.py:121
  67.8 1.1 collective-permute-start.29
  69.0 2.7 %attention.1.own_in_ref = bf16[128,512]{1,0:T(8,128)(2,1)S(1)} custom-call(bf16[128,512]{1,0:T(8,128)(2,1)S(1)} %add_convert_fusion.2.q_ref, bf16[128,1024]{1,0:T(8,128)(2,1)S(1)} %collective-permute-done.17.low_ref, bf16[128,1024]{1,0:T(8,128)(2,1)S(1)} %add_convert_fusion.own_ref, bf16[128,1024]{1,0:T(8,128)(2,1)S(1)} %collective-permute-done.18.high_ref, ...), custom_call_target="tpu_custom_call" | custom-call | flops 100663296 | bytes 1572864 | tf_op jit(solution)/shard_map/attention/pallas_call | solution.py:106
  71.7 1.3 collective-permute-done.21.other_in_ref
  73.1 1.6 %attention_out.1 = (f32[256,256]{1,0:T(8,128)S(1)}, bf16[256,256]{1,0:T(8,128)(2,1)S(1)}, bf16[256,256]{1,0:T(8,128)(2,1)S(1)}, bf16[256,256]{1,0:T(8,128)(2,1)S(1)}) custom-call(s32[2]{0:T(128)S(1)} %pad_add_fusion.place_ref, bf16[128,512]{1,0:T(8,128)(2,1)S(1)} %attention.1.own_in_ref, bf16[128,512]{1,0:T(8,128)(2,1)S(1)} %collective-permute-done.21.other_in_ref, ...), custom_call_target="tpu_custom_call" | custom-call | flops 268435456 | bytes 1048576 | tf_op jit(solution)/shard_map/attention_out/pallas_call | solution.py:388
  74.6 3.3 %collective-permute-start.24 = (bf16[256,256]{1,0:T(8,128)(2,1)S(1)}, bf16[256,256]{1,0:T(8,128)(2,1)S(1)}, u32[]{:S(2)}, u32[]{:S(2)}) collective-permute-start(bf16[256,256]{1,0:T(8,128)(2,1)S(1)} %get-tuple-element.96), channel_id=1, source_target_pairs={{0,3},{1,0},{2,1},{3,2},{4,7},{5,4},{6,5},{7,6},{8,11},{9,8},{10,9... | collective-permute-start | bytes 393224 | tf_op jit(solution)/shard_map/ppermute | solution.py:121
  78.0 1.6 %collective-permute-start.22 = (bf16[256,256]{1,0:T(8,128)(2,1)S(1)}, bf16[256,256]{1,0:T(8,128)(2,1)S(1)}, u32[]{:S(2)}, u32[]{:S(2)}) collective-permute-start(bf16[256,256]{1,0:T(8,128)(2,1)S(1)} %get-tuple-element.94), channel_id=1, source_target_pairs={{0,1},{1,2},{2,3},{3,0},{4,5},{5,6},{6,7},{7,4},{8,9},{9,10},{10,1... | collective-permute-start | bytes 393224 | tf_op jit(solution)/shard_map/ppermute | solution.py:121
  79.6 0.7 pad_maximum_fusion
  80.3 1.6 %collective-permute-done.24 = bf16[256,256]{1,0:T(8,128)(2,1)S(1)} collective-permute-done((bf16[256,256]{1,0:T(8,128)(2,1)S(1)}, bf16[256,256]{1,0:T(8,128)(2,1)S(1)}, u32[]{:S(2)}, u32[]{:S(2)}) %collective-permute-start.24) | collective-permute-done | bytes 131104 | tf_op jit(solution)/shard_map/ppermute | solution.py:121
  81.9 8.0 %collective-permute-done.23 = bf16[256,256]{1,0:T(8,128)(2,1)S(1)} collective-permute-done((bf16[256,256]{1,0:T(8,128)(2,1)S(1)}, bf16[256,256]{1,0:T(8,128)(2,1)S(1)}, u32[]{:S(2)}, u32[]{:S(2)}) %collective-permute-start.23) | collective-permute-done | bytes 131104 | tf_op jit(solution)/shard_map/ppermute | solution.py:121
  90.0 1.2 collective-permute-start.27
  91.2 0.9 collective-permute-start.25
  92.1 2.8 %collective-permute-start.26 = (bf16[256,256]{1,0:T(8,128)(2,1)S(1)}, bf16[256,256]{1,0:T(8,128)(2,1)S(1)}, u32[]{:S(2)}, u32[]{:S(2)}) collective-permute-start(bf16[256,256]{1,0:T(8,128)(2,1)S(1)} %add_convert_fusion.1.refs_0_), channel_id=1, source_target_pairs={{0,2},{1,3},{2,0},{3,1},{4,6},{5,7},{6,4},{7,5},{8,10},{9,11},{10,... | collective-permute-start | bytes 393224 | tf_op jit(solution)/shard_map/ppermute | solution.py:121
  95.1 2.0 %collective-permute-start.32 = (bf16[2,704,256]{2,1,0:T(8,128)(2,1)S(1)}, bf16[2,704,256]{2,1,0:T(8,128)(2,1)S(1)}, u32[]{:S(2)}, u32[]{:S(2)}) collective-permute-start(bf16[2,704,256]{2,1,0:T(8,128)(2,1)S(1)} %get-tuple-element.106), channel_id=1, source_target_pairs={{0,8},{4,12},{8,0},{12,4},{16,24},{20,28},{24,16},{28,20},{1,9},{5... | collective-permute-start | bytes 2162696 | tf_op jit(solution)/shard_map/ppermute | solution.py:121
  97.2 4.4 %collective-permute-done.25.refs_1_ = bf16[256,256]{1,0:T(8,128)(2,1)S(1)} collective-permute-done((bf16[256,256]{1,0:T(8,128)(2,1)S(1)}, bf16[256,256]{1,0:T(8,128)(2,1)S(1)}, u32[]{:S(2)}, u32[]{:S(2)}) %collective-permute-start.25) | collective-permute-done | bytes 131104 | tf_op jit(solution)/shard_map/ppermute | solution.py:121
  101.6 1.0 collective-permute-start.33
  102.6 2.2 %collective-permute-done.26.refs_2_ = bf16[256,256]{1,0:T(8,128)(2,1)S(1)} collective-permute-done((bf16[256,256]{1,0:T(8,128)(2,1)S(1)}, bf16[256,256]{1,0:T(8,128)(2,1)S(1)}, u32[]{:S(2)}, u32[]{:S(2)}) %collective-permute-start.26) | collective-permute-done | bytes 131104 | tf_op jit(solution)/shard_map/ppermute | solution.py:121
  104.9 2.2 %ffn_in.1 = (f32[128,2560]{1,0:T(8,128)S(1)}, bf16[128,2560]{1,0:T(8,128)(2,1)S(1)}) custom-call(s32[2]{0:T(128)S(1)} %pad_add_fusion.place_ref, f32[8,256]{1,0:T(8,128)S(1)} %reshape.21.gain_ref, bf16[256,256]{1,0:T(8,128)(2,1)S(1)} %add_convert_fusion.1.refs_0_, bf16[256,256]{1,0:T(8,128)(2,1)S(1)} %collective-permute-done.25.refs_1_, ...), custom_call_target="tpu_custom_call" | custom-call | flops 1342177280 | bytes 5242880 | tf_op jit(solution)/shard_map/ffn_in/pallas_call | solution.py:333
  107.4 0.6 collective-permute-start.31
  107.9 1.3 collective-permute-done.31
  109.2 5.5 %collective-permute-done.33.refs_4_ = bf16[2,576,256]{2,1,0:T(8,128)(2,1)S(1)} collective-permute-done((bf16[2,576,256]{2,1,0:T(8,128)(2,1)S(1)}, bf16[2,576,256]{2,1,0:T(8,128)(2,1)S(1)}, u32[]{:S(2)}, u32[]{:S(2)}) %collective-permute-start.33) | collective-permute-done | bytes 589856 | tf_op jit(solution)/shard_map/ppermute | solution.py:121
  115.2 1.6 %collective-permute-done.34.other_in_ref = bf16[128,1280]{1,0:T(8,128)(2,1)S(1)} collective-permute-done((bf16[128,1280]{1,0:T(8,128)(2,1)S(1)}, bf16[128,1280]{1,0:T(8,128)(2,1)S(1)}, u32[]{:S(2)}, u32[]{:S(2)}) %collective-permute-start.34) | collective-permute-done | bytes 327712 | tf_op jit(solution)/shard_map/ppermute | solution.py:121
  116.8 1.7 %ffn_out.1 = (f32[256,256]{1,0:T(8,128)S(1)}, bf16[256,256]{1,0:T(8,128)(2,1)S(1)}, bf16[256,256]{1,0:T(8,128)(2,1)S(1)}, bf16[256,256]{1,0:T(8,128)(2,1)S(1)}) custom-call(s32[2]{0:T(128)S(1)} %pad_add_fusion.place_ref, bf16[128,1280]{1,0:T(8,128)(2,1)S(1)} %fusion.8.own_in_ref, bf16[128,1280]{1,0:T(8,128)(2,1)S(1)} %collective-permute-done.34.other_in_ref, ...), custom_call_target="tpu_custom_call" | custom-call | flops 671088640 | bytes 2621440 | tf_op jit(solution)/shard_map/ffn_out/pallas_call | solution.py:388
  118.5 1.6 %collective-permute-start.37 = (bf16[256,256]{1,0:T(8,128)(2,1)S(1)}, bf16[256,256]{1,0:T(8,128)(2,1)S(1)}, u32[]{:S(2)}, u32[]{:S(2)}) collective-permute-start(bf16[256,256]{1,0:T(8,128)(2,1)S(1)} %get-tuple-element.114), channel_id=1, source_target_pairs={{0,3},{1,0},{2,1},{3,2},{4,7},{5,4},{6,5},{7,6},{8,11},{9,8},{10,9... | collective-permute-start | bytes 393224 | tf_op jit(solution)/shard_map/ppermute | solution.py:121
  120.1 1.8 %collective-permute-start.35 = (bf16[256,256]{1,0:T(8,128)(2,1)S(1)}, bf16[256,256]{1,0:T(8,128)(2,1)S(1)}, u32[]{:S(2)}, u32[]{:S(2)}) collective-permute-start(bf16[256,256]{1,0:T(8,128)(2,1)S(1)} %get-tuple-element.112), channel_id=1, source_target_pairs={{0,1},{1,2},{2,3},{3,0},{4,5},{5,6},{6,7},{7,4},{8,9},{9,10},{10,1... | collective-permute-start | bytes 393224 | tf_op jit(solution)/shard_map/ppermute | solution.py:121
  121.9 3.0 %collective-permute-done.37 = bf16[256,256]{1,0:T(8,128)(2,1)S(1)} collective-permute-done((bf16[256,256]{1,0:T(8,128)(2,1)S(1)}, bf16[256,256]{1,0:T(8,128)(2,1)S(1)}, u32[]{:S(2)}, u32[]{:S(2)}) %collective-permute-start.37) | collective-permute-done | bytes 131104 | tf_op jit(solution)/shard_map/ppermute | solution.py:121
  124.9 7.2 %collective-permute-done.36 = bf16[256,256]{1,0:T(8,128)(2,1)S(1)} collective-permute-done((bf16[256,256]{1,0:T(8,128)(2,1)S(1)}, bf16[256,256]{1,0:T(8,128)(2,1)S(1)}, u32[]{:S(2)}, u32[]{:S(2)}) %collective-permute-start.36) | collective-permute-done | bytes 131104 | tf_op jit(solution)/shard_map/ppermute | solution.py:121
  132.3 1.2 collective-permute-done.38
  133.6 0.7 maximum_select_fusion
  (81 shorter events, 4.9 us)
Async XLA Ops:
  0.6 22.2 %collective-permute-start = (bf16[3,256,512]{2,1,0:T(8,128)(2,1)}, bf16[3,256,512]{2,1,0:T(8,128)(2,1)S(1)}, u32[]{:S(2)}, u32[]{:S(2)}) collective-permute-start(bf16[3,256,512]{2,1,0:T(8,128)(2,1)} %refs_0_.4), channel_id=1, source_target_pairs={{0,8},{4,12},{8,0},{12,4},{16,24},{20,28},{24,16},{28,20},{1,9},{5... | collective-permute-start | bytes 2359304 | tf_op jit(solution)/shard_map/ppermute | solution.py:121
  3.6 19.6 %collective-permute-start.1 = (bf16[3,256,512]{2,1,0:T(8,128)(2,1)}, bf16[3,256,512]{2,1,0:T(8,128)(2,1)S(1)}, u32[]{:S(2)}, u32[]{:S(2)}) collective-permute-start(bf16[3,256,512]{2,1,0:T(8,128)(2,1)} %refs_0_.4), channel_id=1, source_target_pairs={{0,16},{4,20},{8,24},{12,28},{16,0},{20,4},{24,8},{28,12},{1,17},{... | collective-permute-start | bytes 2359304 | tf_op jit(solution)/shard_map/ppermute | solution.py:121
  5.2 22.0 %copy-start.14 = (s32[255]{0:T(256)S(1)}, s32[255]{0:T(256)}, u32[]{:S(2)}) copy-start(s32[255]{0:T(256)} %param.13) | copy-start | bytes 3064
  5.2 22.0 %copy-start.11 = (s32[1024]{0:T(1024)S(1)}, s32[1024]{0:T(1024)}, u32[]{:S(2)}) copy-start(s32[1024]{0:T(1024)} %param.12) | copy-start | bytes 12292
  5.2 22.0 %copy-start.12 = (f32[32,8]{0,1:T(8,128)S(1)}, f32[32,8]{0,1:T(8,128)}, u32[]{:S(2)}) copy-start(f32[32,8]{0,1:T(8,128)} %param.16) | copy-start | bytes 3076
  6.1 4.3 %collective-permute-start.5 = (bf16[128,256]{1,0:T(8,128)(2,1)S(1)}, bf16[128,256]{1,0:T(8,128)(2,1)S(1)}, u32[]{:S(2)}, u32[]{:S(2)}) collective-permute-start(bf16[128,256]{1,0:T(8,128)(2,1)S(1)} %get-tuple-element.123), channel_id=1, source_target_pairs={{0,4},{4,0},{8,12},{12,8},{16,20},{20,16},{24,28},{28,24},{1,5},{5... | collective-permute-start | bytes 196616 | tf_op jit(solution)/shard_map/ppermute | solution.py:121
  6.2 8.5 %collective-permute-start.2 = (bf16[128,512]{1,0:T(8,128)(2,1)}, bf16[128,512]{1,0:T(8,128)(2,1)S(1)}, u32[]{:S(2)}, u32[]{:S(2)}) collective-permute-start(bf16[128,512]{1,0:T(8,128)(2,1)} %refs_0_.3), channel_id=1, source_target_pairs={{0,1},{1,2},{2,3},{3,0},{4,5},{5,6},{6,7},{7,4},{8,9},{9,10},{10,1... | collective-permute-start | bytes 393224 | tf_op jit(solution)/shard_map/ppermute | solution.py:121
  7.8 12.0 %collective-permute-start.3 = (bf16[128,512]{1,0:T(8,128)(2,1)}, bf16[128,512]{1,0:T(8,128)(2,1)S(1)}, u32[]{:S(2)}, u32[]{:S(2)}) collective-permute-start(bf16[128,512]{1,0:T(8,128)(2,1)} %refs_0_.3), channel_id=1, source_target_pairs={{0,2},{1,3},{2,0},{3,1},{4,6},{5,7},{6,4},{7,5},{8,10},{9,11},{10,... | collective-permute-start | bytes 393224 | tf_op jit(solution)/shard_map/ppermute | solution.py:121
  10.4 9.9 %collective-permute-start.4 = (bf16[128,512]{1,0:T(8,128)(2,1)}, bf16[128,512]{1,0:T(8,128)(2,1)S(1)}, u32[]{:S(2)}, u32[]{:S(2)}) collective-permute-start(bf16[128,512]{1,0:T(8,128)(2,1)} %refs_0_.3), channel_id=1, source_target_pairs={{0,3},{1,0},{2,1},{3,2},{4,7},{5,4},{6,5},{7,6},{8,11},{9,8},{10,9... | collective-permute-start | bytes 393224 | tf_op jit(solution)/shard_map/ppermute | solution.py:121
  14.6 13.2 %collective-permute-start.6 = (bf16[512,256]{1,0:T(8,128)(2,1)}, bf16[512,256]{1,0:T(8,128)(2,1)S(1)}, u32[]{:S(2)}, u32[]{:S(2)}) collective-permute-start(bf16[512,256]{1,0:T(8,128)(2,1)} %refs_0_.5), channel_id=1, source_target_pairs={{0,8},{4,12},{8,0},{12,4},{16,24},{20,28},{24,16},{28,20},{1,9},{5... | collective-permute-start | bytes 786440 | tf_op jit(solution)/shard_map/ppermute | solution.py:121
  19.8 9.0 %collective-permute-start.7 = (bf16[512,256]{1,0:T(8,128)(2,1)}, bf16[512,256]{1,0:T(8,128)(2,1)S(1)}, u32[]{:S(2)}, u32[]{:S(2)}) collective-permute-start(bf16[512,256]{1,0:T(8,128)(2,1)} %refs_0_.5), channel_id=1, source_target_pairs={{0,16},{4,20},{8,24},{12,28},{16,0},{20,4},{24,8},{28,12},{1,17},{... | collective-permute-start | bytes 786440 | tf_op jit(solution)/shard_map/ppermute | solution.py:121
  20.3 0.9 copy-start.5
  22.1 0.7 copy-start.7
  23.2 3.9 %copy-start.2 = (bf16[3,256,512]{2,1,0:T(8,128)(2,1)}, bf16[3,256,512]{2,1,0:T(8,128)(2,1)S(1)}, u32[]{:S(2)}) copy-start(bf16[3,256,512]{2,1,0:T(8,128)(2,1)S(1)} %collective-permute-done.1.high_in.refs_2_) | copy-start | bytes 2359300
  23.2 5.6 %collective-permute-start.8 = (bf16[4,128,256]{2,1,0:T(8,128)(2,1)S(1)}, bf16[4,128,256]{2,1,0:T(8,128)(2,1)S(1)}, u32[]{:S(2)}, u32[]{:S(2)}) collective-permute-start(bf16[4,128,256]{2,1,0:T(8,128)(2,1)S(1)} %get-tuple-element.63), channel_id=1, source_target_pairs={{0,4},{4,0},{8,12},{12,8},{16,20},{20,16},{24,28},{28,24},{1,5},{5... | collective-permute-start | bytes 786440 | tf_op jit(solution)/shard_map/ppermute | solution.py:121
  24.2 8.5 %copy-start.1 = (bf16[1280,256]{1,0:T(8,128)(2,1)S(1)}, bf16[1280,256]{1,0:T(8,128)(2,1)}, u32[]{:S(2)}) copy-start(bf16[1280,256]{1,0:T(8,128)(2,1)} %refs_0_.6) | copy-start | bytes 1966084
  24.2 17.5 %collective-permute-start.11 = (bf16[3,256,256]{2,1,0:T(8,128)(2,1)}, bf16[3,256,256]{2,1,0:T(8,128)(2,1)}, u32[]{:S(2)}, u32[]{:S(2)}) collective-permute-start(bf16[3,256,256]{2,1,0:T(8,128)(2,1)} %get-tuple-element.73), channel_id=1, source_target_pairs={{0,16},{4,20},{8,24},{12,28},{16,0},{20,4},{24,8},{28,12},{1,17},{... | collective-permute-start | bytes 1179656 | tf_op jit(solution)/shard_map/ppermute | solution.py:121
  26.6 15.1 %collective-permute-start.12 = (bf16[3,256,256]{2,1,0:T(8,128)(2,1)}, bf16[3,256,256]{2,1,0:T(8,128)(2,1)}, u32[]{:S(2)}, u32[]{:S(2)}) collective-permute-start(bf16[3,256,256]{2,1,0:T(8,128)(2,1)} %get-tuple-element.74), channel_id=1, source_target_pairs={{0,8},{4,12},{8,0},{12,4},{16,24},{20,28},{24,16},{28,20},{1,9},{5... | collective-permute-start | bytes 1179656 | tf_op jit(solution)/shard_map/ppermute | solution.py:121
  28.8 0.7 copy-start.9
  30.2 9.6 %collective-permute-start.9 = (bf16[256,256]{1,0:T(8,128)(2,1)}, bf16[256,256]{1,0:T(8,128)(2,1)}, u32[]{:S(2)}, u32[]{:S(2)}) collective-permute-start(bf16[256,256]{1,0:T(8,128)(2,1)} %get-tuple-element.66), channel_id=1, source_target_pairs={{0,16},{4,20},{8,24},{12,28},{16,0},{20,4},{24,8},{28,12},{1,17},{... | collective-permute-start | bytes 393224 | tf_op jit(solution)/shard_map/ppermute | solution.py:121
  31.5 10.2 %collective-permute-start.10 = (bf16[256,256]{1,0:T(8,128)(2,1)}, bf16[256,256]{1,0:T(8,128)(2,1)}, u32[]{:S(2)}, u32[]{:S(2)}) collective-permute-start(bf16[256,256]{1,0:T(8,128)(2,1)} %get-tuple-element.67), channel_id=1, source_target_pairs={{0,8},{4,12},{8,0},{12,4},{16,24},{20,28},{24,16},{28,20},{1,9},{5... | collective-permute-start | bytes 393224 | tf_op jit(solution)/shard_map/ppermute | solution.py:121
  32.7 9.0 %copy-start.3 = (bf16[3,256,512]{2,1,0:T(8,128)(2,1)S(1)}, bf16[3,256,512]{2,1,0:T(8,128)(2,1)}, u32[]{:S(2)}) copy-start(bf16[3,256,512]{2,1,0:T(8,128)(2,1)} %copy-done.2) | copy-start | bytes 2359300
  32.7 9.0 %copy-start.8 = (bf16[4,128,256]{2,1,0:T(8,128)(2,1)S(1)}, bf16[4,128,256]{2,1,0:T(8,128)(2,1)}, u32[]{:S(2)}) copy-start(bf16[4,128,256]{2,1,0:T(8,128)(2,1)} %copy-done.7) | copy-start | bytes 786436
  32.7 9.0 %copy-start.10 = (bf16[4,128,256]{2,1,0:T(8,128)(2,1)S(1)}, bf16[4,128,256]{2,1,0:T(8,128)(2,1)}, u32[]{:S(2)}) copy-start(bf16[4,128,256]{2,1,0:T(8,128)(2,1)} %copy-done.9) | copy-start | bytes 786436
  32.8 12.7 %copy-start = (bf16[2,256,1280]{2,1,0:T(8,128)(2,1)S(1)}, bf16[2,256,1280]{2,1,0:T(8,128)(2,1)}, u32[]{:S(2)}) copy-start(bf16[2,256,1280]{2,1,0:T(8,128)(2,1)} %refs_4_) | copy-start | bytes 3932164
  32.8 14.3 %collective-permute-start.15 = (bf16[576,256]{1,0:T(8,128)(2,1)S(1)}, bf16[576,256]{1,0:T(8,128)(2,1)S(1)}, u32[]{:S(2)}, u32[]{:S(2)}) collective-permute-start(bf16[576,256]{1,0:T(8,128)(2,1)S(1)} %slice.47), channel_id=1, source_target_pairs={{0,8},{4,12},{8,0},{12,4},{16,24},{20,28},{24,16},{28,20},{1,9},{5... | collective-permute-start | bytes 884744 | tf_op jit(solution)/shard_map/ppermute | solution.py:121
  39.8 10.9 %collective-permute-start.16 = (bf16[704,256]{1,0:T(8,128)(2,1)S(1)}, bf16[704,256]{1,0:T(8,128)(2,1)S(1)}, u32[]{:S(2)}, u32[]{:S(2)}) collective-permute-start(bf16[704,256]{1,0:T(8,128)(2,1)S(1)} %slice.48), channel_id=1, source_target_pairs={{0,16},{4,20},{8,24},{12,28},{16,0},{20,4},{24,8},{28,12},{1,17},{... | collective-permute-start | bytes 1081352 | tf_op jit(solution)/shard_map/ppermute | solution.py:121
  41.7 1.1 copy-start.4
  45.0 5.8 %collective-permute-start.13 = (f32[128,1024]{1,0:T(8,128)S(1)}, f32[128,1024]{1,0:T(8,128)S(1)}, u32[]{:S(2)}, u32[]{:S(2)}) collective-permute-start(f32[128,1024]{1,0:T(8,128)S(1)} %get-tuple-element.76), channel_id=1, source_target_pairs={{0,4},{4,0},{8,12},{12,8},{16,20},{20,16},{24,28},{28,24},{1,5},{5... | collective-permute-start | bytes 1572872 | tf_op jit(solution)/shard_map/ppermute | solution.py:121
  45.0 5.7 %collective-permute-start.14 = (f32[128,512]{1,0:T(8,128)S(1)}, f32[128,512]{1,0:T(8,128)S(1)}, u32[]{:S(2)}, u32[]{:S(2)}) collective-permute-start(f32[128,512]{1,0:T(8,128)S(1)} %get-tuple-element.77), channel_id=1, source_target_pairs={{0,4},{4,0},{8,12},{12,8},{16,20},{20,16},{24,28},{28,24},{1,5},{5... | collective-permute-start | bytes 786440 | tf_op jit(solution)/shard_map/ppermute | solution.py:121
  45.6 17.7 %collective-permute-start.19 = (bf16[256,1280]{1,0:T(8,128)(2,1)S(1)}, bf16[256,1280]{1,0:T(8,128)(2,1)S(1)}, u32[]{:S(2)}, u32[]{:S(2)}) collective-permute-start(bf16[256,1280]{1,0:T(8,128)(2,1)S(1)} %get-tuple-element.117), channel_id=1, source_target_pairs={{0,8},{4,12},{8,0},{12,4},{16,24},{20,28},{24,16},{28,20},{1,9},{5... | collective-permute-start | bytes 1966088 | tf_op jit(solution)/shard_map/ppermute | solution.py:121
  47.1 18.2 %collective-permute-start.20 = (bf16[256,1280]{1,0:T(8,128)(2,1)S(1)}, bf16[256,1280]{1,0:T(8,128)(2,1)S(1)}, u32[]{:S(2)}, u32[]{:S(2)}) collective-permute-start(bf16[256,1280]{1,0:T(8,128)(2,1)S(1)} %get-tuple-element.116), channel_id=1, source_target_pairs={{0,16},{4,20},{8,24},{12,28},{16,0},{20,4},{24,8},{28,12},{1,17},{... | collective-permute-start | bytes 1966088 | tf_op jit(solution)/shard_map/ppermute | solution.py:121
  50.8 14.6 %collective-permute-start.17 = (bf16[128,1024]{1,0:T(8,128)(2,1)S(1)}, bf16[128,1024]{1,0:T(8,128)(2,1)S(1)}, u32[]{:S(2)}, u32[]{:S(2)}) collective-permute-start(bf16[128,1024]{1,0:T(8,128)(2,1)S(1)} %add_convert_fusion.own_ref), channel_id=1, source_target_pairs={{0,4},{4,8},{8,12},{12,16},{16,20},{20,24},{24,28},{1,5},{5,9},{9,... | collective-permute-start | bytes 786440 | tf_op jit(solution)/shard_map/ppermute | solution.py:479
  52.1 13.3 %collective-permute-start.18 = (bf16[128,1024]{1,0:T(8,128)(2,1)S(1)}, bf16[128,1024]{1,0:T(8,128)(2,1)S(1)}, u32[]{:S(2)}, u32[]{:S(2)}) collective-permute-start(bf16[128,1024]{1,0:T(8,128)(2,1)S(1)} %add_convert_fusion.own_ref), channel_id=1, source_target_pairs={{4,0},{8,4},{12,8},{16,12},{20,16},{24,20},{28,24},{5,1},{9,5},{13... | collective-permute-start | bytes 786440 | tf_op jit(solution)/shard_map/ppermute | solution.py:480
  65.5 39.3 %collective-permute-start.28 = (bf16[2,256,1280]{2,1,0:T(8,128)(2,1)S(1)}, bf16[2,256,1280]{2,1,0:T(8,128)(2,1)S(1)}, u32[]{:S(2)}, u32[]{:S(2)}) collective-permute-start(bf16[2,256,1280]{2,1,0:T(8,128)(2,1)S(1)} %get-tuple-element.100), channel_id=1, source_target_pairs={{0,8},{4,12},{8,0},{12,4},{16,24},{20,28},{24,16},{28,20},{1,9},{5... | collective-permute-start | bytes 3932168 | tf_op jit(solution)/shard_map/ppermute | solution.py:121
  67.8 37.1 %collective-permute-start.29 = (bf16[2,256,1280]{2,1,0:T(8,128)(2,1)S(1)}, bf16[2,256,1280]{2,1,0:T(8,128)(2,1)S(1)}, u32[]{:S(2)}, u32[]{:S(2)}) collective-permute-start(bf16[2,256,1280]{2,1,0:T(8,128)(2,1)S(1)} %get-tuple-element.101), channel_id=1, source_target_pairs={{0,16},{4,20},{8,24},{12,28},{16,0},{20,4},{24,8},{28,12},{1,17},{... | collective-permute-start | bytes 3932168 | tf_op jit(solution)/shard_map/ppermute | solution.py:121
  69.0 4.1 %copy-start.6 = (bf16[512,256]{1,0:T(8,128)(2,1)S(1)}, bf16[512,256]{1,0:T(8,128)(2,1)}, u32[]{:S(2)}) copy-start(bf16[512,256]{1,0:T(8,128)(2,1)} %refs_0_.5) | copy-start | bytes 786436
  71.6 18.3 %copy-start.13 = (bf16[256,256]{1,0:T(8,128)(2,1)S(1)}, bf16[256,256]{1,0:T(8,128)(2,1)}, u32[]{:S(2)}) copy-start(bf16[256,256]{1,0:T(8,128)(2,1)} %pad_maximum_fusion.1) | copy-start | bytes 393220
  71.7 1.4 %collective-permute-start.21 = (bf16[128,512]{1,0:T(8,128)(2,1)S(1)}, bf16[128,512]{1,0:T(8,128)(2,1)S(1)}, u32[]{:S(2)}, u32[]{:S(2)}) collective-permute-start(bf16[128,512]{1,0:T(8,128)(2,1)S(1)} %attention.1.own_in_ref), channel_id=1, source_target_pairs={{0,4},{4,0},{8,12},{12,8},{16,20},{20,16},{24,28},{28,24},{1,5},{5... | collective-permute-start | bytes 393224 | tf_op jit(solution)/shard_map/ppermute | solution.py:121
  74.6 7.3 %collective-permute-start.24 = (bf16[256,256]{1,0:T(8,128)(2,1)S(1)}, bf16[256,256]{1,0:T(8,128)(2,1)S(1)}, u32[]{:S(2)}, u32[]{:S(2)}) collective-permute-start(bf16[256,256]{1,0:T(8,128)(2,1)S(1)} %get-tuple-element.96), channel_id=1, source_target_pairs={{0,3},{1,0},{2,1},{3,2},{4,7},{5,4},{6,5},{7,6},{8,11},{9,8},{10,9... | collective-permute-start | bytes 393224 | tf_op jit(solution)/shard_map/ppermute | solution.py:121
  77.9 12.0 %collective-permute-start.23 = (bf16[256,256]{1,0:T(8,128)(2,1)S(1)}, bf16[256,256]{1,0:T(8,128)(2,1)S(1)}, u32[]{:S(2)}, u32[]{:S(2)}) collective-permute-start(bf16[256,256]{1,0:T(8,128)(2,1)S(1)} %get-tuple-element.95), channel_id=1, source_target_pairs={{0,2},{1,3},{2,0},{3,1},{4,6},{5,7},{6,4},{7,5},{8,10},{9,11},{10,... | collective-permute-start | bytes 393224 | tf_op jit(solution)/shard_map/ppermute | solution.py:121
  78.0 12.0 %collective-permute-start.22 = (bf16[256,256]{1,0:T(8,128)(2,1)S(1)}, bf16[256,256]{1,0:T(8,128)(2,1)S(1)}, u32[]{:S(2)}, u32[]{:S(2)}) collective-permute-start(bf16[256,256]{1,0:T(8,128)(2,1)S(1)} %get-tuple-element.94), channel_id=1, source_target_pairs={{0,1},{1,2},{2,3},{3,0},{4,5},{5,6},{6,7},{7,4},{8,9},{9,10},{10,1... | collective-permute-start | bytes 393224 | tf_op jit(solution)/shard_map/ppermute | solution.py:121
  90.0 5.1 %collective-permute-start.27 = (bf16[256,256]{1,0:T(8,128)(2,1)S(1)}, bf16[256,256]{1,0:T(8,128)(2,1)S(1)}, u32[]{:S(2)}, u32[]{:S(2)}) collective-permute-start(bf16[256,256]{1,0:T(8,128)(2,1)S(1)} %add_convert_fusion.1.refs_0_), channel_id=1, source_target_pairs={{0,3},{1,0},{2,1},{3,2},{4,7},{5,4},{6,5},{7,6},{8,11},{9,8},{10,9... | collective-permute-start | bytes 393224 | tf_op jit(solution)/shard_map/ppermute | solution.py:121
  91.2 10.4 %collective-permute-start.25 = (bf16[256,256]{1,0:T(8,128)(2,1)S(1)}, bf16[256,256]{1,0:T(8,128)(2,1)S(1)}, u32[]{:S(2)}, u32[]{:S(2)}) collective-permute-start(bf16[256,256]{1,0:T(8,128)(2,1)S(1)} %add_convert_fusion.1.refs_0_), channel_id=1, source_target_pairs={{0,1},{1,2},{2,3},{3,0},{4,5},{5,6},{6,7},{7,4},{8,9},{9,10},{10,1... | collective-permute-start | bytes 393224 | tf_op jit(solution)/shard_map/ppermute | solution.py:121
  92.1 12.7 %collective-permute-start.26 = (bf16[256,256]{1,0:T(8,128)(2,1)S(1)}, bf16[256,256]{1,0:T(8,128)(2,1)S(1)}, u32[]{:S(2)}, u32[]{:S(2)}) collective-permute-start(bf16[256,256]{1,0:T(8,128)(2,1)S(1)} %add_convert_fusion.1.refs_0_), channel_id=1, source_target_pairs={{0,2},{1,3},{2,0},{3,1},{4,6},{5,7},{6,4},{7,5},{8,10},{9,11},{10,... | collective-permute-start | bytes 393224 | tf_op jit(solution)/shard_map/ppermute | solution.py:121
  95.1 19.6 %collective-permute-start.32 = (bf16[2,704,256]{2,1,0:T(8,128)(2,1)S(1)}, bf16[2,704,256]{2,1,0:T(8,128)(2,1)S(1)}, u32[]{:S(2)}, u32[]{:S(2)}) collective-permute-start(bf16[2,704,256]{2,1,0:T(8,128)(2,1)S(1)} %get-tuple-element.106), channel_id=1, source_target_pairs={{0,8},{4,12},{8,0},{12,4},{16,24},{20,28},{24,16},{28,20},{1,9},{5... | collective-permute-start | bytes 2162696 | tf_op jit(solution)/shard_map/ppermute | solution.py:121
  101.6 13.1 %collective-permute-start.33 = (bf16[2,576,256]{2,1,0:T(8,128)(2,1)S(1)}, bf16[2,576,256]{2,1,0:T(8,128)(2,1)S(1)}, u32[]{:S(2)}, u32[]{:S(2)}) collective-permute-start(bf16[2,576,256]{2,1,0:T(8,128)(2,1)S(1)} %get-tuple-element.107), channel_id=1, source_target_pairs={{0,16},{4,20},{8,24},{12,28},{16,0},{20,4},{24,8},{28,12},{1,17},{... | collective-permute-start | bytes 1769480 | tf_op jit(solution)/shard_map/ppermute | solution.py:121
  107.0 7.6 %collective-permute-start.30 = (bf16[128,2560]{1,0:T(8,128)(2,1)S(1)}, bf16[128,2560]{1,0:T(8,128)(2,1)S(1)}, u32[]{:S(2)}, u32[]{:S(2)}) collective-permute-start(bf16[128,2560]{1,0:T(8,128)(2,1)S(1)} %get-tuple-element.103), channel_id=1, source_target_pairs={{0,4},{4,0},{8,12},{12,8},{16,20},{20,16},{24,28},{28,24},{1,5},{5... | collective-permute-start | bytes 1966088 | tf_op jit(solution)/shard_map/ppermute | solution.py:121
  107.4 1.8 %collective-permute-start.31 = (f32[128]{0:T(128)S(1)}, f32[128]{0:T(128)S(1)}, u32[]{:S(2)}, u32[]{:S(2)}) collective-permute-start(f32[128]{0:T(128)S(1)} %slice.54), channel_id=1, source_target_pairs={{0,4},{4,0},{8,12},{12,8},{16,20},{20,16},{24,28},{28,24},{1,5},{5... | collective-permute-start | bytes 1544 | tf_op jit(solution)/shard_map/ppermute | solution.py:121
  115.1 1.7 %collective-permute-start.34 = (bf16[128,1280]{1,0:T(8,128)(2,1)S(1)}, bf16[128,1280]{1,0:T(8,128)(2,1)S(1)}, u32[]{:S(2)}, u32[]{:S(2)}) collective-permute-start(bf16[128,1280]{1,0:T(8,128)(2,1)S(1)} %fusion.8.own_in_ref), channel_id=1, source_target_pairs={{0,4},{4,0},{8,12},{12,8},{16,20},{20,16},{24,28},{28,24},{1,5},{5... | collective-permute-start | bytes 983048 | tf_op jit(solution)/shard_map/ppermute | solution.py:121
  118.5 6.4 %collective-permute-start.37 = (bf16[256,256]{1,0:T(8,128)(2,1)S(1)}, bf16[256,256]{1,0:T(8,128)(2,1)S(1)}, u32[]{:S(2)}, u32[]{:S(2)}) collective-permute-start(bf16[256,256]{1,0:T(8,128)(2,1)S(1)} %get-tuple-element.114), channel_id=1, source_target_pairs={{0,3},{1,0},{2,1},{3,2},{4,7},{5,4},{6,5},{7,6},{8,11},{9,8},{10,9... | collective-permute-start | bytes 393224 | tf_op jit(solution)/shard_map/ppermute | solution.py:121
  120.1 12.0 %collective-permute-start.36 = (bf16[256,256]{1,0:T(8,128)(2,1)S(1)}, bf16[256,256]{1,0:T(8,128)(2,1)S(1)}, u32[]{:S(2)}, u32[]{:S(2)}) collective-permute-start(bf16[256,256]{1,0:T(8,128)(2,1)S(1)} %get-tuple-element.113), channel_id=1, source_target_pairs={{0,2},{1,3},{2,0},{3,1},{4,6},{5,7},{6,4},{7,5},{8,10},{9,11},{10,... | collective-permute-start | bytes 393224 | tf_op jit(solution)/shard_map/ppermute | solution.py:121
  120.1 12.0 %collective-permute-start.35 = (bf16[256,256]{1,0:T(8,128)(2,1)S(1)}, bf16[256,256]{1,0:T(8,128)(2,1)S(1)}, u32[]{:S(2)}, u32[]{:S(2)}) collective-permute-start(bf16[256,256]{1,0:T(8,128)(2,1)S(1)} %get-tuple-element.112), channel_id=1, source_target_pairs={{0,1},{1,2},{2,3},{3,0},{4,5},{5,6},{6,7},{7,4},{8,9},{9,10},{10,1... | collective-permute-start | bytes 393224 | tf_op jit(solution)/shard_map/ppermute | solution.py:121
  132.2 1.3 collective-permute-start.38

commit v10 on v9

--- a/solution.py
+++ b/solution.py
@@ -503,12 +503,12 @@
     own, send = project_ffn(
         place, gain_rows, middle_blocks, in_pieces
     )
-    scale, *down_second = lax.optimization_barrier((scale, *down_second))
     branches = (own + other_core(send).astype(jnp.float32)) * scale
     inner = branches.shape[1] // 2
     hidden = (
         jax.nn.gelu(branches[:, :inner], approximate=True) * branches[:, inner:]
     ).astype(jnp.bfloat16)
+    hidden, *down_second = lax.optimization_barrier((hidden, *down_second))
     own, *sends = columns(
         place, hidden, other_core(hidden), [w_down, *down_first, *down_second], "ffn_out", cut
     )

time: 135 us -> 146 us (1.081)
  waiting for transfers between devices: 66.9 us -> 79.4 us
  starting transfers between devices: 43.4 us -> 41.9 us
    ppermute x37, waiting for transfers between devices: 66.9 us -> 79.4 us  [exchange(): lax.ppermute(value, axis, [(i, partner(i) % count) for i in range(count)])]
    ppermute x37, starting transfers between devices: 40.8 us -> 39.3 us  [exchange(): lax.ppermute(value, axis, [(i, partner(i) % count) for i in range(count)])]
  transfers between devices with their start and end apart: 39 -> 39, of which waited for: 22 -> 22; matrix products, arithmetic and copies ran while one was open for 3% -> 3% of each run, Pallas kernels for 9% -> 7%
where the time goes in v10:
time: 146 us; the launch traced here: 145 us
  waiting for transfers between devices  79.4 us (54%)
  starting transfers between devices  41.9 us (29%)
  Pallas kernels  13.7 us (9%)
  local copies, waits for them, and re-layouts  5.05 us (3%)
  other arithmetic  4.23 us (3%)
    ppermute x37, waiting for transfers between devices, exchange(): lax.ppermute(value, axis, [(i, partner(i) % count) for i in range(count)])  79.4 us
    ppermute x37, starting transfers between devices, exchange(): lax.ppermute(value, axis, [(i, partner(i) % count) for i in range(count)])  39.3 us
    unnamed x30, local copies, waits for them, and re-layouts  3.48 us
    pallas_call x2, Pallas kernels, columns(): pl.pallas_call(functools.partial(columns_kernel, cut), out_shape=(jax.Sha...  3.27 us
  transfers between devices with their start and end apart: 39, of which 22 were waited for; matrix products, arithmetic and copies ran while one was open for 3% of the time, Pallas kernels for 7%

profile of v10, /device:TPU:0, one launch (start us, length us, event | category | flops | bytes accessed | tf_op | source)
XLA Modules:
  0.0 145.2 jit_solution(11613438254672666320)
XLA Ops:
  0.6 3.0 %collective-permute-start = (bf16[3,256,512]{2,1,0:T(8,128)(2,1)}, bf16[3,256,512]{2,1,0:T(8,128)(2,1)S(1)}, u32[]{:S(2)}, u32[]{:S(2)}) collective-permute-start(bf16[3,256,512]{2,1,0:T(8,128)(2,1)} %refs_0_.4), channel_id=1, source_target_pairs={{0,8},{4,12},{8,0},{12,4},{16,24},{20,28},{24,16},{28,20},{1,9},{5... | collective-permute-start | bytes 2359304 | tf_op jit(solution)/shard_map/ppermute | solution.py:121
  3.6 1.5 %collective-permute-start.1 = (bf16[3,256,512]{2,1,0:T(8,128)(2,1)}, bf16[3,256,512]{2,1,0:T(8,128)(2,1)S(1)}, u32[]{:S(2)}, u32[]{:S(2)}) collective-permute-start(bf16[3,256,512]{2,1,0:T(8,128)(2,1)} %refs_0_.4), channel_id=1, source_target_pairs={{0,16},{4,20},{8,24},{12,28},{16,0},{20,4},{24,8},{28,12},{1,17},{... | collective-permute-start | bytes 2359304 | tf_op jit(solution)/shard_map/ppermute | solution.py:121
  5.2 0.9 broadcast_select_fusion.1
  6.2 1.6 %collective-permute-start.2 = (bf16[128,512]{1,0:T(8,128)(2,1)}, bf16[128,512]{1,0:T(8,128)(2,1)S(1)}, u32[]{:S(2)}, u32[]{:S(2)}) collective-permute-start(bf16[128,512]{1,0:T(8,128)(2,1)} %refs_0_.3), channel_id=1, source_target_pairs={{0,1},{1,2},{2,3},{3,0},{4,5},{5,6},{6,7},{7,4},{8,9},{9,10},{10,1... | collective-permute-start | bytes 393224 | tf_op jit(solution)/shard_map/ppermute | solution.py:121
  7.8 2.6 %collective-permute-start.3 = (bf16[128,512]{1,0:T(8,128)(2,1)}, bf16[128,512]{1,0:T(8,128)(2,1)S(1)}, u32[]{:S(2)}, u32[]{:S(2)}) collective-permute-start(bf16[128,512]{1,0:T(8,128)(2,1)} %refs_0_.3), channel_id=1, source_target_pairs={{0,2},{1,3},{2,0},{3,1},{4,6},{5,7},{6,4},{7,5},{8,10},{9,11},{10,... | collective-permute-start | bytes 393224 | tf_op jit(solution)/shard_map/ppermute | solution.py:121
  10.4 1.3 collective-permute-start.4
  11.8 0.7 reshape.21.gain_ref
  12.5 0.7 pad_maximum_fusion.1
  13.2 1.4 collective-permute-done.2.refs_1_
  14.6 0.5 collective-permute-start.6
  15.2 4.7 %collective-permute-done.3.refs_2_ = bf16[128,512]{1,0:T(8,128)(2,1)S(1)} collective-permute-done((bf16[128,512]{1,0:T(8,128)(2,1)}, bf16[128,512]{1,0:T(8,128)(2,1)S(1)}, u32[]{:S(2)}, u32[]{:S(2)}) %collective-permute-start.3) | collective-permute-done | bytes 131104 | tf_op jit(solution)/shard_map/ppermute | solution.py:121
  20.3 0.9 copy-done.5
  21.2 0.8 norm_tokens.1
  22.1 0.7 copy-done.7
  23.2 1.0 relay_qkv.1
  24.2 2.4 %collective-permute-start.11 = (bf16[3,256,256]{2,1,0:T(8,128)(2,1)}, bf16[3,256,256]{2,1,0:T(8,128)(2,1)}, u32[]{:S(2)}, u32[]{:S(2)}) collective-permute-start(bf16[3,256,256]{2,1,0:T(8,128)(2,1)} %get-tuple-element.73), channel_id=1, source_target_pairs={{0,16},{4,20},{8,24},{12,28},{16,0},{20,4},{24,8},{28,12},{1,17},{... | collective-permute-start | bytes 1179656 | tf_op jit(solution)/shard_map/ppermute | solution.py:121
  26.6 0.5 collective-permute-start.12
  27.2 0.6 masked_bias.1.bias_ref
  27.8 1.0 collective-permute-done.7.high_in.refs_2_
  28.8 0.7 copy-done.9
  29.5 0.7 relay_out.1
  30.2 1.3 collective-permute-start.9
  32.0 0.7 reshape.22.gain_ref
  32.8 1.6 %collective-permute-start.15 = (bf16[576,256]{1,0:T(8,128)(2,1)S(1)}, bf16[576,256]{1,0:T(8,128)(2,1)S(1)}, u32[]{:S(2)}, u32[]{:S(2)}) collective-permute-start(bf16[576,256]{1,0:T(8,128)(2,1)S(1)} %slice.47), channel_id=1, source_target_pairs={{0,8},{4,12},{8,0},{12,4},{16,24},{20,28},{24,16},{28,20},{1,9},{5... | collective-permute-start | bytes 884744 | tf_op jit(solution)/shard_map/ppermute | solution.py:121
  34.4 5.4 %collective-permute-done.9.refs_3_ = bf16[256,256]{1,0:T(8,128)(2,1)} collective-permute-done((bf16[256,256]{1,0:T(8,128)(2,1)}, bf16[256,256]{1,0:T(8,128)(2,1)}, u32[]{:S(2)}, u32[]{:S(2)}) %collective-permute-start.9) | collective-permute-done | bytes 131104 | tf_op jit(solution)/shard_map/ppermute | solution.py:121
  39.8 1.5 %collective-permute-start.16 = (bf16[704,256]{1,0:T(8,128)(2,1)S(1)}, bf16[704,256]{1,0:T(8,128)(2,1)S(1)}, u32[]{:S(2)}, u32[]{:S(2)}) collective-permute-start(bf16[704,256]{1,0:T(8,128)(2,1)S(1)} %slice.48), channel_id=1, source_target_pairs={{0,16},{4,20},{8,24},{12,28},{16,0},{20,4},{24,8},{28,12},{1,17},{... | collective-permute-start | bytes 1081352 | tf_op jit(solution)/shard_map/ppermute | solution.py:121
  41.7 1.1 copy-done.4
  42.8 2.1 %qkv.1 = (f32[128,512]{1,0:T(8,128)S(1)}, f32[128,1024]{1,0:T(8,128)S(1)}, f32[128,512]{1,0:T(8,128)S(1)}, f32[128,1024]{1,0:T(8,128)S(1)}) custom-call(s32[2]{0:T(128)S(1)} %pad_add_fusion.place_ref, bf16[4,128,256]{2,1,0:T(8,128)(2,1)S(1)} %copy-done.8, bf16[4,128,256]{2,1,0:T(8,128)(2,1)S(1)} %copy-done.10, bf16[3,256,512]{2,1,0:T(8,128)(2,1)S(1)} %copy-done.4, ...), custom_call_target="tpu_custom_call" | custom-call | flops 805306368 | bytes 3145728 | tf_op jit(solution)/shard_map/qkv/pallas_call | solution.py:297
  45.6 0.6 collective-permute-start.19
  46.2 0.9 collective-permute-done.15.low_in.refs_1_
  47.4 3.3 %collective-permute-done.16.high_in.refs_2_ = bf16[704,256]{1,0:T(8,128)(2,1)S(1)} collective-permute-done((bf16[704,256]{1,0:T(8,128)(2,1)S(1)}, bf16[704,256]{1,0:T(8,128)(2,1)S(1)}, u32[]{:S(2)}, u32[]{:S(2)}) %collective-permute-start.16) | collective-permute-done | bytes 360480 | tf_op jit(solution)/shard_map/ppermute | solution.py:121
  50.8 1.3 collective-permute-start.17
  52.1 1.3 collective-permute-start.18
  53.5 9.8 %collective-permute-done.19.low_in.refs_5_ = bf16[256,1280]{1,0:T(8,128)(2,1)S(1)} collective-permute-done((bf16[256,1280]{1,0:T(8,128)(2,1)S(1)}, bf16[256,1280]{1,0:T(8,128)(2,1)S(1)}, u32[]{:S(2)}, u32[]{:S(2)}) %collective-permute-start.19) | collective-permute-done | bytes 655392 | tf_op jit(solution)/shard_map/ppermute | solution.py:121
  63.3 2.1 %collective-permute-done.20.high_in.refs_6_ = bf16[256,1280]{1,0:T(8,128)(2,1)S(1)} collective-permute-done((bf16[256,1280]{1,0:T(8,128)(2,1)S(1)}, bf16[256,1280]{1,0:T(8,128)(2,1)S(1)}, u32[]{:S(2)}, u32[]{:S(2)}) %collective-permute-start.20) | collective-permute-done | bytes 655392 | tf_op jit(solution)/shard_map/ppermute | solution.py:121
  65.5 2.3 %collective-permute-start.28 = (bf16[2,256,1280]{2,1,0:T(8,128)(2,1)S(1)}, bf16[2,256,1280]{2,1,0:T(8,128)(2,1)S(1)}, u32[]{:S(2)}, u32[]{:S(2)}) collective-permute-start(bf16[2,256,1280]{2,1,0:T(8,128)(2,1)S(1)} %get-tuple-element.100), channel_id=1, source_target_pairs={{0,8},{4,12},{8,0},{12,4},{16,24},{20,28},{24,16},{28,20},{1,9},{5... | collective-permute-start | bytes 3932168 | tf_op jit(solution)/shard_map/ppermute | solution.py:121
  67.8 1.1 collective-permute-start.29
  69.0 2.7 %attention.1.own_in_ref = bf16[128,512]{1,0:T(8,128)(2,1)S(1)} custom-call(bf16[128,512]{1,0:T(8,128)(2,1)S(1)} %add_convert_fusion.2.q_ref, bf16[128,1024]{1,0:T(8,128)(2,1)S(1)} %collective-permute-done.17.low_ref, bf16[128,1024]{1,0:T(8,128)(2,1)S(1)} %add_convert_fusion.own_ref, bf16[128,1024]{1,0:T(8,128)(2,1)S(1)} %collective-permute-done.18.high_ref, ...), custom_call_target="tpu_custom_call" | custom-call | flops 100663296 | bytes 1572864 | tf_op jit(solution)/shard_map/attention/pallas_call | solution.py:106
  71.7 1.3 collective-permute-done.21.other_in_ref
  73.1 1.6 %attention_out.1 = (f32[256,256]{1,0:T(8,128)S(1)}, bf16[256,256]{1,0:T(8,128)(2,1)S(1)}, bf16[256,256]{1,0:T(8,128)(2,1)S(1)}, bf16[256,256]{1,0:T(8,128)(2,1)S(1)}) custom-call(s32[2]{0:T(128)S(1)} %pad_add_fusion.place_ref, bf16[128,512]{1,0:T(8,128)(2,1)S(1)} %attention.1.own_in_ref, bf16[128,512]{1,0:T(8,128)(2,1)S(1)} %collective-permute-done.21.other_in_ref, ...), custom_call_target="tpu_custom_call" | custom-call | flops 268435456 | bytes 1048576 | tf_op jit(solution)/shard_map/attention_out/pallas_call | solution.py:388
  74.6 3.3 %collective-permute-start.24 = (bf16[256,256]{1,0:T(8,128)(2,1)S(1)}, bf16[256,256]{1,0:T(8,128)(2,1)S(1)}, u32[]{:S(2)}, u32[]{:S(2)}) collective-permute-start(bf16[256,256]{1,0:T(8,128)(2,1)S(1)} %get-tuple-element.96), channel_id=1, source_target_pairs={{0,3},{1,0},{2,1},{3,2},{4,7},{5,4},{6,5},{7,6},{8,11},{9,8},{10,9... | collective-permute-start | bytes 393224 | tf_op jit(solution)/shard_map/ppermute | solution.py:121
  78.0 1.6 %collective-permute-start.22 = (bf16[256,256]{1,0:T(8,128)(2,1)S(1)}, bf16[256,256]{1,0:T(8,128)(2,1)S(1)}, u32[]{:S(2)}, u32[]{:S(2)}) collective-permute-start(bf16[256,256]{1,0:T(8,128)(2,1)S(1)} %get-tuple-element.94), channel_id=1, source_target_pairs={{0,1},{1,2},{2,3},{3,0},{4,5},{5,6},{6,7},{7,4},{8,9},{9,10},{10,1... | collective-permute-start | bytes 393224 | tf_op jit(solution)/shard_map/ppermute | solution.py:121
  79.6 0.7 pad_maximum_fusion
  80.3 1.6 %collective-permute-done.24 = bf16[256,256]{1,0:T(8,128)(2,1)S(1)} collective-permute-done((bf16[256,256]{1,0:T(8,128)(2,1)S(1)}, bf16[256,256]{1,0:T(8,128)(2,1)S(1)}, u32[]{:S(2)}, u32[]{:S(2)}) %collective-permute-start.24) | collective-permute-done | bytes 131104 | tf_op jit(solution)/shard_map/ppermute | solution.py:121
  81.9 8.0 %collective-permute-done.23 = bf16[256,256]{1,0:T(8,128)(2,1)S(1)} collective-permute-done((bf16[256,256]{1,0:T(8,128)(2,1)S(1)}, bf16[256,256]{1,0:T(8,128)(2,1)S(1)}, u32[]{:S(2)}, u32[]{:S(2)}) %collective-permute-start.23) | collective-permute-done | bytes 131104 | tf_op jit(solution)/shard_map/ppermute | solution.py:121
  90.0 1.2 collective-permute-start.27
  91.2 0.9 collective-permute-start.25
  92.1 2.8 %collective-permute-start.26 = (bf16[256,256]{1,0:T(8,128)(2,1)S(1)}, bf16[256,256]{1,0:T(8,128)(2,1)S(1)}, u32[]{:S(2)}, u32[]{:S(2)}) collective-permute-start(bf16[256,256]{1,0:T(8,128)(2,1)S(1)} %add_convert_fusion.1.refs_0_), channel_id=1, source_target_pairs={{0,2},{1,3},{2,0},{3,1},{4,6},{5,7},{6,4},{7,5},{8,10},{9,11},{10,... | collective-permute-start | bytes 393224 | tf_op jit(solution)/shard_map/ppermute | solution.py:121
  95.2 6.4 %collective-permute-done.25.refs_1_ = bf16[256,256]{1,0:T(8,128)(2,1)S(1)} collective-permute-done((bf16[256,256]{1,0:T(8,128)(2,1)S(1)}, bf16[256,256]{1,0:T(8,128)(2,1)S(1)}, u32[]{:S(2)}, u32[]{:S(2)}) %collective-permute-start.25) | collective-permute-done | bytes 131104 | tf_op jit(solution)/shard_map/ppermute | solution.py:121
  101.6 3.3 %collective-permute-done.26.refs_2_ = bf16[256,256]{1,0:T(8,128)(2,1)S(1)} collective-permute-done((bf16[256,256]{1,0:T(8,128)(2,1)S(1)}, bf16[256,256]{1,0:T(8,128)(2,1)S(1)}, u32[]{:S(2)}, u32[]{:S(2)}) %collective-permute-start.26) | collective-permute-done | bytes 131104 | tf_op jit(solution)/shard_map/ppermute | solution.py:121
  104.9 2.2 %ffn_in.1 = (f32[128,2560]{1,0:T(8,128)S(1)}, bf16[128,2560]{1,0:T(8,128)(2,1)S(1)}) custom-call(s32[2]{0:T(128)S(1)} %pad_add_fusion.place_ref, f32[8,256]{1,0:T(8,128)S(1)} %reshape.22.gain_ref, bf16[256,256]{1,0:T(8,128)(2,1)S(1)} %add_convert_fusion.1.refs_0_, bf16[256,256]{1,0:T(8,128)(2,1)S(1)} %collective-permute-done.25.refs_1_, ...), custom_call_target="tpu_custom_call" | custom-call | flops 1342177280 | bytes 5242880 | tf_op jit(solution)/shard_map/ffn_in/pallas_call | solution.py:333
  107.4 0.6 collective-permute-start.31
  107.9 1.9 %collective-permute-start.32 = (bf16[2,704,256]{2,1,0:T(8,128)(2,1)S(1)}, bf16[2,704,256]{2,1,0:T(8,128)(2,1)S(1)}, u32[]{:S(2)}, u32[]{:S(2)}) collective-permute-start(bf16[2,704,256]{2,1,0:T(8,128)(2,1)S(1)} %get-tuple-element.106), channel_id=1, source_target_pairs={{0,8},{4,12},{8,0},{12,4},{16,24},{20,28},{24,16},{28,20},{1,9},{5... | collective-permute-start | bytes 2162696 | tf_op jit(solution)/shard_map/ppermute | solution.py:121
  109.9 0.6 collective-permute-start.33
  110.9 14.0 %collective-permute-done.33.refs_4_ = bf16[2,576,256]{2,1,0:T(8,128)(2,1)S(1)} collective-permute-done((bf16[2,576,256]{2,1,0:T(8,128)(2,1)S(1)}, bf16[2,576,256]{2,1,0:T(8,128)(2,1)S(1)}, u32[]{:S(2)}, u32[]{:S(2)}) %collective-permute-start.33) | collective-permute-done | bytes 589856 | tf_op jit(solution)/shard_map/ppermute | solution.py:121
  124.9 1.3 collective-permute-done.32.refs_3_
  126.3 1.6 %collective-permute-done.34.other_in_ref = bf16[128,1280]{1,0:T(8,128)(2,1)S(1)} collective-permute-done((bf16[128,1280]{1,0:T(8,128)(2,1)S(1)}, bf16[128,1280]{1,0:T(8,128)(2,1)S(1)}, u32[]{:S(2)}, u32[]{:S(2)}) %collective-permute-start.34) | collective-permute-done | bytes 327712 | tf_op jit(solution)/shard_map/ppermute | solution.py:121
  127.9 1.7 %ffn_out.1 = (f32[256,256]{1,0:T(8,128)S(1)}, bf16[256,256]{1,0:T(8,128)(2,1)S(1)}, bf16[256,256]{1,0:T(8,128)(2,1)S(1)}, bf16[256,256]{1,0:T(8,128)(2,1)S(1)}) custom-call(s32[2]{0:T(128)S(1)} %pad_add_fusion.place_ref, bf16[128,1280]{1,0:T(8,128)(2,1)S(1)} %fusion.8.own_in_ref, bf16[128,1280]{1,0:T(8,128)(2,1)S(1)} %collective-permute-done.34.other_in_ref, ...), custom_call_target="tpu_custom_call" | custom-call | flops 671088640 | bytes 2621440 | tf_op jit(solution)/shard_map/ffn_out/pallas_call | solution.py:388
  129.6 1.7 %collective-permute-start.37 = (bf16[256,256]{1,0:T(8,128)(2,1)S(1)}, bf16[256,256]{1,0:T(8,128)(2,1)S(1)}, u32[]{:S(2)}, u32[]{:S(2)}) collective-permute-start(bf16[256,256]{1,0:T(8,128)(2,1)S(1)} %get-tuple-element.114), channel_id=1, source_target_pairs={{0,3},{1,0},{2,1},{3,2},{4,7},{5,4},{6,5},{7,6},{8,11},{9,8},{10,9... | collective-permute-start | bytes 393224 | tf_op jit(solution)/shard_map/ppermute | solution.py:121
  131.3 0.6 collective-permute-start.35
  131.9 3.7 %collective-permute-done.37 = bf16[256,256]{1,0:T(8,128)(2,1)S(1)} collective-permute-done((bf16[256,256]{1,0:T(8,128)(2,1)S(1)}, bf16[256,256]{1,0:T(8,128)(2,1)S(1)}, u32[]{:S(2)}, u32[]{:S(2)}) %collective-permute-start.37) | collective-permute-done | bytes 131104 | tf_op jit(solution)/shard_map/ppermute | solution.py:121
  135.7 7.4 %collective-permute-done.36 = bf16[256,256]{1,0:T(8,128)(2,1)S(1)} collective-permute-done((bf16[256,256]{1,0:T(8,128)(2,1)S(1)}, bf16[256,256]{1,0:T(8,128)(2,1)S(1)}, u32[]{:S(2)}, u32[]{:S(2)}) %collective-permute-start.36) | collective-permute-done | bytes 131104 | tf_op jit(solution)/shard_map/ppermute | solution.py:121
  143.2 1.2 collective-permute-done.38
  144.5 0.7 maximum_select_fusion
  (81 shorter events, 4.8 us)
Async XLA Ops:
  0.6 22.2 %collective-permute-start = (bf16[3,256,512]{2,1,0:T(8,128)(2,1)}, bf16[3,256,512]{2,1,0:T(8,128)(2,1)S(1)}, u32[]{:S(2)}, u32[]{:S(2)}) collective-permute-start(bf16[3,256,512]{2,1,0:T(8,128)(2,1)} %refs_0_.4), channel_id=1, source_target_pairs={{0,8},{4,12},{8,0},{12,4},{16,24},{20,28},{24,16},{28,20},{1,9},{5... | collective-permute-start | bytes 2359304 | tf_op jit(solution)/shard_map/ppermute | solution.py:121
  3.6 19.6 %collective-permute-start.1 = (bf16[3,256,512]{2,1,0:T(8,128)(2,1)}, bf16[3,256,512]{2,1,0:T(8,128)(2,1)S(1)}, u32[]{:S(2)}, u32[]{:S(2)}) collective-permute-start(bf16[3,256,512]{2,1,0:T(8,128)(2,1)} %refs_0_.4), channel_id=1, source_target_pairs={{0,16},{4,20},{8,24},{12,28},{16,0},{20,4},{24,8},{28,12},{1,17},{... | collective-permute-start | bytes 2359304 | tf_op jit(solution)/shard_map/ppermute | solution.py:121
  5.2 22.0 %copy-start.14 = (s32[255]{0:T(256)S(1)}, s32[255]{0:T(256)}, u32[]{:S(2)}) copy-start(s32[255]{0:T(256)} %param.13) | copy-start | bytes 3064
  5.2 22.0 %copy-start.11 = (s32[1024]{0:T(1024)S(1)}, s32[1024]{0:T(1024)}, u32[]{:S(2)}) copy-start(s32[1024]{0:T(1024)} %param.12) | copy-start | bytes 12292
  5.2 22.0 %copy-start.12 = (f32[32,8]{0,1:T(8,128)S(1)}, f32[32,8]{0,1:T(8,128)}, u32[]{:S(2)}) copy-start(f32[32,8]{0,1:T(8,128)} %param.16) | copy-start | bytes 3076
  6.1 4.3 %collective-permute-start.5 = (bf16[128,256]{1,0:T(8,128)(2,1)S(1)}, bf16[128,256]{1,0:T(8,128)(2,1)S(1)}, u32[]{:S(2)}, u32[]{:S(2)}) collective-permute-start(bf16[128,256]{1,0:T(8,128)(2,1)S(1)} %get-tuple-element.123), channel_id=1, source_target_pairs={{0,4},{4,0},{8,12},{12,8},{16,20},{20,16},{24,28},{28,24},{1,5},{5... | collective-permute-start | bytes 196616 | tf_op jit(solution)/shard_map/ppermute | solution.py:121
  6.2 8.5 %collective-permute-start.2 = (bf16[128,512]{1,0:T(8,128)(2,1)}, bf16[128,512]{1,0:T(8,128)(2,1)S(1)}, u32[]{:S(2)}, u32[]{:S(2)}) collective-permute-start(bf16[128,512]{1,0:T(8,128)(2,1)} %refs_0_.3), channel_id=1, source_target_pairs={{0,1},{1,2},{2,3},{3,0},{4,5},{5,6},{6,7},{7,4},{8,9},{9,10},{10,1... | collective-permute-start | bytes 393224 | tf_op jit(solution)/shard_map/ppermute | solution.py:121
  7.8 12.0 %collective-permute-start.3 = (bf16[128,512]{1,0:T(8,128)(2,1)}, bf16[128,512]{1,0:T(8,128)(2,1)S(1)}, u32[]{:S(2)}, u32[]{:S(2)}) collective-permute-start(bf16[128,512]{1,0:T(8,128)(2,1)} %refs_0_.3), channel_id=1, source_target_pairs={{0,2},{1,3},{2,0},{3,1},{4,6},{5,7},{6,4},{7,5},{8,10},{9,11},{10,... | collective-permute-start | bytes 393224 | tf_op jit(solution)/shard_map/ppermute | solution.py:121
  10.4 9.9 %collective-permute-start.4 = (bf16[128,512]{1,0:T(8,128)(2,1)}, bf16[128,512]{1,0:T(8,128)(2,1)S(1)}, u32[]{:S(2)}, u32[]{:S(2)}) collective-permute-start(bf16[128,512]{1,0:T(8,128)(2,1)} %refs_0_.3), channel_id=1, source_target_pairs={{0,3},{1,0},{2,1},{3,2},{4,7},{5,4},{6,5},{7,6},{8,11},{9,8},{10,9... | collective-permute-start | bytes 393224 | tf_op jit(solution)/shard_map/ppermute | solution.py:121
  14.6 13.2 %collective-permute-start.6 = (bf16[512,256]{1,0:T(8,128)(2,1)}, bf16[512,256]{1,0:T(8,128)(2,1)S(1)}, u32[]{:S(2)}, u32[]{:S(2)}) collective-permute-start(bf16[512,256]{1,0:T(8,128)(2,1)} %refs_0_.5), channel_id=1, source_target_pairs={{0,8},{4,12},{8,0},{12,4},{16,24},{20,28},{24,16},{28,20},{1,9},{5... | collective-permute-start | bytes 786440 | tf_op jit(solution)/shard_map/ppermute | solution.py:121
  19.8 9.0 %collective-permute-start.7 = (bf16[512,256]{1,0:T(8,128)(2,1)}, bf16[512,256]{1,0:T(8,128)(2,1)S(1)}, u32[]{:S(2)}, u32[]{:S(2)}) collective-permute-start(bf16[512,256]{1,0:T(8,128)(2,1)} %refs_0_.5), channel_id=1, source_target_pairs={{0,16},{4,20},{8,24},{12,28},{16,0},{20,4},{24,8},{28,12},{1,17},{... | collective-permute-start | bytes 786440 | tf_op jit(solution)/shard_map/ppermute | solution.py:121
  20.3 0.9 copy-start.5
  22.1 0.7 copy-start.7
  23.2 3.9 %copy-start.2 = (bf16[3,256,512]{2,1,0:T(8,128)(2,1)}, bf16[3,256,512]{2,1,0:T(8,128)(2,1)S(1)}, u32[]{:S(2)}) copy-start(bf16[3,256,512]{2,1,0:T(8,128)(2,1)S(1)} %collective-permute-done.1.high_in.refs_2_) | copy-start | bytes 2359300
  23.2 5.6 %collective-permute-start.8 = (bf16[4,128,256]{2,1,0:T(8,128)(2,1)S(1)}, bf16[4,128,256]{2,1,0:T(8,128)(2,1)S(1)}, u32[]{:S(2)}, u32[]{:S(2)}) collective-permute-start(bf16[4,128,256]{2,1,0:T(8,128)(2,1)S(1)} %get-tuple-element.63), channel_id=1, source_target_pairs={{0,4},{4,0},{8,12},{12,8},{16,20},{20,16},{24,28},{28,24},{1,5},{5... | collective-permute-start | bytes 786440 | tf_op jit(solution)/shard_map/ppermute | solution.py:121
  24.2 8.5 %copy-start.1 = (bf16[1280,256]{1,0:T(8,128)(2,1)S(1)}, bf16[1280,256]{1,0:T(8,128)(2,1)}, u32[]{:S(2)}) copy-start(bf16[1280,256]{1,0:T(8,128)(2,1)} %refs_0_.6) | copy-start | bytes 1966084
  24.2 17.5 %collective-permute-start.11 = (bf16[3,256,256]{2,1,0:T(8,128)(2,1)}, bf16[3,256,256]{2,1,0:T(8,128)(2,1)}, u32[]{:S(2)}, u32[]{:S(2)}) collective-permute-start(bf16[3,256,256]{2,1,0:T(8,128)(2,1)} %get-tuple-element.73), channel_id=1, source_target_pairs={{0,16},{4,20},{8,24},{12,28},{16,0},{20,4},{24,8},{28,12},{1,17},{... | collective-permute-start | bytes 1179656 | tf_op jit(solution)/shard_map/ppermute | solution.py:121
  26.6 15.1 %collective-permute-start.12 = (bf16[3,256,256]{2,1,0:T(8,128)(2,1)}, bf16[3,256,256]{2,1,0:T(8,128)(2,1)}, u32[]{:S(2)}, u32[]{:S(2)}) collective-permute-start(bf16[3,256,256]{2,1,0:T(8,128)(2,1)} %get-tuple-element.74), channel_id=1, source_target_pairs={{0,8},{4,12},{8,0},{12,4},{16,24},{20,28},{24,16},{28,20},{1,9},{5... | collective-permute-start | bytes 1179656 | tf_op jit(solution)/shard_map/ppermute | solution.py:121
  28.8 0.7 copy-start.9
  30.2 9.6 %collective-permute-start.9 = (bf16[256,256]{1,0:T(8,128)(2,1)}, bf16[256,256]{1,0:T(8,128)(2,1)}, u32[]{:S(2)}, u32[]{:S(2)}) collective-permute-start(bf16[256,256]{1,0:T(8,128)(2,1)} %get-tuple-element.66), channel_id=1, source_target_pairs={{0,16},{4,20},{8,24},{12,28},{16,0},{20,4},{24,8},{28,12},{1,17},{... | collective-permute-start | bytes 393224 | tf_op jit(solution)/shard_map/ppermute | solution.py:121
  31.5 10.2 %collective-permute-start.10 = (bf16[256,256]{1,0:T(8,128)(2,1)}, bf16[256,256]{1,0:T(8,128)(2,1)}, u32[]{:S(2)}, u32[]{:S(2)}) collective-permute-start(bf16[256,256]{1,0:T(8,128)(2,1)} %get-tuple-element.67), channel_id=1, source_target_pairs={{0,8},{4,12},{8,0},{12,4},{16,24},{20,28},{24,16},{28,20},{1,9},{5... | collective-permute-start | bytes 393224 | tf_op jit(solution)/shard_map/ppermute | solution.py:121
  32.7 9.0 %copy-start.3 = (bf16[3,256,512]{2,1,0:T(8,128)(2,1)S(1)}, bf16[3,256,512]{2,1,0:T(8,128)(2,1)}, u32[]{:S(2)}) copy-start(bf16[3,256,512]{2,1,0:T(8,128)(2,1)} %copy-done.2) | copy-start | bytes 2359300
  32.7 9.0 %copy-start.8 = (bf16[4,128,256]{2,1,0:T(8,128)(2,1)S(1)}, bf16[4,128,256]{2,1,0:T(8,128)(2,1)}, u32[]{:S(2)}) copy-start(bf16[4,128,256]{2,1,0:T(8,128)(2,1)} %copy-done.7) | copy-start | bytes 786436
  32.7 9.0 %copy-start.10 = (bf16[4,128,256]{2,1,0:T(8,128)(2,1)S(1)}, bf16[4,128,256]{2,1,0:T(8,128)(2,1)}, u32[]{:S(2)}) copy-start(bf16[4,128,256]{2,1,0:T(8,128)(2,1)} %copy-done.9) | copy-start | bytes 786436
  32.8 12.8 %copy-start = (bf16[2,256,1280]{2,1,0:T(8,128)(2,1)S(1)}, bf16[2,256,1280]{2,1,0:T(8,128)(2,1)}, u32[]{:S(2)}) copy-start(bf16[2,256,1280]{2,1,0:T(8,128)(2,1)} %refs_4_) | copy-start | bytes 3932164
  32.8 14.3 %collective-permute-start.15 = (bf16[576,256]{1,0:T(8,128)(2,1)S(1)}, bf16[576,256]{1,0:T(8,128)(2,1)S(1)}, u32[]{:S(2)}, u32[]{:S(2)}) collective-permute-start(bf16[576,256]{1,0:T(8,128)(2,1)S(1)} %slice.47), channel_id=1, source_target_pairs={{0,8},{4,12},{8,0},{12,4},{16,24},{20,28},{24,16},{28,20},{1,9},{5... | collective-permute-start | bytes 884744 | tf_op jit(solution)/shard_map/ppermute | solution.py:121
  39.8 10.9 %collective-permute-start.16 = (bf16[704,256]{1,0:T(8,128)(2,1)S(1)}, bf16[704,256]{1,0:T(8,128)(2,1)S(1)}, u32[]{:S(2)}, u32[]{:S(2)}) collective-permute-start(bf16[704,256]{1,0:T(8,128)(2,1)S(1)} %slice.48), channel_id=1, source_target_pairs={{0,16},{4,20},{8,24},{12,28},{16,0},{20,4},{24,8},{28,12},{1,17},{... | collective-permute-start | bytes 1081352 | tf_op jit(solution)/shard_map/ppermute | solution.py:121
  41.7 1.1 copy-start.4
  45.0 5.8 %collective-permute-start.13 = (f32[128,1024]{1,0:T(8,128)S(1)}, f32[128,1024]{1,0:T(8,128)S(1)}, u32[]{:S(2)}, u32[]{:S(2)}) collective-permute-start(f32[128,1024]{1,0:T(8,128)S(1)} %get-tuple-element.76), channel_id=1, source_target_pairs={{0,4},{4,0},{8,12},{12,8},{16,20},{20,16},{24,28},{28,24},{1,5},{5... | collective-permute-start | bytes 1572872 | tf_op jit(solution)/shard_map/ppermute | solution.py:121
  45.0 5.7 %collective-permute-start.14 = (f32[128,512]{1,0:T(8,128)S(1)}, f32[128,512]{1,0:T(8,128)S(1)}, u32[]{:S(2)}, u32[]{:S(2)}) collective-permute-start(f32[128,512]{1,0:T(8,128)S(1)} %get-tuple-element.77), channel_id=1, source_target_pairs={{0,4},{4,0},{8,12},{12,8},{16,20},{20,16},{24,28},{28,24},{1,5},{5... | collective-permute-start | bytes 786440 | tf_op jit(solution)/shard_map/ppermute | solution.py:121
  45.6 17.7 %collective-permute-start.19 = (bf16[256,1280]{1,0:T(8,128)(2,1)S(1)}, bf16[256,1280]{1,0:T(8,128)(2,1)S(1)}, u32[]{:S(2)}, u32[]{:S(2)}) collective-permute-start(bf16[256,1280]{1,0:T(8,128)(2,1)S(1)} %get-tuple-element.117), channel_id=1, source_target_pairs={{0,8},{4,12},{8,0},{12,4},{16,24},{20,28},{24,16},{28,20},{1,9},{5... | collective-permute-start | bytes 1966088 | tf_op jit(solution)/shard_map/ppermute | solution.py:121
  47.1 18.2 %collective-permute-start.20 = (bf16[256,1280]{1,0:T(8,128)(2,1)S(1)}, bf16[256,1280]{1,0:T(8,128)(2,1)S(1)}, u32[]{:S(2)}, u32[]{:S(2)}) collective-permute-start(bf16[256,1280]{1,0:T(8,128)(2,1)S(1)} %get-tuple-element.116), channel_id=1, source_target_pairs={{0,16},{4,20},{8,24},{12,28},{16,0},{20,4},{24,8},{28,12},{1,17},{... | collective-permute-start | bytes 1966088 | tf_op jit(solution)/shard_map/ppermute | solution.py:121
  50.8 14.6 %collective-permute-start.17 = (bf16[128,1024]{1,0:T(8,128)(2,1)S(1)}, bf16[128,1024]{1,0:T(8,128)(2,1)S(1)}, u32[]{:S(2)}, u32[]{:S(2)}) collective-permute-start(bf16[128,1024]{1,0:T(8,128)(2,1)S(1)} %add_convert_fusion.own_ref), channel_id=1, source_target_pairs={{0,4},{4,8},{8,12},{12,16},{16,20},{20,24},{24,28},{1,5},{5,9},{9,... | collective-permute-start | bytes 786440 | tf_op jit(solution)/shard_map/ppermute | solution.py:479
  52.1 13.3 %collective-permute-start.18 = (bf16[128,1024]{1,0:T(8,128)(2,1)S(1)}, bf16[128,1024]{1,0:T(8,128)(2,1)S(1)}, u32[]{:S(2)}, u32[]{:S(2)}) collective-permute-start(bf16[128,1024]{1,0:T(8,128)(2,1)S(1)} %add_convert_fusion.own_ref), channel_id=1, source_target_pairs={{4,0},{8,4},{12,8},{16,12},{20,16},{24,20},{28,24},{5,1},{9,5},{13... | collective-permute-start | bytes 786440 | tf_op jit(solution)/shard_map/ppermute | solution.py:480
  65.5 39.3 %collective-permute-start.28 = (bf16[2,256,1280]{2,1,0:T(8,128)(2,1)S(1)}, bf16[2,256,1280]{2,1,0:T(8,128)(2,1)S(1)}, u32[]{:S(2)}, u32[]{:S(2)}) collective-permute-start(bf16[2,256,1280]{2,1,0:T(8,128)(2,1)S(1)} %get-tuple-element.100), channel_id=1, source_target_pairs={{0,8},{4,12},{8,0},{12,4},{16,24},{20,28},{24,16},{28,20},{1,9},{5... | collective-permute-start | bytes 3932168 | tf_op jit(solution)/shard_map/ppermute | solution.py:121
  67.8 37.1 %collective-permute-start.29 = (bf16[2,256,1280]{2,1,0:T(8,128)(2,1)S(1)}, bf16[2,256,1280]{2,1,0:T(8,128)(2,1)S(1)}, u32[]{:S(2)}, u32[]{:S(2)}) collective-permute-start(bf16[2,256,1280]{2,1,0:T(8,128)(2,1)S(1)} %get-tuple-element.101), channel_id=1, source_target_pairs={{0,16},{4,20},{8,24},{12,28},{16,0},{20,4},{24,8},{28,12},{1,17},{... | collective-permute-start | bytes 3932168 | tf_op jit(solution)/shard_map/ppermute | solution.py:121
  69.0 4.1 %copy-start.6 = (bf16[512,256]{1,0:T(8,128)(2,1)S(1)}, bf16[512,256]{1,0:T(8,128)(2,1)}, u32[]{:S(2)}) copy-start(bf16[512,256]{1,0:T(8,128)(2,1)} %refs_0_.5) | copy-start | bytes 786436
  71.6 18.3 %copy-start.13 = (bf16[256,256]{1,0:T(8,128)(2,1)S(1)}, bf16[256,256]{1,0:T(8,128)(2,1)}, u32[]{:S(2)}) copy-start(bf16[256,256]{1,0:T(8,128)(2,1)} %pad_maximum_fusion.1) | copy-start | bytes 393220
  71.6 1.4 collective-permute-start.21
  74.6 7.3 %collective-permute-start.24 = (bf16[256,256]{1,0:T(8,128)(2,1)S(1)}, bf16[256,256]{1,0:T(8,128)(2,1)S(1)}, u32[]{:S(2)}, u32[]{:S(2)}) collective-permute-start(bf16[256,256]{1,0:T(8,128)(2,1)S(1)} %get-tuple-element.96), channel_id=1, source_target_pairs={{0,3},{1,0},{2,1},{3,2},{4,7},{5,4},{6,5},{7,6},{8,11},{9,8},{10,9... | collective-permute-start | bytes 393224 | tf_op jit(solution)/shard_map/ppermute | solution.py:121
  77.9 12.0 %collective-permute-start.23 = (bf16[256,256]{1,0:T(8,128)(2,1)S(1)}, bf16[256,256]{1,0:T(8,128)(2,1)S(1)}, u32[]{:S(2)}, u32[]{:S(2)}) collective-permute-start(bf16[256,256]{1,0:T(8,128)(2,1)S(1)} %get-tuple-element.95), channel_id=1, source_target_pairs={{0,2},{1,3},{2,0},{3,1},{4,6},{5,7},{6,4},{7,5},{8,10},{9,11},{10,... | collective-permute-start | bytes 393224 | tf_op jit(solution)/shard_map/ppermute | solution.py:121
  78.0 12.0 %collective-permute-start.22 = (bf16[256,256]{1,0:T(8,128)(2,1)S(1)}, bf16[256,256]{1,0:T(8,128)(2,1)S(1)}, u32[]{:S(2)}, u32[]{:S(2)}) collective-permute-start(bf16[256,256]{1,0:T(8,128)(2,1)S(1)} %get-tuple-element.94), channel_id=1, source_target_pairs={{0,1},{1,2},{2,3},{3,0},{4,5},{5,6},{6,7},{7,4},{8,9},{9,10},{10,1... | collective-permute-start | bytes 393224 | tf_op jit(solution)/shard_map/ppermute | solution.py:121
  90.0 5.1 %collective-permute-start.27 = (bf16[256,256]{1,0:T(8,128)(2,1)S(1)}, bf16[256,256]{1,0:T(8,128)(2,1)S(1)}, u32[]{:S(2)}, u32[]{:S(2)}) collective-permute-start(bf16[256,256]{1,0:T(8,128)(2,1)S(1)} %add_convert_fusion.1.refs_0_), channel_id=1, source_target_pairs={{0,3},{1,0},{2,1},{3,2},{4,7},{5,4},{6,5},{7,6},{8,11},{9,8},{10,9... | collective-permute-start | bytes 393224 | tf_op jit(solution)/shard_map/ppermute | solution.py:121
  91.2 10.4 %collective-permute-start.25 = (bf16[256,256]{1,0:T(8,128)(2,1)S(1)}, bf16[256,256]{1,0:T(8,128)(2,1)S(1)}, u32[]{:S(2)}, u32[]{:S(2)}) collective-permute-start(bf16[256,256]{1,0:T(8,128)(2,1)S(1)} %add_convert_fusion.1.refs_0_), channel_id=1, source_target_pairs={{0,1},{1,2},{2,3},{3,0},{4,5},{5,6},{6,7},{7,4},{8,9},{9,10},{10,1... | collective-permute-start | bytes 393224 | tf_op jit(solution)/shard_map/ppermute | solution.py:121
  92.1 12.7 %collective-permute-start.26 = (bf16[256,256]{1,0:T(8,128)(2,1)S(1)}, bf16[256,256]{1,0:T(8,128)(2,1)S(1)}, u32[]{:S(2)}, u32[]{:S(2)}) collective-permute-start(bf16[256,256]{1,0:T(8,128)(2,1)S(1)} %add_convert_fusion.1.refs_0_), channel_id=1, source_target_pairs={{0,2},{1,3},{2,0},{3,1},{4,6},{5,7},{6,4},{7,5},{8,10},{9,11},{10,... | collective-permute-start | bytes 393224 | tf_op jit(solution)/shard_map/ppermute | solution.py:121
  107.0 3.4 %collective-permute-start.30 = (bf16[128,2560]{1,0:T(8,128)(2,1)S(1)}, bf16[128,2560]{1,0:T(8,128)(2,1)S(1)}, u32[]{:S(2)}, u32[]{:S(2)}) collective-permute-start(bf16[128,2560]{1,0:T(8,128)(2,1)S(1)} %get-tuple-element.103), channel_id=1, source_target_pairs={{0,4},{4,0},{8,12},{12,8},{16,20},{20,16},{24,28},{28,24},{1,5},{5... | collective-permute-start | bytes 1966088 | tf_op jit(solution)/shard_map/ppermute | solution.py:121
  107.4 3.1 %collective-permute-start.31 = (f32[128]{0:T(128)S(1)}, f32[128]{0:T(128)S(1)}, u32[]{:S(2)}, u32[]{:S(2)}) collective-permute-start(f32[128]{0:T(128)S(1)} %slice.54), channel_id=1, source_target_pairs={{0,4},{4,0},{8,12},{12,8},{16,20},{20,16},{24,28},{28,24},{1,5},{5... | collective-permute-start | bytes 1544 | tf_op jit(solution)/shard_map/ppermute | solution.py:121
  107.9 18.3 %collective-permute-start.32 = (bf16[2,704,256]{2,1,0:T(8,128)(2,1)S(1)}, bf16[2,704,256]{2,1,0:T(8,128)(2,1)S(1)}, u32[]{:S(2)}, u32[]{:S(2)}) collective-permute-start(bf16[2,704,256]{2,1,0:T(8,128)(2,1)S(1)} %get-tuple-element.106), channel_id=1, source_target_pairs={{0,8},{4,12},{8,0},{12,4},{16,24},{20,28},{24,16},{28,20},{1,9},{5... | collective-permute-start | bytes 2162696 | tf_op jit(solution)/shard_map/ppermute | solution.py:121
  109.9 15.0 %collective-permute-start.33 = (bf16[2,576,256]{2,1,0:T(8,128)(2,1)S(1)}, bf16[2,576,256]{2,1,0:T(8,128)(2,1)S(1)}, u32[]{:S(2)}, u32[]{:S(2)}) collective-permute-start(bf16[2,576,256]{2,1,0:T(8,128)(2,1)S(1)} %get-tuple-element.107), channel_id=1, source_target_pairs={{0,16},{4,20},{8,24},{12,28},{16,0},{20,4},{24,8},{28,12},{1,17},{... | collective-permute-start | bytes 1769480 | tf_op jit(solution)/shard_map/ppermute | solution.py:121
  126.3 1.6 %collective-permute-start.34 = (bf16[128,1280]{1,0:T(8,128)(2,1)S(1)}, bf16[128,1280]{1,0:T(8,128)(2,1)S(1)}, u32[]{:S(2)}, u32[]{:S(2)}) collective-permute-start(bf16[128,1280]{1,0:T(8,128)(2,1)S(1)} %fusion.8.own_in_ref), channel_id=1, source_target_pairs={{0,4},{4,0},{8,12},{12,8},{16,20},{20,16},{24,28},{28,24},{1,5},{5... | collective-permute-start | bytes 983048 | tf_op jit(solution)/shard_map/ppermute | solution.py:121
  129.6 6.1 %collective-permute-start.37 = (bf16[256,256]{1,0:T(8,128)(2,1)S(1)}, bf16[256,256]{1,0:T(8,128)(2,1)S(1)}, u32[]{:S(2)}, u32[]{:S(2)}) collective-permute-start(bf16[256,256]{1,0:T(8,128)(2,1)S(1)} %get-tuple-element.114), channel_id=1, source_target_pairs={{0,3},{1,0},{2,1},{3,2},{4,7},{5,4},{6,5},{7,6},{8,11},{9,8},{10,9... | collective-permute-start | bytes 393224 | tf_op jit(solution)/shard_map/ppermute | solution.py:121
  131.3 11.8 %collective-permute-start.36 = (bf16[256,256]{1,0:T(8,128)(2,1)S(1)}, bf16[256,256]{1,0:T(8,128)(2,1)S(1)}, u32[]{:S(2)}, u32[]{:S(2)}) collective-permute-start(bf16[256,256]{1,0:T(8,128)(2,1)S(1)} %get-tuple-element.113), channel_id=1, source_target_pairs={{0,2},{1,3},{2,0},{3,1},{4,6},{5,7},{6,4},{7,5},{8,10},{9,11},{10,... | collective-permute-start | bytes 393224 | tf_op jit(solution)/shard_map/ppermute | solution.py:121
  131.3 11.8 %collective-permute-start.35 = (bf16[256,256]{1,0:T(8,128)(2,1)S(1)}, bf16[256,256]{1,0:T(8,128)(2,1)S(1)}, u32[]{:S(2)}, u32[]{:S(2)}) collective-permute-start(bf16[256,256]{1,0:T(8,128)(2,1)S(1)} %get-tuple-element.112), channel_id=1, source_target_pairs={{0,1},{1,2},{2,3},{3,0},{4,5},{5,6},{6,7},{7,4},{8,9},{9,10},{10,1... | collective-permute-start | bytes 393224 | tf_op jit(solution)/shard_map/ppermute | solution.py:121
  143.2 1.3 collective-permute-start.38
